TPU v7x, 256 devices: a whole 4x4x8 slice. The times are simulated.
256 devices in a mesh: rhombus: 8 (over z), tile: 32 (over y, x, core).
Axes of the slice: x: 4, y: 4, z: 8, core: 2. Of those that a mesh axis runs over, the one named last changes fastest.
Arguments:
- fine_latent: bfloat16 [131072, 512], P(('rhombus', 'tile')), may hold values from -6 to 6
- mid_latent: bfloat16 [8192, 512], P(('rhombus', 'tile')), may hold values from -6 to 6
- coarse_latent: bfloat16 [642, 512], replicated, may hold values from -6 to 6
- fine_parent: int32 [131072], P(('rhombus', 'tile')), may hold values from 0 to 95, as said below
- mid_parent: int32 [8192], P(('rhombus', 'tile')), may hold values from 0 to 641
- halo_rows: int32 [65536], P(('rhombus', 'tile')), may hold values from 0 to 511
- edge_source: int32 [786432], P(('rhombus', 'tile')), may hold values from 0 to 767
- edge_target: int32 [786432], P(('rhombus', 'tile')), may hold values from 0 to 512, as said below
- w_child: bfloat16 [512, 512], replicated, may hold values from -1 to 1
- mid_w1: bfloat16 [512, 512], replicated, may hold values from -0.25 to 0.25
- mid_w2: bfloat16 [512, 512], replicated, may hold values from -0.5 to 0.5
- mid_w3: bfloat16 [512, 512], replicated, may hold values from -0.25 to 0.25
- w_coarse: bfloat16 [512, 512], replicated, may hold values from -1 to 1
- coarse_w1: bfloat16 [512, 512], replicated, may hold values from -0.25 to 0.25
- coarse_w2: bfloat16 [512, 512], replicated, may hold values from -0.5 to 0.5
- coarse_w3: bfloat16 [512, 512], replicated, may hold values from -0.25 to 0.25
- w_descend: bfloat16 [512, 512], replicated, may hold values from -0.25 to 0.25
- w_fine: bfloat16 [512, 512], replicated, may hold values from -0.25 to 0.25
- edge_w_src: bfloat16 [512, 512], replicated, may hold values from -1 to 1
- edge_w_dst: bfloat16 [512, 512], replicated, may hold values from -0.25 to 0.25
- edge_w2: bfloat16 [512, 512], replicated, may hold values from -0.25 to 0.25
- node_w1: bfloat16 [512, 512], replicated, may hold values from -0.25 to 0.25
- node_w2: bfloat16 [512, 512], replicated, may hold values from -0.125 to 0.125
- node_w3: bfloat16 [512, 512], replicated, may hold values from -0.25 to 0.25
Outputs:
- fine_out: bfloat16 [131072, 512], P(('rhombus', 'tile'))
- mid_out: bfloat16 [8192, 512], P(('rhombus', 'tile'))
- coarse_out: bfloat16 [642, 512], replicated
Inputs may be any that keep to these rules, and one draw needn't show every extreme that they name: `fine_parent`: in tile t of a group, an entry p < 32 names a middle slot of the same tile, 32 <= p < 64 a slot of tile t - 1, 64 <= p a slot of tile t + 1; tile 0 never names the tile before and the last tile of a group never names the tile after. `edge_target`: in each tile the live slots come first and name a fine row of that tile; the remaining slots hold 512. Each tile has at least 1536 live slots, and some tile has all 3072 slots live.
All inputs are finite; a program needn't handle non-finite values.
Results may differ from a plain program's by a relative error of at most 0.013.
Values may be sent and summed in bfloat16 or wider, within the bound.
No kernel may reach another device: no remote copies, remote signals or barrier semaphores. Data moves between devices by JAX's collectives and lax.ppermute only.
A program may use at most 64 MiB of HBM per device.

v0:
```python
import jax
import jax.numpy as jnp
from jax import lax
from jax.sharding import PartitionSpec as P

EPSILON = 1e-05


def extended_2(shard, sides, width):
    for axis, dim in sides:
        size, length = (lax.axis_size(axis), shard.shape[dim])
        up = [(i, (i + 1) % size) for i in range(size - 1)]
        down = [(j, i) for i, j in up]
        last = lax.slice_in_dim(shard, length - width, length, axis=dim)
        leading = lax.slice_in_dim(shard, 0, width, axis=dim)
        before = lax.ppermute(last, axis, up)
        after = lax.ppermute(leading, axis, down)
        shard = jnp.concatenate([before, shard, after], axis=dim)
    return shard


def product(left, right):
    return jnp.dot(left, right, preferred_element_type=jnp.float32)


def normed(values):
    return values / jnp.sqrt(jnp.mean(values * values, axis=-1, keepdims=True) + EPSILON)


def node_update(latent, incoming, first, second, third):
    hidden = jax.nn.silu(product(latent, first) + product(incoming, second)).astype(jnp.bfloat16)
    return (latent.astype(jnp.float32) + normed(product(hidden, third))).astype(jnp.bfloat16)


def coarse_update(latent, incoming, coarse_w1, coarse_w2, coarse_w3, w_descend):
    updated = node_update(latent, incoming.astype(jnp.bfloat16), coarse_w1, coarse_w2, coarse_w3)
    return (updated, product(updated, w_descend).astype(jnp.bfloat16))


def selector_rows(row_ids, width):
    columns = lax.broadcasted_iota(jnp.int32, (row_ids.shape[0], width), 1)
    return (columns == row_ids[:, None]).astype(jnp.bfloat16)


def edge_update(
    node_table, lifted, source, target, edge_w_src, edge_w_dst, edge_w2, node_w1, node_w2, node_w3
):
    fine_count = lifted.shape[0]
    sender = product(node_table, edge_w_src).astype(jnp.bfloat16)
    receiver = product(lifted, edge_w_dst).astype(jnp.bfloat16)
    source_pick = selector_rows(source, node_table.shape[0])
    target_pick = selector_rows(target, fine_count)
    edge_sum = product(source_pick, sender) + product(target_pick, receiver)
    edge_hidden = jax.nn.silu(edge_sum).astype(jnp.bfloat16)
    hidden_sums = lax.dot_general(
        target_pick, edge_hidden, (((0,), (0,)), ((), ())), preferred_element_type=jnp.float32
    )
    aggregate = jnp.dot(hidden_sums, edge_w2.astype(jnp.float32), precision=lax.Precision.HIGHEST)
    return node_update(lifted, aggregate.astype(jnp.bfloat16), node_w1, node_w2, node_w3)


def on_device(
    fine_latent,
    mid_latent,
    coarse_latent,
    fine_parent,
    mid_parent,
    halo_rows,
    edge_source,
    edge_target,
    w_child,
    mid_w1,
    mid_w2,
    mid_w3,
    w_coarse,
    coarse_w1,
    coarse_w2,
    coarse_w3,
    w_descend,
    w_fine,
    edge_w_src,
    edge_w_dst,
    edge_w2,
    node_w1,
    node_w2,
    node_w3,
):
    fine_count = fine_latent.shape[0]
    mid_count = mid_latent.shape[0]
    coarse_count = coarse_latent.shape[0]
    rim_count = halo_rows.shape[0] // 2
    child_msg = product(fine_latent, w_child).astype(jnp.bfloat16)
    slot_ids = lax.broadcasted_iota(jnp.int32, (3 * mid_count, fine_count), 0)
    picker = (slot_ids == fine_parent[None, :]).astype(jnp.bfloat16)
    partial_sums = product(picker, child_msg)
    extended = extended_2(partial_sums[mid_count:], (("tile", 0),), mid_count)
    mid_in = partial_sums[:mid_count] + extended[:mid_count] + extended[3 * mid_count :]
    mid_up = node_update(mid_latent, mid_in.astype(jnp.bfloat16), mid_w1, mid_w2, mid_w3)
    mid_msg = product(mid_up, w_coarse).astype(jnp.bfloat16)
    coarse_ids = lax.broadcasted_iota(jnp.int32, (coarse_count, mid_count), 0)
    selector = (coarse_ids == mid_parent[None, :]).astype(jnp.bfloat16)
    coarse_in = lax.psum(product(selector, mid_msg), ("rhombus", "tile"))
    coarse_out, down_coarse = coarse_update(
        coarse_latent, coarse_in, coarse_w1, coarse_w2, coarse_w3, w_descend
    )
    lookup = selector_rows(mid_parent, coarse_count)
    mid_out = (mid_up.astype(jnp.float32) + product(lookup, down_coarse)).astype(jnp.bfloat16)
    fine_down = product(mid_out, w_fine).astype(jnp.bfloat16)
    nearby = extended_2(fine_down, (("tile", 0),), mid_count)
    remapped = jnp.where(
        fine_parent < mid_count,
        fine_parent + mid_count,
        jnp.where(fine_parent < 2 * mid_count, fine_parent - mid_count, fine_parent),
    )
    parent_pick = selector_rows(remapped, 3 * mid_count)
    lifted = (fine_latent.astype(jnp.float32) + product(parent_pick, nearby)).astype(jnp.bfloat16)
    boundary = product(selector_rows(halo_rows, fine_count), lifted).astype(jnp.bfloat16)
    bordered = extended_2(boundary, (("tile", 0),), rim_count)
    node_table = jnp.concatenate([lifted, bordered[:rim_count], bordered[3 * rim_count :]], axis=0)
    fine_out = edge_update(
        node_table,
        lifted,
        edge_source,
        edge_target,
        edge_w_src,
        edge_w_dst,
        edge_w2,
        node_w1,
        node_w2,
        node_w3,
    )
    return (fine_out, mid_out, coarse_out)


def solution(mesh):
    placed = (
        P(("rhombus", "tile"), None),
        P(("rhombus", "tile"), None),
        P(),
        P(("rhombus", "tile")),
        P(("rhombus", "tile")),
        P(("rhombus", "tile")),
        P(("rhombus", "tile")),
        P(("rhombus", "tile")),
        P(),
        P(),
        P(),
        P(),
        P(),
        P(),
        P(),
        P(),
        P(),
        P(),
        P(),
        P(),
        P(),
        P(),
        P(),
        P(),
    )
    return jax.shard_map(
        on_device,
        mesh=mesh,
        in_specs=placed,
        out_specs=(P(("rhombus", "tile"), None), P(("rhombus", "tile"), None), P()),
        check_vma=False,
    )
```

profile of v0, /device:TPU:1, one launch (start us, length us, event | category | flops | bytes accessed | tf_op | source)
XLA Modules:
  0.0 144.4 jit_solution(7383957612705457493)
XLA Ops:
  0.6 0.0 copy-start
  0.7 1.9 %fusion.9 = f32[96,512]{1,0:T(8,128)S(1)} fusion(bf16[512,512]{1,0:T(8,128)(2,1)} %param.24, bf16[512,512]{1,0:T(8,128)(2,1)} %param.32, s32[512]{0:T(512)} %param.27), kind=kOutput, calls=%fused_computation.23 | convolution fusion | flops 319078400 | bytes 1247232 | tf_op jit(solution)/shard_map/dot_general | solution.py:23
  2.6 0.0 copy-start.6
  2.7 4.6 %collective-permute-start = (f32[32,512]{1,0:T(8,128)S(1)}, f32[32,512]{1,0:T(8,128)S(1)}, u32[]{:S(2)}, u32[]{:S(2)}) collective-permute-start(f32[32,512]{1,0:T(8,128)S(1)} %get-tuple-element.5), channel_id=1, source_target_pairs={{0,1},{1,2},{2,3},{3,4},{4,5},{5,6},{6,7},{7,8},{8,9},{9,10},{10,1... | collective-permute-start | bytes 196616 | tf_op jit(solution)/shard_map/ppermute | solution.py:16
  7.3 1.9 %collective-permute-start.1 = (f32[32,512]{1,0:T(8,128)S(1)}, f32[32,512]{1,0:T(8,128)S(1)}, u32[]{:S(2)}, u32[]{:S(2)}) collective-permute-start(f32[32,512]{1,0:T(8,128)S(1)} %get-tuple-element.6), channel_id=1, source_target_pairs={{1,0},{2,1},{3,2},{4,3},{5,4},{6,5},{7,6},{8,7},{9,8},{10,9},{11,1... | collective-permute-start | bytes 196616 | tf_op jit(solution)/shard_map/ppermute | solution.py:17
  9.3 1.6 %fusion.51 = f32[642,512]{1,0:T(8,128)} fusion(bf16[642,512]{1,0:T(8,128)(2,1)S(1)} %copy-done.1, bf16[512,512]{1,0:T(8,128)(2,1)S(1)} %copy-done.3), kind=kOutput, calls=%fused_computation.80 | convolution fusion | flops 336592896 | bytes 2496512 | tf_op jit(solution)/shard_map/dot_general | solution.py:23
  10.9 0.2 fusion.50
  11.1 1.8 %collective-permute-done.1 = f32[32,512]{1,0:T(8,128)S(1)} collective-permute-done((f32[32,512]{1,0:T(8,128)S(1)}, f32[32,512]{1,0:T(8,128)S(1)}, u32[]{:S(2)}, u32[]{:S(2)}) %collective-permute-start.1) | collective-permute-done | bytes 65568 | tf_op jit(solution)/shard_map/ppermute | solution.py:17
  12.9 0.5 multiply_reduce_fusion.2
  13.4 0.1 add_convert_fusion.2
  13.5 0.5 fusion.12
  14.0 88.7 %all-reduce.1 = bf16[642,512]{1,0:T(8,128)(2,1)S(1)} all-reduce(f32[642,512]{1,0:T(8,128)S(1)} %fusion.12), channel_id=1, replica_groups=mesh['rhombus'=8,'tile'=32] {'rhombus','tile'}, use_global_device_ids=true, to_apply=%region_1.2 | all-reduce | flops 328704 | bytes 1972224 | tf_op jit(solution)/shard_map/psum | solution.py:102
  102.7 2.8 %multiply_reduce_fusion = (f32[642]{0:T(1024)S(1)}, f32[642,512]{1,0:T(8,128)S(1)}) fusion(bf16[512,512]{1,0:T(8,128)(2,1)} %param.39, f32[642,512]{1,0:T(8,128)} %fusion.51, bf16[512,512]{1,0:T(8,128)(2,1)} %param.38, bf16[642,512]{1,0:T(8,128)(2,1)S(1)} %all-reduce.1), kind=kOutput, calls=%fused_computation.15 | convolution fusion | flops 675814784 | bytes 4338184 | tf_op jit(solution)/shard_map/dot_general | solution.py:23
  105.5 0.3 add_convert_fusion
  105.8 2.0 %fusion.11 = bf16[32,512]{1,0:T(8,128)(2,1)S(1)} fusion(bf16[642,512]{1,0:T(8,128)(2,1)S(1)} %add_convert_fusion, bf16[512,512]{1,0:T(8,128)(2,1)} %param.40, bf16[32,512]{1,0:T(8,128)(2,1)S(1)} %add_convert_fusion.2, s32[32]{0:T(128)S(1)} %copy-done.14), kind=kOutput, calls=%fused_computation.27 | convolution fusion | flops 358028352 | bytes 1247360 | tf_op jit(solution)/shard_map/dot_general | solution.py:23
  107.8 0.2 convolution_convert_fusion.6
  108.0 1.9 %collective-permute-start.2 = (bf16[32,512]{1,0:T(8,128)(2,1)S(1)}, bf16[32,512]{1,0:T(8,128)(2,1)S(1)}, u32[]{:S(2)}, u32[]{:S(2)}) collective-permute-start(bf16[32,512]{1,0:T(8,128)(2,1)S(1)} %convolution_convert_fusion.6), channel_id=1, source_target_pairs={{0,1},{1,2},{2,3},{3,4},{4,5},{5,6},{6,7},{7,8},{8,9},{9,10},{10,1... | collective-permute-start | bytes 98312 | tf_op jit(solution)/shard_map/ppermute | solution.py:16
  109.9 2.4 %collective-permute-start.3 = (bf16[32,512]{1,0:T(8,128)(2,1)S(1)}, bf16[32,512]{1,0:T(8,128)(2,1)S(1)}, u32[]{:S(2)}, u32[]{:S(2)}) collective-permute-start(bf16[32,512]{1,0:T(8,128)(2,1)S(1)} %convolution_convert_fusion.6), channel_id=1, source_target_pairs={{1,0},{2,1},{3,2},{4,3},{5,4},{6,5},{7,6},{8,7},{9,8},{10,9},{11,1... | collective-permute-start | bytes 98312 | tf_op jit(solution)/shard_map/ppermute | solution.py:17
  112.4 2.8 %collective-permute-done.3 = bf16[32,512]{1,0:T(8,128)(2,1)S(1)} collective-permute-done((bf16[32,512]{1,0:T(8,128)(2,1)S(1)}, bf16[32,512]{1,0:T(8,128)(2,1)S(1)}, u32[]{:S(2)}, u32[]{:S(2)}) %collective-permute-start.3) | collective-permute-done | bytes 32800 | tf_op jit(solution)/shard_map/ppermute | solution.py:17
  115.2 0.3 fusion.6
  115.5 0.3 convolution_convert_fusion.5
  115.9 1.9 %collective-permute-start.4 = (bf16[128,512]{1,0:T(8,128)(2,1)S(1)}, bf16[128,512]{1,0:T(8,128)(2,1)}, u32[]{:S(2)}, u32[]{:S(2)}) collective-permute-start(bf16[128,512]{1,0:T(8,128)(2,1)S(1)} %get-tuple-element.3), channel_id=1, source_target_pairs={{0,1},{1,2},{2,3},{3,4},{4,5},{5,6},{6,7},{7,8},{8,9},{9,10},{10,1... | collective-permute-start | bytes 393224 | tf_op jit(solution)/shard_map/ppermute | solution.py:16
  117.9 3.3 %collective-permute-start.5 = (bf16[128,512]{1,0:T(8,128)(2,1)S(1)}, bf16[128,512]{1,0:T(8,128)(2,1)}, u32[]{:S(2)}, u32[]{:S(2)}) collective-permute-start(bf16[128,512]{1,0:T(8,128)(2,1)S(1)} %get-tuple-element.4), channel_id=1, source_target_pairs={{1,0},{2,1},{3,2},{4,3},{5,4},{6,5},{7,6},{8,7},{9,8},{10,9},{11,1... | collective-permute-start | bytes 393224 | tf_op jit(solution)/shard_map/ppermute | solution.py:17
  121.2 4.8 %fusion.2 = f32[3072,512]{1,0:T(8,128)} fusion(s32[3072]{0:T(1024)S(1)} %copy-done.16, bf16[512,512]{1,0:T(8,128)(2,1)S(1)} %fusion.6, bf16[512,512]{1,0:T(8,128)(2,1)S(1)} %copy-done), kind=kOutput, calls=%fused_computation.5 | convolution fusion | flops 1880883200 | bytes 7352320 | tf_op jit(solution)/shard_map/dot_general | solution.py:23
  126.0 0.4 fusion.52
  126.5 0.6 copy-done.15
  127.1 2.4 %convolution_convert_fusion = bf16[768,512]{1,0:T(8,128)(2,1)} fusion(bf16[512,512]{1,0:T(8,128)(2,1)S(1)} %copy-done.15, bf16[128,512]{1,0:T(8,128)(2,1)} %collective-permute-done.5, bf16[128,512]{1,0:T(8,128)(2,1)} %collective-permute-done.4, bf16[512,512]{1,0:T(8,128)(2,1)S(1)} %fusion.6), kind=kOutput, calls=%fused_computation.10 | convolution fusion | flops 405405696 | bytes 2097152 | tf_op jit(solution)/shard_map/dot_general | solution.py:23
  129.5 8.3 %fusion.1 = f32[512,512]{1,0:T(8,128)S(1)} fusion(s32[3072]{0:T(1024)S(1)} %copy-done.16, f32[3072,512]{1,0:T(8,128)} %fusion.2, bf16[768,512]{1,0:T(8,128)(2,1)} %convolution_convert_fusion, s32[3072]{0:T(1024)S(1)} %copy-done.17), kind=kOutput, calls=%fused_computation.4 | convolution fusion | flops 4039901184 | bytes 8151040 | tf_op jit(solution)/shard_map/dot_general | solution.py:55
  137.8 2.8 %convolution_convert_fusion.4 = bf16[512,512]{1,0:T(8,128)(2,1)} fusion(f32[512,512]{1,0:T(8,128)S(1)} %fusion.1, bf16[512,512]{1,0:T(8,128)(2,1)} %param.44), kind=kOutput, calls=%fused_computation.20 | convolution fusion | flops 1610874880 | bytes 2097152 | tf_op jit(solution)/shard_map/dot_general | solution.py:58
  140.7 2.4 %multiply_reduce_fusion.1 = (f32[512]{0:T(512)S(1)}, f32[512,512]{0,1:T(8,128)S(1)}) fusion(bf16[512,512]{1,0:T(8,128)(2,1)} %param.47, f32[512,512]{1,0:T(8,128)S(1)} %fusion.52, bf16[512,512]{1,0:T(8,128)(2,1)} %convolution_convert_fusion.4, bf16[512,512]{1,0:T(8,128)(2,1)} %param.46), kind=kOutput, calls=%fused_computation.32 | convolution fusion | flops 538967552 | bytes 3672064 | tf_op jit(solution)/shard_map/dot_general | solution.py:23
  143.0 0.3 copy.27
  143.4 1.0 add_convert_fusion.1
  (45 shorter events, 0.2 us)
Async XLA Ops:
  0.6 120.6 %copy-start = (bf16[512,512]{1,0:T(8,128)(2,1)S(1)}, bf16[512,512]{1,0:T(8,128)(2,1)}, u32[]{:S(2)}) copy-start(bf16[512,512]{1,0:T(8,128)(2,1)} %param.43) | copy-start | bytes 1572868
  0.6 8.6 %copy-start.1 = (bf16[642,512]{1,0:T(8,128)(2,1)S(1)}, bf16[642,512]{1,0:T(8,128)(2,1)}, u32[]{:S(2)}) copy-start(bf16[642,512]{1,0:T(8,128)(2,1)} %param.26) | copy-start | bytes 1972228
  0.7 8.6 %copy-start.3 = (bf16[512,512]{1,0:T(8,128)(2,1)S(1)}, bf16[512,512]{1,0:T(8,128)(2,1)}, u32[]{:S(2)}) copy-start(bf16[512,512]{1,0:T(8,128)(2,1)} %param.37) | copy-start | bytes 1572868
  2.6 8.3 %copy-start.6 = (bf16[512,512]{1,0:T(8,128)(2,1)S(1)}, bf16[512,512]{1,0:T(8,128)(2,1)}, u32[]{:S(2)}) copy-start(bf16[512,512]{1,0:T(8,128)(2,1)} %param.33) | copy-start | bytes 1572868
  2.6 8.3 %copy-start.11 = (bf16[32,512]{1,0:T(8,128)(2,1)S(1)}, bf16[32,512]{1,0:T(8,128)(2,1)}, u32[]{:S(2)}) copy-start(bf16[32,512]{1,0:T(8,128)(2,1)} %param.25) | copy-start | bytes 98308
  2.6 10.3 %copy-start.4 = (bf16[512,512]{1,0:T(8,128)(2,1)S(1)}, bf16[512,512]{1,0:T(8,128)(2,1)}, u32[]{:S(2)}) copy-start(bf16[512,512]{1,0:T(8,128)(2,1)} %param.35) | copy-start | bytes 1572868
  2.7 10.3 %copy-start.5 = (bf16[512,512]{1,0:T(8,128)(2,1)S(1)}, bf16[512,512]{1,0:T(8,128)(2,1)}, u32[]{:S(2)}) copy-start(bf16[512,512]{1,0:T(8,128)(2,1)} %param.34) | copy-start | bytes 1572868
  2.7 8.4 %collective-permute-start = (f32[32,512]{1,0:T(8,128)S(1)}, f32[32,512]{1,0:T(8,128)S(1)}, u32[]{:S(2)}, u32[]{:S(2)}) collective-permute-start(f32[32,512]{1,0:T(8,128)S(1)} %get-tuple-element.5), channel_id=1, source_target_pairs={{0,1},{1,2},{2,3},{3,4},{4,5},{5,6},{6,7},{7,8},{8,9},{9,10},{10,1... | collective-permute-start | bytes 196616 | tf_op jit(solution)/shard_map/ppermute | solution.py:16
  7.3 5.6 %collective-permute-start.1 = (f32[32,512]{1,0:T(8,128)S(1)}, f32[32,512]{1,0:T(8,128)S(1)}, u32[]{:S(2)}, u32[]{:S(2)}) collective-permute-start(f32[32,512]{1,0:T(8,128)S(1)} %get-tuple-element.6), channel_id=1, source_target_pairs={{1,0},{2,1},{3,2},{4,3},{5,4},{6,5},{7,6},{8,7},{9,8},{10,9},{11,1... | collective-permute-start | bytes 196616 | tf_op jit(solution)/shard_map/ppermute | solution.py:17
  10.9 2.6 %copy-start.9 = (bf16[512,512]{1,0:T(8,128)(2,1)S(1)}, bf16[512,512]{1,0:T(8,128)(2,1)}, u32[]{:S(2)}) copy-start(bf16[512,512]{1,0:T(8,128)(2,1)} %param.36) | copy-start | bytes 1572868
  10.9 2.6 %copy-start.14 = (s32[32]{0:T(128)S(1)}, s32[32]{0:T(128)}, u32[]{:S(2)}) copy-start(s32[32]{0:T(128)} %param.28) | copy-start | bytes 388
  105.7 9.8 %copy-start.2 = (bf16[642,512]{1,0:T(8,128)(2,1)}, bf16[642,512]{1,0:T(8,128)(2,1)S(1)}, u32[]{:S(2)}) copy-start(bf16[642,512]{1,0:T(8,128)(2,1)S(1)} %add_convert_fusion) | copy-start | bytes 1972228
  105.8 2.0 %copy-start.7 = (bf16[512,512]{1,0:T(8,128)(2,1)S(1)}, bf16[512,512]{1,0:T(8,128)(2,1)}, u32[]{:S(2)}) copy-start(bf16[512,512]{1,0:T(8,128)(2,1)} %param.41) | copy-start | bytes 1572868
  105.8 6.6 %copy-start.13 = (s32[512]{0:T(512)S(1)}, s32[512]{0:T(512)}, u32[]{:S(2)}) copy-start(s32[512]{0:T(512)} %param.27) | copy-start | bytes 6148
  105.8 9.4 %copy-start.8 = (bf16[512,512]{1,0:T(8,128)(2,1)S(1)}, bf16[512,512]{1,0:T(8,128)(2,1)}, u32[]{:S(2)}) copy-start(bf16[512,512]{1,0:T(8,128)(2,1)} %param.24) | copy-start | bytes 1572868
  105.8 9.7 %copy-start.18 = (s32[256]{0:T(256)S(1)}, s32[256]{0:T(256)}, u32[]{:S(2)}) copy-start(s32[256]{0:T(256)} %param.29) | copy-start | bytes 3076
  107.8 18.2 %copy-start.12 = (bf16[32,512]{1,0:T(8,128)(2,1)}, bf16[32,512]{1,0:T(8,128)(2,1)S(1)}, u32[]{:S(2)}) copy-start(bf16[32,512]{1,0:T(8,128)(2,1)S(1)} %fusion.11) | copy-start | bytes 98308
  107.8 13.4 %copy-start.16 = (s32[3072]{0:T(1024)S(1)}, s32[3072]{0:T(1024)}, u32[]{:S(2)}) copy-start(s32[3072]{0:T(1024)} %param.31) | copy-start | bytes 36868
  108.0 4.4 %collective-permute-start.2 = (bf16[32,512]{1,0:T(8,128)(2,1)S(1)}, bf16[32,512]{1,0:T(8,128)(2,1)S(1)}, u32[]{:S(2)}, u32[]{:S(2)}) collective-permute-start(bf16[32,512]{1,0:T(8,128)(2,1)S(1)} %convolution_convert_fusion.6), channel_id=1, source_target_pairs={{0,1},{1,2},{2,3},{3,4},{4,5},{5,6},{6,7},{7,8},{8,9},{9,10},{10,1... | collective-permute-start | bytes 98312 | tf_op jit(solution)/shard_map/ppermute | solution.py:16
  109.9 5.2 %collective-permute-start.3 = (bf16[32,512]{1,0:T(8,128)(2,1)S(1)}, bf16[32,512]{1,0:T(8,128)(2,1)S(1)}, u32[]{:S(2)}, u32[]{:S(2)}) collective-permute-start(bf16[32,512]{1,0:T(8,128)(2,1)S(1)} %convolution_convert_fusion.6), channel_id=1, source_target_pairs={{1,0},{2,1},{3,2},{4,3},{5,4},{6,5},{7,6},{8,7},{9,8},{10,9},{11,1... | collective-permute-start | bytes 98312 | tf_op jit(solution)/shard_map/ppermute | solution.py:17
  115.9 10.6 %collective-permute-start.4 = (bf16[128,512]{1,0:T(8,128)(2,1)S(1)}, bf16[128,512]{1,0:T(8,128)(2,1)}, u32[]{:S(2)}, u32[]{:S(2)}) collective-permute-start(bf16[128,512]{1,0:T(8,128)(2,1)S(1)} %get-tuple-element.3), channel_id=1, source_target_pairs={{0,1},{1,2},{2,3},{3,4},{4,5},{5,6},{6,7},{7,8},{8,9},{9,10},{10,1... | collective-permute-start | bytes 393224 | tf_op jit(solution)/shard_map/ppermute | solution.py:16
  117.8 8.2 %copy-start.10 = (bf16[512,512]{1,0:T(8,128)(2,1)S(1)}, bf16[512,512]{1,0:T(8,128)(2,1)}, u32[]{:S(2)}) copy-start(bf16[512,512]{1,0:T(8,128)(2,1)} %param.45) | copy-start | bytes 1572868
  117.9 8.6 %collective-permute-start.5 = (bf16[128,512]{1,0:T(8,128)(2,1)S(1)}, bf16[128,512]{1,0:T(8,128)(2,1)}, u32[]{:S(2)}, u32[]{:S(2)}) collective-permute-start(bf16[128,512]{1,0:T(8,128)(2,1)S(1)} %get-tuple-element.4), channel_id=1, source_target_pairs={{1,0},{2,1},{3,2},{4,3},{5,4},{6,5},{7,6},{8,7},{9,8},{10,9},{11,1... | collective-permute-start | bytes 393224 | tf_op jit(solution)/shard_map/ppermute | solution.py:17
  126.0 1.0 copy-start.15
  126.5 3.1 %copy-start.17 = (s32[3072]{0:T(1024)S(1)}, s32[3072]{0:T(1024)}, u32[]{:S(2)}) copy-start(s32[3072]{0:T(1024)} %param.30) | copy-start | bytes 36868
where the time goes:
time: 147 us; the launch traced here: 144 us
  blocking collectives  88.7 us (60%)
  matrix products  31.5 us (21%)
  starting transfers between devices  16.2 us (11%)
  waiting for transfers between devices  4.62 us (3%)
    psum x1, blocking collectives, on_device(): coarse_in = lax.psum(product(selector, mid_msg), ('rhombus', 'tile'))  88.7 us
    dot_general x14, matrix products, product(): return jnp.dot(left, right, preferred_element_type=jnp.float32)  20.3 us
    ppermute x3, starting transfers between devices, extended_2(): before = lax.ppermute(last, axis, up)  8.49 us
    dot_general x1, matrix products, edge_update(): lax.dot_general(target_pick, edge_hidden, (((0,), (0,)), ((), ())), prefe...  8.29 us
    ppermute x3, starting transfers between devices, extended_2(): after = lax.ppermute(leading, axis, down)  7.68 us
    ppermute x3, waiting for transfers between devices, extended_2(): after = lax.ppermute(leading, axis, down)  4.61 us
  transfers between devices with their start and end apart: 6, of which 2 were waited for; matrix products, arithmetic and copies ran while one was open for 5% of the time, Pallas kernels for 0%

commit v1 on v0

v1 whole, which is shorter than its diff:
```python
import jax
import jax.numpy as jnp
from jax import lax
from jax.sharding import PartitionSpec as P

EPSILON = 1e-05
BLOCK = 24
PLANE = ("y", "x")
TILE = ("y", "x", "c")


def product(left, right):
    return jnp.dot(left, right, preferred_element_type=jnp.float32)


def bf(values):
    return values.astype(jnp.bfloat16)


def normed(values):
    return values / jnp.sqrt(jnp.mean(values * values, axis=-1, keepdims=True) + EPSILON)


def node_update(latent, incoming, first, second, third):
    hidden = bf(jax.nn.silu(product(latent, first) + product(incoming, second)))
    return bf(latent.astype(jnp.float32) + normed(product(hidden, third)))


def selector_rows(row_ids, width):
    columns = lax.broadcasted_iota(jnp.int32, (row_ids.shape[0], width), 1)
    return bf(columns == row_ids[:, None])


def selector_columns(row_ids, height):
    rows = lax.broadcasted_iota(jnp.int32, (height, row_ids.shape[0]), 0)
    return bf(rows == row_ids[None, :])


def shifted(values, axis, step, size):
    pairs = [(i, i + step) for i in range(size) if 0 <= i + step < size]
    return lax.ppermute(values, axis, pairs)


def swapped(values):
    return lax.ppermute(values, "c", [(0, 1), (1, 0)])


def with_columns(rows, columns):
    count = rows.shape[0]
    extra = jnp.stack(columns, axis=1).astype(jnp.bfloat16)
    extra = jnp.concatenate([extra, jnp.zeros((count, 128 - extra.shape[1]), jnp.bfloat16)], axis=1)
    return jnp.concatenate([rows, extra], axis=1)


def on_device(
    fine_latent,
    mid_latent,
    coarse_latent,
    fine_parent,
    mid_parent,
    halo_rows,
    edge_source,
    edge_target,
    w_child,
    mid_w1,
    mid_w2,
    mid_w3,
    w_coarse,
    coarse_w1,
    coarse_w2,
    coarse_w3,
    w_descend,
    w_fine,
    edge_w_src,
    edge_w_dst,
    edge_w2,
    node_w1,
    node_w2,
    node_w3,
):
    fine_count, width = fine_latent.shape
    mid_count = mid_latent.shape[0]
    coarse_count = coarse_latent.shape[0]
    rim = halo_rows.shape[0] // 2
    planes, chips = lax.axis_size("z"), lax.axis_size("y") * lax.axis_size("x")
    tiles = 2 * chips
    half = chips * BLOCK
    core = lax.axis_index("c")
    chip = lax.axis_index("y") * lax.axis_size("x") + lax.axis_index("x")

    child_msg = bf(product(fine_latent, w_child))
    partial_sums = product(selector_columns(fine_parent, 3 * mid_count), child_msg)
    from_before = shifted(partial_sums[2 * mid_count :], TILE, 1, tiles)
    from_after = shifted(partial_sums[mid_count : 2 * mid_count], TILE, -1, tiles)
    mid_in = partial_sums[:mid_count] + from_before + from_after
    mid_up = node_update(mid_latent, bf(mid_in), mid_w1, mid_w2, mid_w3)

    labelled = with_columns(mid_up, [mid_parent // 32, mid_parent % 32])
    other = swapped(labelled)
    pair = jnp.where(core == 0, jnp.concatenate([labelled, other]), jnp.concatenate([other, labelled]))
    pair_ids = pair[:, width].astype(jnp.int32) * 32 + pair[:, width + 1].astype(jnp.int32)

    pair_msg = bf(product(pair[:, :width], w_coarse))
    blocks = bf(product(selector_columns(pair_ids - core * half, half), pair_msg))
    blocks = lax.all_to_all(blocks.reshape(chips, BLOCK, width), PLANE, 0, 0)
    own = bf(jnp.sum(blocks.astype(jnp.float32), axis=0))
    planes_of = lax.all_to_all(jnp.broadcast_to(own, (planes, BLOCK, width)), "z", 0, 0)
    coarse_in = bf(jnp.sum(planes_of.astype(jnp.float32), axis=0))

    padded = jnp.pad(coarse_latent, ((0, 2 * half - coarse_count), (0, 0)))
    own_latent = lax.dynamic_slice_in_dim(padded, core * half + chip * BLOCK, BLOCK)
    own_out = node_update(own_latent, coarse_in, coarse_w1, coarse_w2, coarse_w3)
    mine = lax.all_to_all(jnp.broadcast_to(own_out, (chips, BLOCK, width)), PLANE, 0, 0).reshape(half, width)
    theirs = swapped(mine)
    coarse_all = jnp.where(core == 0, jnp.concatenate([mine, theirs]), jnp.concatenate([theirs, mine]))

    before = shifted(pair, PLANE, 1, chips)
    after = shifted(pair, PLANE, -1, chips)
    window = lax.dynamic_slice_in_dim(jnp.concatenate([before, pair, after]), core * mid_count, 5 * mid_count)
    window_ids = window[:, width].astype(jnp.int32) * 32 + window[:, width + 1].astype(jnp.int32)

    sent = with_columns(fine_latent, [fine_parent + 1])
    boundary = bf(product(selector_rows(halo_rows, fine_count), sent))
    halo_before = shifted(boundary[rim:], TILE, 1, tiles)
    halo_after = shifted(boundary[:rim], TILE, -1, tiles)

    def placed(code, tile):
        parent = code - 1
        side = parent // mid_count
        away = jnp.where(side == 1, -1, jnp.where(side == 2, 1, 0))
        return jnp.where(code > 0, (tile + away) * mid_count + parent % mid_count, -1)

    table = jnp.concatenate([fine_latent, halo_before[:, :width], halo_after[:, :width]])
    own_slot = placed(fine_parent + 1, 2)
    table_slot = jnp.concatenate(
        [
            own_slot,
            placed(halo_before[:, width].astype(jnp.int32), 1),
            placed(halo_after[:, width].astype(jnp.int32), 3),
        ]
    )

    parents = bf(product(selector_rows(window_ids, 2 * half), coarse_all))
    down = bf(product(parents, w_descend))
    window_out = bf(window[:, :width].astype(jnp.float32) + down.astype(jnp.float32))
    mid_out = window_out[2 * mid_count : 3 * mid_count]
    fine_down = bf(product(window_out, w_fine))
    lifted_table = bf(
        table.astype(jnp.float32) + product(selector_rows(table_slot, 5 * mid_count), fine_down)
    )
    lifted = lifted_table[:fine_count]

    sender = bf(product(lifted_table, edge_w_src))
    receiver = bf(product(lifted, edge_w_dst))
    source_pick = selector_rows(edge_source, table.shape[0])
    target_pick = selector_rows(edge_target, fine_count)
    edge_sum = product(source_pick, sender) + product(target_pick, receiver)
    edge_hidden = bf(jax.nn.silu(edge_sum))
    hidden_sums = lax.dot_general(
        target_pick, edge_hidden, (((0,), (0,)), ((), ())), preferred_element_type=jnp.float32
    )
    aggregate = jnp.dot(hidden_sums, edge_w2.astype(jnp.float32), precision=lax.Precision.HIGHEST)
    fine_out = node_update(lifted, bf(aggregate), node_w1, node_w2, node_w3)
    return (fine_out, mid_out, coarse_all[:coarse_count])


def solution(mesh):
    groups, tiles = mesh.shape["rhombus"], mesh.shape["tile"]
    side = {32: (4, 4), 8: (2, 2)}[tiles]
    physical = jax.sharding.Mesh(mesh.devices.reshape(groups, *side, 2), ("z", "y", "x", "c"))
    every = ("z", "y", "x", "c")
    split, copied = P(every), P()
    return jax.shard_map(
        on_device,
        mesh=physical,
        in_specs=(split, split, copied) + (split,) * 5 + (copied,) * 16,
        out_specs=(split, split, copied),
        check_vma=False,
    )
```

time: 147 us -> 99.9 us (0.68); the launches traced: 144 us -> 99 us
  blocking collectives: 88.7 us -> 0 us
  starting transfers between devices: 16.2 us -> 41.4 us
  waiting for transfers between devices: 4.62 us -> 17.9 us
  local copies, waits for them, and re-layouts: 1.04 us -> 5.76 us
  matrix products: 31.5 us -> 28.4 us
  other arithmetic: 1.4 us -> 4.39 us
    psum x1 -> x0, blocking collectives: 88.7 us -> none  [on_device(): coarse_in = lax.psum(product(selector, mid_msg), ('rhombus', 'tile'))]
    all_to_all x0 -> x3, starting transfers between devices: none -> 23.9 us  [the longest x1 8.3 us: on_device(): blocks = lax.all_to_all(blocks.reshape(chips, BLOCK, width), PLANE, 0, 0)]
    all_to_all x0 -> x3, waiting for transfers between devices: none -> 13.8 us  [the longest x1 7.69 us: on_device(): lax.all_to_all(jnp.broadcast_to(own_out, (chips, BLOCK, width)), PLANE, 0...]
    slice x2 -> x7, local copies, waits for them, and re-layouts: 0.03 us -> 3.18 us  [the longest x1 0.91 us: on_device(): halo_before[:, :width]]
    dot_general x14 -> x13, matrix products: 20.3 us -> 17.3 us  [product(): return jnp.dot(left, right, preferred_element_type=jnp.float32)]
    broadcast_in_dim x0 -> x4, local copies, waits for them, and re-layouts: none -> 1.48 us  [the longest x1 0.78 us: on_device(): jnp.broadcast_to(own_out, (chips, BLOCK, width))]
    ppermute x6 -> x8, starting transfers between devices: 16.2 us -> 17.4 us  [the longest x6 15.8 us: shifted(): return lax.ppermute(values, axis, pairs)]
    ppermute x6 -> x8, waiting for transfers between devices: 4.62 us -> 4.16 us  [the longest x6 3.22 us: shifted(): return lax.ppermute(values, axis, pairs)]
  transfers between devices with their start and end apart: 6 -> 11, of which waited for: 2 -> 5; matrix products, arithmetic and copies ran while one was open for 5% -> 9% of each run, Pallas kernels for 0% -> 0%
where the time goes in v1:
time: 99.9 us; the launch traced here: 99 us
  starting transfers between devices  41.4 us (41%)
  matrix products  28.4 us (28%)
  waiting for transfers between devices  17.9 us (18%)
  local copies, waits for them, and re-layouts  5.76 us (6%)
  other arithmetic  4.39 us (4%)
  between operations  1.18 us (1%)
    dot_general x13, matrix products, product(): return jnp.dot(left, right, preferred_element_type=jnp.float32)  17.3 us
    ppermute x6, starting transfers between devices, shifted(): return lax.ppermute(values, axis, pairs)  15.8 us
    all_to_all x1, starting transfers between devices, on_device(): blocks = lax.all_to_all(blocks.reshape(chips, BLOCK, width), PLANE, 0, 0)  8.3 us
    dot_general x1, matrix products, on_device(): lax.dot_general(target_pick, edge_hidden, (((0,), (0,)), ((), ())), prefe...  8.29 us
    all_to_all x1, starting transfers between devices, on_device(): lax.all_to_all(jnp.broadcast_to(own, (planes, BLOCK, width)), 'z', 0, 0)  8.18 us
    all_to_all x1, waiting for transfers between devices, on_device(): lax.all_to_all(jnp.broadcast_to(own_out, (chips, BLOCK, width)), PLANE, 0...  7.69 us
    all_to_all x1, starting transfers between devices, on_device(): lax.all_to_all(jnp.broadcast_to(own_out, (chips, BLOCK, width)), PLANE, 0...  7.45 us
    all_to_all x1, waiting for transfers between devices, on_device(): lax.all_to_all(jnp.broadcast_to(own, (planes, BLOCK, width)), 'z', 0, 0)  4.79 us
  transfers between devices with their start and end apart: 11, of which 5 were waited for; matrix products, arithmetic and copies ran while one was open for 9% of the time, Pallas kernels for 0%

profile of v1, /device:TPU:1, one launch (start us, length us, event | category | flops | bytes accessed | tf_op | source)
XLA Modules:
  0.0 99.0 jit_solution(9328102804030791898)
XLA Ops:
  0.7 1.9 %fusion.6 = f32[96,512]{1,0:T(8,128)S(1)} fusion(bf16[512,512]{1,0:T(8,128)(2,1)} %param.24, bf16[512,512]{1,0:T(8,128)(2,1)} %param.32, s32[512]{0:T(512)} %param.27), kind=kOutput, calls=%fused_computation.16 | convolution fusion | flops 319078400 | bytes 1247232 | tf_op jit(solution)/shard_map/dot_general | solution.py:13
  2.7 4.6 %collective-permute-start.2 = (f32[32,512]{1,0:T(8,128)S(1)}, f32[32,512]{1,0:T(8,128)S(1)}, u32[]{:S(2)}, u32[]{:S(2)}) collective-permute-start(f32[32,512]{1,0:T(8,128)S(1)} %get-tuple-element.5), channel_id=1, source_target_pairs={{0,1},{1,2},{2,3},{3,4},{4,5},{5,6},{6,7},{7,8},{8,9},{9,10},{10,1... | collective-permute-start | bytes 196616 | tf_op jit(solution)/shard_map/ppermute | solution.py:41
  7.3 1.9 %collective-permute-start.3 = (f32[32,512]{1,0:T(8,128)S(1)}, f32[32,512]{1,0:T(8,128)S(1)}, u32[]{:S(2)}, u32[]{:S(2)}) collective-permute-start(f32[32,512]{1,0:T(8,128)S(1)} %get-tuple-element.6), channel_id=1, source_target_pairs={{1,0},{2,1},{3,2},{4,3},{5,4},{6,5},{7,6},{8,7},{9,8},{10,9},{11,1... | collective-permute-start | bytes 196616 | tf_op jit(solution)/shard_map/ppermute | solution.py:41
  9.7 3.2 %collective-permute-done.3 = f32[32,512]{1,0:T(8,128)S(1)} collective-permute-done((f32[32,512]{1,0:T(8,128)S(1)}, f32[32,512]{1,0:T(8,128)S(1)}, u32[]{:S(2)}, u32[]{:S(2)}) %collective-permute-start.3) | collective-permute-done | bytes 65568 | tf_op jit(solution)/shard_map/ppermute | solution.py:41
  13.9 0.9 collective-permute-done.4
  15.1 1.2 %convolution_convert_fusion.4 = bf16[384,512]{1,0:T(8,128)(2,1)} fusion(bf16[512,512]{1,0:T(8,128)(2,1)S(1)} %copy-done.4, s32[64]{0:T(128)S(1)} %subtract_reduce_fusion, bf16[64,640]{1,0:T(8,128)(2,1)S(1)} %maximum_select_fusion.1), kind=kOutput, calls=%fused_computation.15 | convolution fusion | flops 58974208 | bytes 983552 | tf_op jit(solution)/shard_map/dot_general | solution.py:13
  16.3 8.3 %all-to-all-start = ((bf16[16,24,512]{2,1,0:T(8,128)(2,1)}), bf16[16,24,512]{2,1,0:T(8,128)(2,1)S(1)}, u32[]{:S(2)}, u32[]{:S(2)}) async-start(bf16[16,24,512]{2,1,0:T(8,128)(2,1)} %bitcast.2), calls=%async_computation | async-start | bytes 786432 | tf_op jit(solution)/shard_map/all_to_all | solution.py:105
  24.7 1.6 %convolution_convert_fusion.5 = bf16[256,640]{1,0:T(8,128)(2,1)S(1)} fusion(bf16[512,1]{1,0:T(8,128)(2,1)S(1)} %convert_element_type.165, bf16[512,512]{1,0:T(8,128)(2,1)} %param.24, bf16[640]{0:T(1024)(128)(2,1)S(1)} %pad.34.clone, s32[256]{0:T(256)S(1)} %copy-done.18), kind=kOutput, calls=%fused_computation.17 | convolution fusion | flops 170033152 | bytes 855296 | tf_op jit(solution)/shard_map/dot_general | solution.py:13
  26.3 0.7 fusion.61
  27.0 2.3 %collective-permute-start.1 = (bf16[128,640]{1,0:T(8,128)(2,1)}, bf16[128,640]{1,0:T(8,128)(2,1)S(1)}, u32[]{:S(2)}, u32[]{:S(2)}) collective-permute-start(bf16[128,640]{1,0:T(8,128)(2,1)} %get-tuple-element.4), channel_id=1, source_target_pairs={{1,0},{2,1},{3,2},{4,3},{5,4},{6,5},{7,6},{8,7},{9,8},{10,9},{11,1... | collective-permute-start | bytes 491528 | tf_op jit(solution)/shard_map/ppermute | solution.py:41
  29.4 3.4 %collective-permute-start = (bf16[128,640]{1,0:T(8,128)(2,1)}, bf16[128,640]{1,0:T(8,128)(2,1)}, u32[]{:S(2)}, u32[]{:S(2)}) collective-permute-start(bf16[128,640]{1,0:T(8,128)(2,1)} %get-tuple-element.3), channel_id=1, source_target_pairs={{0,1},{1,2},{2,3},{3,4},{4,5},{5,6},{6,7},{7,8},{8,9},{9,10},{10,1... | collective-permute-start | bytes 491528 | tf_op jit(solution)/shard_map/ppermute | solution.py:41
  32.8 1.3 %all-to-all-done = bf16[16,24,512]{2,1,0:T(8,128)(2,1)S(1)} async-done(((bf16[16,24,512]{2,1,0:T(8,128)(2,1)}), bf16[16,24,512]{2,1,0:T(8,128)(2,1)S(1)}, u32[]{:S(2)}, u32[]{:S(2)}) %all-to-all-start) | async-done | bytes 393248 | tf_op jit(solution)/shard_map/all_to_all | solution.py:105
  34.2 0.7 broadcast_in_dim.44
  34.9 8.2 %all-to-all-start.1 = ((bf16[8,24,512]{2,1,0:T(8,128)(2,1)}), bf16[8,24,512]{2,1,0:T(8,128)(2,1)S(1)}, u32[]{:S(2)}, u32[]{:S(2)}) async-start(bf16[8,24,512]{2,1,0:T(8,128)(2,1)} %broadcast_in_dim.44), calls=%async_computation.1 | async-start | bytes 393216 | tf_op jit(solution)/shard_map/all_to_all | solution.py:107
  43.2 2.2 %collective-permute-start.5 = (bf16[64,640]{1,0:T(8,128)(2,1)S(1)}, bf16[64,640]{1,0:T(8,128)(2,1)S(1)}, u32[]{:S(2)}, u32[]{:S(2)}) collective-permute-start(bf16[64,640]{1,0:T(8,128)(2,1)S(1)} %maximum_select_fusion.1), channel_id=1, source_target_pairs={{0,2},{2,4},{4,6},{6,8},{8,10},{10,12},{12,14},{14,16},{16,18},{18... | collective-permute-start | bytes 245768 | tf_op jit(solution)/shard_map/ppermute | solution.py:41
  45.5 1.3 %collective-permute-start.6 = (bf16[64,640]{1,0:T(8,128)(2,1)S(1)}, bf16[64,640]{1,0:T(8,128)(2,1)S(1)}, u32[]{:S(2)}, u32[]{:S(2)}) collective-permute-start(bf16[64,640]{1,0:T(8,128)(2,1)S(1)} %maximum_select_fusion.1), channel_id=1, source_target_pairs={{2,0},{4,2},{6,4},{8,6},{10,8},{12,10},{14,12},{16,14},{18,16},{20... | collective-permute-start | bytes 245768 | tf_op jit(solution)/shard_map/ppermute | solution.py:41
  47.0 4.8 %all-to-all-done.1 = bf16[8,24,512]{2,1,0:T(8,128)(2,1)S(1)} async-done(((bf16[8,24,512]{2,1,0:T(8,128)(2,1)}), bf16[8,24,512]{2,1,0:T(8,128)(2,1)S(1)}, u32[]{:S(2)}, u32[]{:S(2)}) %all-to-all-start.1) | async-done | bytes 196640 | tf_op jit(solution)/shard_map/all_to_all | solution.py:107
  52.4 0.8 broadcast_in_dim.45
  53.2 7.4 %all-to-all-start.2 = ((bf16[16,24,512]{2,1,0:T(8,128)(2,1)}), bf16[16,24,512]{2,1,0:T(8,128)(2,1)S(1)}, u32[]{:S(2)}, u32[]{:S(2)}) async-start(bf16[16,24,512]{2,1,0:T(8,128)(2,1)} %broadcast_in_dim.45), calls=%async_computation.2 | async-start | bytes 786432 | tf_op jit(solution)/shard_map/all_to_all | solution.py:113
  60.7 0.9 fusion.28
  61.5 0.9 fusion.35
  62.4 7.7 %all-to-all-done.2 = bf16[16,24,512]{2,1,0:T(8,128)(2,1)S(1)} async-done(((bf16[16,24,512]{2,1,0:T(8,128)(2,1)}), bf16[16,24,512]{2,1,0:T(8,128)(2,1)S(1)}, u32[]{:S(2)}, u32[]{:S(2)}) %all-to-all-start.2) | async-done | bytes 393248 | tf_op jit(solution)/shard_map/all_to_all | solution.py:113
  70.1 1.6 %collective-permute-start.7 = (bf16[384,512]{1,0:T(8,128)(2,1)S(1)}, bf16[384,512]{1,0:T(8,128)(2,1)S(1)}, u32[]{:S(2)}, u32[]{:S(2)}) collective-permute-start(bf16[384,512]{1,0:T(8,128)(2,1)S(1)} %bitcast.31), channel_id=1, source_target_pairs={{0,1},{1,0},{2,3},{3,2},{4,5},{5,4},{6,7},{7,6},{8,9},{9,8},{10,11... | collective-permute-start | bytes 1179656 | tf_op jit(solution)/shard_map/ppermute | solution.py:45
  71.7 0.9 slice.73
  73.4 0.9 slice.89
  75.5 1.7 %add_convert_fusion = bf16[768,512]{1,0:T(8,128)(2,1)S(1)} fusion(bf16[128,512]{1,0:T(8,128)(2,1)S(1)} %slice-done, bf16[128,512]{1,0:T(8,128)(2,1)S(1)} %slice.73, bf16[512,512]{1,0:T(8,128)(2,1)S(1)} %copy-done.14, bf16[160,512]{1,0:T(8,128)(2,1)S(1)} %add_convert_fusion.2, bf16[512,512]{1,0:T(8,128)(2,1)} %param.41, s32[768]{0:T(1024)S(1)} %pad_add_fusion), kind=kOutput, calls=%fused_computation.9 | convolution fusion | flops 213065728 | bytes 2264064 | tf_op jit(solution)/shard_map/dot_general | solution.py:13
  77.2 1.5 %convolution_convert_fusion = bf16[768,512]{1,0:T(8,128)(2,1)} fusion(bf16[768,512]{1,0:T(8,128)(2,1)S(1)} %add_convert_fusion, bf16[512,512]{1,0:T(8,128)(2,1)S(1)} %copy-done.15), kind=kOutput, calls=%fused_computation.10 | convolution fusion | flops 403046400 | bytes 2097152 | tf_op jit(solution)/shard_map/dot_general | solution.py:13
  79.4 4.8 %fusion.2 = f32[3072,512]{1,0:T(8,128)} fusion(s32[3072]{0:T(1024)S(1)} %copy-done.16, bf16[512,512]{1,0:T(8,128)(2,1)S(1)} %copy-done, bf16[768,512]{1,0:T(8,128)(2,1)S(1)} %add_convert_fusion), kind=kOutput, calls=%fused_computation.5 | convolution fusion | flops 1880883200 | bytes 7352320 | tf_op jit(solution)/shard_map/dot_general | solution.py:13
  84.2 8.3 %fusion.1 = f32[512,512]{1,0:T(8,128)S(1)} fusion(s32[3072]{0:T(1024)S(1)} %copy-done.16, f32[3072,512]{1,0:T(8,128)} %fusion.2, bf16[768,512]{1,0:T(8,128)(2,1)} %convolution_convert_fusion, s32[3072]{0:T(1024)S(1)} %copy-done.17), kind=kOutput, calls=%fused_computation.4 | convolution fusion | flops 4039901184 | bytes 8151040 | tf_op jit(solution)/shard_map/dot_general | solution.py:159
  92.5 2.8 %convolution_convert_fusion.3 = bf16[512,512]{1,0:T(8,128)(2,1)} fusion(f32[512,512]{1,0:T(8,128)S(1)} %fusion.1, bf16[512,512]{1,0:T(8,128)(2,1)} %param.44), kind=kOutput, calls=%fused_computation.14 | convolution fusion | flops 1610874880 | bytes 2097152 | tf_op jit(solution)/shard_map/dot_general | solution.py:162
  95.3 2.4 %multiply_reduce_fusion = (f32[512]{0:T(512)S(1)}, f32[512,512]{0,1:T(8,128)S(1)}) fusion(bf16[512,512]{1,0:T(8,128)(2,1)} %param.47, f32[512,512]{1,0:T(8,128)S(1)} %fusion.17, bf16[512,512]{1,0:T(8,128)(2,1)} %convolution_convert_fusion.3, bf16[512,512]{1,0:T(8,128)(2,1)} %param.46), kind=kOutput, calls=%fused_computation.27 | convolution fusion | flops 538967552 | bytes 3672064 | tf_op jit(solution)/shard_map/dot_general | solution.py:13
  98.0 1.0 %add_convert_fusion.1 = bf16[512,512]{1,0:T(8,128)(2,1)} fusion(f32[512,512]{1,0:T(8,128)S(1)} %copy.37, f32[512]{0:T(512)S(1)} %add_sqrt_fusion, bf16[768,512]{1,0:T(8,128)(2,1)S(1)} %add_convert_fusion), kind=kLoop, calls=%fused_computation.26 | loop fusion | flops 1048576 | bytes 2099200 | tf_op jit(solution)/shard_map/convert_element_type | solution.py:17
  (84 shorter events, 5.7 us)
Async XLA Ops:
  0.6 78.5 %copy-start = (bf16[512,512]{1,0:T(8,128)(2,1)S(1)}, bf16[512,512]{1,0:T(8,128)(2,1)}, u32[]{:S(2)}) copy-start(bf16[512,512]{1,0:T(8,128)(2,1)} %param.43) | copy-start | bytes 1572868
  0.6 8.6 %copy-start.11 = (bf16[32,512]{1,0:T(8,128)(2,1)S(1)}, bf16[32,512]{1,0:T(8,128)(2,1)}, u32[]{:S(2)}) copy-start(bf16[32,512]{1,0:T(8,128)(2,1)} %param.25) | copy-start | bytes 98308
  0.7 8.6 %copy-start.5 = (bf16[512,512]{1,0:T(8,128)(2,1)S(1)}, bf16[512,512]{1,0:T(8,128)(2,1)}, u32[]{:S(2)}) copy-start(bf16[512,512]{1,0:T(8,128)(2,1)} %param.33) | copy-start | bytes 1572868
  0.7 8.8 %copy-start.19 = (s32[32]{0:T(128)S(1)}, s32[32]{0:T(128)}, u32[]{:S(2)}) copy-start(s32[32]{0:T(128)} %param.28) | copy-start | bytes 388
  0.7 12.2 %copy-start.3 = (bf16[512,512]{1,0:T(8,128)(2,1)S(1)}, bf16[512,512]{1,0:T(8,128)(2,1)}, u32[]{:S(2)}) copy-start(bf16[512,512]{1,0:T(8,128)(2,1)} %param.34) | copy-start | bytes 1572868
  0.7 12.2 %copy-start.2 = (bf16[512,512]{1,0:T(8,128)(2,1)S(1)}, bf16[512,512]{1,0:T(8,128)(2,1)}, u32[]{:S(2)}) copy-start(bf16[512,512]{1,0:T(8,128)(2,1)} %param.35) | copy-start | bytes 1572868
  2.6 11.0 %copy-start.12 = (s32[512]{0:T(512)S(1)}, s32[512]{0:T(512)}, u32[]{:S(2)}) copy-start(s32[512]{0:T(512)} %param.27) | copy-start | bytes 6148
  2.7 12.5 %copy-start.4 = (bf16[512,512]{1,0:T(8,128)(2,1)S(1)}, bf16[512,512]{1,0:T(8,128)(2,1)}, u32[]{:S(2)}) copy-start(bf16[512,512]{1,0:T(8,128)(2,1)} %param.36) | copy-start | bytes 1572868
  2.7 7.0 %collective-permute-start.2 = (f32[32,512]{1,0:T(8,128)S(1)}, f32[32,512]{1,0:T(8,128)S(1)}, u32[]{:S(2)}, u32[]{:S(2)}) collective-permute-start(f32[32,512]{1,0:T(8,128)S(1)} %get-tuple-element.5), channel_id=1, source_target_pairs={{0,1},{1,2},{2,3},{3,4},{4,5},{5,6},{6,7},{7,8},{8,9},{9,10},{10,1... | collective-permute-start | bytes 196616 | tf_op jit(solution)/shard_map/ppermute | solution.py:41
  7.3 5.6 %collective-permute-start.3 = (f32[32,512]{1,0:T(8,128)S(1)}, f32[32,512]{1,0:T(8,128)S(1)}, u32[]{:S(2)}, u32[]{:S(2)}) collective-permute-start(f32[32,512]{1,0:T(8,128)S(1)} %get-tuple-element.6), channel_id=1, source_target_pairs={{1,0},{2,1},{3,2},{4,3},{5,4},{6,5},{7,6},{8,7},{9,8},{10,9},{11,1... | collective-permute-start | bytes 196616 | tf_op jit(solution)/shard_map/ppermute | solution.py:41
  9.7 14.9 %copy-start.18 = (s32[256]{0:T(256)S(1)}, s32[256]{0:T(256)}, u32[]{:S(2)}) copy-start(s32[256]{0:T(256)} %param.29) | copy-start | bytes 3076
  13.6 1.2 %collective-permute-start.4 = (bf16[32,640]{1,0:T(8,128)(2,1)S(1)}, bf16[32,640]{1,0:T(8,128)(2,1)S(1)}, u32[]{:S(2)}, u32[]{:S(2)}) collective-permute-start(bf16[32,640]{1,0:T(8,128)(2,1)S(1)} %pad_maximum_fusion), channel_id=1, source_target_pairs={{0,1},{1,0},{2,3},{3,2},{4,5},{5,4},{6,7},{7,6},{8,9},{9,8},{10,11... | collective-permute-start | bytes 122888 | tf_op jit(solution)/shard_map/ppermute | solution.py:45
  16.3 17.8 %all-to-all-start = ((bf16[16,24,512]{2,1,0:T(8,128)(2,1)}), bf16[16,24,512]{2,1,0:T(8,128)(2,1)S(1)}, u32[]{:S(2)}, u32[]{:S(2)}) async-start(bf16[16,24,512]{2,1,0:T(8,128)(2,1)} %bitcast.2), calls=%async_computation | async-start | bytes 786432 | tf_op jit(solution)/shard_map/all_to_all | solution.py:105
  24.7 18.4 %copy-start.1 = (bf16[642,512]{1,0:T(8,128)(2,1)S(1)}, bf16[642,512]{1,0:T(8,128)(2,1)}, u32[]{:S(2)}) copy-start(bf16[642,512]{1,0:T(8,128)(2,1)} %param.26) | copy-start | bytes 1972228
  24.7 18.4 %copy-start.6 = (bf16[512,512]{1,0:T(8,128)(2,1)S(1)}, bf16[512,512]{1,0:T(8,128)(2,1)}, u32[]{:S(2)}) copy-start(bf16[512,512]{1,0:T(8,128)(2,1)} %param.37) | copy-start | bytes 1572868
  26.3 25.6 %copy-start.7 = (bf16[512,512]{1,0:T(8,128)(2,1)S(1)}, bf16[512,512]{1,0:T(8,128)(2,1)}, u32[]{:S(2)}) copy-start(bf16[512,512]{1,0:T(8,128)(2,1)} %param.39) | copy-start | bytes 1572868
  26.3 25.6 %copy-start.8 = (bf16[512,512]{1,0:T(8,128)(2,1)S(1)}, bf16[512,512]{1,0:T(8,128)(2,1)}, u32[]{:S(2)}) copy-start(bf16[512,512]{1,0:T(8,128)(2,1)} %param.38) | copy-start | bytes 1572868
  27.0 19.7 %collective-permute-start.1 = (bf16[128,640]{1,0:T(8,128)(2,1)}, bf16[128,640]{1,0:T(8,128)(2,1)S(1)}, u32[]{:S(2)}, u32[]{:S(2)}) collective-permute-start(bf16[128,640]{1,0:T(8,128)(2,1)} %get-tuple-element.4), channel_id=1, source_target_pairs={{1,0},{2,1},{3,2},{4,3},{5,4},{6,5},{7,6},{8,7},{9,8},{10,9},{11,1... | collective-permute-start | bytes 491528 | tf_op jit(solution)/shard_map/ppermute | solution.py:41
  29.4 31.3 %collective-permute-start = (bf16[128,640]{1,0:T(8,128)(2,1)}, bf16[128,640]{1,0:T(8,128)(2,1)}, u32[]{:S(2)}, u32[]{:S(2)}) collective-permute-start(bf16[128,640]{1,0:T(8,128)(2,1)} %get-tuple-element.3), channel_id=1, source_target_pairs={{0,1},{1,2},{2,3},{3,4},{4,5},{5,6},{6,7},{7,8},{8,9},{9,10},{10,1... | collective-permute-start | bytes 491528 | tf_op jit(solution)/shard_map/ppermute | solution.py:41
  34.9 16.9 %all-to-all-start.1 = ((bf16[8,24,512]{2,1,0:T(8,128)(2,1)}), bf16[8,24,512]{2,1,0:T(8,128)(2,1)S(1)}, u32[]{:S(2)}, u32[]{:S(2)}) async-start(bf16[8,24,512]{2,1,0:T(8,128)(2,1)} %broadcast_in_dim.44), calls=%async_computation.1 | async-start | bytes 393216 | tf_op jit(solution)/shard_map/all_to_all | solution.py:107
  43.2 29.4 %collective-permute-start.5 = (bf16[64,640]{1,0:T(8,128)(2,1)S(1)}, bf16[64,640]{1,0:T(8,128)(2,1)S(1)}, u32[]{:S(2)}, u32[]{:S(2)}) collective-permute-start(bf16[64,640]{1,0:T(8,128)(2,1)S(1)} %maximum_select_fusion.1), channel_id=1, source_target_pairs={{0,2},{2,4},{4,6},{6,8},{8,10},{10,12},{12,14},{14,16},{16,18},{18... | collective-permute-start | bytes 245768 | tf_op jit(solution)/shard_map/ppermute | solution.py:41
  45.5 27.2 %collective-permute-start.6 = (bf16[64,640]{1,0:T(8,128)(2,1)S(1)}, bf16[64,640]{1,0:T(8,128)(2,1)S(1)}, u32[]{:S(2)}, u32[]{:S(2)}) collective-permute-start(bf16[64,640]{1,0:T(8,128)(2,1)S(1)} %maximum_select_fusion.1), channel_id=1, source_target_pairs={{2,0},{4,2},{6,4},{8,6},{10,8},{12,10},{14,12},{16,14},{18,16},{20... | collective-permute-start | bytes 245768 | tf_op jit(solution)/shard_map/ppermute | solution.py:41
  46.8 25.9 %copy-start.10 = (bf16[128,640]{1,0:T(8,128)(2,1)}, bf16[128,640]{1,0:T(8,128)(2,1)S(1)}, u32[]{:S(2)}) copy-start(bf16[128,640]{1,0:T(8,128)(2,1)S(1)} %collective-permute-done.1) | copy-start | bytes 491524
  53.2 16.9 %all-to-all-start.2 = ((bf16[16,24,512]{2,1,0:T(8,128)(2,1)}), bf16[16,24,512]{2,1,0:T(8,128)(2,1)S(1)}, u32[]{:S(2)}, u32[]{:S(2)}) async-start(bf16[16,24,512]{2,1,0:T(8,128)(2,1)} %broadcast_in_dim.45), calls=%async_computation.2 | async-start | bytes 786432 | tf_op jit(solution)/shard_map/all_to_all | solution.py:113
  70.1 3.0 %collective-permute-start.7 = (bf16[384,512]{1,0:T(8,128)(2,1)S(1)}, bf16[384,512]{1,0:T(8,128)(2,1)S(1)}, u32[]{:S(2)}, u32[]{:S(2)}) collective-permute-start(bf16[384,512]{1,0:T(8,128)(2,1)S(1)} %bitcast.31), channel_id=1, source_target_pairs={{0,1},{1,0},{2,3},{3,2},{4,5},{5,4},{6,7},{7,6},{8,9},{9,8},{10,11... | collective-permute-start | bytes 1179656 | tf_op jit(solution)/shard_map/ppermute | solution.py:45
  72.9 1.4 %copy-start.13 = (bf16[512,512]{1,0:T(8,128)(2,1)S(1)}, bf16[512,512]{1,0:T(8,128)(2,1)}, u32[]{:S(2)}) copy-start(bf16[512,512]{1,0:T(8,128)(2,1)} %param.40) | copy-start | bytes 1572868
  73.4 2.1 %slice-start = ((bf16[128,640]{1,0:T(8,128)(2,1)}), bf16[128,512]{1,0:T(8,128)(2,1)S(1)}, s32[]{:S(2)}) async-start(bf16[128,640]{1,0:T(8,128)(2,1)} %copy-done.10), calls=%async_computation.3 | async-start | bytes 262144 | tf_op jit(solution)/shard_map/slice | solution.py:133
  73.4 2.0 %copy-start.14 = (bf16[512,512]{1,0:T(8,128)(2,1)S(1)}, bf16[512,512]{1,0:T(8,128)(2,1)}, u32[]{:S(2)}) copy-start(bf16[512,512]{1,0:T(8,128)(2,1)} %param.24) | copy-start | bytes 1572868
  75.5 1.7 %copy-start.15 = (bf16[512,512]{1,0:T(8,128)(2,1)S(1)}, bf16[512,512]{1,0:T(8,128)(2,1)}, u32[]{:S(2)}) copy-start(bf16[512,512]{1,0:T(8,128)(2,1)} %param.42) | copy-start | bytes 1572868
  77.2 1.5 %copy-start.9 = (bf16[512,512]{1,0:T(8,128)(2,1)S(1)}, bf16[512,512]{1,0:T(8,128)(2,1)}, u32[]{:S(2)}) copy-start(bf16[512,512]{1,0:T(8,128)(2,1)} %param.45) | copy-start | bytes 1572868
  78.7 0.7 copy-start.16
  79.4 4.8 %copy-start.17 = (s32[3072]{0:T(1024)S(1)}, s32[3072]{0:T(1024)}, u32[]{:S(2)}) copy-start(s32[3072]{0:T(1024)} %param.30) | copy-start | bytes 36868

commit v2 on v1

v2 whole, which is shorter than its diff:
```python
import functools

import jax
import jax.numpy as jnp
from jax import lax
from jax.experimental import pallas as pl
from jax.experimental.pallas import tpu as pltpu
from jax.sharding import PartitionSpec as P

EPSILON = 1e-05
BLOCK = 24
LANES = 128
CHUNK = 512
PLANE = ("y", "x")
TILE = ("y", "x", "c")
F32, BF16, I32 = jnp.float32, jnp.bfloat16, jnp.int32
VMEM = pl.BlockSpec(memory_space=pltpu.VMEM)
UNREAD = pl.BlockSpec(memory_space=pl.ANY)


def kernel_call(body, outs, operands, after=(), scratch=(), limit=24, flops=0, name=None):
    count, skipped = len(operands), len(after)

    def kernel(*refs):
        body(*refs[:count], *refs[count + skipped :])

    return pl.pallas_call(
        kernel,
        out_shape=[jax.ShapeDtypeStruct(shape, dtype) for shape, dtype in outs],
        in_specs=[VMEM] * count + [UNREAD] * skipped,
        out_specs=[VMEM] * len(outs),
        scratch_shapes=list(scratch),
        compiler_params=pltpu.CompilerParams(vmem_limit_bytes=limit << 20),
        cost_estimate=pl.CostEstimate(flops=flops, bytes_accessed=1 << 20, transcendentals=0),
        name=name,
    )(*operands, *after)


def product(left, right):
    return jnp.dot(left, right, preferred_element_type=F32)


def silu(values):
    half = 0.5 * values
    return half + half * jnp.tanh(half)


def updated(latent, hidden, third):
    values = product(hidden.astype(BF16), third)
    scale = lax.rsqrt(jnp.mean(values * values, axis=-1, keepdims=True) + EPSILON)
    return (latent.astype(F32) + values * scale).astype(BF16)


def lanes(height, first=0):
    return lax.broadcasted_iota(I32, (height, LANES), 1) + first


def spread(row):
    return jnp.broadcast_to(row, (LANES, LANES)).T


def hot(mask):
    return jnp.where(mask, 1.0, 0.0).astype(BF16)


def picks(spread_ids, first, blocks):
    return [hot(spread_ids == lanes(LANES, first + LANES * q)) for q in range(blocks)]


def sums_body(parent, fine, own, up, down):
    count = own.shape[0]
    rows = lax.broadcasted_iota(I32, (3 * count, LANES), 0)
    blocks = [hot(rows == parent[r : r + 1, :]) for r in range(parent.shape[0])]
    sums = product(jnp.concatenate(blocks, axis=1), fine[...])
    own[...] = sums[:count]
    down[...] = sums[count : 2 * count].astype(BF16)
    up[...] = sums[2 * count :].astype(BF16)


def mid_body(own, before, after, latent, ids, w_child, first, second, third, out):
    count, width = latent.shape
    total = own[...] + before[...].astype(F32) + after[...].astype(F32)
    incoming = product(total.astype(BF16), w_child[...]).astype(BF16)
    hidden = silu(product(latent[...], first[...]) + product(incoming, second[...]))
    out[:, :width] = updated(latent[...], hidden, third[...])
    spread_ids = spread(jnp.concatenate([ids[...], jnp.zeros((1, LANES - count), I32)], axis=1))[:count]
    place = lanes(count)
    label = jnp.where(place == 0, spread_ids >> 5, jnp.where(place == 1, spread_ids & 31, 0))
    out[:, width:] = label.astype(F32).astype(BF16)


def row_ids(labelled, width):
    label = labelled[:, width:].astype(F32)
    return (label[:, :1] * 32.0 + label[:, 1:2]).astype(I32)


def blocks_body(mine, theirs, pair, out):
    count, width = mine.shape[0], out.shape[1]
    half = out.shape[0]
    core = lax.axis_index("c")
    pair[pl.ds(pl.multiple_of(core * count, count), count), :] = mine[...]
    pair[pl.ds(pl.multiple_of((1 - core) * count, count), count), :] = theirs[...]
    both = pair[...]
    columns = lax.broadcasted_iota(I32, (2 * count, half), 1) + core * half
    picked = hot(row_ids(both, width) == columns)
    out[...] = lax.dot_general(
        picked, both[:, :width], (((0,), (0,)), ((), ())), preferred_element_type=F32
    ).astype(BF16)


def tables_body(
    fine, parent, halo, coarse, w_src, w_dst, w_node, w_coarse, coarse_w1, coarse_w2,
    sender, receiver, node, boundary, both, own_latent, own_hidden,
):
    count, width = fine.shape
    blocks = count // LANES
    values = fine[...]
    sender[...] = product(values, w_src[...]).astype(BF16)
    receiver[...] = product(values, w_dst[...]).astype(BF16)
    node[...] = product(values, w_node[...])
    codes = [(spread(parent[r : r + 1, :]) + 1).astype(F32).astype(BF16) for r in range(blocks)]
    codes = jnp.concatenate(codes, axis=0)
    for r in range(halo.shape[0]):
        picked = jnp.concatenate(picks(spread(halo[r : r + 1, :]), 0, blocks), axis=1)
        boundary[r * LANES : (r + 1) * LANES, :width] = product(picked, values).astype(BF16)
        boundary[r * LANES : (r + 1) * LANES, width:] = product(picked, codes).astype(BF16)
    both[...] = product(w_coarse[...], coarse_w2[...]).astype(BF16)
    rows, total = own_latent.shape[0], coarse.shape[0]
    chip = lax.axis_index("y") * lax.axis_size("x") + lax.axis_index("x")
    chips = lax.axis_size("y") * lax.axis_size("x")
    first = (lax.axis_index("c") * chips + chip) * rows
    place = lax.broadcasted_iota(I32, (rows, total), 0) + first
    picked = hot(place == lax.broadcasted_iota(I32, (rows, total), 1))
    latent = product(picked, coarse[...]).astype(BF16)
    own_latent[...] = latent
    own_hidden[...] = product(latent, coarse_w1[...])


def gather_body(parts, out):
    total = jnp.sum(parts[...].astype(F32), axis=0).astype(BF16)
    for i in range(out.shape[0]):
        out[i] = total


def coarse_body(parts, own_latent, own_hidden, both, third, out):
    total = jnp.sum(parts[...].astype(F32), axis=0).astype(BF16)
    hidden = silu(own_hidden[...] + product(total, both[...]))
    result = updated(own_latent[...], hidden, third[...])
    for i in range(out.shape[0]):
        out[i] = result


def own_edges_body(source, target, sender, receiver, out, table):
    count = sender.shape[0]
    table[:count] = sender[...]
    table[count:] = receiver[...]
    for k in range(out.shape[0] // CHUNK):
        rows = []
        for r in range(k * CHUNK // LANES, (k + 1) * CHUNK // LANES):
            row = picks(spread(source[r : r + 1, :]), 0, count // LANES)
            row += picks(spread(target[r : r + 1, :]), 0, count // LANES)
            rows.append(jnp.concatenate(row, axis=1))
        picked = jnp.concatenate(rows, axis=0)
        out[k * CHUNK : (k + 1) * CHUNK, :] = product(picked, table[...]).astype(BF16)


def slots(codes, tile, count):
    parent = codes - 1
    side = parent // count
    away = jnp.where(side == 1, -1, jnp.where(side == 2, 1, 0))
    return jnp.where(codes > 0, (tile + away) * count + (parent & (count - 1)), -1)


def rest_edges_body(mid_count, source, target, parent, before, after, w_src, first, out, select, own_pick, table, where):
    count = own_pick.shape[0]
    width = out.shape[1]
    blocks = count // LANES
    for r in range(blocks):
        place = slots(spread(parent[r : r + 1, :]) + 1, 2, mid_count)
        rows = slice(r * LANES, (r + 1) * LANES)
        where[rows, :] = jnp.concatenate(picks(place, 0, 2), axis=1)
        near = place - mid_count
        own_pick[rows, :] = hot(near == lanes(LANES))
        far = place + 4 * mid_count
        there = slice(count + 2 * LANES + r * LANES, count + 2 * LANES + (r + 1) * LANES)
        where[there, :] = jnp.concatenate(picks(far, 0, 2), axis=1)
    for r, (halo, tile) in enumerate(((before, 1), (after, 3))):
        values = halo[...]
        rows = slice(r * LANES, (r + 1) * LANES)
        table[rows, :] = product(values[:, :width], w_src[...]).astype(BF16)
        place = slots(values[:, width:].astype(F32).astype(I32), tile, mid_count)
        where[count + r * LANES : count + (r + 1) * LANES, :] = jnp.concatenate(picks(place, 0, 2), axis=1)
    for k in range(out.shape[0] // CHUNK):
        rows = []
        for r in range(k * CHUNK // LANES, (k + 1) * CHUNK // LANES):
            row = picks(spread(source[r : r + 1, :]), 0, blocks + 2)
            row += picks(spread(target[r : r + 1, :]), 0, blocks)
            rows.append(jnp.concatenate(row, axis=1))
        picked = jnp.concatenate(rows, axis=0)
        here = slice(k * CHUNK, (k + 1) * CHUNK)
        select[here, :] = product(picked, where[...]).astype(BF16)
        rest = product(picked[:, count : count + 2 * LANES], table[...])
        out[here, :] = (first[here, :].astype(F32) + rest).astype(BF16)


def final_body(
    mine, theirs, before, pair, after, edges, select, target, fine, own_pick, node,
    w_descend, w_fine, w_src, w_dst, w_node, edge_w2, node_w2, node_w3,
    fine_out, mid_out, coarse_out, coarse, window, table, sums,
):
    core = lax.axis_index("c")
    half, width = mine.shape
    two = pair.shape[0]
    count = two // 2
    coarse[pl.ds(pl.multiple_of(core * half, half), half), :] = mine[...]
    coarse[pl.ds(pl.multiple_of((1 - core) * half, half), half), :] = theirs[...]
    window[:two] = before[...]
    window[two : 2 * two] = pair[...]
    window[2 * two :] = after[...]
    near = window[pl.ds(pl.multiple_of(core * count, count), 5 * count), :]
    columns = lax.broadcasted_iota(I32, (5 * count, 2 * half), 1)
    picked = hot(row_ids(near, width) == columns)
    parents = product(picked, coarse[...]).astype(BF16)
    down = product(parents, w_descend[...]).astype(BF16)
    middle = (near[:, :width].astype(F32) + down.astype(F32)).astype(BF16)
    mid_out[...] = middle[2 * count : 3 * count]
    fine_down = product(middle, w_fine[...]).astype(BF16)
    closer = fine_down[count : 4 * count]
    table[: 5 * count] = product(fine_down, w_src[...]).astype(BF16)
    table[5 * count :] = product(closer, w_dst[...]).astype(BF16)
    rows = lax.broadcasted_iota(I32, (fine.shape[0], LANES), 0)
    for k in range(edges.shape[0] // CHUNK):
        here = slice(k * CHUNK, (k + 1) * CHUNK)
        edge_sum = edges[here, :].astype(F32) + product(select[here, :], table[...])
        hidden = silu(edge_sum).astype(BF16)
        marks = range(k * CHUNK // LANES, (k + 1) * CHUNK // LANES)
        scatter = jnp.concatenate([hot(rows == target[r : r + 1, :]) for r in marks], axis=1)
        part = product(scatter, hidden)
        if k == 0:
            sums[...] = part
        else:
            sums[...] += part
    coarse_out[...] = coarse[: coarse_out.shape[0], :]
    reach = fine_down[count : 5 * count]
    lifted = (fine[...].astype(F32) + product(own_pick[...], reach)).astype(BF16)
    near_node = product(reach, w_node[...]).astype(BF16)
    aggregate = product(sums[...].astype(BF16), edge_w2[...]).astype(BF16)
    hidden = silu(node[...] + product(own_pick[...], near_node) + product(aggregate, node_w2[...]))
    fine_out[...] = updated(lifted, hidden, node_w3[...])


def shifted(values, axis, step, size):
    pairs = [(i, i + step) for i in range(size) if 0 <= i + step < size]
    return lax.ppermute(values, axis, pairs)


def swapped(values):
    return lax.ppermute(values, "c", [(0, 1), (1, 0)])


def on_device(
    fine_latent,
    mid_latent,
    coarse_latent,
    fine_parent,
    mid_parent,
    halo_rows,
    edge_source,
    edge_target,
    w_child,
    mid_w1,
    mid_w2,
    mid_w3,
    w_coarse,
    coarse_w1,
    coarse_w2,
    coarse_w3,
    w_descend,
    w_fine,
    edge_w_src,
    edge_w_dst,
    edge_w2,
    node_w1,
    node_w2,
    node_w3,
):
    count, width = fine_latent.shape
    mids = mid_latent.shape[0]
    coarse_count = coarse_latent.shape[0]
    edge_count = edge_source.shape[0]
    planes, chips = lax.axis_size("z"), lax.axis_size("y") * lax.axis_size("x")
    tiles = 2 * chips
    half = chips * BLOCK
    wide = width + LANES
    parent = fine_parent.reshape(-1, LANES)
    source = edge_source.reshape(-1, LANES)
    target = edge_target.reshape(-1, LANES)
    halo = halo_rows.reshape(-1, LANES)

    own, up, down = kernel_call(
        sums_body,
        [((mids, width), F32), ((mids, width), BF16), ((mids, width), BF16)],
        [parent, fine_latent],
        name="child_sums",
    )
    from_before = shifted(up, TILE, 1, tiles)
    from_after = shifted(down, TILE, -1, tiles)
    (labelled,) = kernel_call(
        mid_body,
        [((mids, wide), BF16)],
        [own, from_before, from_after, mid_latent, mid_parent[None], w_child, mid_w1, mid_w2, mid_w3],
        name="mid_update",
    )
    other = swapped(labelled)
    pair, blocks = kernel_call(
        blocks_body,
        [((2 * mids, wide), BF16), ((half, width), BF16)],
        [labelled, other],
        name="coarse_blocks",
    )

    blocks = blocks.reshape(chips, BLOCK, width)
    parts = lax.all_to_all(blocks, PLANE, 0, 0)
    sender, receiver, node, boundary, both, own_latent, own_hidden = kernel_call(
        tables_body,
        [
            ((count, width), BF16),
            ((count, width), BF16),
            ((count, width), F32),
            ((2 * LANES, wide), BF16),
            ((width, width), BF16),
            ((BLOCK, width), BF16),
            ((BLOCK, width), F32),
        ],
        [fine_latent, parent, halo, coarse_latent, edge_w_src, edge_w_dst, node_w1, w_coarse, coarse_w1, coarse_w2],
        after=[blocks],
        flops=2_000_000_000,
        name="tables",
    )

    (own_parts,) = kernel_call(
        gather_body, [((planes, BLOCK, width), BF16)], [parts], after=[own_latent], name="plane_sum"
    )
    in_planes = lax.all_to_all(own_parts, "z", 0, 0)
    pair_sent, boundary, _ = lax.optimization_barrier((pair, boundary, own_parts))
    before = shifted(pair_sent, PLANE, 1, chips)
    after = shifted(pair_sent, PLANE, -1, chips)
    halo_before = shifted(boundary[LANES:], TILE, 1, tiles)
    halo_after = shifted(boundary[:LANES], TILE, -1, tiles)
    (own_edges,) = kernel_call(
        own_edges_body,
        [((edge_count, width), BF16)],
        [source, target, sender, receiver],
        after=[own_parts],
        scratch=[pltpu.VMEM((2 * count, width), BF16)],
        limit=32,
        flops=3_200_000_000,
        name="own_edges",
    )

    (results,) = kernel_call(
        coarse_body,
        [((chips, BLOCK, width), BF16)],
        [in_planes, own_latent, own_hidden, both, coarse_w3],
        after=[own_edges],
        name="coarse_update",
    )
    mine = lax.all_to_all(results, PLANE, 0, 0).reshape(half, width)
    edges, select, own_pick = kernel_call(
        functools.partial(rest_edges_body, mids),
        [((edge_count, width), BF16), ((edge_count, 2 * LANES), BF16), ((count, LANES), BF16)],
        [source, target, parent, halo_before, halo_after, edge_w_src, own_edges],
        after=[results],
        scratch=[pltpu.VMEM((2 * LANES, width), BF16), pltpu.VMEM((2 * count + 2 * LANES, 2 * LANES), BF16)],
        limit=32,
        flops=3_000_000_000,
        name="rest_edges",
    )
    theirs = swapped(mine)

    fine_out, mid_out, coarse_out = kernel_call(
        final_body,
        [((count, width), BF16), ((mids, width), BF16), ((coarse_count, width), BF16)],
        [mine, theirs, before, pair, after, edges, select, target, fine_latent, own_pick, node]
        + [w_descend, w_fine, edge_w_src, edge_w_dst, node_w1, edge_w2, node_w2, node_w3],
        scratch=[
            pltpu.VMEM((2 * half, width), BF16),
            pltpu.VMEM((6 * mids, wide), BF16),
            pltpu.VMEM((8 * mids, width), BF16),
            pltpu.VMEM((count, width), F32),
        ],
        limit=32,
        name="final",
    )
    return (fine_out, mid_out, coarse_out)


def solution(mesh):
    groups, tiles = mesh.shape["rhombus"], mesh.shape["tile"]
    side = {32: (4, 4), 8: (2, 2)}[tiles]
    physical = jax.sharding.Mesh(mesh.devices.reshape(groups, *side, 2), ("z", "y", "x", "c"))
    every = ("z", "y", "x", "c")
    split, copied = P(every), P()
    return jax.shard_map(
        on_device,
        mesh=physical,
        in_specs=(split, split, copied) + (split,) * 5 + (copied,) * 16,
        out_specs=(split, split, copied),
        check_vma=False,
    )
```

time: 99.9 us -> 110 us (1.10)
  the two profiles are of different devices: /device:TPU:1 before, /device:TPU:8 now
where the time goes in v2:
time: 110 us; the launch traced here: 109 us
  starting transfers between devices  47.6 us (43%)
  local copies, waits for them, and re-layouts  30.5 us (28%)
  Pallas kernels  22.5 us (20%)
  waiting for transfers between devices  7.02 us (6%)
    unnamed x98, local copies, waits for them, and re-layouts  28.7 us
    ppermute x6, starting transfers between devices, shifted(): return lax.ppermute(values, axis, pairs)  23.6 us
    pallas_call x9, Pallas kernels, kernel_call(): pl.pallas_call(kernel, out_shape=[jax.ShapeDtypeStruct(shape, dtype) for...  22.5 us
    all_to_all x1, starting transfers between devices, on_device(): in_planes = lax.all_to_all(own_parts, 'z', 0, 0)  8.46 us
    all_to_all x1, starting transfers between devices, on_device(): parts = lax.all_to_all(blocks, PLANE, 0, 0)  8.09 us
    all_to_all x1, starting transfers between devices, on_device(): mine = lax.all_to_all(results, PLANE, 0, 0).reshape(half, width)  7.23 us
    all_to_all x1, waiting for transfers between devices, on_device(): in_planes = lax.all_to_all(own_parts, 'z', 0, 0)  4.22 us
  transfers between devices with their start and end apart: 11, of which 3 were waited for; matrix products, arithmetic and copies ran while one was open for 2% of the time, Pallas kernels for 9%

profile of v2, /device:TPU:8, one launch (start us, length us, event | category | flops | bytes accessed | tf_op | source)
XLA Modules:
  0.0 108.6 jit_solution(13662525221707766355)
XLA Ops:
  2.6 1.9 %collective-permute-start = (bf16[32,512]{1,0:T(8,128)(2,1)S(1)}, bf16[32,512]{1,0:T(8,128)(2,1)S(1)}, u32[]{:S(2)}, u32[]{:S(2)}) collective-permute-start(bf16[32,512]{1,0:T(8,128)(2,1)S(1)} %get-tuple-element.21), channel_id=1, source_target_pairs={{0,1},{1,2},{2,3},{3,4},{4,5},{5,6},{6,7},{7,8},{8,9},{9,10},{10,1... | collective-permute-start | bytes 98312 | tf_op jit(solution)/shard_map/ppermute | solution.py:254
  4.5 5.8 %collective-permute-start.1 = (bf16[32,512]{1,0:T(8,128)(2,1)S(1)}, bf16[32,512]{1,0:T(8,128)(2,1)S(1)}, u32[]{:S(2)}, u32[]{:S(2)}) collective-permute-start(bf16[32,512]{1,0:T(8,128)(2,1)S(1)} %get-tuple-element.22), channel_id=1, source_target_pairs={{1,0},{2,1},{3,2},{4,3},{5,4},{6,5},{7,6},{8,7},{9,8},{10,9},{11,1... | collective-permute-start | bytes 98312 | tf_op jit(solution)/shard_map/ppermute | solution.py:254
  10.3 1.6 %collective-permute-done.1.refs_2_ = bf16[32,512]{1,0:T(8,128)(2,1)S(1)} collective-permute-done((bf16[32,512]{1,0:T(8,128)(2,1)S(1)}, bf16[32,512]{1,0:T(8,128)(2,1)S(1)}, u32[]{:S(2)}, u32[]{:S(2)}) %collective-permute-start.1) | collective-permute-done | bytes 32800 | tf_op jit(solution)/shard_map/ppermute | solution.py:254
  11.9 1.0 copy-done.7
  12.9 1.0 copy-done.8
  15.0 1.0 copy-done.10
  18.3 1.2 %collective-permute-done.2.refs_1_ = bf16[32,640]{1,0:T(8,128)(2,1)S(1)} collective-permute-done((bf16[32,640]{1,0:T(8,128)(2,1)S(1)}, bf16[32,640]{1,0:T(8,128)(2,1)S(1)}, u32[]{:S(2)}, u32[]{:S(2)}) %collective-permute-start.2) | collective-permute-done | bytes 40992 | tf_op jit(solution)/shard_map/ppermute | solution.py:258
  19.5 1.2 %coarse_blocks.1 = (bf16[64,640]{1,0:T(8,128)(2,1)S(1)}, bf16[384,512]{1,0:T(8,128)(2,1)}) custom-call(bf16[32,640]{1,0:T(8,128)(2,1)S(1)} %mid_update.1.refs_0_, bf16[32,640]{1,0:T(8,128)(2,1)S(1)} %collective-permute-done.2.refs_1_), custom_call_target="tpu_custom_call" | custom-call | bytes 1048576 | tf_op jit(solution)/shard_map/coarse_blocks/pallas_call | solution.py:27
  20.7 8.1 %all-to-all-start = ((bf16[16,24,512]{2,1,0:T(8,128)(2,1)}), bf16[16,24,512]{2,1,0:T(8,128)(2,1)}, u32[]{:S(2)}, u32[]{:S(2)}) async-start(bf16[16,24,512]{2,1,0:T(8,128)(2,1)} %bitcast.2.refs_10_), calls=%async_computation | async-start | bytes 786432 | tf_op jit(solution)/shard_map/all_to_all | solution.py:323
  29.8 1.0 copy-done.15
  30.9 1.0 copy-done.17
  31.9 1.1 %copy-done.38 = bf16[642,512]{1,0:T(8,128)(2,1)S(1)} copy-done((bf16[642,512]{1,0:T(8,128)(2,1)S(1)}, bf16[642,512]{1,0:T(8,128)(2,1)}, u32[]{:S(2)}) %copy-start.38) | copy-done | bytes 657432
  33.0 1.0 copy-done.39
  34.1 1.0 copy-done.40
  35.1 1.0 copy-done.41
  36.1 1.7 %tables.1 = (bf16[512,512]{1,0:T(8,128)(2,1)S(1)}, bf16[512,512]{1,0:T(8,128)(2,1)S(1)}, f32[512,512]{1,0:T(8,128)S(1)}, bf16[256,640]{1,0:T(8,128)(2,1)S(1)}, b...) custom-call(bf16[512,512]{1,0:T(8,128)(2,1)S(1)} %copy-done.1, ...), custom_call_target="tpu_custom_call" | custom-call | flops 2000000000 | bytes 1048576 | tf_op jit(solution)/shard_map/tables/pallas_call | solution.py:27
  42.0 1.8 %plane_sum.1.refs_4_ = bf16[8,24,512]{2,1,0:T(8,128)(2,1)} custom-call(bf16[16,24,512]{2,1,0:T(8,128)(2,1)} %all-to-all-done.refs_0_, bf16[24,512]{1,0:T(8,128)(2,1)S(1)} %get-tuple-element.24.refs_1_), custom_call_target="tpu_custom_call" | custom-call | bytes 1048576 | tf_op jit(solution)/shard_map/plane_sum/pallas_call | solution.py:27
  43.7 8.5 %all-to-all-start.1 = ((bf16[8,24,512]{2,1,0:T(8,128)(2,1)}), bf16[8,24,512]{2,1,0:T(8,128)(2,1)}, u32[]{:S(2)}, u32[]{:S(2)}) async-start(bf16[8,24,512]{2,1,0:T(8,128)(2,1)} %plane_sum.1.refs_4_), calls=%async_computation.1 | async-start | bytes 393216 | tf_op jit(solution)/shard_map/all_to_all | solution.py:344
  52.9 1.0 copy-done.46
  55.0 3.5 %own_edges.1.refs_5_.refs_6_ = bf16[3072,512]{1,0:T(8,128)(2,1)S(1)} custom-call(s32[24,128]{1,0:T(8,128)S(1)} %bitcast.16, s32[24,128]{1,0:T(8,128)S(1)} %bitcast.9, bf16[512,512]{1,0:T(8,128)(2,1)S(1)} %copy-done.46, bf16[512,512]{1,0:T(8,128)(2,1)S(1)} %copy-done.48, bf16[8,24,512]{2,1,0:T(8,128)(2,1)} %plane_sum.1.refs_4_), custom_call_target="tpu_custom_call" | custom-call | flops 3200000000 | bytes 1048576 | tf_op jit(solution)/shard_map/own_edges/pallas_call | solution.py:27
  58.5 4.2 %all-to-all-done.1.refs_0_ = bf16[8,24,512]{2,1,0:T(8,128)(2,1)} async-done(((bf16[8,24,512]{2,1,0:T(8,128)(2,1)}), bf16[8,24,512]{2,1,0:T(8,128)(2,1)}, u32[]{:S(2)}, u32[]{:S(2)}) %all-to-all-start.1) | async-done | bytes 196640 | tf_op jit(solution)/shard_map/all_to_all | solution.py:344
  62.7 1.0 copy-done.11
  63.8 1.0 copy-done.25
  66.3 1.4 %coarse_update.1.refs_7_ = bf16[16,24,512]{2,1,0:T(8,128)(2,1)S(1)} custom-call(bf16[8,24,512]{2,1,0:T(8,128)(2,1)} %all-to-all-done.1.refs_0_, bf16[24,512]{1,0:T(8,128)(2,1)S(1)} %copy-done.28, f32[24,512]{1,0:T(8,128)S(1)} %copy-done.32, bf16[512,512]{1,0:T(8,128)(2,1)S(1)} %copy-done.25, bf16[512,512]{1,0:T(8,128)(2,1)S(1)} %copy-done.11, ...), custom_call_target="tpu_custom_call" | custom-call | bytes 1048576 | tf_op jit(solution)/shard_map/coarse_update/pallas_call | solution.py:27
  68.5 7.2 %all-to-all-start.2 = ((bf16[16,24,512]{2,1,0:T(8,128)(2,1)}), bf16[16,24,512]{2,1,0:T(8,128)(2,1)S(1)}, u32[]{:S(2)}, u32[]{:S(2)}) async-start(bf16[16,24,512]{2,1,0:T(8,128)(2,1)} %copy-done.3), calls=%async_computation.2 | async-start | bytes 786432 | tf_op jit(solution)/shard_map/all_to_all | solution.py:368
  75.7 1.7 %fusion = (bf16[128,640]{1,0:T(8,128)(2,1)}, bf16[128,640]{1,0:T(8,128)(2,1)}) fusion(bf16[256,640]{1,0:T(8,128)(2,1)} %copy-done.26), kind=kLoop, calls=%fused_computation | loop fusion | bytes 655360 | tf_op jit(solution)/shard_map/slice | solution.py:349
  77.5 1.9 %collective-permute-start.6 = (bf16[128,640]{1,0:T(8,128)(2,1)}, bf16[128,640]{1,0:T(8,128)(2,1)}, u32[]{:S(2)}, u32[]{:S(2)}) collective-permute-start(bf16[128,640]{1,0:T(8,128)(2,1)} %get-tuple-element.38), channel_id=1, source_target_pairs={{0,1},{1,2},{2,3},{3,4},{4,5},{5,6},{6,7},{7,8},{8,9},{9,10},{10,1... | collective-permute-start | bytes 491528 | tf_op jit(solution)/shard_map/ppermute | solution.py:254
  79.4 5.8 %collective-permute-start.7 = (bf16[128,640]{1,0:T(8,128)(2,1)}, bf16[128,640]{1,0:T(8,128)(2,1)}, u32[]{:S(2)}, u32[]{:S(2)}) collective-permute-start(bf16[128,640]{1,0:T(8,128)(2,1)} %get-tuple-element.37), channel_id=1, source_target_pairs={{1,0},{2,1},{3,2},{4,3},{5,4},{6,5},{7,6},{8,7},{9,8},{10,9},{11,1... | collective-permute-start | bytes 491528 | tf_op jit(solution)/shard_map/ppermute | solution.py:254
  85.3 2.1 %collective-permute-start.4 = (bf16[64,640]{1,0:T(8,128)(2,1)}, bf16[64,640]{1,0:T(8,128)(2,1)S(1)}, u32[]{:S(2)}, u32[]{:S(2)}) collective-permute-start(bf16[64,640]{1,0:T(8,128)(2,1)} %copy-done.29), channel_id=1, source_target_pairs={{0,2},{2,4},{4,6},{6,8},{8,10},{10,12},{12,14},{14,16},{16,18},{18... | collective-permute-start | bytes 245768 | tf_op jit(solution)/shard_map/ppermute | solution.py:254
  87.3 6.2 %collective-permute-start.5 = (bf16[64,640]{1,0:T(8,128)(2,1)}, bf16[64,640]{1,0:T(8,128)(2,1)S(1)}, u32[]{:S(2)}, u32[]{:S(2)}) collective-permute-start(bf16[64,640]{1,0:T(8,128)(2,1)} %copy-done.29), channel_id=1, source_target_pairs={{2,0},{4,2},{6,4},{8,6},{10,8},{12,10},{14,12},{16,14},{18,16},{20... | collective-permute-start | bytes 245768 | tf_op jit(solution)/shard_map/ppermute | solution.py:254
  96.4 4.8 %rest_edges.1 = (bf16[3072,512]{1,0:T(8,128)(2,1)S(1)}, bf16[3072,256]{1,0:T(8,128)(2,1)S(1)}, bf16[512,128]{1,0:T(8,128)(2,1)S(1)}) custom-call(s32[24,128]{1,0:T(8,128)S(1)} %bitcast.17, s32[24,128]{1,0:T(8,128)S(1)} %bitcast.10, s32[4,128]{1,0:T(4,128)S(1)} %bitcast.14, bf16[128,640]{1,0:T(8,128)(2,1)} %collective-permute-done.6.refs_3_, ...), custom_call_target="tpu_custom_call" | custom-call | flops 3000000000 | bytes 1048576 | tf_op jit(solution)/shard_map/rest_edges/pallas_call | solution.py:27
  101.3 7.3 %final.1 = (bf16[512,512]{1,0:T(8,128)(2,1)}, bf16[32,512]{1,0:T(8,128)(2,1)}, bf16[642,512]{1,0:T(8,128)(2,1)}) custom-call(bf16[384,512]{1,0:T(8,128)(2,1)S(1)} %bitcast.8, bf16[384,512]{1,0:T(8,128)(2,1)S(1)} %collective-permute-done.3.refs_1_, bf16[64,640]{1,0:T(8,128)(2,1)S(1)} %collective-permute-done.4.refs_2_, bf16[64,640]{1,0:T(8,128)(2,1)S(1)} %copy-done.30, ...), custom_call_target="tpu_custom_call" | custom-call | bytes 1048576 | tf_op jit(solution)/shard_map/final/pallas_call | solution.py:27
  (98 shorter events, 17.3 us)
Async XLA Ops:
  0.6 28.1 %copy-start.44 = (s32[256]{0:T(256)S(1)}, s32[256]{0:T(256)}, u32[]{:S(2)}) copy-start(s32[256]{0:T(256)} %param.29) | copy-start | bytes 3076
  0.6 1.0 copy-start
  2.4 26.4 %copy-start.1 = (bf16[512,512]{1,0:T(8,128)(2,1)S(1)}, bf16[512,512]{1,0:T(8,128)(2,1)}, u32[]{:S(2)}) copy-start(bf16[512,512]{1,0:T(8,128)(2,1)} %refs_8_.5) | copy-start | bytes 1572868
  2.4 26.4 %copy-start.36 = (s32[512]{0:T(512)S(1)}, s32[512]{0:T(512)}, u32[]{:S(2)}) copy-start(s32[512]{0:T(512)} %param.27) | copy-start | bytes 6148
  2.6 7.7 %collective-permute-start = (bf16[32,512]{1,0:T(8,128)(2,1)S(1)}, bf16[32,512]{1,0:T(8,128)(2,1)S(1)}, u32[]{:S(2)}, u32[]{:S(2)}) collective-permute-start(bf16[32,512]{1,0:T(8,128)(2,1)S(1)} %get-tuple-element.21), channel_id=1, source_target_pairs={{0,1},{1,2},{2,3},{3,4},{4,5},{5,6},{6,7},{7,8},{8,9},{9,10},{10,1... | collective-permute-start | bytes 98312 | tf_op jit(solution)/shard_map/ppermute | solution.py:254
  4.5 7.3 %collective-permute-start.1 = (bf16[32,512]{1,0:T(8,128)(2,1)S(1)}, bf16[32,512]{1,0:T(8,128)(2,1)S(1)}, u32[]{:S(2)}, u32[]{:S(2)}) collective-permute-start(bf16[32,512]{1,0:T(8,128)(2,1)S(1)} %get-tuple-element.22), channel_id=1, source_target_pairs={{1,0},{2,1},{3,2},{4,3},{5,4},{6,5},{7,6},{8,7},{9,8},{10,9},{11,1... | collective-permute-start | bytes 98312 | tf_op jit(solution)/shard_map/ppermute | solution.py:254
  18.2 1.3 %collective-permute-start.2 = (bf16[32,640]{1,0:T(8,128)(2,1)S(1)}, bf16[32,640]{1,0:T(8,128)(2,1)S(1)}, u32[]{:S(2)}, u32[]{:S(2)}) collective-permute-start(bf16[32,640]{1,0:T(8,128)(2,1)S(1)} %mid_update.1.refs_0_), channel_id=1, source_target_pairs={{0,1},{1,0},{2,3},{3,2},{4,5},{5,4},{6,7},{7,6},{8,9},{9,8},{10,11... | collective-permute-start | bytes 122888 | tf_op jit(solution)/shard_map/ppermute | solution.py:258
  20.7 8.1 %copy-start.29 = (bf16[64,640]{1,0:T(8,128)(2,1)}, bf16[64,640]{1,0:T(8,128)(2,1)S(1)}, u32[]{:S(2)}) copy-start(bf16[64,640]{1,0:T(8,128)(2,1)S(1)} %get-tuple-element.31.refs_3_) | copy-start | bytes 245764
  20.7 21.3 %all-to-all-start = ((bf16[16,24,512]{2,1,0:T(8,128)(2,1)}), bf16[16,24,512]{2,1,0:T(8,128)(2,1)}, u32[]{:S(2)}, u32[]{:S(2)}) async-start(bf16[16,24,512]{2,1,0:T(8,128)(2,1)} %bitcast.2.refs_10_), calls=%async_computation | async-start | bytes 786432 | tf_op jit(solution)/shard_map/all_to_all | solution.py:323
  28.8 1.0 copy-start.12
  31.9 1.1 %copy-start.38 = (bf16[642,512]{1,0:T(8,128)(2,1)S(1)}, bf16[642,512]{1,0:T(8,128)(2,1)}, u32[]{:S(2)}) copy-start(bf16[642,512]{1,0:T(8,128)(2,1)} %refs_3_.3) | copy-start | bytes 1972228
  36.1 16.1 %copy-start.34 = (s32[3072]{0:T(1024)S(1)}, s32[3072]{0:T(1024)}, u32[]{:S(2)}) copy-start(s32[3072]{0:T(1024)} %param.31) | copy-start | bytes 36868
  42.0 10.2 %copy-start.27 = (bf16[24,512]{1,0:T(8,128)(2,1)}, bf16[24,512]{1,0:T(8,128)(2,1)S(1)}, u32[]{:S(2)}) copy-start(bf16[24,512]{1,0:T(8,128)(2,1)S(1)} %get-tuple-element.24.refs_1_) | copy-start | bytes 73732
  42.0 10.2 %copy-start.31 = (f32[24,512]{1,0:T(8,128)}, f32[24,512]{1,0:T(8,128)S(1)}, u32[]{:S(2)}) copy-start(f32[24,512]{1,0:T(8,128)S(1)} %get-tuple-element.25.refs_2_) | copy-start | bytes 147460
  43.7 19.0 %all-to-all-start.1 = ((bf16[8,24,512]{2,1,0:T(8,128)(2,1)}), bf16[8,24,512]{2,1,0:T(8,128)(2,1)}, u32[]{:S(2)}, u32[]{:S(2)}) async-start(bf16[8,24,512]{2,1,0:T(8,128)(2,1)} %plane_sum.1.refs_4_), calls=%async_computation.1 | async-start | bytes 393216 | tf_op jit(solution)/shard_map/all_to_all | solution.py:344
  68.5 16.6 %all-to-all-start.2 = ((bf16[16,24,512]{2,1,0:T(8,128)(2,1)}), bf16[16,24,512]{2,1,0:T(8,128)(2,1)S(1)}, u32[]{:S(2)}, u32[]{:S(2)}) async-start(bf16[16,24,512]{2,1,0:T(8,128)(2,1)} %copy-done.3), calls=%async_computation.2 | async-start | bytes 786432 | tf_op jit(solution)/shard_map/all_to_all | solution.py:368
  77.5 16.1 %collective-permute-start.6 = (bf16[128,640]{1,0:T(8,128)(2,1)}, bf16[128,640]{1,0:T(8,128)(2,1)}, u32[]{:S(2)}, u32[]{:S(2)}) collective-permute-start(bf16[128,640]{1,0:T(8,128)(2,1)} %get-tuple-element.38), channel_id=1, source_target_pairs={{0,1},{1,2},{2,3},{3,4},{4,5},{5,6},{6,7},{7,8},{8,9},{9,10},{10,1... | collective-permute-start | bytes 491528 | tf_op jit(solution)/shard_map/ppermute | solution.py:254
  79.4 14.2 %collective-permute-start.7 = (bf16[128,640]{1,0:T(8,128)(2,1)}, bf16[128,640]{1,0:T(8,128)(2,1)}, u32[]{:S(2)}, u32[]{:S(2)}) collective-permute-start(bf16[128,640]{1,0:T(8,128)(2,1)} %get-tuple-element.37), channel_id=1, source_target_pairs={{1,0},{2,1},{3,2},{4,3},{5,4},{6,5},{7,6},{8,7},{9,8},{10,9},{11,1... | collective-permute-start | bytes 491528 | tf_op jit(solution)/shard_map/ppermute | solution.py:254
  85.2 16.0 %copy-start.2 = (bf16[512,512]{1,0:T(8,128)(2,1)S(1)}, bf16[512,512]{1,0:T(8,128)(2,1)}, u32[]{:S(2)}) copy-start(bf16[512,512]{1,0:T(8,128)(2,1)} %refs_8_.5) | copy-start | bytes 1572868
  85.2 16.0 %collective-permute-start.3 = (bf16[384,512]{1,0:T(8,128)(2,1)S(1)}, bf16[384,512]{1,0:T(8,128)(2,1)S(1)}, u32[]{:S(2)}, u32[]{:S(2)}) collective-permute-start(bf16[384,512]{1,0:T(8,128)(2,1)S(1)} %bitcast.7), channel_id=1, source_target_pairs={{0,1},{1,0},{2,3},{3,2},{4,5},{5,4},{6,7},{7,6},{8,9},{9,8},{10,11... | collective-permute-start | bytes 1179656 | tf_op jit(solution)/shard_map/ppermute | solution.py:258
  85.3 15.9 %collective-permute-start.4 = (bf16[64,640]{1,0:T(8,128)(2,1)}, bf16[64,640]{1,0:T(8,128)(2,1)S(1)}, u32[]{:S(2)}, u32[]{:S(2)}) collective-permute-start(bf16[64,640]{1,0:T(8,128)(2,1)} %copy-done.29), channel_id=1, source_target_pairs={{0,2},{2,4},{4,6},{6,8},{8,10},{10,12},{12,14},{14,16},{16,18},{18... | collective-permute-start | bytes 245768 | tf_op jit(solution)/shard_map/ppermute | solution.py:254
  87.3 13.9 %collective-permute-start.5 = (bf16[64,640]{1,0:T(8,128)(2,1)}, bf16[64,640]{1,0:T(8,128)(2,1)S(1)}, u32[]{:S(2)}, u32[]{:S(2)}) collective-permute-start(bf16[64,640]{1,0:T(8,128)(2,1)} %copy-done.29), channel_id=1, source_target_pairs={{2,0},{4,2},{6,4},{8,6},{10,8},{12,10},{14,12},{16,14},{18,16},{20... | collective-permute-start | bytes 245768 | tf_op jit(solution)/shard_map/ppermute | solution.py:254
  96.3 4.9 %copy-start.6 = (f32[512,512]{1,0:T(8,128)S(1)}, f32[512,512]{1,0:T(8,128)}, u32[]{:S(2)}) copy-start(f32[512,512]{1,0:T(8,128)} %copy-done.5) | copy-start | bytes 3145732
  96.3 4.9 %copy-start.14 = (bf16[512,512]{1,0:T(8,128)(2,1)S(1)}, bf16[512,512]{1,0:T(8,128)(2,1)}, u32[]{:S(2)}) copy-start(bf16[512,512]{1,0:T(8,128)(2,1)} %refs_13_.1) | copy-start | bytes 1572868
  96.3 4.9 %copy-start.16 = (bf16[512,512]{1,0:T(8,128)(2,1)S(1)}, bf16[512,512]{1,0:T(8,128)(2,1)}, u32[]{:S(2)}) copy-start(bf16[512,512]{1,0:T(8,128)(2,1)} %refs_14_.1) | copy-start | bytes 1572868
  96.3 4.9 %copy-start.18 = (bf16[512,512]{1,0:T(8,128)(2,1)S(1)}, bf16[512,512]{1,0:T(8,128)(2,1)}, u32[]{:S(2)}) copy-start(bf16[512,512]{1,0:T(8,128)(2,1)} %refs_15_.1) | copy-start | bytes 1572868
  96.3 4.9 %copy-start.19 = (bf16[512,512]{1,0:T(8,128)(2,1)S(1)}, bf16[512,512]{1,0:T(8,128)(2,1)}, u32[]{:S(2)}) copy-start(bf16[512,512]{1,0:T(8,128)(2,1)} %refs_11_.1) | copy-start | bytes 1572868
  96.3 4.9 %copy-start.20 = (bf16[512,512]{1,0:T(8,128)(2,1)S(1)}, bf16[512,512]{1,0:T(8,128)(2,1)}, u32[]{:S(2)}) copy-start(bf16[512,512]{1,0:T(8,128)(2,1)} %refs_12_.1) | copy-start | bytes 1572868
  96.4 4.9 %copy-start.21 = (bf16[512,512]{1,0:T(8,128)(2,1)S(1)}, bf16[512,512]{1,0:T(8,128)(2,1)}, u32[]{:S(2)}) copy-start(bf16[512,512]{1,0:T(8,128)(2,1)} %refs_16_.1) | copy-start | bytes 1572868
  96.4 4.9 %copy-start.22 = (bf16[512,512]{1,0:T(8,128)(2,1)S(1)}, bf16[512,512]{1,0:T(8,128)(2,1)}, u32[]{:S(2)}) copy-start(bf16[512,512]{1,0:T(8,128)(2,1)} %refs_17_.1) | copy-start | bytes 1572868
  96.4 4.9 %copy-start.23 = (bf16[512,512]{1,0:T(8,128)(2,1)S(1)}, bf16[512,512]{1,0:T(8,128)(2,1)}, u32[]{:S(2)}) copy-start(bf16[512,512]{1,0:T(8,128)(2,1)} %refs_18_.1) | copy-start | bytes 1572868
  96.4 4.9 %copy-start.30 = (bf16[64,640]{1,0:T(8,128)(2,1)S(1)}, bf16[64,640]{1,0:T(8,128)(2,1)}, u32[]{:S(2)}) copy-start(bf16[64,640]{1,0:T(8,128)(2,1)} %copy-done.29) | copy-start | bytes 245764
  (28 other events, 25.5 us)

commit v3 on v2

--- a/solution.py
+++ b/solution.py
@@ -15,25 +15,61 @@
 TILE = ("y", "x", "c")
 F32, BF16, I32 = jnp.float32, jnp.bfloat16, jnp.int32
 VMEM = pl.BlockSpec(memory_space=pltpu.VMEM)
+STORED = pl.BlockSpec(memory_space=pltpu.HBM)
 UNREAD = pl.BlockSpec(memory_space=pl.ANY)
 
 
-def kernel_call(body, outs, operands, after=(), scratch=(), limit=24, flops=0, name=None):
-    count, skipped = len(operands), len(after)
+class Copied:
+    def __init__(self, source, target, semaphore):
+        self.copy = pltpu.make_async_copy(source, target, semaphore)
+        self.target, self.waiting = target, True
+        self.copy.start()
+
+    def get(self):
+        if self.waiting:
+            self.copy.wait()
+            self.waiting = False
+        return self.target
+
+    def __getitem__(self, index):
+        return self.get()[index]
+
+    @property
+    def shape(self):
+        return self.target.shape
+
+
+def kernel_call(body, outs, operands, stored=(), after=(), scratch=(), keep=(), limit=8, flops=0, name=None):
+    count, held, skipped, given = len(operands), len(stored), len(after), len(outs)
+    target = dict(keep)
 
     def kernel(*refs):
-        body(*refs[:count], *refs[count + skipped :])
-
+        inputs, refs = refs[:count], refs[count:]
+        sources, refs = refs[:held], refs[held + skipped :]
+        results, refs = refs[:given], refs[given:]
+        own, refs = refs[: len(scratch)], refs[len(scratch) :]
+        buffers = iter(refs)
+        places = [results[target[i]] if i in target else next(buffers) for i in range(held)]
+        semaphores = next(buffers) if held else None
+        copies = [Copied(sources[i], places[i], semaphores.at[i]) for i in range(held)]
+        fresh = [results[o] for o in range(given) if o not in target.values()]
+        body(*inputs, *copies, *fresh, *own)
+        for copy in copies:
+            copy.get()
+
+    buffers = [pltpu.VMEM(stored[i].shape, stored[i].dtype) for i in range(held) if i not in target]
+    if held:
+        buffers.append(pltpu.SemaphoreType.DMA((held,)))
     return pl.pallas_call(
         kernel,
-        out_shape=[jax.ShapeDtypeStruct(shape, dtype) for shape, dtype in outs],
-        in_specs=[VMEM] * count + [UNREAD] * skipped,
-        out_specs=[VMEM] * len(outs),
-        scratch_shapes=list(scratch),
+        out_shape=outs,
+        in_specs=[VMEM] * count + [STORED] * held + [UNREAD] * skipped,
+        out_specs=[VMEM] * given,
+        scratch_shapes=[*scratch, *buffers],
         compiler_params=pltpu.CompilerParams(vmem_limit_bytes=limit << 20),
         cost_estimate=pl.CostEstimate(flops=flops, bytes_accessed=1 << 20, transcendentals=0),
         name=name,
-    )(*operands, *after)
+    )(*operands, *[pltpu.with_memory_space_constraint(array, pltpu.HBM) for array in stored], *after)
 
 
 def product(left, right):
@@ -77,16 +113,24 @@
     up[...] = sums[2 * count :].astype(BF16)
 
 
-def mid_body(own, before, after, latent, ids, w_child, first, second, third, out):
-    count, width = latent.shape
-    total = own[...] + before[...].astype(F32) + after[...].astype(F32)
-    incoming = product(total.astype(BF16), w_child[...]).astype(BF16)
-    hidden = silu(product(latent[...], first[...]) + product(incoming, second[...]))
-    out[:, :width] = updated(latent[...], hidden, third[...])
+def mid_ready_body(latent, ids, first, w_child, second, third, kept, hidden, labels):
+    count = hidden.shape[0]
     spread_ids = spread(jnp.concatenate([ids[...], jnp.zeros((1, LANES - count), I32)], axis=1))[:count]
     place = lanes(count)
     label = jnp.where(place == 0, spread_ids >> 5, jnp.where(place == 1, spread_ids & 31, 0))
-    out[:, width:] = label.astype(F32).astype(BF16)
+    labels[...] = label.astype(F32).astype(BF16)
+    values = latent[...]
+    kept[...] = values
+    hidden[...] = product(values, first[...])
+
+
+def mid_body(own, before, after, latent, hidden, labels, w_child, second, third, out):
+    width = latent.shape[1]
+    total = own[...] + before[...].astype(F32) + after[...].astype(F32)
+    incoming = product(total.astype(BF16), w_child[...]).astype(BF16)
+    value = silu(hidden[...] + product(incoming, second[...]))
+    out[:, :width] = updated(latent[...], value, third[...])
+    out[:, width:] = labels[...]
 
 
 def row_ids(labelled, width):
@@ -108,60 +152,59 @@
     ).astype(BF16)
 
 
-def tables_body(
-    fine, parent, halo, coarse, w_src, w_dst, w_node, w_coarse, coarse_w1, coarse_w2,
-    sender, receiver, node, boundary, both, own_latent, own_hidden,
-):
+def tables_body(parent, halo, fine, w_src, w_dst, w_node, sender, receiver, node, down, up, token):
+    token[...] = jnp.zeros_like(token)
     count, width = fine.shape
     blocks = count // LANES
     values = fine[...]
+    codes = [(spread(parent[r : r + 1, :]) + 1).astype(F32).astype(BF16) for r in range(blocks)]
+    codes = jnp.concatenate(codes, axis=0)
+    for r, out in enumerate((down, up)):
+        picked = jnp.concatenate(picks(spread(halo[r : r + 1, :]), 0, blocks), axis=1)
+        out[:, :width] = product(picked, values).astype(BF16)
+        out[:, width:] = product(picked, codes).astype(BF16)
     sender[...] = product(values, w_src[...]).astype(BF16)
     receiver[...] = product(values, w_dst[...]).astype(BF16)
     node[...] = product(values, w_node[...])
-    codes = [(spread(parent[r : r + 1, :]) + 1).astype(F32).astype(BF16) for r in range(blocks)]
-    codes = jnp.concatenate(codes, axis=0)
-    for r in range(halo.shape[0]):
-        picked = jnp.concatenate(picks(spread(halo[r : r + 1, :]), 0, blocks), axis=1)
-        boundary[r * LANES : (r + 1) * LANES, :width] = product(picked, values).astype(BF16)
-        boundary[r * LANES : (r + 1) * LANES, width:] = product(picked, codes).astype(BF16)
-    both[...] = product(w_coarse[...], coarse_w2[...]).astype(BF16)
+
+
+def gather_body(parts, out):
+    total = jnp.sum(parts[...].astype(F32), axis=0).astype(BF16)
+    for i in range(out.shape[0]):
+        out[i] = total
+
+
+def coarse_body(parts, own_latent, own_hidden, both, third, out):
+    total = jnp.sum(parts[...].astype(F32), axis=0).astype(BF16)
+    hidden = silu(own_hidden[...] + product(total, both[...]))
+    result = updated(own_latent[...], hidden, third[...])
+    for i in range(out.shape[0]):
+        out[i] = result
+
+
+def own_edges_body(
+    source, target, sender, receiver, coarse, coarse_w1, w_coarse, coarse_w2, third, out, both, own_latent, own_hidden
+):
+    count = sender.shape[0]
+    blocks = count // LANES
+    sent, received = sender[...], receiver[...]
+    for k in range(out.shape[0] // CHUNK):
+        marks = range(k * CHUNK // LANES, (k + 1) * CHUNK // LANES)
+        picked = [jnp.concatenate(picks(spread(source[r : r + 1, :]), 0, blocks), axis=1) for r in marks]
+        total = product(jnp.concatenate(picked, axis=0), sent)
+        picked = [jnp.concatenate(picks(spread(target[r : r + 1, :]), 0, blocks), axis=1) for r in marks]
+        total += product(jnp.concatenate(picked, axis=0), received)
+        out[k * CHUNK : (k + 1) * CHUNK, :] = total.astype(BF16)
     rows, total = own_latent.shape[0], coarse.shape[0]
+    chips = lax.axis_size("y") * lax.axis_size("x")
     chip = lax.axis_index("y") * lax.axis_size("x") + lax.axis_index("x")
-    chips = lax.axis_size("y") * lax.axis_size("x")
     first = (lax.axis_index("c") * chips + chip) * rows
     place = lax.broadcasted_iota(I32, (rows, total), 0) + first
     picked = hot(place == lax.broadcasted_iota(I32, (rows, total), 1))
     latent = product(picked, coarse[...]).astype(BF16)
     own_latent[...] = latent
     own_hidden[...] = product(latent, coarse_w1[...])
-
-
-def gather_body(parts, out):
-    total = jnp.sum(parts[...].astype(F32), axis=0).astype(BF16)
-    for i in range(out.shape[0]):
-        out[i] = total
-
-
-def coarse_body(parts, own_latent, own_hidden, both, third, out):
-    total = jnp.sum(parts[...].astype(F32), axis=0).astype(BF16)
-    hidden = silu(own_hidden[...] + product(total, both[...]))
-    result = updated(own_latent[...], hidden, third[...])
-    for i in range(out.shape[0]):
-        out[i] = result
-
-
-def own_edges_body(source, target, sender, receiver, out, table):
-    count = sender.shape[0]
-    table[:count] = sender[...]
-    table[count:] = receiver[...]
-    for k in range(out.shape[0] // CHUNK):
-        rows = []
-        for r in range(k * CHUNK // LANES, (k + 1) * CHUNK // LANES):
-            row = picks(spread(source[r : r + 1, :]), 0, count // LANES)
-            row += picks(spread(target[r : r + 1, :]), 0, count // LANES)
-            rows.append(jnp.concatenate(row, axis=1))
-        picked = jnp.concatenate(rows, axis=0)
-        out[k * CHUNK : (k + 1) * CHUNK, :] = product(picked, table[...]).astype(BF16)
+    both[...] = product(w_coarse[...], coarse_w2[...]).astype(BF16)
 
 
 def slots(codes, tile, count):
@@ -171,7 +214,10 @@
     return jnp.where(codes > 0, (tile + away) * count + (parent & (count - 1)), -1)
 
 
-def rest_edges_body(mid_count, source, target, parent, before, after, w_src, first, out, select, own_pick, table, where):
+def rest_edges_body(
+    mid_count, first, source, target, parent, before, after, w_src, out, select, own_pick, token, table, where
+):
+    token[...] = jnp.zeros_like(token)
     count = own_pick.shape[0]
     width = out.shape[1]
     blocks = count // LANES
@@ -203,26 +249,29 @@
         out[here, :] = (first[here, :].astype(F32) + rest).astype(BF16)
 
 
+def ready_body(rows, before, pair, after, w_descend, w_fine, w_src, w_dst, middle, picked, window):
+    two = pair.shape[0]
+    count, width = two // 2, middle.shape[1]
+    window[:two] = before[...]
+    window[two : 2 * two] = pair[...]
+    window[2 * two :] = after[...]
+    near = window[pl.ds(pl.multiple_of(lax.axis_index("c") * count, count), 5 * count), :]
+    middle[...] = near[:, :width]
+    picked[...] = hot(row_ids(near, width) == lax.broadcasted_iota(I32, (5 * count, rows), 1))
+
+
 def final_body(
-    mine, theirs, before, pair, after, edges, select, target, fine, own_pick, node,
-    w_descend, w_fine, w_src, w_dst, w_node, edge_w2, node_w2, node_w3,
-    fine_out, mid_out, coarse_out, coarse, window, table, sums,
+    mine, theirs, w_descend, w_fine, w_src, w_dst, near, picked, target, select, edges, edge_w2, own_pick, fine,
+    w_node, node, node_w2, node_w3, fine_out, mid_out, coarse_out, coarse, table, sums,
 ):
     core = lax.axis_index("c")
     half, width = mine.shape
-    two = pair.shape[0]
-    count = two // 2
+    count = near.shape[0] // 5
     coarse[pl.ds(pl.multiple_of(core * half, half), half), :] = mine[...]
     coarse[pl.ds(pl.multiple_of((1 - core) * half, half), half), :] = theirs[...]
-    window[:two] = before[...]
-    window[two : 2 * two] = pair[...]
-    window[2 * two :] = after[...]
-    near = window[pl.ds(pl.multiple_of(core * count, count), 5 * count), :]
-    columns = lax.broadcasted_iota(I32, (5 * count, 2 * half), 1)
-    picked = hot(row_ids(near, width) == columns)
-    parents = product(picked, coarse[...]).astype(BF16)
+    parents = product(picked[...], coarse[...]).astype(BF16)
     down = product(parents, w_descend[...]).astype(BF16)
-    middle = (near[:, :width].astype(F32) + down.astype(F32)).astype(BF16)
+    middle = (near[...].astype(F32) + down.astype(F32)).astype(BF16)
     mid_out[...] = middle[2 * count : 3 * count]
     fine_down = product(middle, w_fine[...]).astype(BF16)
     closer = fine_down[count : 4 * count]
@@ -297,99 +346,134 @@
     target = edge_target.reshape(-1, LANES)
     halo = halo_rows.reshape(-1, LANES)
 
+    def near(*shape, dtype=BF16):
+        return pltpu.VMEM(shape, dtype)
+
+    def far(*shape, dtype=BF16):
+        return pltpu.HBM(shape, dtype)
+
+    def here(array):
+        return pltpu.with_memory_space_constraint(array, pltpu.VMEM)
+
+    def free(*shape, dtype=BF16):
+        return jax.ShapeDtypeStruct(shape, dtype)
+
+    square = near(width, width)
     own, up, down = kernel_call(
         sums_body,
-        [((mids, width), F32), ((mids, width), BF16), ((mids, width), BF16)],
-        [parent, fine_latent],
+        [near(mids, width, dtype=F32), free(mids, width), free(mids, width)],
+        [],
+        stored=[parent, fine_latent],
         name="child_sums",
     )
     from_before = shifted(up, TILE, 1, tiles)
     from_after = shifted(down, TILE, -1, tiles)
+    w_child, mid_w2, mid_w3, kept, hidden, labels = kernel_call(
+        mid_ready_body,
+        [square, square, square, near(mids, width), near(mids, width, dtype=F32), near(mids, LANES)],
+        [],
+        stored=[mid_latent, mid_parent[None], mid_w1, w_child, mid_w2, mid_w3],
+        keep=[(3, 0), (4, 1), (5, 2)],
+        after=[own],
+        flops=1_000_000_000,
+        name="mid_ready",
+    )
     (labelled,) = kernel_call(
         mid_body,
-        [((mids, wide), BF16)],
-        [own, from_before, from_after, mid_latent, mid_parent[None], w_child, mid_w1, mid_w2, mid_w3],
+        [free(mids, wide)],
+        [here(own), from_before, from_after] + [here(a) for a in (kept, hidden, labels, w_child, mid_w2, mid_w3)],
         name="mid_update",
     )
     other = swapped(labelled)
     pair, blocks = kernel_call(
         blocks_body,
-        [((2 * mids, wide), BF16), ((half, width), BF16)],
+        [free(2 * mids, wide), near(half, width)],
         [labelled, other],
         name="coarse_blocks",
     )
 
     blocks = blocks.reshape(chips, BLOCK, width)
     parts = lax.all_to_all(blocks, PLANE, 0, 0)
-    sender, receiver, node, boundary, both, own_latent, own_hidden = kernel_call(
+    before = shifted(pair, PLANE, 1, chips)
+    after = shifted(pair, PLANE, -1, chips)
+    sender, receiver, node, halo_down, halo_up, token = kernel_call(
         tables_body,
-        [
-            ((count, width), BF16),
-            ((count, width), BF16),
-            ((count, width), F32),
-            ((2 * LANES, wide), BF16),
-            ((width, width), BF16),
-            ((BLOCK, width), BF16),
-            ((BLOCK, width), F32),
-        ],
-        [fine_latent, parent, halo, coarse_latent, edge_w_src, edge_w_dst, node_w1, w_coarse, coarse_w1, coarse_w2],
+        [far(count, width), far(count, width), far(count, width, dtype=F32), free(LANES, wide), free(LANES, wide), free(8, LANES)],
+        [],
+        stored=[parent, halo, fine_latent, edge_w_src, edge_w_dst, node_w1],
         after=[blocks],
+        limit=12,
         flops=2_000_000_000,
         name="tables",
     )
 
     (own_parts,) = kernel_call(
-        gather_body, [((planes, BLOCK, width), BF16)], [parts], after=[own_latent], name="plane_sum"
+        gather_body,
+        [near(planes, BLOCK, width)],
+        [parts],
+        after=[token, before, after],
+        name="plane_sum",
     )
     in_planes = lax.all_to_all(own_parts, "z", 0, 0)
-    pair_sent, boundary, _ = lax.optimization_barrier((pair, boundary, own_parts))
-    before = shifted(pair_sent, PLANE, 1, chips)
-    after = shifted(pair_sent, PLANE, -1, chips)
-    halo_before = shifted(boundary[LANES:], TILE, 1, tiles)
-    halo_after = shifted(boundary[:LANES], TILE, -1, tiles)
-    (own_edges,) = kernel_call(
+    halo_down, halo_up, _ = lax.optimization_barrier((halo_down, halo_up, own_parts))
+    halo_before = shifted(halo_up, TILE, 1, tiles)
+    halo_after = shifted(halo_down, TILE, -1, tiles)
+    coarse_w3, own_edges, both, own_latent, own_hidden = kernel_call(
         own_edges_body,
-        [((edge_count, width), BF16)],
-        [source, target, sender, receiver],
+        [square, far(edge_count, width), square, near(BLOCK, width), near(BLOCK, width, dtype=F32)],
+        [],
+        stored=[source, target, sender, receiver, coarse_latent, coarse_w1, w_coarse, coarse_w2, coarse_w3],
+        keep=[(8, 0)],
         after=[own_parts],
-        scratch=[pltpu.VMEM((2 * count, width), BF16)],
-        limit=32,
-        flops=3_200_000_000,
+        limit=16,
+        flops=3_500_000_000,
         name="own_edges",
     )
 
     (results,) = kernel_call(
         coarse_body,
-        [((chips, BLOCK, width), BF16)],
-        [in_planes, own_latent, own_hidden, both, coarse_w3],
-        after=[own_edges],
+        [near(chips, BLOCK, width)],
+        [in_planes] + [here(a) for a in (own_latent, own_hidden, both, coarse_w3)],
+        after=[halo_before, halo_after],
         name="coarse_update",
     )
     mine = lax.all_to_all(results, PLANE, 0, 0).reshape(half, width)
-    edges, select, own_pick = kernel_call(
+    edges, select, own_pick, token = kernel_call(
         functools.partial(rest_edges_body, mids),
-        [((edge_count, width), BF16), ((edge_count, 2 * LANES), BF16), ((count, LANES), BF16)],
-        [source, target, parent, halo_before, halo_after, edge_w_src, own_edges],
+        [far(edge_count, width), far(edge_count, 2 * LANES), far(count, LANES), free(8, LANES)],
+        [],
+        stored=[own_edges, source, target, parent, halo_before, halo_after, edge_w_src],
         after=[results],
         scratch=[pltpu.VMEM((2 * LANES, width), BF16), pltpu.VMEM((2 * count + 2 * LANES, 2 * LANES), BF16)],
-        limit=32,
-        flops=3_000_000_000,
+        limit=24,
+        flops=3_500_000_000,
         name="rest_edges",
     )
+    mine, own_pick = lax.optimization_barrier((mine, own_pick))
     theirs = swapped(mine)
+    w_descend, w_fine, w_src, w_dst, middle, picked = kernel_call(
+        functools.partial(ready_body, 2 * half),
+        [square] * 4 + [near(5 * mids, width), near(5 * mids, 2 * half)],
+        [],
+        stored=[before, pair, after, w_descend, w_fine, edge_w_src, edge_w_dst],
+        keep=[(3, 0), (4, 1), (5, 2), (6, 3)],
+        after=[mine, token],
+        scratch=[pltpu.VMEM((6 * mids, wide), BF16)],
+        flops=1_000_000_000,
+        name="final_ready",
+    )
 
     fine_out, mid_out, coarse_out = kernel_call(
         final_body,
-        [((count, width), BF16), ((mids, width), BF16), ((coarse_count, width), BF16)],
-        [mine, theirs, before, pair, after, edges, select, target, fine_latent, own_pick, node]
-        + [w_descend, w_fine, edge_w_src, edge_w_dst, node_w1, edge_w2, node_w2, node_w3],
+        [free(count, width), free(mids, width), free(coarse_count, width)],
+        [mine, theirs] + [here(a) for a in (w_descend, w_fine, w_src, w_dst, middle, picked)],
+        stored=[target, select, edges, edge_w2, own_pick, fine_latent, node_w1, node, node_w2, node_w3],
         scratch=[
             pltpu.VMEM((2 * half, width), BF16),
-            pltpu.VMEM((6 * mids, wide), BF16),
             pltpu.VMEM((8 * mids, width), BF16),
             pltpu.VMEM((count, width), F32),
         ],
-        limit=32,
+        limit=24,
         name="final",
     )
     return (fine_out, mid_out, coarse_out)

time: 110 us -> 90.2 us (0.82)
  the two profiles are of different devices: /device:TPU:8 before, /device:TPU:1 now
where the time goes in v3:
time: 90.2 us; the launch traced here: 89.5 us
  starting transfers between devices  46 us (51%)
  Pallas kernels  39.2 us (43%)
  waiting for transfers between devices  3.29 us (4%)
  between operations  1.05 us (1%)
    pallas_call x11, Pallas kernels, kernel_call(): pl.pallas_call(kernel, out_shape=outs, in_specs=[VMEM] * count + [STORED]...  39.2 us
    ppermute x6, starting transfers between devices, shifted(): return lax.ppermute(values, axis, pairs)  18.4 us
    all_to_all x1, starting transfers between devices, on_device(): mine = lax.all_to_all(results, PLANE, 0, 0).reshape(half, width)  9.09 us
    all_to_all x1, starting transfers between devices, on_device(): parts = lax.all_to_all(blocks, PLANE, 0, 0)  8.3 us
    all_to_all x1, starting transfers between devices, on_device(): in_planes = lax.all_to_all(own_parts, 'z', 0, 0)  8.18 us
    ppermute x2, starting transfers between devices, swapped(): return lax.ppermute(values, 'c', [(0, 1), (1, 0)])  1.95 us
  transfers between devices with their start and end apart: 11, of which 3 were waited for; matrix products, arithmetic and copies ran while one was open for 0% of the time, Pallas kernels for 27%

profile of v3, /device:TPU:1, one launch (start us, length us, event | category | flops | bytes accessed | tf_op | source)
XLA Modules:
  0.0 89.5 jit_solution(639611091852292033)
XLA Ops:
  0.6 1.3 %child_sums.1 = (f32[32,512]{1,0:T(8,128)S(1)}, bf16[32,512]{1,0:T(8,128)(2,1)S(1)}, bf16[32,512]{1,0:T(8,128)(2,1)S(1)}) custom-call(s32[4,128]{1,0:T(4,128)} %bitcast.13, bf16[512,512]{1,0:T(8,128)(2,1)} %refs_13_.1), custom_call_target="tpu_custom_call" | custom-call | bytes 1048576 | tf_op jit(solution)/shard_map/child_sums/pallas_call | solution.py:63
  1.9 4.5 %collective-permute-start = (bf16[32,512]{1,0:T(8,128)(2,1)S(1)}, bf16[32,512]{1,0:T(8,128)(2,1)S(1)}, u32[]{:S(2)}, u32[]{:S(2)}) collective-permute-start(bf16[32,512]{1,0:T(8,128)(2,1)S(1)} %get-tuple-element.40), channel_id=1, source_target_pairs={{0,1},{1,2},{2,3},{3,4},{4,5},{5,6},{6,7},{7,8},{8,9},{9,10},{10,1... | collective-permute-start | bytes 98312 | tf_op jit(solution)/shard_map/ppermute | solution.py:303
  6.5 1.9 %collective-permute-start.1 = (bf16[32,512]{1,0:T(8,128)(2,1)S(1)}, bf16[32,512]{1,0:T(8,128)(2,1)S(1)}, u32[]{:S(2)}, u32[]{:S(2)}) collective-permute-start(bf16[32,512]{1,0:T(8,128)(2,1)S(1)} %get-tuple-element.41), channel_id=1, source_target_pairs={{1,0},{2,1},{3,2},{4,3},{5,4},{6,5},{7,6},{8,7},{9,8},{10,9},{11,1... | collective-permute-start | bytes 98312 | tf_op jit(solution)/shard_map/ppermute | solution.py:303
  8.4 1.6 %mid_ready.1 = (bf16[512,512]{1,0:T(8,128)(2,1)S(1)}, bf16[512,512]{1,0:T(8,128)(2,1)S(1)}, bf16[512,512]{1,0:T(8,128)(2,1)S(1)}, bf16[32,512]{1,0:T(8,128)(2,1)...) custom-call(bf16[32,512]{1,0:T(8,128)(2,1)} %refs_0_.1, s32[1,32]{1,0:T(1,128)} %bitcast.19, ...), custom_call_target="tpu_custom_call" | custom-call | flops 1000000000 | bytes 1048576 | tf_op jit(solution)/shard_map/mid_ready/pallas_call | solution.py:63
  10.0 0.0 collective-permute-done.refs_1_
  10.0 1.7 %collective-permute-done.1.refs_2_ = bf16[32,512]{1,0:T(8,128)(2,1)S(1)} collective-permute-done((bf16[32,512]{1,0:T(8,128)(2,1)S(1)}, bf16[32,512]{1,0:T(8,128)(2,1)S(1)}, u32[]{:S(2)}, u32[]{:S(2)}) %collective-permute-start.1) | collective-permute-done | bytes 32800 | tf_op jit(solution)/shard_map/ppermute | solution.py:303
  11.7 0.6 mid_update.1.refs_0_
  12.3 0.1 collective-permute-start.2
  12.4 1.2 %collective-permute-done.2.refs_1_ = bf16[32,640]{1,0:T(8,128)(2,1)S(1)} collective-permute-done((bf16[32,640]{1,0:T(8,128)(2,1)S(1)}, bf16[32,640]{1,0:T(8,128)(2,1)S(1)}, u32[]{:S(2)}, u32[]{:S(2)}) %collective-permute-start.2) | collective-permute-done | bytes 40992 | tf_op jit(solution)/shard_map/ppermute | solution.py:307
  13.6 1.2 %coarse_blocks.1 = (bf16[64,640]{1,0:T(8,128)(2,1)S(1)}, bf16[384,512]{1,0:T(8,128)(2,1)}) custom-call(bf16[32,640]{1,0:T(8,128)(2,1)S(1)} %mid_update.1.refs_0_, bf16[32,640]{1,0:T(8,128)(2,1)S(1)} %collective-permute-done.2.refs_1_), custom_call_target="tpu_custom_call" | custom-call | bytes 1048576 | tf_op jit(solution)/shard_map/coarse_blocks/pallas_call | solution.py:63
  14.8 8.3 %all-to-all-start = ((bf16[16,24,512]{2,1,0:T(8,128)(2,1)}), bf16[16,24,512]{2,1,0:T(8,128)(2,1)S(1)}, u32[]{:S(2)}, u32[]{:S(2)}) async-start(bf16[16,24,512]{2,1,0:T(8,128)(2,1)} %bitcast.2.refs_6_), calls=%async_computation | async-start | bytes 786432 | tf_op jit(solution)/shard_map/all_to_all | solution.py:396
  23.1 1.3 %collective-permute-start.4 = (bf16[64,640]{1,0:T(8,128)(2,1)S(1)}, bf16[64,640]{1,0:T(8,128)(2,1)S(1)}, u32[]{:S(2)}, u32[]{:S(2)}) collective-permute-start(bf16[64,640]{1,0:T(8,128)(2,1)S(1)} %get-tuple-element.50.refs_1_), channel_id=1, source_target_pairs={{2,0},{4,2},{6,4},{8,6},{10,8},{12,10},{14,12},{16,14},{18,16},{20... | collective-permute-start | bytes 245768 | tf_op jit(solution)/shard_map/ppermute | solution.py:303
  24.4 4.0 %collective-permute-start.3 = (bf16[64,640]{1,0:T(8,128)(2,1)S(1)}, bf16[64,640]{1,0:T(8,128)(2,1)S(1)}, u32[]{:S(2)}, u32[]{:S(2)}) collective-permute-start(bf16[64,640]{1,0:T(8,128)(2,1)S(1)} %get-tuple-element.50.refs_1_), channel_id=1, source_target_pairs={{0,2},{2,4},{4,6},{6,8},{8,10},{10,12},{12,14},{14,16},{16,18},{18... | collective-permute-start | bytes 245768 | tf_op jit(solution)/shard_map/ppermute | solution.py:303
  28.4 4.1 %tables.1 = (bf16[512,512]{1,0:T(8,128)(2,1)}, bf16[512,512]{1,0:T(8,128)(2,1)}, f32[512,512]{1,0:T(8,128)}, bf16[128,640]{1,0:T(8,128)(2,1)S(1)}, bf16[128,640]...) custom-call(s32[4,128]{1,0:T(4,128)} %bitcast.14, s32[2,128]{1,0:T(2,128)} %bitcast.18, bf16[512,512]{1,0:T(8,128)(2,1)} %refs_13_.1, ...), custom_call_target="tpu_custom_call" | custom-call | flops 2000000000 | bytes 1048576 | tf_op jit(solution)/shard_map/tables/pallas_call | solution.py:63
  32.5 0.0 collective-permute-done.4.refs_3_.refs_2_
  32.6 0.0 all-to-all-done.refs_0_
  32.6 0.7 plane_sum.1.refs_9_
  33.3 8.2 %all-to-all-start.1 = ((bf16[8,24,512]{2,1,0:T(8,128)(2,1)}), bf16[8,24,512]{2,1,0:T(8,128)(2,1)S(1)}, u32[]{:S(2)}, u32[]{:S(2)}) async-start(bf16[8,24,512]{2,1,0:T(8,128)(2,1)} %plane_sum.1.refs_9_), calls=%async_computation.1 | async-start | bytes 393216 | tf_op jit(solution)/shard_map/all_to_all | solution.py:417
  41.5 4.8 %collective-permute-start.5 = (bf16[128,640]{1,0:T(8,128)(2,1)S(1)}, bf16[128,640]{1,0:T(8,128)(2,1)S(1)}, u32[]{:S(2)}, u32[]{:S(2)}) collective-permute-start(bf16[128,640]{1,0:T(8,128)(2,1)S(1)} %get-tuple-element.59), channel_id=1, source_target_pairs={{0,1},{1,2},{2,3},{3,4},{4,5},{5,6},{6,7},{7,8},{8,9},{9,10},{10,1... | collective-permute-start | bytes 491528 | tf_op jit(solution)/shard_map/ppermute | solution.py:303
  46.3 1.9 %collective-permute-start.6 = (bf16[128,640]{1,0:T(8,128)(2,1)S(1)}, bf16[128,640]{1,0:T(8,128)(2,1)S(1)}, u32[]{:S(2)}, u32[]{:S(2)}) collective-permute-start(bf16[128,640]{1,0:T(8,128)(2,1)S(1)} %get-tuple-element.60), channel_id=1, source_target_pairs={{1,0},{2,1},{3,2},{4,3},{5,4},{6,5},{7,6},{8,7},{9,8},{10,9},{11,1... | collective-permute-start | bytes 491528 | tf_op jit(solution)/shard_map/ppermute | solution.py:303
  48.2 7.6 %own_edges.1 = (bf16[512,512]{1,0:T(8,128)(2,1)S(1)}, bf16[3072,512]{1,0:T(8,128)(2,1)}, bf16[512,512]{1,0:T(8,128)(2,1)S(1)}, bf16[24,512]{1,0:T(8,128)(2,1)S(1)}, f32[24,512]{1,0:T(8,128)S(1)}) custom-call(s32[24,128]{1,0:T(8,128)} %bitcast.16, s32[24,128]{1,0:T(8,128)} %bitcast.10, bf16[512,512]{1,0:T(8,128)(2,1)} %get-tuple-element.51.refs_2_, ...), custom_call_target="tpu_custom_call" | custom-call | flops 3500000000 | bytes 1048576 | tf_op jit(solution)/shard_map/own_edges/pallas_call | solution.py:63
  55.9 0.0 copy-start
  55.9 0.0 collective-permute-done.6.refs_6_.refs_5_
  55.9 0.0 all-to-all-done.1.refs_0_
  55.9 1.2 %coarse_update.1.refs_7_ = bf16[16,24,512]{2,1,0:T(8,128)(2,1)} custom-call(bf16[8,24,512]{2,1,0:T(8,128)(2,1)S(1)} %all-to-all-done.1.refs_0_, bf16[24,512]{1,0:T(8,128)(2,1)S(1)} %get-tuple-element.53.refs_1_, f32[24,512]{1,0:T(8,128)S(1)} %get-tuple-element.54.refs_2_, bf16[512,512]{1,0:T(8,128)(2,1)S(1)} %get-tuple-element.55.refs_3_, ...), custom_call_target="tpu_custom_call" | custom-call | bytes 1048576 | tf_op jit(solution)/shard_map/coarse_update/pallas_call | solution.py:63
  57.1 9.1 %all-to-all-start.2 = ((bf16[16,24,512]{2,1,0:T(8,128)(2,1)}), bf16[16,24,512]{2,1,0:T(8,128)(2,1)S(1)}, u32[]{:S(2)}, u32[]{:S(2)}) async-start(bf16[16,24,512]{2,1,0:T(8,128)(2,1)} %coarse_update.1.refs_7_), calls=%async_computation.2 | async-start | bytes 786432 | tf_op jit(solution)/shard_map/all_to_all | solution.py:440
  66.3 8.8 %rest_edges.1 = (bf16[3072,512]{1,0:T(8,128)(2,1)}, bf16[3072,256]{1,0:T(8,128)(2,1)}, bf16[512,128]{1,0:T(8,128)(2,1)}, bf16[8,128]{1,0:T(8,128)(2,1)S(1)}) custom-call(bf16[3072,512]{1,0:T(8,128)(2,1)} %get-tuple-element.61.refs_0_, s32[24,128]{1,0:T(8,128)} %bitcast.17, s32[24,128]{1,0:T(8,128)} %bitcast.11, s32[4,128]{1,0:T(4,128)} %bitcast.15, ...), custom_call_target="tpu_custom_call" | custom-call | flops 3500000000 | bytes 1048576 | tf_op jit(solution)/shard_map/rest_edges/pallas_call | solution.py:63
  75.0 0.4 all-to-all-done.2
  75.4 1.9 %collective-permute-start.7 = (bf16[384,512]{1,0:T(8,128)(2,1)S(1)}, bf16[384,512]{1,0:T(8,128)(2,1)S(1)}, u32[]{:S(2)}, u32[]{:S(2)}) collective-permute-start(bf16[384,512]{1,0:T(8,128)(2,1)S(1)} %bitcast.7), channel_id=1, source_target_pairs={{0,1},{1,0},{2,3},{3,2},{4,5},{5,4},{6,7},{7,6},{8,9},{9,8},{10,11... | collective-permute-start | bytes 1179656 | tf_op jit(solution)/shard_map/ppermute | solution.py:307
  77.3 1.7 %final_ready.1 = (bf16[512,512]{1,0:T(8,128)(2,1)S(1)}, bf16[512,512]{1,0:T(8,128)(2,1)S(1)}, bf16[512,512]{1,0:T(8,128)(2,1)S(1)}, bf16[512,512]{1,0:T(8,128)(2...) custom-call(bf16[64,640]{1,0:T(8,128)(2,1)} %copy-done.3, bf16[64,640]{1,0:T(8,128)(2,1)} %copy-done.4, ...), custom_call_target="tpu_custom_call" | custom-call | flops 1000000000 | bytes 1048576 | tf_op jit(solution)/shard_map/final_ready/pallas_call | solution.py:63
  79.0 0.0 collective-permute-done.7.refs_1_
  79.0 10.4 %final.1 = (bf16[512,512]{1,0:T(8,128)(2,1)}, bf16[32,512]{1,0:T(8,128)(2,1)}, bf16[642,512]{1,0:T(8,128)(2,1)}) custom-call(bf16[384,512]{1,0:T(8,128)(2,1)S(1)} %bitcast.9, bf16[384,512]{1,0:T(8,128)(2,1)S(1)} %collective-permute-done.7.refs_1_, bf16[512,512]{1,0:T(8,128)(2,1)S(1)} %get-tuple-element.65.refs_2_, ...), custom_call_target="tpu_custom_call" | custom-call | bytes 1048576 | tf_op jit(solution)/shard_map/final/pallas_call | solution.py:63
  (11 shorter events, 0.0 us)
Async XLA Ops:
  1.9 8.1 %collective-permute-start = (bf16[32,512]{1,0:T(8,128)(2,1)S(1)}, bf16[32,512]{1,0:T(8,128)(2,1)S(1)}, u32[]{:S(2)}, u32[]{:S(2)}) collective-permute-start(bf16[32,512]{1,0:T(8,128)(2,1)S(1)} %get-tuple-element.40), channel_id=1, source_target_pairs={{0,1},{1,2},{2,3},{3,4},{4,5},{5,6},{6,7},{7,8},{8,9},{9,10},{10,1... | collective-permute-start | bytes 98312 | tf_op jit(solution)/shard_map/ppermute | solution.py:303
  6.5 5.2 %collective-permute-start.1 = (bf16[32,512]{1,0:T(8,128)(2,1)S(1)}, bf16[32,512]{1,0:T(8,128)(2,1)S(1)}, u32[]{:S(2)}, u32[]{:S(2)}) collective-permute-start(bf16[32,512]{1,0:T(8,128)(2,1)S(1)} %get-tuple-element.41), channel_id=1, source_target_pairs={{1,0},{2,1},{3,2},{4,3},{5,4},{6,5},{7,6},{8,7},{9,8},{10,9},{11,1... | collective-permute-start | bytes 98312 | tf_op jit(solution)/shard_map/ppermute | solution.py:303
  12.3 1.3 %collective-permute-start.2 = (bf16[32,640]{1,0:T(8,128)(2,1)S(1)}, bf16[32,640]{1,0:T(8,128)(2,1)S(1)}, u32[]{:S(2)}, u32[]{:S(2)}) collective-permute-start(bf16[32,640]{1,0:T(8,128)(2,1)S(1)} %mid_update.1.refs_0_), channel_id=1, source_target_pairs={{0,1},{1,0},{2,3},{3,2},{4,5},{5,4},{6,7},{7,6},{8,9},{9,8},{10,11... | collective-permute-start | bytes 122888 | tf_op jit(solution)/shard_map/ppermute | solution.py:307
  14.8 17.7 %copy-start.4 = (bf16[64,640]{1,0:T(8,128)(2,1)}, bf16[64,640]{1,0:T(8,128)(2,1)S(1)}, u32[]{:S(2)}) copy-start(bf16[64,640]{1,0:T(8,128)(2,1)S(1)} %get-tuple-element.50.refs_1_) | copy-start | bytes 245764
  14.8 17.8 %all-to-all-start = ((bf16[16,24,512]{2,1,0:T(8,128)(2,1)}), bf16[16,24,512]{2,1,0:T(8,128)(2,1)S(1)}, u32[]{:S(2)}, u32[]{:S(2)}) async-start(bf16[16,24,512]{2,1,0:T(8,128)(2,1)} %bitcast.2.refs_6_), calls=%async_computation | async-start | bytes 786432 | tf_op jit(solution)/shard_map/all_to_all | solution.py:396
  23.1 9.4 %collective-permute-start.4 = (bf16[64,640]{1,0:T(8,128)(2,1)S(1)}, bf16[64,640]{1,0:T(8,128)(2,1)S(1)}, u32[]{:S(2)}, u32[]{:S(2)}) collective-permute-start(bf16[64,640]{1,0:T(8,128)(2,1)S(1)} %get-tuple-element.50.refs_1_), channel_id=1, source_target_pairs={{2,0},{4,2},{6,4},{8,6},{10,8},{12,10},{14,12},{16,14},{18,16},{20... | collective-permute-start | bytes 245768 | tf_op jit(solution)/shard_map/ppermute | solution.py:303
  24.4 8.1 %collective-permute-start.3 = (bf16[64,640]{1,0:T(8,128)(2,1)S(1)}, bf16[64,640]{1,0:T(8,128)(2,1)S(1)}, u32[]{:S(2)}, u32[]{:S(2)}) collective-permute-start(bf16[64,640]{1,0:T(8,128)(2,1)S(1)} %get-tuple-element.50.refs_1_), channel_id=1, source_target_pairs={{0,2},{2,4},{4,6},{6,8},{8,10},{10,12},{12,14},{14,16},{16,18},{18... | collective-permute-start | bytes 245768 | tf_op jit(solution)/shard_map/ppermute | solution.py:303
  32.5 23.3 %copy-start.2 = (bf16[64,640]{1,0:T(8,128)(2,1)}, bf16[64,640]{1,0:T(8,128)(2,1)S(1)}, u32[]{:S(2)}) copy-start(bf16[64,640]{1,0:T(8,128)(2,1)S(1)} %collective-permute-done.4.refs_3_.refs_2_) | copy-start | bytes 245764
  32.6 23.3 %copy-start.3 = (bf16[64,640]{1,0:T(8,128)(2,1)}, bf16[64,640]{1,0:T(8,128)(2,1)S(1)}, u32[]{:S(2)}) copy-start(bf16[64,640]{1,0:T(8,128)(2,1)S(1)} %collective-permute-done.3.refs_2_.refs_0_) | copy-start | bytes 245764
  33.3 22.6 %all-to-all-start.1 = ((bf16[8,24,512]{2,1,0:T(8,128)(2,1)}), bf16[8,24,512]{2,1,0:T(8,128)(2,1)S(1)}, u32[]{:S(2)}, u32[]{:S(2)}) async-start(bf16[8,24,512]{2,1,0:T(8,128)(2,1)} %plane_sum.1.refs_9_), calls=%async_computation.1 | async-start | bytes 393216 | tf_op jit(solution)/shard_map/all_to_all | solution.py:417
  41.5 14.4 %collective-permute-start.5 = (bf16[128,640]{1,0:T(8,128)(2,1)S(1)}, bf16[128,640]{1,0:T(8,128)(2,1)S(1)}, u32[]{:S(2)}, u32[]{:S(2)}) collective-permute-start(bf16[128,640]{1,0:T(8,128)(2,1)S(1)} %get-tuple-element.59), channel_id=1, source_target_pairs={{0,1},{1,2},{2,3},{3,4},{4,5},{5,6},{6,7},{7,8},{8,9},{9,10},{10,1... | collective-permute-start | bytes 491528 | tf_op jit(solution)/shard_map/ppermute | solution.py:303
  46.3 9.6 %collective-permute-start.6 = (bf16[128,640]{1,0:T(8,128)(2,1)S(1)}, bf16[128,640]{1,0:T(8,128)(2,1)S(1)}, u32[]{:S(2)}, u32[]{:S(2)}) collective-permute-start(bf16[128,640]{1,0:T(8,128)(2,1)S(1)} %get-tuple-element.60), channel_id=1, source_target_pairs={{1,0},{2,1},{3,2},{4,3},{5,4},{6,5},{7,6},{8,7},{9,8},{10,9},{11,1... | collective-permute-start | bytes 491528 | tf_op jit(solution)/shard_map/ppermute | solution.py:303
  55.9 10.4 %copy-start = (bf16[128,640]{1,0:T(8,128)(2,1)}, bf16[128,640]{1,0:T(8,128)(2,1)S(1)}, u32[]{:S(2)}) copy-start(bf16[128,640]{1,0:T(8,128)(2,1)S(1)} %collective-permute-done.5.refs_5_.refs_4_) | copy-start | bytes 491524
  55.9 10.4 %copy-start.1 = (bf16[128,640]{1,0:T(8,128)(2,1)}, bf16[128,640]{1,0:T(8,128)(2,1)S(1)}, u32[]{:S(2)}) copy-start(bf16[128,640]{1,0:T(8,128)(2,1)S(1)} %collective-permute-done.6.refs_6_.refs_5_) | copy-start | bytes 491524
  57.1 18.3 %all-to-all-start.2 = ((bf16[16,24,512]{2,1,0:T(8,128)(2,1)}), bf16[16,24,512]{2,1,0:T(8,128)(2,1)S(1)}, u32[]{:S(2)}, u32[]{:S(2)}) async-start(bf16[16,24,512]{2,1,0:T(8,128)(2,1)} %coarse_update.1.refs_7_), calls=%async_computation.2 | async-start | bytes 786432 | tf_op jit(solution)/shard_map/all_to_all | solution.py:440
  75.4 3.6 %collective-permute-start.7 = (bf16[384,512]{1,0:T(8,128)(2,1)S(1)}, bf16[384,512]{1,0:T(8,128)(2,1)S(1)}, u32[]{:S(2)}, u32[]{:S(2)}) collective-permute-start(bf16[384,512]{1,0:T(8,128)(2,1)S(1)} %bitcast.7), channel_id=1, source_target_pairs={{0,1},{1,0},{2,3},{3,2},{4,5},{5,4},{6,7},{7,6},{8,9},{9,8},{10,11... | collective-permute-start | bytes 1179656 | tf_op jit(solution)/shard_map/ppermute | solution.py:307

commit v4 on v3

--- a/solution.py
+++ b/solution.py
@@ -20,15 +20,25 @@
 
 
 class Copied:
-    def __init__(self, source, target, semaphore):
-        self.copy = pltpu.make_async_copy(source, target, semaphore)
-        self.target, self.waiting = target, True
-        self.copy.start()
-
-    def get(self):
-        if self.waiting:
-            self.copy.wait()
-            self.waiting = False
+    def __init__(self, source, target, semaphores, first=0, pieces=1):
+        rows = target.shape[0] // pieces
+        self.target, self.copies = target, []
+        for k in range(pieces):
+            part = slice(k * rows, (k + 1) * rows) if pieces > 1 else slice(None)
+            self.copies.append(pltpu.make_async_copy(source.at[part], target.at[part], semaphores.at[first + k]))
+        self.waiting = [False] * pieces
+
+    def start(self, k=None):
+        for i in range(len(self.copies)) if k is None else (k,):
+            self.copies[i].start()
+            self.waiting[i] = True
+        return self
+
+    def get(self, k=None):
+        for i in range(len(self.copies)) if k is None else (k,):
+            if self.waiting[i]:
+                self.copies[i].wait()
+                self.waiting[i] = False
         return self.target
 
     def __getitem__(self, index):
@@ -39,9 +49,13 @@
         return self.target.shape
 
 
-def kernel_call(body, outs, operands, stored=(), after=(), scratch=(), keep=(), limit=8, flops=0, name=None):
+def kernel_call(
+    body, outs, operands, stored=(), after=(), scratch=(), keep=(), streams=(), pieces=(), limit=8, flops=0, name=None
+):
     count, held, skipped, given = len(operands), len(stored), len(after), len(outs)
     target = dict(keep)
+    cuts = [stored[i].shape[0] // CHUNK if i in pieces else 1 for i in range(held)]
+    flows = {o: outs[o].shape[0] // CHUNK for o in streams}
 
     def kernel(*refs):
         inputs, refs = refs[:count], refs[count:]
@@ -50,21 +64,32 @@
         own, refs = refs[: len(scratch)], refs[len(scratch) :]
         buffers = iter(refs)
         places = [results[target[i]] if i in target else next(buffers) for i in range(held)]
-        semaphores = next(buffers) if held else None
-        copies = [Copied(sources[i], places[i], semaphores.at[i]) for i in range(held)]
-        fresh = [results[o] for o in range(given) if o not in target.values()]
-        body(*inputs, *copies, *fresh, *own)
-        for copy in copies:
-            copy.get()
+        leaving = {o: next(buffers) for o in streams}
+        semaphores = next(buffers) if held or streams else None
+        first, copies, fresh = 0, [], []
+        for i in range(held):
+            copies.append(Copied(sources[i], places[i], semaphores, first, cuts[i]).start())
+            first += cuts[i]
+        for o in range(given):
+            if o in flows:
+                fresh.append(Copied(leaving[o], results[o], semaphores, first, flows[o]))
+                first += flows[o]
+            elif o not in target.values():
+                fresh.append(results[o])
+        body(*inputs, *copies, *fresh, *[leaving[o] for o in streams], *own)
+        for copy in copies + fresh:
+            if isinstance(copy, Copied):
+                copy.get()
 
     buffers = [pltpu.VMEM(stored[i].shape, stored[i].dtype) for i in range(held) if i not in target]
-    if held:
-        buffers.append(pltpu.SemaphoreType.DMA((held,)))
+    buffers += [pltpu.VMEM(outs[o].shape, outs[o].dtype) for o in streams]
+    if held or streams:
+        buffers.append(pltpu.SemaphoreType.DMA((sum(cuts) + sum(flows.values()),)))
     return pl.pallas_call(
         kernel,
         out_shape=outs,
         in_specs=[VMEM] * count + [STORED] * held + [UNREAD] * skipped,
-        out_specs=[VMEM] * given,
+        out_specs=[STORED if o in flows else VMEM for o in range(given)],
         scratch_shapes=[*scratch, *buffers],
         compiler_params=pltpu.CompilerParams(vmem_limit_bytes=limit << 20),
         cost_estimate=pl.CostEstimate(flops=flops, bytes_accessed=1 << 20, transcendentals=0),
@@ -103,14 +128,16 @@
     return [hot(spread_ids == lanes(LANES, first + LANES * q)) for q in range(blocks)]
 
 
-def sums_body(parent, fine, own, up, down):
+def sums_body(parent, fine, own, swap, cross):
     count = own.shape[0]
+    core = lax.axis_index("c")
     rows = lax.broadcasted_iota(I32, (3 * count, LANES), 0)
     blocks = [hot(rows == parent[r : r + 1, :]) for r in range(parent.shape[0])]
     sums = product(jnp.concatenate(blocks, axis=1), fine[...])
     own[...] = sums[:count]
-    down[...] = sums[count : 2 * count].astype(BF16)
-    up[...] = sums[2 * count :].astype(BF16)
+    down, up = sums[count : 2 * count].astype(BF16), sums[2 * count :].astype(BF16)
+    swap[...] = jnp.where(core == 0, up, down)
+    cross[...] = jnp.where(core == 0, down, up)
 
 
 def mid_ready_body(latent, ids, first, w_child, second, third, kept, hidden, labels):
@@ -152,17 +179,26 @@
     ).astype(BF16)
 
 
-def tables_body(parent, halo, fine, w_src, w_dst, w_node, sender, receiver, node, down, up, token):
-    token[...] = jnp.zeros_like(token)
+def boundary_body(parent, halo, fine, pair, swap, cross):
     count, width = fine.shape
-    blocks = count // LANES
-    values = fine[...]
+    two, blocks = pair.shape[0], count // LANES
+    core = lax.axis_index("c")
     codes = [(spread(parent[r : r + 1, :]) + 1).astype(F32).astype(BF16) for r in range(blocks)]
     codes = jnp.concatenate(codes, axis=0)
-    for r, out in enumerate((down, up)):
-        picked = jnp.concatenate(picks(spread(halo[r : r + 1, :]), 0, blocks), axis=1)
-        out[:, :width] = product(picked, values).astype(BF16)
-        out[:, width:] = product(picked, codes).astype(BF16)
+    rows = halo[...]
+    for out, first, row in (
+        (swap, 0, jnp.where(core == 0, rows[1:2], rows[:1])),
+        (cross, two, jnp.where(core == 0, rows[:1], rows[1:2])),
+    ):
+        picked = jnp.concatenate(picks(spread(row), 0, blocks), axis=1)
+        out[first : first + LANES, :width] = product(picked, fine[...]).astype(BF16)
+        out[first : first + LANES, width:] = product(picked, codes).astype(BF16)
+    cross[:two] = pair[...]
+
+
+def tables_body(fine, w_src, w_dst, w_node, sender, receiver, node, token):
+    token[...] = jnp.zeros_like(token)
+    values = fine[...]
     sender[...] = product(values, w_src[...]).astype(BF16)
     receiver[...] = product(values, w_dst[...]).astype(BF16)
     node[...] = product(values, w_node[...])
@@ -183,7 +219,8 @@
 
 
 def own_edges_body(
-    source, target, sender, receiver, coarse, coarse_w1, w_coarse, coarse_w2, third, out, both, own_latent, own_hidden
+    source, target, sender, receiver, coarse, coarse_w1, w_coarse, coarse_w2, edge_w2, node_w2, third,
+    sent_out, both, last, own_latent, own_hidden, out,
 ):
     count = sender.shape[0]
     blocks = count // LANES
@@ -195,6 +232,8 @@
         picked = [jnp.concatenate(picks(spread(target[r : r + 1, :]), 0, blocks), axis=1) for r in marks]
         total += product(jnp.concatenate(picked, axis=0), received)
         out[k * CHUNK : (k + 1) * CHUNK, :] = total.astype(BF16)
+        sent_out.start(k)
+    last[...] = product(edge_w2[...], node_w2[...]).astype(BF16)
     rows, total = own_latent.shape[0], coarse.shape[0]
     chips = lax.axis_size("y") * lax.axis_size("x")
     chip = lax.axis_index("y") * lax.axis_size("x") + lax.axis_index("x")
@@ -215,12 +254,15 @@
 
 
 def rest_edges_body(
-    mid_count, first, source, target, parent, before, after, w_src, out, select, own_pick, token, table, where
+    mid_count, source, target, parent, cross, swap, w_src, first, sent_out, sent_select, own_pick, token,
+    out, select, table, where
 ):
     token[...] = jnp.zeros_like(token)
+    core = lax.axis_index("c")
     count = own_pick.shape[0]
     width = out.shape[1]
     blocks = count // LANES
+    two = cross.shape[0] - LANES
     for r in range(blocks):
         place = slots(spread(parent[r : r + 1, :]) + 1, 2, mid_count)
         rows = slice(r * LANES, (r + 1) * LANES)
@@ -230,12 +272,12 @@
         far = place + 4 * mid_count
         there = slice(count + 2 * LANES + r * LANES, count + 2 * LANES + (r + 1) * LANES)
         where[there, :] = jnp.concatenate(picks(far, 0, 2), axis=1)
-    for r, (halo, tile) in enumerate(((before, 1), (after, 3))):
-        values = halo[...]
-        rows = slice(r * LANES, (r + 1) * LANES)
+    for values, late in ((cross[two:], core), (swap[...], 1 - core)):
+        rows = pl.ds(pl.multiple_of(late * LANES, LANES), LANES)
         table[rows, :] = product(values[:, :width], w_src[...]).astype(BF16)
-        place = slots(values[:, width:].astype(F32).astype(I32), tile, mid_count)
-        where[count + r * LANES : count + (r + 1) * LANES, :] = jnp.concatenate(picks(place, 0, 2), axis=1)
+        place = slots(values[:, width:].astype(F32).astype(I32), 1 + 2 * late, mid_count)
+        rows = pl.ds(pl.multiple_of(count + late * LANES, LANES), LANES)
+        where[rows, :] = jnp.concatenate(picks(place, 0, 2), axis=1)
     for k in range(out.shape[0] // CHUNK):
         rows = []
         for r in range(k * CHUNK // LANES, (k + 1) * CHUNK // LANES):
@@ -245,24 +287,27 @@
         picked = jnp.concatenate(rows, axis=0)
         here = slice(k * CHUNK, (k + 1) * CHUNK)
         select[here, :] = product(picked, where[...]).astype(BF16)
+        sent_select.start(k)
         rest = product(picked[:, count : count + 2 * LANES], table[...])
-        out[here, :] = (first[here, :].astype(F32) + rest).astype(BF16)
-
-
-def ready_body(rows, before, pair, after, w_descend, w_fine, w_src, w_dst, middle, picked, window):
+        out[here, :] = (first.get(k)[here, :].astype(F32) + rest).astype(BF16)
+        sent_out.start(k)
+
+
+def ready_body(rows, cross, pair, swap, w_descend, w_fine, w_src, w_dst, middle, picked, window):
+    core = lax.axis_index("c")
     two = pair.shape[0]
     count, width = two // 2, middle.shape[1]
-    window[:two] = before[...]
-    window[two : 2 * two] = pair[...]
-    window[2 * two :] = after[...]
-    near = window[pl.ds(pl.multiple_of(lax.axis_index("c") * count, count), 5 * count), :]
+    window[pl.ds(pl.multiple_of((1 - core) * 4 * count, count), count), :] = swap[...]
+    window[pl.ds(pl.multiple_of(core * 3 * count, count), two), :] = cross[:two]
+    window[pl.ds(pl.multiple_of((2 - core) * count, count), two), :] = pair[...]
+    near = window[...]
     middle[...] = near[:, :width]
     picked[...] = hot(row_ids(near, width) == lax.broadcasted_iota(I32, (5 * count, rows), 1))
 
 
 def final_body(
-    mine, theirs, w_descend, w_fine, w_src, w_dst, near, picked, target, select, edges, edge_w2, own_pick, fine,
-    w_node, node, node_w2, node_w3, fine_out, mid_out, coarse_out, coarse, table, sums,
+    mine, theirs, w_descend, w_fine, w_src, w_dst, near, picked, target, select, edges, own_pick, fine,
+    w_node, last, node, node_w3, fine_out, mid_out, coarse_out, coarse, table, sums,
 ):
     core = lax.axis_index("c")
     half, width = mine.shape
@@ -280,7 +325,7 @@
     rows = lax.broadcasted_iota(I32, (fine.shape[0], LANES), 0)
     for k in range(edges.shape[0] // CHUNK):
         here = slice(k * CHUNK, (k + 1) * CHUNK)
-        edge_sum = edges[here, :].astype(F32) + product(select[here, :], table[...])
+        edge_sum = edges.get(k)[here, :].astype(F32) + product(select.get(k)[here, :], table[...])
         hidden = silu(edge_sum).astype(BF16)
         marks = range(k * CHUNK // LANES, (k + 1) * CHUNK // LANES)
         scatter = jnp.concatenate([hot(rows == target[r : r + 1, :]) for r in marks], axis=1)
@@ -293,18 +338,17 @@
     reach = fine_down[count : 5 * count]
     lifted = (fine[...].astype(F32) + product(own_pick[...], reach)).astype(BF16)
     near_node = product(reach, w_node[...]).astype(BF16)
-    aggregate = product(sums[...].astype(BF16), edge_w2[...]).astype(BF16)
-    hidden = silu(node[...] + product(own_pick[...], near_node) + product(aggregate, node_w2[...]))
+    hidden = silu(node[...] + product(own_pick[...], near_node) + product(sums[...].astype(BF16), last[...]))
     fine_out[...] = updated(lifted, hidden, node_w3[...])
-
-
-def shifted(values, axis, step, size):
-    pairs = [(i, i + step) for i in range(size) if 0 <= i + step < size]
-    return lax.ppermute(values, axis, pairs)
 
 
 def swapped(values):
     return lax.ppermute(values, "c", [(0, 1), (1, 0)])
+
+
+def crossed(values, tiles):
+    pairs = [(t, t + 1) for t in range(1, tiles - 1, 2)]
+    return lax.ppermute(values, TILE, pairs + [(b, a) for a, b in pairs])
 
 
 def on_device(
@@ -359,15 +403,15 @@
         return jax.ShapeDtypeStruct(shape, dtype)
 
     square = near(width, width)
-    own, up, down = kernel_call(
+    own, swap, cross = kernel_call(
         sums_body,
         [near(mids, width, dtype=F32), free(mids, width), free(mids, width)],
         [],
         stored=[parent, fine_latent],
         name="child_sums",
     )
-    from_before = shifted(up, TILE, 1, tiles)
-    from_after = shifted(down, TILE, -1, tiles)
+    from_cross = crossed(cross, tiles)
+    from_swap = swapped(swap)
     w_child, mid_w2, mid_w3, kept, hidden, labels = kernel_call(
         mid_ready_body,
         [square, square, square, near(mids, width), near(mids, width, dtype=F32), near(mids, LANES)],
@@ -381,27 +425,36 @@
     (labelled,) = kernel_call(
         mid_body,
         [free(mids, wide)],
-        [here(own), from_before, from_after] + [here(a) for a in (kept, hidden, labels, w_child, mid_w2, mid_w3)],
+        [here(own), from_swap, from_cross] + [here(a) for a in (kept, hidden, labels, w_child, mid_w2, mid_w3)],
         name="mid_update",
     )
     other = swapped(labelled)
     pair, blocks = kernel_call(
         blocks_body,
-        [free(2 * mids, wide), near(half, width)],
+        [far(2 * mids, wide), near(half, width)],
         [labelled, other],
         name="coarse_blocks",
     )
 
     blocks = blocks.reshape(chips, BLOCK, width)
     parts = lax.all_to_all(blocks, PLANE, 0, 0)
-    before = shifted(pair, PLANE, 1, chips)
-    after = shifted(pair, PLANE, -1, chips)
-    sender, receiver, node, halo_down, halo_up, token = kernel_call(
+    halo_swap, cross = kernel_call(
+        boundary_body,
+        [free(LANES, wide), free(2 * mids + LANES, wide)],
+        [],
+        stored=[parent, halo, fine_latent, pair],
+        after=[blocks],
+        flops=500_000_000,
+        name="boundary",
+    )
+    cross_in = crossed(cross, tiles)
+    halo_in = swapped(halo_swap)
+    sender, receiver, node, token = kernel_call(
         tables_body,
-        [far(count, width), far(count, width), far(count, width, dtype=F32), free(LANES, wide), free(LANES, wide), free(8, LANES)],
-        [],
-        stored=[parent, halo, fine_latent, edge_w_src, edge_w_dst, node_w1],
-        after=[blocks],
+        [far(count, width), far(count, width), far(count, width, dtype=F32), free(8, LANES)],
+        [],
+        stored=[fine_latent, edge_w_src, edge_w_dst, node_w1],
+        after=[halo_swap],
         limit=12,
         flops=2_000_000_000,
         name="tables",
@@ -411,21 +464,20 @@
         gather_body,
         [near(planes, BLOCK, width)],
         [parts],
-        after=[token, before, after],
+        after=[token, cross_in, halo_in],
         name="plane_sum",
     )
     in_planes = lax.all_to_all(own_parts, "z", 0, 0)
-    halo_down, halo_up, _ = lax.optimization_barrier((halo_down, halo_up, own_parts))
-    halo_before = shifted(halo_up, TILE, 1, tiles)
-    halo_after = shifted(halo_down, TILE, -1, tiles)
-    coarse_w3, own_edges, both, own_latent, own_hidden = kernel_call(
+    mid_in = swapped(jnp.where(lax.axis_index("c") == 0, cross_in[mids : 2 * mids], cross_in[:mids]))
+    coarse_w3, own_edges, both, last, own_latent, own_hidden = kernel_call(
         own_edges_body,
-        [square, far(edge_count, width), square, near(BLOCK, width), near(BLOCK, width, dtype=F32)],
-        [],
-        stored=[source, target, sender, receiver, coarse_latent, coarse_w1, w_coarse, coarse_w2, coarse_w3],
-        keep=[(8, 0)],
+        [square, far(edge_count, width), square, far(width, width), near(BLOCK, width), near(BLOCK, width, dtype=F32)],
+        [],
+        stored=[source, target, sender, receiver, coarse_latent, coarse_w1, w_coarse, coarse_w2, edge_w2, node_w2, coarse_w3],
+        keep=[(10, 0)],
+        streams=[1],
         after=[own_parts],
-        limit=16,
+        limit=20,
         flops=3_500_000_000,
         name="own_edges",
     )
@@ -434,7 +486,7 @@
         coarse_body,
         [near(chips, BLOCK, width)],
         [in_planes] + [here(a) for a in (own_latent, own_hidden, both, coarse_w3)],
-        after=[halo_before, halo_after],
+        after=[mid_in],
         name="coarse_update",
     )
     mine = lax.all_to_all(results, PLANE, 0, 0).reshape(half, width)
@@ -442,7 +494,9 @@
         functools.partial(rest_edges_body, mids),
         [far(edge_count, width), far(edge_count, 2 * LANES), far(count, LANES), free(8, LANES)],
         [],
-        stored=[own_edges, source, target, parent, halo_before, halo_after, edge_w_src],
+        stored=[source, target, parent, cross_in, halo_in, edge_w_src, own_edges],
+        pieces=[6],
+        streams=[0, 1],
         after=[results],
         scratch=[pltpu.VMEM((2 * LANES, width), BF16), pltpu.VMEM((2 * count + 2 * LANES, 2 * LANES), BF16)],
         limit=24,
@@ -455,10 +509,10 @@
         functools.partial(ready_body, 2 * half),
         [square] * 4 + [near(5 * mids, width), near(5 * mids, 2 * half)],
         [],
-        stored=[before, pair, after, w_descend, w_fine, edge_w_src, edge_w_dst],
+        stored=[cross_in, pair, mid_in, w_descend, w_fine, edge_w_src, edge_w_dst],
         keep=[(3, 0), (4, 1), (5, 2), (6, 3)],
         after=[mine, token],
-        scratch=[pltpu.VMEM((6 * mids, wide), BF16)],
+        scratch=[pltpu.VMEM((5 * mids, wide), BF16)],
         flops=1_000_000_000,
         name="final_ready",
     )
@@ -467,7 +521,8 @@
         final_body,
         [free(count, width), free(mids, width), free(coarse_count, width)],
         [mine, theirs] + [here(a) for a in (w_descend, w_fine, w_src, w_dst, middle, picked)],
-        stored=[target, select, edges, edge_w2, own_pick, fine_latent, node_w1, node, node_w2, node_w3],
+        stored=[target, select, edges, own_pick, fine_latent, node_w1, last, node, node_w3],
+        pieces=[1, 2],
         scratch=[
             pltpu.VMEM((2 * half, width), BF16),
             pltpu.VMEM((8 * mids, width), BF16),

time: 90.2 us -> 81.5 us (0.904)
  starting transfers between devices: 46 us -> 36.1 us
  Pallas kernels: 39.2 us -> 40.3 us
    ppermute x6 -> x2, starting transfers between devices: 18.4 us -> 5.78 us  [crossed(): return lax.ppermute(values, TILE, pairs + [(b, a) for a, b in pairs])]
    ppermute x2 -> x5, starting transfers between devices: 1.95 us -> 6.39 us  [swapped(): return lax.ppermute(values, 'c', [(0, 1), (1, 0)])]
    all_to_all x1, starting transfers between devices: 8.3 us -> 6.86 us  [on_device(): parts = lax.all_to_all(blocks, PLANE, 0, 0)]
    pallas_call x11 -> x12, Pallas kernels: 39.2 us -> 40.3 us  [kernel_call(): pl.pallas_call(kernel, out_shape=outs, in_specs=[VMEM] * count + [STORED]...]
    ppermute x6 -> x2, waiting for transfers between devices: 1.68 us -> 2.22 us  [crossed(): return lax.ppermute(values, TILE, pairs + [(b, a) for a, b in pairs])]
  transfers between devices with their start and end apart: 11 -> 10, of which waited for: 3 -> 4; matrix products, arithmetic and copies ran while one was open for 0% -> 0% of each run, Pallas kernels for 27% -> 32%
where the time goes in v4:
time: 81.5 us; the launch traced here: 80.9 us
  Pallas kernels  40.3 us (49%)
  starting transfers between devices  36.1 us (44%)
  waiting for transfers between devices  3.5 us (4%)
  between operations  1.01 us (1%)
    pallas_call x12, Pallas kernels, kernel_call(): pl.pallas_call(kernel, out_shape=outs, in_specs=[VMEM] * count + [STORED]...  40.3 us
    all_to_all x1, starting transfers between devices, on_device(): mine = lax.all_to_all(results, PLANE, 0, 0).reshape(half, width)  8.89 us
    all_to_all x1, starting transfers between devices, on_device(): in_planes = lax.all_to_all(own_parts, 'z', 0, 0)  8.19 us
    all_to_all x1, starting transfers between devices, on_device(): parts = lax.all_to_all(blocks, PLANE, 0, 0)  6.86 us
    ppermute x5, starting transfers between devices, swapped(): return lax.ppermute(values, 'c', [(0, 1), (1, 0)])  6.39 us
    ppermute x2, starting transfers between devices, crossed(): return lax.ppermute(values, TILE, pairs + [(b, a) for a, b in pairs])  5.78 us
    ppermute x2, waiting for transfers between devices, crossed(): return lax.ppermute(values, TILE, pairs + [(b, a) for a, b in pairs])  2.22 us
  transfers between devices with their start and end apart: 10, of which 4 were waited for; matrix products, arithmetic and copies ran while one was open for 0% of the time, Pallas kernels for 32%

profile of v4, /device:TPU:1, one launch (start us, length us, event | category | flops | bytes accessed | tf_op | source)
XLA Modules:
  0.0 80.9 jit_solution(12037933696164043539)
XLA Ops:
  0.6 1.3 %child_sums.1 = (f32[32,512]{1,0:T(8,128)S(1)}, bf16[32,512]{1,0:T(8,128)(2,1)S(1)}, bf16[32,512]{1,0:T(8,128)(2,1)S(1)}) custom-call(s32[4,128]{1,0:T(4,128)} %bitcast.13, bf16[512,512]{1,0:T(8,128)(2,1)} %refs_12_.1), custom_call_target="tpu_custom_call" | custom-call | bytes 1048576 | tf_op jit(solution)/shard_map/child_sums/pallas_call | solution.py:88
  1.9 3.3 %collective-permute-start = (bf16[32,512]{1,0:T(8,128)(2,1)S(1)}, bf16[32,512]{1,0:T(8,128)(2,1)S(1)}, u32[]{:S(2)}, u32[]{:S(2)}) collective-permute-start(bf16[32,512]{1,0:T(8,128)(2,1)S(1)} %get-tuple-element.39), channel_id=1, source_target_pairs={{0,1},{1,0},{2,3},{3,2},{4,5},{5,4},{6,7},{7,6},{8,9},{9,8},{10,11... | collective-permute-start | bytes 98312 | tf_op jit(solution)/shard_map/ppermute | solution.py:346
  5.3 1.9 %collective-permute-start.1 = (bf16[32,512]{1,0:T(8,128)(2,1)S(1)}, bf16[32,512]{1,0:T(8,128)(2,1)S(1)}, u32[]{:S(2)}, u32[]{:S(2)}) collective-permute-start(bf16[32,512]{1,0:T(8,128)(2,1)S(1)} %get-tuple-element.40), channel_id=1, source_target_pairs={{1,2},{3,4},{5,6},{7,8},{9,10},{11,12},{13,14},{15,16},{17,18},{19... | collective-permute-start | bytes 98312 | tf_op jit(solution)/shard_map/ppermute | solution.py:351
  7.2 1.6 %mid_ready.1 = (bf16[512,512]{1,0:T(8,128)(2,1)S(1)}, bf16[512,512]{1,0:T(8,128)(2,1)S(1)}, bf16[512,512]{1,0:T(8,128)(2,1)S(1)}, bf16[32,512]{1,0:T(8,128)(2,1)...) custom-call(bf16[32,512]{1,0:T(8,128)(2,1)} %refs_0_.2, s32[1,32]{1,0:T(1,128)} %bitcast.19, ...), custom_call_target="tpu_custom_call" | custom-call | flops 1000000000 | bytes 1048576 | tf_op jit(solution)/shard_map/mid_ready/pallas_call | solution.py:88
  8.8 0.0 collective-permute-done.refs_1_
  8.8 1.7 %collective-permute-done.1.refs_2_ = bf16[32,512]{1,0:T(8,128)(2,1)S(1)} collective-permute-done((bf16[32,512]{1,0:T(8,128)(2,1)S(1)}, bf16[32,512]{1,0:T(8,128)(2,1)S(1)}, u32[]{:S(2)}, u32[]{:S(2)}) %collective-permute-start.1) | collective-permute-done | bytes 32800 | tf_op jit(solution)/shard_map/ppermute | solution.py:351
  10.5 0.6 mid_update.1.refs_0_
  11.1 0.1 collective-permute-start.2
  11.2 1.2 %collective-permute-done.2.refs_1_ = bf16[32,640]{1,0:T(8,128)(2,1)S(1)} collective-permute-done((bf16[32,640]{1,0:T(8,128)(2,1)S(1)}, bf16[32,640]{1,0:T(8,128)(2,1)S(1)}, u32[]{:S(2)}, u32[]{:S(2)}) %collective-permute-start.2) | collective-permute-done | bytes 40992 | tf_op jit(solution)/shard_map/ppermute | solution.py:346
  12.4 1.2 %coarse_blocks.1 = (bf16[64,640]{1,0:T(8,128)(2,1)}, bf16[384,512]{1,0:T(8,128)(2,1)}) custom-call(bf16[32,640]{1,0:T(8,128)(2,1)S(1)} %mid_update.1.refs_0_, bf16[32,640]{1,0:T(8,128)(2,1)S(1)} %collective-permute-done.2.refs_1_), custom_call_target="tpu_custom_call" | custom-call | bytes 1048576 | tf_op jit(solution)/shard_map/coarse_blocks/pallas_call | solution.py:88
  13.6 6.9 %all-to-all-start = ((bf16[16,24,512]{2,1,0:T(8,128)(2,1)}), bf16[16,24,512]{2,1,0:T(8,128)(2,1)S(1)}, u32[]{:S(2)}, u32[]{:S(2)}) async-start(bf16[16,24,512]{2,1,0:T(8,128)(2,1)} %bitcast.2.refs_4_), calls=%async_computation | async-start | bytes 786432 | tf_op jit(solution)/shard_map/all_to_all | solution.py:440
  20.5 1.5 %boundary.1 = (bf16[128,640]{1,0:T(8,128)(2,1)S(1)}, bf16[192,640]{1,0:T(8,128)(2,1)S(1)}) custom-call(s32[4,128]{1,0:T(4,128)} %bitcast.14, s32[2,128]{1,0:T(2,128)} %bitcast.18, bf16[512,512]{1,0:T(8,128)(2,1)} %refs_12_.1, bf16[64,640]{1,0:T(8,128)(2,1)} %get-tuple-element.48.refs_3_.refs_1_, bf16[16,24,512]{2,1,0:T(8,128)(2,1)} %bitcast.2.refs_4_), custom_call_target="tpu_custom_call" | custom-call | flops 500000000 | bytes 1048576 | tf_op jit(solution)/shard_map/boundary/pallas_call | solution.py:88
  22.0 3.9 %collective-permute-start.3 = (bf16[192,640]{1,0:T(8,128)(2,1)S(1)}, bf16[192,640]{1,0:T(8,128)(2,1)S(1)}, u32[]{:S(2)}, u32[]{:S(2)}) collective-permute-start(bf16[192,640]{1,0:T(8,128)(2,1)S(1)} %get-tuple-element.51), channel_id=1, source_target_pairs={{1,2},{3,4},{5,6},{7,8},{9,10},{11,12},{13,14},{15,16},{17,18},{19... | collective-permute-start | bytes 737288 | tf_op jit(solution)/shard_map/ppermute | solution.py:351
  25.9 0.1 collective-permute-start.4
  26.0 3.6 %tables.1 = (bf16[512,512]{1,0:T(8,128)(2,1)}, bf16[512,512]{1,0:T(8,128)(2,1)}, f32[512,512]{1,0:T(8,128)}, bf16[8,128]{1,0:T(8,128)(2,1)S(1)}) custom-call(bf16[512,512]{1,0:T(8,128)(2,1)} %refs_12_.1, bf16[512,512]{1,0:T(8,128)(2,1)} %refs_5_.7, bf16[512,512]{1,0:T(8,128)(2,1)} %refs_6_.3, bf16[512,512]{1,0:T(8,128)(2,1)} %refs_13_.1, ...), custom_call_target="tpu_custom_call" | custom-call | flops 2000000000 | bytes 1048576 | tf_op jit(solution)/shard_map/tables/pallas_call | solution.py:88
  29.6 0.0 collective-permute-done.4.refs_3_.refs_4_
  29.6 0.5 collective-permute-done.3.refs_2_.refs_3_.refs_0_
  30.1 0.0 all-to-all-done.refs_0_
  30.1 0.8 plane_sum.1.refs_11_
  30.9 8.2 %all-to-all-start.1 = ((bf16[8,24,512]{2,1,0:T(8,128)(2,1)}), bf16[8,24,512]{2,1,0:T(8,128)(2,1)S(1)}, u32[]{:S(2)}, u32[]{:S(2)}) async-start(bf16[8,24,512]{2,1,0:T(8,128)(2,1)} %plane_sum.1.refs_11_), calls=%async_computation.1 | async-start | bytes 393216 | tf_op jit(solution)/shard_map/all_to_all | solution.py:470
  39.1 1.7 %collective-permute-start.5 = (bf16[32,640]{1,0:T(8,128)(2,1)S(1)}, bf16[32,640]{1,0:T(8,128)(2,1)S(1)}, u32[]{:S(2)}, u32[]{:S(2)}) collective-permute-start(bf16[32,640]{1,0:T(8,128)(2,1)S(1)} %slice_select_fusion), channel_id=1, source_target_pairs={{0,1},{1,0},{2,3},{3,2},{4,5},{5,4},{6,7},{7,6},{8,9},{9,8},{10,11... | collective-permute-start | bytes 122888 | tf_op jit(solution)/shard_map/ppermute | solution.py:346
  40.8 7.3 %own_edges.1 = (bf16[512,512]{1,0:T(8,128)(2,1)S(1)}, bf16[3072,512]{1,0:T(8,128)(2,1)}, bf16[512,512]{1,0:T(8,128)(2,1)S(1)}, bf16[512,512]{1,0:T(8,128)(2,1)},...) custom-call(s32[24,128]{1,0:T(8,128)} %bitcast.16, s32[24,128]{1,0:T(8,128)} %bitcast.10, ...), custom_call_target="tpu_custom_call" | custom-call | flops 3500000000 | bytes 1048576 | tf_op jit(solution)/shard_map/own_edges/pallas_call | solution.py:88
  48.1 0.0 collective-permute-done.5.refs_5_.refs_2_
  48.1 0.0 copy-start.2
  48.1 0.0 all-to-all-done.1.refs_0_
  48.1 1.2 %coarse_update.1.refs_7_ = bf16[16,24,512]{2,1,0:T(8,128)(2,1)} custom-call(bf16[8,24,512]{2,1,0:T(8,128)(2,1)S(1)} %all-to-all-done.1.refs_0_, bf16[24,512]{1,0:T(8,128)(2,1)S(1)} %get-tuple-element.54.refs_1_, f32[24,512]{1,0:T(8,128)S(1)} %get-tuple-element.55.refs_2_, bf16[512,512]{1,0:T(8,128)(2,1)S(1)} %get-tuple-element.56.refs_3_, ...), custom_call_target="tpu_custom_call" | custom-call | bytes 1048576 | tf_op jit(solution)/shard_map/coarse_update/pallas_call | solution.py:88
  49.4 8.9 %all-to-all-start.2 = ((bf16[16,24,512]{2,1,0:T(8,128)(2,1)}), bf16[16,24,512]{2,1,0:T(8,128)(2,1)S(1)}, u32[]{:S(2)}, u32[]{:S(2)}) async-start(bf16[16,24,512]{2,1,0:T(8,128)(2,1)} %coarse_update.1.refs_7_), calls=%async_computation.2 | async-start | bytes 786432 | tf_op jit(solution)/shard_map/all_to_all | solution.py:492
  58.3 9.8 %rest_edges.1 = (bf16[3072,512]{1,0:T(8,128)(2,1)}, bf16[3072,256]{1,0:T(8,128)(2,1)}, bf16[512,128]{1,0:T(8,128)(2,1)}, bf16[8,128]{1,0:T(8,128)(2,1)S(1)}) custom-call(s32[24,128]{1,0:T(8,128)} %bitcast.17, s32[24,128]{1,0:T(8,128)} %bitcast.11, s32[4,128]{1,0:T(4,128)} %bitcast.15, bf16[192,640]{1,0:T(8,128)(2,1)} %copy-done, bf16[128,640]{1,0:T(8,128)(2,1)} %copy-done.1, ...), custom_call_target="tpu_custom_call" | custom-call | flops 3500000000 | bytes 1048576 | tf_op jit(solution)/shard_map/rest_edges/pallas_call | solution.py:88
  68.1 0.1 all-to-all-done.2
  68.2 1.2 %collective-permute-start.6 = (bf16[384,512]{1,0:T(8,128)(2,1)S(1)}, bf16[384,512]{1,0:T(8,128)(2,1)S(1)}, u32[]{:S(2)}, u32[]{:S(2)}) collective-permute-start(bf16[384,512]{1,0:T(8,128)(2,1)S(1)} %bitcast.7), channel_id=1, source_target_pairs={{0,1},{1,0},{2,3},{3,2},{4,5},{5,4},{6,7},{7,6},{8,9},{9,8},{10,11... | collective-permute-start | bytes 1179656 | tf_op jit(solution)/shard_map/ppermute | solution.py:346
  69.4 1.8 %final_ready.1 = (bf16[512,512]{1,0:T(8,128)(2,1)S(1)}, bf16[512,512]{1,0:T(8,128)(2,1)S(1)}, bf16[512,512]{1,0:T(8,128)(2,1)S(1)}, bf16[512,512]{1,0:T(8,128)(2...) custom-call(bf16[192,640]{1,0:T(8,128)(2,1)} %copy-done, ...), custom_call_target="tpu_custom_call" | custom-call | flops 1000000000 | bytes 1048576 | tf_op jit(solution)/shard_map/final_ready/pallas_call | solution.py:88
  71.1 9.6 %final.1 = (bf16[512,512]{1,0:T(8,128)(2,1)}, bf16[32,512]{1,0:T(8,128)(2,1)}, bf16[642,512]{1,0:T(8,128)(2,1)}) custom-call(bf16[384,512]{1,0:T(8,128)(2,1)S(1)} %bitcast.9, bf16[384,512]{1,0:T(8,128)(2,1)S(1)} %collective-permute-done.6.refs_1_, bf16[512,512]{1,0:T(8,128)(2,1)S(1)} %get-tuple-element.62.refs_2_, ...), custom_call_target="tpu_custom_call" | custom-call | bytes 1048576 | tf_op jit(solution)/shard_map/final/pallas_call | solution.py:88
  (7 shorter events, 0.0 us)
Async XLA Ops:
  1.9 6.9 %collective-permute-start = (bf16[32,512]{1,0:T(8,128)(2,1)S(1)}, bf16[32,512]{1,0:T(8,128)(2,1)S(1)}, u32[]{:S(2)}, u32[]{:S(2)}) collective-permute-start(bf16[32,512]{1,0:T(8,128)(2,1)S(1)} %get-tuple-element.39), channel_id=1, source_target_pairs={{0,1},{1,0},{2,3},{3,2},{4,5},{5,4},{6,7},{7,6},{8,9},{9,8},{10,11... | collective-permute-start | bytes 98312 | tf_op jit(solution)/shard_map/ppermute | solution.py:346
  5.3 5.2 %collective-permute-start.1 = (bf16[32,512]{1,0:T(8,128)(2,1)S(1)}, bf16[32,512]{1,0:T(8,128)(2,1)S(1)}, u32[]{:S(2)}, u32[]{:S(2)}) collective-permute-start(bf16[32,512]{1,0:T(8,128)(2,1)S(1)} %get-tuple-element.40), channel_id=1, source_target_pairs={{1,2},{3,4},{5,6},{7,8},{9,10},{11,12},{13,14},{15,16},{17,18},{19... | collective-permute-start | bytes 98312 | tf_op jit(solution)/shard_map/ppermute | solution.py:351
  11.1 1.3 %collective-permute-start.2 = (bf16[32,640]{1,0:T(8,128)(2,1)S(1)}, bf16[32,640]{1,0:T(8,128)(2,1)S(1)}, u32[]{:S(2)}, u32[]{:S(2)}) collective-permute-start(bf16[32,640]{1,0:T(8,128)(2,1)S(1)} %mid_update.1.refs_0_), channel_id=1, source_target_pairs={{0,1},{1,0},{2,3},{3,2},{4,5},{5,4},{6,7},{7,6},{8,9},{9,8},{10,11... | collective-permute-start | bytes 122888 | tf_op jit(solution)/shard_map/ppermute | solution.py:346
  13.6 16.5 %all-to-all-start = ((bf16[16,24,512]{2,1,0:T(8,128)(2,1)}), bf16[16,24,512]{2,1,0:T(8,128)(2,1)S(1)}, u32[]{:S(2)}, u32[]{:S(2)}) async-start(bf16[16,24,512]{2,1,0:T(8,128)(2,1)} %bitcast.2.refs_4_), calls=%async_computation | async-start | bytes 786432 | tf_op jit(solution)/shard_map/all_to_all | solution.py:440
  22.0 8.1 %collective-permute-start.3 = (bf16[192,640]{1,0:T(8,128)(2,1)S(1)}, bf16[192,640]{1,0:T(8,128)(2,1)S(1)}, u32[]{:S(2)}, u32[]{:S(2)}) collective-permute-start(bf16[192,640]{1,0:T(8,128)(2,1)S(1)} %get-tuple-element.51), channel_id=1, source_target_pairs={{1,2},{3,4},{5,6},{7,8},{9,10},{11,12},{13,14},{15,16},{17,18},{19... | collective-permute-start | bytes 737288 | tf_op jit(solution)/shard_map/ppermute | solution.py:351
  25.9 3.7 %collective-permute-start.4 = (bf16[128,640]{1,0:T(8,128)(2,1)S(1)}, bf16[128,640]{1,0:T(8,128)(2,1)S(1)}, u32[]{:S(2)}, u32[]{:S(2)}) collective-permute-start(bf16[128,640]{1,0:T(8,128)(2,1)S(1)} %get-tuple-element.49.refs_4_), channel_id=1, source_target_pairs={{0,1},{1,0},{2,3},{3,2},{4,5},{5,4},{6,7},{7,6},{8,9},{9,8},{10,11... | collective-permute-start | bytes 491528 | tf_op jit(solution)/shard_map/ppermute | solution.py:346
  29.6 18.5 %copy-start.1 = (bf16[128,640]{1,0:T(8,128)(2,1)}, bf16[128,640]{1,0:T(8,128)(2,1)S(1)}, u32[]{:S(2)}) copy-start(bf16[128,640]{1,0:T(8,128)(2,1)S(1)} %collective-permute-done.4.refs_3_.refs_4_) | copy-start | bytes 491524
  30.1 18.0 %copy-start = (bf16[192,640]{1,0:T(8,128)(2,1)}, bf16[192,640]{1,0:T(8,128)(2,1)S(1)}, u32[]{:S(2)}) copy-start(bf16[192,640]{1,0:T(8,128)(2,1)S(1)} %collective-permute-done.3.refs_2_.refs_3_.refs_0_) | copy-start | bytes 737284
  30.9 17.2 %all-to-all-start.1 = ((bf16[8,24,512]{2,1,0:T(8,128)(2,1)}), bf16[8,24,512]{2,1,0:T(8,128)(2,1)S(1)}, u32[]{:S(2)}, u32[]{:S(2)}) async-start(bf16[8,24,512]{2,1,0:T(8,128)(2,1)} %plane_sum.1.refs_11_), calls=%async_computation.1 | async-start | bytes 393216 | tf_op jit(solution)/shard_map/all_to_all | solution.py:470
  39.1 9.0 %collective-permute-start.5 = (bf16[32,640]{1,0:T(8,128)(2,1)S(1)}, bf16[32,640]{1,0:T(8,128)(2,1)S(1)}, u32[]{:S(2)}, u32[]{:S(2)}) collective-permute-start(bf16[32,640]{1,0:T(8,128)(2,1)S(1)} %slice_select_fusion), channel_id=1, source_target_pairs={{0,1},{1,0},{2,3},{3,2},{4,5},{5,4},{6,7},{7,6},{8,9},{9,8},{10,11... | collective-permute-start | bytes 122888 | tf_op jit(solution)/shard_map/ppermute | solution.py:346
  48.1 20.0 %copy-start.2 = (bf16[32,640]{1,0:T(8,128)(2,1)}, bf16[32,640]{1,0:T(8,128)(2,1)S(1)}, u32[]{:S(2)}) copy-start(bf16[32,640]{1,0:T(8,128)(2,1)S(1)} %collective-permute-done.5.refs_5_.refs_2_) | copy-start | bytes 122884
  49.4 18.8 %all-to-all-start.2 = ((bf16[16,24,512]{2,1,0:T(8,128)(2,1)}), bf16[16,24,512]{2,1,0:T(8,128)(2,1)S(1)}, u32[]{:S(2)}, u32[]{:S(2)}) async-start(bf16[16,24,512]{2,1,0:T(8,128)(2,1)} %coarse_update.1.refs_7_), calls=%async_computation.2 | async-start | bytes 786432 | tf_op jit(solution)/shard_map/all_to_all | solution.py:492
  68.2 2.9 %collective-permute-start.6 = (bf16[384,512]{1,0:T(8,128)(2,1)S(1)}, bf16[384,512]{1,0:T(8,128)(2,1)S(1)}, u32[]{:S(2)}, u32[]{:S(2)}) collective-permute-start(bf16[384,512]{1,0:T(8,128)(2,1)S(1)} %bitcast.7), channel_id=1, source_target_pairs={{0,1},{1,0},{2,3},{3,2},{4,5},{5,4},{6,7},{7,6},{8,9},{9,8},{10,11... | collective-permute-start | bytes 1179656 | tf_op jit(solution)/shard_map/ppermute | solution.py:346

commit v5 on v4

--- a/solution.py
+++ b/solution.py
@@ -11,6 +11,7 @@
 BLOCK = 24
 LANES = 128
 CHUNK = 512
+PIECE = 1536
 PLANE = ("y", "x")
 TILE = ("y", "x", "c")
 F32, BF16, I32 = jnp.float32, jnp.bfloat16, jnp.int32
@@ -54,8 +55,8 @@
 ):
     count, held, skipped, given = len(operands), len(stored), len(after), len(outs)
     target = dict(keep)
-    cuts = [stored[i].shape[0] // CHUNK if i in pieces else 1 for i in range(held)]
-    flows = {o: outs[o].shape[0] // CHUNK for o in streams}
+    cuts = [stored[i].shape[0] // PIECE if i in pieces else 1 for i in range(held)]
+    flows = {o: outs[o].shape[0] // PIECE for o in streams}
 
     def kernel(*refs):
         inputs, refs = refs[:count], refs[count:]
@@ -205,35 +206,20 @@
 
 
 def gather_body(parts, out):
-    total = jnp.sum(parts[...].astype(F32), axis=0).astype(BF16)
-    for i in range(out.shape[0]):
-        out[i] = total
-
-
-def coarse_body(parts, own_latent, own_hidden, both, third, out):
-    total = jnp.sum(parts[...].astype(F32), axis=0).astype(BF16)
+    out[...] = jnp.sum(parts[...].astype(F32), axis=0).astype(BF16)
+
+
+def coarse_body(mine, theirs, own_latent, own_hidden, both, third, out):
+    total = (mine[...].astype(F32) + theirs[...].astype(F32)).astype(BF16)
     hidden = silu(own_hidden[...] + product(total, both[...]))
     result = updated(own_latent[...], hidden, third[...])
     for i in range(out.shape[0]):
         out[i] = result
 
 
-def own_edges_body(
-    source, target, sender, receiver, coarse, coarse_w1, w_coarse, coarse_w2, edge_w2, node_w2, third,
-    sent_out, both, last, own_latent, own_hidden, out,
+def coarse_ready_body(
+    coarse, coarse_w1, w_coarse, coarse_w2, edge_w2, node_w2, third, both, last, own_latent, own_hidden
 ):
-    count = sender.shape[0]
-    blocks = count // LANES
-    sent, received = sender[...], receiver[...]
-    for k in range(out.shape[0] // CHUNK):
-        marks = range(k * CHUNK // LANES, (k + 1) * CHUNK // LANES)
-        picked = [jnp.concatenate(picks(spread(source[r : r + 1, :]), 0, blocks), axis=1) for r in marks]
-        total = product(jnp.concatenate(picked, axis=0), sent)
-        picked = [jnp.concatenate(picks(spread(target[r : r + 1, :]), 0, blocks), axis=1) for r in marks]
-        total += product(jnp.concatenate(picked, axis=0), received)
-        out[k * CHUNK : (k + 1) * CHUNK, :] = total.astype(BF16)
-        sent_out.start(k)
-    last[...] = product(edge_w2[...], node_w2[...]).astype(BF16)
     rows, total = own_latent.shape[0], coarse.shape[0]
     chips = lax.axis_size("y") * lax.axis_size("x")
     chip = lax.axis_index("y") * lax.axis_size("x") + lax.axis_index("x")
@@ -244,6 +230,7 @@
     own_latent[...] = latent
     own_hidden[...] = product(latent, coarse_w1[...])
     both[...] = product(w_coarse[...], coarse_w2[...]).astype(BF16)
+    last[...] = product(edge_w2[...], node_w2[...]).astype(BF16)
 
 
 def slots(codes, tile, count):
@@ -253,8 +240,8 @@
     return jnp.where(codes > 0, (tile + away) * count + (parent & (count - 1)), -1)
 
 
-def rest_edges_body(
-    mid_count, source, target, parent, cross, swap, w_src, first, sent_out, sent_select, own_pick, token,
+def edges_body(
+    mid_count, parent, source, target, cross, swap, w_src, sender, receiver, sent_out, sent_select, own_pick, token,
     out, select, table, where
 ):
     token[...] = jnp.zeros_like(token)
@@ -273,11 +260,12 @@
         there = slice(count + 2 * LANES + r * LANES, count + 2 * LANES + (r + 1) * LANES)
         where[there, :] = jnp.concatenate(picks(far, 0, 2), axis=1)
     for values, late in ((cross[two:], core), (swap[...], 1 - core)):
-        rows = pl.ds(pl.multiple_of(late * LANES, LANES), LANES)
+        rows = pl.ds(pl.multiple_of(count + late * LANES, LANES), LANES)
         table[rows, :] = product(values[:, :width], w_src[...]).astype(BF16)
         place = slots(values[:, width:].astype(F32).astype(I32), 1 + 2 * late, mid_count)
-        rows = pl.ds(pl.multiple_of(count + late * LANES, LANES), LANES)
         where[rows, :] = jnp.concatenate(picks(place, 0, 2), axis=1)
+    table[:count] = sender[...]
+    table[count + 2 * LANES :] = receiver[...]
     for k in range(out.shape[0] // CHUNK):
         rows = []
         for r in range(k * CHUNK // LANES, (k + 1) * CHUNK // LANES):
@@ -287,10 +275,10 @@
         picked = jnp.concatenate(rows, axis=0)
         here = slice(k * CHUNK, (k + 1) * CHUNK)
         select[here, :] = product(picked, where[...]).astype(BF16)
-        sent_select.start(k)
-        rest = product(picked[:, count : count + 2 * LANES], table[...])
-        out[here, :] = (first.get(k)[here, :].astype(F32) + rest).astype(BF16)
-        sent_out.start(k)
+        out[here, :] = product(picked, table[...]).astype(BF16)
+        if (k + 1) * CHUNK % PIECE == 0:
+            sent_out.start(k * CHUNK // PIECE)
+            sent_select.start(k * CHUNK // PIECE)
 
 
 def ready_body(rows, cross, pair, swap, w_descend, w_fine, w_src, w_dst, middle, picked, window):
@@ -325,7 +313,8 @@
     rows = lax.broadcasted_iota(I32, (fine.shape[0], LANES), 0)
     for k in range(edges.shape[0] // CHUNK):
         here = slice(k * CHUNK, (k + 1) * CHUNK)
-        edge_sum = edges.get(k)[here, :].astype(F32) + product(select.get(k)[here, :], table[...])
+        piece = k * CHUNK // PIECE
+        edge_sum = edges.get(piece)[here, :].astype(F32) + product(select.get(piece)[here, :], table[...])
         hidden = silu(edge_sum).astype(BF16)
         marks = range(k * CHUNK // LANES, (k + 1) * CHUNK // LANES)
         scatter = jnp.concatenate([hot(rows == target[r : r + 1, :]) for r in marks], axis=1)
@@ -344,6 +333,10 @@
 
 def swapped(values):
     return lax.ppermute(values, "c", [(0, 1), (1, 0)])
+
+
+def paired(values, step):
+    return lax.ppermute(values, "z", [(i, i ^ step) for i in range(lax.axis_size("z"))])
 
 
 def crossed(values, tiles):
@@ -460,48 +453,45 @@
         name="tables",
     )
 
-    (own_parts,) = kernel_call(
-        gather_body,
-        [near(planes, BLOCK, width)],
-        [parts],
-        after=[token, cross_in, halo_in],
-        name="plane_sum",
-    )
-    in_planes = lax.all_to_all(own_parts, "z", 0, 0)
+    (total,) = kernel_call(
+        gather_body, [free(BLOCK, width)], [parts], after=[token, cross_in, halo_in], name="plane_sum"
+    )
     mid_in = swapped(jnp.where(lax.axis_index("c") == 0, cross_in[mids : 2 * mids], cross_in[:mids]))
-    coarse_w3, own_edges, both, last, own_latent, own_hidden = kernel_call(
-        own_edges_body,
-        [square, far(edge_count, width), square, far(width, width), near(BLOCK, width), near(BLOCK, width, dtype=F32)],
-        [],
-        stored=[source, target, sender, receiver, coarse_latent, coarse_w1, w_coarse, coarse_w2, edge_w2, node_w2, coarse_w3],
-        keep=[(10, 0)],
-        streams=[1],
-        after=[own_parts],
-        limit=20,
-        flops=3_500_000_000,
-        name="own_edges",
+    step = 1
+    while 2 * step < planes:
+        total = (total.astype(F32) + paired(total, step).astype(F32)).astype(BF16)
+        step *= 2
+    other = paired(total, step)
+    coarse_w3, both, last, own_latent, own_hidden = kernel_call(
+        coarse_ready_body,
+        [square, square, far(width, width), near(BLOCK, width), near(BLOCK, width, dtype=F32)],
+        [],
+        stored=[coarse_latent, coarse_w1, w_coarse, coarse_w2, edge_w2, node_w2, coarse_w3],
+        keep=[(6, 0)],
+        after=[total],
+        flops=1_500_000_000,
+        name="coarse_ready",
     )
 
     (results,) = kernel_call(
         coarse_body,
         [near(chips, BLOCK, width)],
-        [in_planes] + [here(a) for a in (own_latent, own_hidden, both, coarse_w3)],
+        [total, other] + [here(a) for a in (own_latent, own_hidden, both, coarse_w3)],
         after=[mid_in],
         name="coarse_update",
     )
     mine = lax.all_to_all(results, PLANE, 0, 0).reshape(half, width)
     edges, select, own_pick, token = kernel_call(
-        functools.partial(rest_edges_body, mids),
+        functools.partial(edges_body, mids),
         [far(edge_count, width), far(edge_count, 2 * LANES), far(count, LANES), free(8, LANES)],
         [],
-        stored=[source, target, parent, cross_in, halo_in, edge_w_src, own_edges],
-        pieces=[6],
+        stored=[parent, source, target, cross_in, halo_in, edge_w_src, sender, receiver],
         streams=[0, 1],
         after=[results],
-        scratch=[pltpu.VMEM((2 * LANES, width), BF16), pltpu.VMEM((2 * count + 2 * LANES, 2 * LANES), BF16)],
+        scratch=[pltpu.VMEM((2 * count + 2 * LANES, width), BF16), pltpu.VMEM((2 * count + 2 * LANES, 2 * LANES), BF16)],
         limit=24,
-        flops=3_500_000_000,
-        name="rest_edges",
+        flops=6_500_000_000,
+        name="edges",
     )
     mine, own_pick = lax.optimization_barrier((mine, own_pick))
     theirs = swapped(mine)

time: 81.5 us -> 80.4 us (0.987)
  Pallas kernels: 40.3 us -> 36.2 us
  starting transfers between devices: 36.1 us -> 38 us
  waiting for transfers between devices: 3.5 us -> 4.71 us
    ppermute x0 -> x3, starting transfers between devices: none -> 10 us  [paired(): lax.ppermute(values, 'z', [(i, i ^ step) for i in range(lax.axis_size('z'...]
    all_to_all x1 -> x0, starting transfers between devices: 8.19 us -> none  [on_device(): in_planes = lax.all_to_all(own_parts, 'z', 0, 0)]
    pallas_call x12, Pallas kernels: 40.3 us -> 36.2 us  [kernel_call(): pl.pallas_call(kernel, out_shape=outs, in_specs=[VMEM] * count + [STORED]...]
    ppermute x5, starting transfers between devices: 6.39 us -> 7.75 us  [swapped(): return lax.ppermute(values, 'c', [(0, 1), (1, 0)])]
    all_to_all x1, starting transfers between devices: 8.89 us -> 7.65 us  [on_device(): mine = lax.all_to_all(results, PLANE, 0, 0).reshape(half, width)]
    ppermute x0 -> x3, waiting for transfers between devices: none -> 1.22 us  [paired(): lax.ppermute(values, 'z', [(i, i ^ step) for i in range(lax.axis_size('z'...]
  transfers between devices with their start and end apart: 10 -> 12, of which waited for: 4 -> 4; matrix products, arithmetic and copies ran while one was open for 0% -> 0% of each run, Pallas kernels for 32% -> 28%
where the time goes in v5:
time: 80.4 us; the launch traced here: 80 us
  starting transfers between devices  38 us (47%)
  Pallas kernels  36.2 us (45%)
  waiting for transfers between devices  4.71 us (6%)
  between operations  1.01 us (1%)
    pallas_call x12, Pallas kernels, kernel_call(): pl.pallas_call(kernel, out_shape=outs, in_specs=[VMEM] * count + [STORED]...  36.2 us
    ppermute x3, starting transfers between devices, paired(): lax.ppermute(values, 'z', [(i, i ^ step) for i in range(lax.axis_size('z'...  10 us
    ppermute x5, starting transfers between devices, swapped(): return lax.ppermute(values, 'c', [(0, 1), (1, 0)])  7.75 us
    all_to_all x1, starting transfers between devices, on_device(): mine = lax.all_to_all(results, PLANE, 0, 0).reshape(half, width)  7.65 us
    all_to_all x1, starting transfers between devices, on_device(): parts = lax.all_to_all(blocks, PLANE, 0, 0)  6.86 us
    ppermute x2, starting transfers between devices, crossed(): return lax.ppermute(values, TILE, pairs + [(b, a) for a, b in pairs])  5.78 us
    ppermute x2, waiting for transfers between devices, crossed(): return lax.ppermute(values, TILE, pairs + [(b, a) for a, b in pairs])  2.26 us
  transfers between devices with their start and end apart: 12, of which 4 were waited for; matrix products, arithmetic and copies ran while one was open for 0% of the time, Pallas kernels for 28%

profile of v5, /device:TPU:1, one launch (start us, length us, event | category | flops | bytes accessed | tf_op | source)
XLA Modules:
  0.0 80.0 jit_solution(2182833837398187869)
XLA Ops:
  0.6 1.3 %child_sums.1 = (f32[32,512]{1,0:T(8,128)S(1)}, bf16[32,512]{1,0:T(8,128)(2,1)S(1)}, bf16[32,512]{1,0:T(8,128)(2,1)S(1)}) custom-call(s32[4,128]{1,0:T(4,128)} %bitcast.12, bf16[512,512]{1,0:T(8,128)(2,1)} %refs_12_.1), custom_call_target="tpu_custom_call" | custom-call | bytes 1048576 | tf_op jit(solution)/shard_map/child_sums/pallas_call | solution.py:89
  1.9 3.3 %collective-permute-start = (bf16[32,512]{1,0:T(8,128)(2,1)S(1)}, bf16[32,512]{1,0:T(8,128)(2,1)S(1)}, u32[]{:S(2)}, u32[]{:S(2)}) collective-permute-start(bf16[32,512]{1,0:T(8,128)(2,1)S(1)} %get-tuple-element.38), channel_id=1, source_target_pairs={{0,1},{1,0},{2,3},{3,2},{4,5},{5,4},{6,7},{7,6},{8,9},{9,8},{10,11... | collective-permute-start | bytes 98312 | tf_op jit(solution)/shard_map/ppermute | solution.py:335
  5.3 1.9 %collective-permute-start.1 = (bf16[32,512]{1,0:T(8,128)(2,1)S(1)}, bf16[32,512]{1,0:T(8,128)(2,1)S(1)}, u32[]{:S(2)}, u32[]{:S(2)}) collective-permute-start(bf16[32,512]{1,0:T(8,128)(2,1)S(1)} %get-tuple-element.39), channel_id=1, source_target_pairs={{1,2},{3,4},{5,6},{7,8},{9,10},{11,12},{13,14},{15,16},{17,18},{19... | collective-permute-start | bytes 98312 | tf_op jit(solution)/shard_map/ppermute | solution.py:344
  7.2 1.6 %mid_ready.1 = (bf16[512,512]{1,0:T(8,128)(2,1)S(1)}, bf16[512,512]{1,0:T(8,128)(2,1)S(1)}, bf16[512,512]{1,0:T(8,128)(2,1)S(1)}, bf16[32,512]{1,0:T(8,128)(2,1)...) custom-call(bf16[32,512]{1,0:T(8,128)(2,1)} %refs_0_.3, s32[1,32]{1,0:T(1,128)} %bitcast.17, ...), custom_call_target="tpu_custom_call" | custom-call | flops 1000000000 | bytes 1048576 | tf_op jit(solution)/shard_map/mid_ready/pallas_call | solution.py:89
  8.8 0.0 collective-permute-done.refs_1_
  8.8 1.7 %collective-permute-done.1.refs_2_ = bf16[32,512]{1,0:T(8,128)(2,1)S(1)} collective-permute-done((bf16[32,512]{1,0:T(8,128)(2,1)S(1)}, bf16[32,512]{1,0:T(8,128)(2,1)S(1)}, u32[]{:S(2)}, u32[]{:S(2)}) %collective-permute-start.1) | collective-permute-done | bytes 32800 | tf_op jit(solution)/shard_map/ppermute | solution.py:344
  10.5 0.6 mid_update.1.refs_0_
  11.1 0.1 collective-permute-start.2
  11.2 1.2 %collective-permute-done.2.refs_1_ = bf16[32,640]{1,0:T(8,128)(2,1)S(1)} collective-permute-done((bf16[32,640]{1,0:T(8,128)(2,1)S(1)}, bf16[32,640]{1,0:T(8,128)(2,1)S(1)}, u32[]{:S(2)}, u32[]{:S(2)}) %collective-permute-start.2) | collective-permute-done | bytes 40992 | tf_op jit(solution)/shard_map/ppermute | solution.py:335
  12.4 1.2 %coarse_blocks.1 = (bf16[64,640]{1,0:T(8,128)(2,1)}, bf16[384,512]{1,0:T(8,128)(2,1)}) custom-call(bf16[32,640]{1,0:T(8,128)(2,1)S(1)} %mid_update.1.refs_0_, bf16[32,640]{1,0:T(8,128)(2,1)S(1)} %collective-permute-done.2.refs_1_), custom_call_target="tpu_custom_call" | custom-call | bytes 1048576 | tf_op jit(solution)/shard_map/coarse_blocks/pallas_call | solution.py:89
  13.6 6.9 %all-to-all-start = ((bf16[16,24,512]{2,1,0:T(8,128)(2,1)}), bf16[16,24,512]{2,1,0:T(8,128)(2,1)S(1)}, u32[]{:S(2)}, u32[]{:S(2)}) async-start(bf16[16,24,512]{2,1,0:T(8,128)(2,1)} %bitcast.2.refs_4_), calls=%async_computation | async-start | bytes 786432 | tf_op jit(solution)/shard_map/all_to_all | solution.py:433
  20.5 1.5 %boundary.1 = (bf16[128,640]{1,0:T(8,128)(2,1)S(1)}, bf16[192,640]{1,0:T(8,128)(2,1)S(1)}) custom-call(s32[4,128]{1,0:T(4,128)} %bitcast.13, s32[2,128]{1,0:T(2,128)} %bitcast.16, bf16[512,512]{1,0:T(8,128)(2,1)} %refs_12_.1, bf16[64,640]{1,0:T(8,128)(2,1)} %get-tuple-element.47.refs_3_.refs_1_, bf16[16,24,512]{2,1,0:T(8,128)(2,1)} %bitcast.2.refs_4_), custom_call_target="tpu_custom_call" | custom-call | flops 500000000 | bytes 1048576 | tf_op jit(solution)/shard_map/boundary/pallas_call | solution.py:89
  22.0 3.9 %collective-permute-start.3 = (bf16[192,640]{1,0:T(8,128)(2,1)S(1)}, bf16[192,640]{1,0:T(8,128)(2,1)S(1)}, u32[]{:S(2)}, u32[]{:S(2)}) collective-permute-start(bf16[192,640]{1,0:T(8,128)(2,1)S(1)} %get-tuple-element.50), channel_id=1, source_target_pairs={{1,2},{3,4},{5,6},{7,8},{9,10},{11,12},{13,14},{15,16},{17,18},{19... | collective-permute-start | bytes 737288 | tf_op jit(solution)/shard_map/ppermute | solution.py:344
  25.9 0.1 collective-permute-start.4
  26.0 3.5 %tables.1 = (bf16[512,512]{1,0:T(8,128)(2,1)}, bf16[512,512]{1,0:T(8,128)(2,1)}, f32[512,512]{1,0:T(8,128)}, bf16[8,128]{1,0:T(8,128)(2,1)S(1)}) custom-call(bf16[512,512]{1,0:T(8,128)(2,1)} %refs_12_.1, bf16[512,512]{1,0:T(8,128)(2,1)} %refs_5_.7, bf16[512,512]{1,0:T(8,128)(2,1)} %refs_6_.3, bf16[512,512]{1,0:T(8,128)(2,1)} %refs_13_.1, ...), custom_call_target="tpu_custom_call" | custom-call | flops 2000000000 | bytes 1048576 | tf_op jit(solution)/shard_map/tables/pallas_call | solution.py:89
  29.6 0.6 collective-permute-done.3.refs_2_.refs_3_.refs_0_
  30.1 0.0 all-to-all-done.refs_0_
  30.2 0.1 plane_sum.1
  30.2 1.7 %collective-permute-start.5 = (bf16[24,512]{1,0:T(8,128)(2,1)S(1)}, bf16[24,512]{1,0:T(8,128)(2,1)S(1)}, u32[]{:S(2)}, u32[]{:S(2)}) collective-permute-start(bf16[24,512]{1,0:T(8,128)(2,1)S(1)} %plane_sum.1), channel_id=1, source_target_pairs={{0,32},{32,0},{64,96},{96,64},{128,160},{160,128},{192,224},{224,1... | collective-permute-start | bytes 73736 | tf_op jit(solution)/shard_map/ppermute | solution.py:339
  31.9 1.2 %collective-permute-done.5 = bf16[24,512]{1,0:T(8,128)(2,1)S(1)} collective-permute-done((bf16[24,512]{1,0:T(8,128)(2,1)S(1)}, bf16[24,512]{1,0:T(8,128)(2,1)S(1)}, u32[]{:S(2)}, u32[]{:S(2)}) %collective-permute-start.5) | collective-permute-done | bytes 24608 | tf_op jit(solution)/shard_map/ppermute | solution.py:339
  33.2 3.1 %collective-permute-start.6 = (bf16[24,512]{1,0:T(8,128)(2,1)S(1)}, bf16[24,512]{1,0:T(8,128)(2,1)S(1)}, u32[]{:S(2)}, u32[]{:S(2)}) collective-permute-start(bf16[24,512]{1,0:T(8,128)(2,1)S(1)} %add_convert_fusion.1), channel_id=1, source_target_pairs={{0,64},{32,96},{64,0},{96,32},{128,192},{160,224},{192,128},{224,1... | collective-permute-start | bytes 73736 | tf_op jit(solution)/shard_map/ppermute | solution.py:339
  36.3 2.7 %collective-permute-start.8 = (bf16[32,640]{1,0:T(8,128)(2,1)S(1)}, bf16[32,640]{1,0:T(8,128)(2,1)S(1)}, u32[]{:S(2)}, u32[]{:S(2)}) collective-permute-start(bf16[32,640]{1,0:T(8,128)(2,1)S(1)} %slice_select_fusion), channel_id=1, source_target_pairs={{0,1},{1,0},{2,3},{3,2},{4,5},{5,4},{6,7},{7,6},{8,9},{9,8},{10,11... | collective-permute-start | bytes 122888 | tf_op jit(solution)/shard_map/ppermute | solution.py:335
  39.0 0.0 collective-permute-done.6
  39.0 5.2 %collective-permute-start.7 = (bf16[24,512]{1,0:T(8,128)(2,1)S(1)}, bf16[24,512]{1,0:T(8,128)(2,1)S(1)}, u32[]{:S(2)}, u32[]{:S(2)}) collective-permute-start(bf16[24,512]{1,0:T(8,128)(2,1)S(1)} %add_convert_fusion.refs_7_.refs_0_), channel_id=1, source_target_pairs={{0,128},{32,160},{64,192},{96,224},{128,0},{160,32},{192,64},{224,... | collective-permute-start | bytes 73736 | tf_op jit(solution)/shard_map/ppermute | solution.py:339
  44.2 3.3 %coarse_ready.1 = (bf16[512,512]{1,0:T(8,128)(2,1)S(1)}, bf16[512,512]{1,0:T(8,128)(2,1)S(1)}, bf16[512,512]{1,0:T(8,128)(2,1)}, bf16[24,512]{1,0:T(8,128)(2,1)S(1)}, f32[24,512]{1,0:T(8,128)S(1)}) custom-call(bf16[642,512]{1,0:T(8,128)(2,1)} %refs_0_.5, bf16[512,512]{1,0:T(8,128)(2,1)} %refs_1_.5, bf16[512,512]{1,0:T(8,128)(2,1)} %refs_2_.7, ...), custom_call_target="tpu_custom_call" | custom-call | flops 1500000000 | bytes 1048576 | tf_op jit(solution)/shard_map/coarse_ready/pallas_call | solution.py:89
  47.6 0.0 collective-permute-done.7.refs_1_
  47.6 1.3 %coarse_update.1.refs_8_ = bf16[16,24,512]{2,1,0:T(8,128)(2,1)} custom-call(bf16[24,512]{1,0:T(8,128)(2,1)S(1)} %add_convert_fusion.refs_7_.refs_0_, bf16[24,512]{1,0:T(8,128)(2,1)S(1)} %collective-permute-done.7.refs_1_, bf16[24,512]{1,0:T(8,128)(2,1)S(1)} %get-tuple-element.51.refs_2_, f32[24,512]{1,0:T(8,128)S(1)} %get-tuple-element.52.refs_3_, ...), custom_call_target="tpu_custom_call" | custom-call | bytes 1048576 | tf_op jit(solution)/shard_map/coarse_update/pallas_call | solution.py:89
  48.8 7.7 %all-to-all-start.1 = ((bf16[16,24,512]{2,1,0:T(8,128)(2,1)}), bf16[16,24,512]{2,1,0:T(8,128)(2,1)S(1)}, u32[]{:S(2)}, u32[]{:S(2)}) async-start(bf16[16,24,512]{2,1,0:T(8,128)(2,1)} %coarse_update.1.refs_8_), calls=%async_computation.1 | async-start | bytes 786432 | tf_op jit(solution)/shard_map/all_to_all | solution.py:483
  56.5 10.4 %edges.1 = (bf16[3072,512]{1,0:T(8,128)(2,1)}, bf16[3072,256]{1,0:T(8,128)(2,1)}, bf16[512,128]{1,0:T(8,128)(2,1)}, bf16[8,128]{1,0:T(8,128)(2,1)S(1)}) custom-call(s32[4,128]{1,0:T(4,128)} %bitcast.14, s32[24,128]{1,0:T(8,128)} %bitcast.15, s32[24,128]{1,0:T(8,128)} %bitcast.10, bf16[192,640]{1,0:T(8,128)(2,1)} %copy-done, bf16[128,640]{1,0:T(8,128)(2,1)} %copy-done.1, ...), custom_call_target="tpu_custom_call" | custom-call | flops 6499999744 | bytes 1048576 | tf_op jit(solution)/shard_map/edges/pallas_call | solution.py:89
  67.0 1.5 %collective-permute-start.9 = (bf16[384,512]{1,0:T(8,128)(2,1)S(1)}, bf16[384,512]{1,0:T(8,128)(2,1)S(1)}, u32[]{:S(2)}, u32[]{:S(2)}) collective-permute-start(bf16[384,512]{1,0:T(8,128)(2,1)S(1)} %bitcast.7), channel_id=1, source_target_pairs={{0,1},{1,0},{2,3},{3,2},{4,5},{5,4},{6,7},{7,6},{8,9},{9,8},{10,11... | collective-permute-start | bytes 1179656 | tf_op jit(solution)/shard_map/ppermute | solution.py:335
  68.5 1.8 %final_ready.1 = (bf16[512,512]{1,0:T(8,128)(2,1)S(1)}, bf16[512,512]{1,0:T(8,128)(2,1)S(1)}, bf16[512,512]{1,0:T(8,128)(2,1)S(1)}, bf16[512,512]{1,0:T(8,128)(2...) custom-call(bf16[192,640]{1,0:T(8,128)(2,1)} %copy-done, ...), custom_call_target="tpu_custom_call" | custom-call | flops 1000000000 | bytes 1048576 | tf_op jit(solution)/shard_map/final_ready/pallas_call | solution.py:89
  70.2 9.6 %final.1 = (bf16[512,512]{1,0:T(8,128)(2,1)}, bf16[32,512]{1,0:T(8,128)(2,1)}, bf16[642,512]{1,0:T(8,128)(2,1)}) custom-call(bf16[384,512]{1,0:T(8,128)(2,1)S(1)} %bitcast.9, bf16[384,512]{1,0:T(8,128)(2,1)S(1)} %collective-permute-done.9.refs_1_, bf16[512,512]{1,0:T(8,128)(2,1)S(1)} %get-tuple-element.60.refs_2_, ...), custom_call_target="tpu_custom_call" | custom-call | bytes 1048576 | tf_op jit(solution)/shard_map/final/pallas_call | solution.py:89
  (13 shorter events, 0.1 us)
Async XLA Ops:
  1.9 6.9 %collective-permute-start = (bf16[32,512]{1,0:T(8,128)(2,1)S(1)}, bf16[32,512]{1,0:T(8,128)(2,1)S(1)}, u32[]{:S(2)}, u32[]{:S(2)}) collective-permute-start(bf16[32,512]{1,0:T(8,128)(2,1)S(1)} %get-tuple-element.38), channel_id=1, source_target_pairs={{0,1},{1,0},{2,3},{3,2},{4,5},{5,4},{6,7},{7,6},{8,9},{9,8},{10,11... | collective-permute-start | bytes 98312 | tf_op jit(solution)/shard_map/ppermute | solution.py:335
  5.3 5.2 %collective-permute-start.1 = (bf16[32,512]{1,0:T(8,128)(2,1)S(1)}, bf16[32,512]{1,0:T(8,128)(2,1)S(1)}, u32[]{:S(2)}, u32[]{:S(2)}) collective-permute-start(bf16[32,512]{1,0:T(8,128)(2,1)S(1)} %get-tuple-element.39), channel_id=1, source_target_pairs={{1,2},{3,4},{5,6},{7,8},{9,10},{11,12},{13,14},{15,16},{17,18},{19... | collective-permute-start | bytes 98312 | tf_op jit(solution)/shard_map/ppermute | solution.py:344
  11.1 1.3 %collective-permute-start.2 = (bf16[32,640]{1,0:T(8,128)(2,1)S(1)}, bf16[32,640]{1,0:T(8,128)(2,1)S(1)}, u32[]{:S(2)}, u32[]{:S(2)}) collective-permute-start(bf16[32,640]{1,0:T(8,128)(2,1)S(1)} %mid_update.1.refs_0_), channel_id=1, source_target_pairs={{0,1},{1,0},{2,3},{3,2},{4,5},{5,4},{6,7},{7,6},{8,9},{9,8},{10,11... | collective-permute-start | bytes 122888 | tf_op jit(solution)/shard_map/ppermute | solution.py:335
  13.6 16.5 %all-to-all-start = ((bf16[16,24,512]{2,1,0:T(8,128)(2,1)}), bf16[16,24,512]{2,1,0:T(8,128)(2,1)S(1)}, u32[]{:S(2)}, u32[]{:S(2)}) async-start(bf16[16,24,512]{2,1,0:T(8,128)(2,1)} %bitcast.2.refs_4_), calls=%async_computation | async-start | bytes 786432 | tf_op jit(solution)/shard_map/all_to_all | solution.py:433
  22.0 8.1 %collective-permute-start.3 = (bf16[192,640]{1,0:T(8,128)(2,1)S(1)}, bf16[192,640]{1,0:T(8,128)(2,1)S(1)}, u32[]{:S(2)}, u32[]{:S(2)}) collective-permute-start(bf16[192,640]{1,0:T(8,128)(2,1)S(1)} %get-tuple-element.50), channel_id=1, source_target_pairs={{1,2},{3,4},{5,6},{7,8},{9,10},{11,12},{13,14},{15,16},{17,18},{19... | collective-permute-start | bytes 737288 | tf_op jit(solution)/shard_map/ppermute | solution.py:344
  25.9 3.7 %collective-permute-start.4 = (bf16[128,640]{1,0:T(8,128)(2,1)S(1)}, bf16[128,640]{1,0:T(8,128)(2,1)S(1)}, u32[]{:S(2)}, u32[]{:S(2)}) collective-permute-start(bf16[128,640]{1,0:T(8,128)(2,1)S(1)} %get-tuple-element.48.refs_4_), channel_id=1, source_target_pairs={{0,1},{1,0},{2,3},{3,2},{4,5},{5,4},{6,7},{7,6},{8,9},{9,8},{10,11... | collective-permute-start | bytes 491528 | tf_op jit(solution)/shard_map/ppermute | solution.py:335
  29.6 18.0 %copy-start.1 = (bf16[128,640]{1,0:T(8,128)(2,1)}, bf16[128,640]{1,0:T(8,128)(2,1)S(1)}, u32[]{:S(2)}) copy-start(bf16[128,640]{1,0:T(8,128)(2,1)S(1)} %collective-permute-done.4.refs_3_.refs_4_) | copy-start | bytes 491524
  30.1 17.4 %copy-start = (bf16[192,640]{1,0:T(8,128)(2,1)}, bf16[192,640]{1,0:T(8,128)(2,1)S(1)}, u32[]{:S(2)}) copy-start(bf16[192,640]{1,0:T(8,128)(2,1)S(1)} %collective-permute-done.3.refs_2_.refs_3_.refs_0_) | copy-start | bytes 737284
  30.2 2.9 %collective-permute-start.5 = (bf16[24,512]{1,0:T(8,128)(2,1)S(1)}, bf16[24,512]{1,0:T(8,128)(2,1)S(1)}, u32[]{:S(2)}, u32[]{:S(2)}) collective-permute-start(bf16[24,512]{1,0:T(8,128)(2,1)S(1)} %plane_sum.1), channel_id=1, source_target_pairs={{0,32},{32,0},{64,96},{96,64},{128,160},{160,128},{192,224},{224,1... | collective-permute-start | bytes 73736 | tf_op jit(solution)/shard_map/ppermute | solution.py:339
  33.2 5.8 %collective-permute-start.6 = (bf16[24,512]{1,0:T(8,128)(2,1)S(1)}, bf16[24,512]{1,0:T(8,128)(2,1)S(1)}, u32[]{:S(2)}, u32[]{:S(2)}) collective-permute-start(bf16[24,512]{1,0:T(8,128)(2,1)S(1)} %add_convert_fusion.1), channel_id=1, source_target_pairs={{0,64},{32,96},{64,0},{96,32},{128,192},{160,224},{192,128},{224,1... | collective-permute-start | bytes 73736 | tf_op jit(solution)/shard_map/ppermute | solution.py:339
  36.3 11.3 %collective-permute-start.8 = (bf16[32,640]{1,0:T(8,128)(2,1)S(1)}, bf16[32,640]{1,0:T(8,128)(2,1)S(1)}, u32[]{:S(2)}, u32[]{:S(2)}) collective-permute-start(bf16[32,640]{1,0:T(8,128)(2,1)S(1)} %slice_select_fusion), channel_id=1, source_target_pairs={{0,1},{1,0},{2,3},{3,2},{4,5},{5,4},{6,7},{7,6},{8,9},{9,8},{10,11... | collective-permute-start | bytes 122888 | tf_op jit(solution)/shard_map/ppermute | solution.py:335
  39.0 8.6 %collective-permute-start.7 = (bf16[24,512]{1,0:T(8,128)(2,1)S(1)}, bf16[24,512]{1,0:T(8,128)(2,1)S(1)}, u32[]{:S(2)}, u32[]{:S(2)}) collective-permute-start(bf16[24,512]{1,0:T(8,128)(2,1)S(1)} %add_convert_fusion.refs_7_.refs_0_), channel_id=1, source_target_pairs={{0,128},{32,160},{64,192},{96,224},{128,0},{160,32},{192,64},{224,... | collective-permute-start | bytes 73736 | tf_op jit(solution)/shard_map/ppermute | solution.py:339
  47.6 19.4 %copy-start.2 = (bf16[32,640]{1,0:T(8,128)(2,1)}, bf16[32,640]{1,0:T(8,128)(2,1)S(1)}, u32[]{:S(2)}) copy-start(bf16[32,640]{1,0:T(8,128)(2,1)S(1)} %collective-permute-done.8.refs_6_.refs_2_) | copy-start | bytes 122884
  48.8 18.1 %all-to-all-start.1 = ((bf16[16,24,512]{2,1,0:T(8,128)(2,1)}), bf16[16,24,512]{2,1,0:T(8,128)(2,1)S(1)}, u32[]{:S(2)}, u32[]{:S(2)}) async-start(bf16[16,24,512]{2,1,0:T(8,128)(2,1)} %coarse_update.1.refs_8_), calls=%async_computation.1 | async-start | bytes 786432 | tf_op jit(solution)/shard_map/all_to_all | solution.py:483
  67.0 3.3 %collective-permute-start.9 = (bf16[384,512]{1,0:T(8,128)(2,1)S(1)}, bf16[384,512]{1,0:T(8,128)(2,1)S(1)}, u32[]{:S(2)}, u32[]{:S(2)}) collective-permute-start(bf16[384,512]{1,0:T(8,128)(2,1)S(1)} %bitcast.7), channel_id=1, source_target_pairs={{0,1},{1,0},{2,3},{3,2},{4,5},{5,4},{6,7},{7,6},{8,9},{9,8},{10,11... | collective-permute-start | bytes 1179656 | tf_op jit(solution)/shard_map/ppermute | solution.py:335

commit v6 on v5

--- a/solution.py
+++ b/solution.py
@@ -11,7 +11,7 @@
 BLOCK = 24
 LANES = 128
 CHUNK = 512
-PIECE = 1536
+PIECE = 1024
 PLANE = ("y", "x")
 TILE = ("y", "x", "c")
 F32, BF16, I32 = jnp.float32, jnp.bfloat16, jnp.int32
@@ -180,46 +180,53 @@
     ).astype(BF16)
 
 
-def boundary_body(parent, halo, fine, pair, swap, cross):
+def own_edges_body(
+    parent, halo, source, target, fine, w_src, w_dst, pair, sent_out, swap, cross, token, out
+):
+    token[...] = jnp.zeros_like(token)
     count, width = fine.shape
     two, blocks = pair.shape[0], count // LANES
     core = lax.axis_index("c")
     codes = [(spread(parent[r : r + 1, :]) + 1).astype(F32).astype(BF16) for r in range(blocks)]
     codes = jnp.concatenate(codes, axis=0)
     rows = halo[...]
-    for out, first, row in (
+    values = fine[...]
+    sent = product(values, w_src[...]).astype(BF16)
+    received = product(values, w_dst[...]).astype(BF16)
+    for k in range(out.shape[0] // CHUNK):
+        marks = range(k * CHUNK // LANES, (k + 1) * CHUNK // LANES)
+        picked = [jnp.concatenate(picks(spread(source[r : r + 1, :]), 0, blocks), axis=1) for r in marks]
+        total = product(jnp.concatenate(picked, axis=0), sent)
+        picked = [jnp.concatenate(picks(spread(target[r : r + 1, :]), 0, blocks), axis=1) for r in marks]
+        total += product(jnp.concatenate(picked, axis=0), received)
+        out[k * CHUNK : (k + 1) * CHUNK, :] = total.astype(BF16)
+        if (k + 1) * CHUNK % PIECE == 0:
+            sent_out.start(k * CHUNK // PIECE)
+    for place, first, row in (
         (swap, 0, jnp.where(core == 0, rows[1:2], rows[:1])),
         (cross, two, jnp.where(core == 0, rows[:1], rows[1:2])),
     ):
         picked = jnp.concatenate(picks(spread(row), 0, blocks), axis=1)
-        out[first : first + LANES, :width] = product(picked, fine[...]).astype(BF16)
-        out[first : first + LANES, width:] = product(picked, codes).astype(BF16)
+        place[first : first + LANES, :width] = product(picked, values).astype(BF16)
+        place[first : first + LANES, width:] = product(picked, codes).astype(BF16)
     cross[:two] = pair[...]
 
 
-def tables_body(fine, w_src, w_dst, w_node, sender, receiver, node, token):
-    token[...] = jnp.zeros_like(token)
-    values = fine[...]
-    sender[...] = product(values, w_src[...]).astype(BF16)
-    receiver[...] = product(values, w_dst[...]).astype(BF16)
-    node[...] = product(values, w_node[...])
-
-
 def gather_body(parts, out):
-    out[...] = jnp.sum(parts[...].astype(F32), axis=0).astype(BF16)
-
-
-def coarse_body(mine, theirs, own_latent, own_hidden, both, third, out):
-    total = (mine[...].astype(F32) + theirs[...].astype(F32)).astype(BF16)
+    total = jnp.sum(parts[...].astype(F32), axis=0).astype(BF16)
+    for i in range(out.shape[0]):
+        out[i] = total
+
+
+def coarse_body(parts, own_latent, own_hidden, both, third, out):
+    total = jnp.sum(parts[...].astype(F32), axis=0).astype(BF16)
     hidden = silu(own_hidden[...] + product(total, both[...]))
     result = updated(own_latent[...], hidden, third[...])
     for i in range(out.shape[0]):
         out[i] = result
 
 
-def coarse_ready_body(
-    coarse, coarse_w1, w_coarse, coarse_w2, edge_w2, node_w2, third, both, last, own_latent, own_hidden
-):
+def coarse_rows_body(coarse, coarse_w1, own_latent, own_hidden):
     rows, total = own_latent.shape[0], coarse.shape[0]
     chips = lax.axis_size("y") * lax.axis_size("x")
     chip = lax.axis_index("y") * lax.axis_size("x") + lax.axis_index("x")
@@ -229,6 +236,11 @@
     latent = product(picked, coarse[...]).astype(BF16)
     own_latent[...] = latent
     own_hidden[...] = product(latent, coarse_w1[...])
+
+
+def weights_body(w_coarse, coarse_w2, edge_w2, node_w2, third, rows, hidden, both, last, own_latent, own_hidden):
+    own_latent[...] = rows[...]
+    own_hidden[...] = hidden[...]
     both[...] = product(w_coarse[...], coarse_w2[...]).astype(BF16)
     last[...] = product(edge_w2[...], node_w2[...]).astype(BF16)
 
@@ -240,16 +252,15 @@
     return jnp.where(codes > 0, (tile + away) * count + (parent & (count - 1)), -1)
 
 
-def edges_body(
-    mid_count, parent, source, target, cross, swap, w_src, sender, receiver, sent_out, sent_select, own_pick, token,
-    out, select, table, where
+def rest_edges_body(
+    mid_count, parent, source, target, cross, swap, w_src, pair, mid_swap, first, w_descend, w_fine,
+    sent_out, sent_select, own_pick, middle, picked, out, select, table, where, window
 ):
-    token[...] = jnp.zeros_like(token)
     core = lax.axis_index("c")
     count = own_pick.shape[0]
     width = out.shape[1]
     blocks = count // LANES
-    two = cross.shape[0] - LANES
+    two = pair.shape[0]
     for r in range(blocks):
         place = slots(spread(parent[r : r + 1, :]) + 1, 2, mid_count)
         rows = slice(r * LANES, (r + 1) * LANES)
@@ -260,42 +271,36 @@
         there = slice(count + 2 * LANES + r * LANES, count + 2 * LANES + (r + 1) * LANES)
         where[there, :] = jnp.concatenate(picks(far, 0, 2), axis=1)
     for values, late in ((cross[two:], core), (swap[...], 1 - core)):
-        rows = pl.ds(pl.multiple_of(count + late * LANES, LANES), LANES)
+        rows = pl.ds(pl.multiple_of(late * LANES, LANES), LANES)
         table[rows, :] = product(values[:, :width], w_src[...]).astype(BF16)
         place = slots(values[:, width:].astype(F32).astype(I32), 1 + 2 * late, mid_count)
+        rows = pl.ds(pl.multiple_of(count + late * LANES, LANES), LANES)
         where[rows, :] = jnp.concatenate(picks(place, 0, 2), axis=1)
-    table[:count] = sender[...]
-    table[count + 2 * LANES :] = receiver[...]
+    window[pl.ds(pl.multiple_of((1 - core) * 4 * mid_count, mid_count), mid_count), :] = mid_swap[...]
+    window[pl.ds(pl.multiple_of(core * 3 * mid_count, mid_count), two), :] = cross[:two]
+    window[pl.ds(pl.multiple_of((2 - core) * mid_count, mid_count), two), :] = pair[...]
+    near = window[...]
+    middle[...] = near[:, :width]
+    picked[...] = hot(row_ids(near, width) == lax.broadcasted_iota(I32, picked.shape, 1))
     for k in range(out.shape[0] // CHUNK):
         rows = []
         for r in range(k * CHUNK // LANES, (k + 1) * CHUNK // LANES):
             row = picks(spread(source[r : r + 1, :]), 0, blocks + 2)
             row += picks(spread(target[r : r + 1, :]), 0, blocks)
             rows.append(jnp.concatenate(row, axis=1))
-        picked = jnp.concatenate(rows, axis=0)
+        marks = jnp.concatenate(rows, axis=0)
         here = slice(k * CHUNK, (k + 1) * CHUNK)
-        select[here, :] = product(picked, where[...]).astype(BF16)
-        out[here, :] = product(picked, table[...]).astype(BF16)
+        select[here, :] = product(marks, where[...]).astype(BF16)
+        rest = product(marks[:, count : count + 2 * LANES], table[...])
+        out[here, :] = (first.get(k * CHUNK // PIECE)[here, :].astype(F32) + rest).astype(BF16)
         if (k + 1) * CHUNK % PIECE == 0:
             sent_out.start(k * CHUNK // PIECE)
             sent_select.start(k * CHUNK // PIECE)
 
 
-def ready_body(rows, cross, pair, swap, w_descend, w_fine, w_src, w_dst, middle, picked, window):
-    core = lax.axis_index("c")
-    two = pair.shape[0]
-    count, width = two // 2, middle.shape[1]
-    window[pl.ds(pl.multiple_of((1 - core) * 4 * count, count), count), :] = swap[...]
-    window[pl.ds(pl.multiple_of(core * 3 * count, count), two), :] = cross[:two]
-    window[pl.ds(pl.multiple_of((2 - core) * count, count), two), :] = pair[...]
-    near = window[...]
-    middle[...] = near[:, :width]
-    picked[...] = hot(row_ids(near, width) == lax.broadcasted_iota(I32, (5 * count, rows), 1))
-
-
 def final_body(
-    mine, theirs, w_descend, w_fine, w_src, w_dst, near, picked, target, select, edges, own_pick, fine,
-    w_node, last, node, node_w3, fine_out, mid_out, coarse_out, coarse, table, sums,
+    mine, theirs, w_descend, w_fine, near, picked, w_src, w_dst, target, select, edges, own_pick, fine,
+    w_node, last, node_w3, fine_out, mid_out, coarse_out, coarse, table, sums,
 ):
     core = lax.axis_index("c")
     half, width = mine.shape
@@ -326,17 +331,12 @@
     coarse_out[...] = coarse[: coarse_out.shape[0], :]
     reach = fine_down[count : 5 * count]
     lifted = (fine[...].astype(F32) + product(own_pick[...], reach)).astype(BF16)
-    near_node = product(reach, w_node[...]).astype(BF16)
-    hidden = silu(node[...] + product(own_pick[...], near_node) + product(sums[...].astype(BF16), last[...]))
+    hidden = silu(product(lifted, w_node[...]) + product(sums[...].astype(BF16), last[...]))
     fine_out[...] = updated(lifted, hidden, node_w3[...])
 
 
 def swapped(values):
     return lax.ppermute(values, "c", [(0, 1), (1, 0)])
-
-
-def paired(values, step):
-    return lax.ppermute(values, "z", [(i, i ^ step) for i in range(lax.axis_size("z"))])
 
 
 def crossed(values, tiles):
@@ -431,88 +431,82 @@
 
     blocks = blocks.reshape(chips, BLOCK, width)
     parts = lax.all_to_all(blocks, PLANE, 0, 0)
-    halo_swap, cross = kernel_call(
-        boundary_body,
-        [free(LANES, wide), free(2 * mids + LANES, wide)],
+    own_edges, halo_swap, cross, token = kernel_call(
+        own_edges_body,
+        [far(edge_count, width), far(LANES, wide), far(2 * mids + LANES, wide), free(8, LANES)],
         [],
-        stored=[parent, halo, fine_latent, pair],
+        stored=[parent, halo, source, target, fine_latent, edge_w_src, edge_w_dst, pair],
+        streams=[0],
         after=[blocks],
-        flops=500_000_000,
-        name="boundary",
-    )
+        limit=24,
+        flops=4_000_000_000,
+        name="own_edges",
+    )
+
+    (own_parts,) = kernel_call(
+        gather_body, [near(planes, BLOCK, width)], [parts], after=[token], name="plane_sum"
+    )
+    in_planes = lax.all_to_all(own_parts, "z", 0, 0)
+    rows, hidden = kernel_call(
+        coarse_rows_body,
+        [far(BLOCK, width), far(BLOCK, width, dtype=F32)],
+        [],
+        stored=[coarse_latent, coarse_w1],
+        after=[own_parts],
+
+        name="coarse_rows",
+    )
+    halo_swap, cross, rows = lax.optimization_barrier((halo_swap, cross, rows))
     cross_in = crossed(cross, tiles)
     halo_in = swapped(halo_swap)
-    sender, receiver, node, token = kernel_call(
-        tables_body,
-        [far(count, width), far(count, width), far(count, width, dtype=F32), free(8, LANES)],
-        [],
-        stored=[fine_latent, edge_w_src, edge_w_dst, node_w1],
-        after=[halo_swap],
-        limit=12,
-        flops=2_000_000_000,
-        name="tables",
-    )
-
-    (total,) = kernel_call(
-        gather_body, [free(BLOCK, width)], [parts], after=[token, cross_in, halo_in], name="plane_sum"
-    )
-    mid_in = swapped(jnp.where(lax.axis_index("c") == 0, cross_in[mids : 2 * mids], cross_in[:mids]))
-    step = 1
-    while 2 * step < planes:
-        total = (total.astype(F32) + paired(total, step).astype(F32)).astype(BF16)
-        step *= 2
-    other = paired(total, step)
     coarse_w3, both, last, own_latent, own_hidden = kernel_call(
-        coarse_ready_body,
+        weights_body,
         [square, square, far(width, width), near(BLOCK, width), near(BLOCK, width, dtype=F32)],
         [],
-        stored=[coarse_latent, coarse_w1, w_coarse, coarse_w2, edge_w2, node_w2, coarse_w3],
-        keep=[(6, 0)],
-        after=[total],
-        flops=1_500_000_000,
-        name="coarse_ready",
-    )
+        stored=[w_coarse, coarse_w2, edge_w2, node_w2, coarse_w3, rows, hidden],
+        keep=[(4, 0)],
+        flops=3_000_000_000,
+        name="weights",
+    )
+    nearest, own_latent = lax.optimization_barrier((cross_in, own_latent))
+    mid_in = swapped(jnp.where(lax.axis_index("c") == 0, nearest[mids : 2 * mids], nearest[:mids]))
 
     (results,) = kernel_call(
         coarse_body,
         [near(chips, BLOCK, width)],
-        [total, other] + [here(a) for a in (own_latent, own_hidden, both, coarse_w3)],
-        after=[mid_in],
+        [in_planes] + [here(a) for a in (own_latent, own_hidden, both, coarse_w3)],
+        after=[cross_in, halo_in],
         name="coarse_update",
     )
     mine = lax.all_to_all(results, PLANE, 0, 0).reshape(half, width)
-    edges, select, own_pick, token = kernel_call(
-        functools.partial(edges_body, mids),
-        [far(edge_count, width), far(edge_count, 2 * LANES), far(count, LANES), free(8, LANES)],
+    w_descend, w_fine, edges, select, own_pick, middle, picked = kernel_call(
+        functools.partial(rest_edges_body, mids),
+        [square, square, far(edge_count, width), far(edge_count, 2 * LANES), far(count, LANES)]
+        + [near(5 * mids, width), near(5 * mids, 2 * half)],
         [],
-        stored=[parent, source, target, cross_in, halo_in, edge_w_src, sender, receiver],
-        streams=[0, 1],
+        stored=[parent, source, target, cross_in, halo_in, edge_w_src, pair, mid_in, own_edges, w_descend, w_fine],
+        keep=[(9, 0), (10, 1)],
+        pieces=[8],
+        streams=[2, 3],
         after=[results],
-        scratch=[pltpu.VMEM((2 * count + 2 * LANES, width), BF16), pltpu.VMEM((2 * count + 2 * LANES, 2 * LANES), BF16)],
+        scratch=[
+            pltpu.VMEM((2 * LANES, width), BF16),
+            pltpu.VMEM((2 * count + 2 * LANES, 2 * LANES), BF16),
+            pltpu.VMEM((5 * mids, wide), BF16),
+        ],
         limit=24,
-        flops=6_500_000_000,
-        name="edges",
+        flops=4_000_000_000,
+        name="rest_edges",
     )
     mine, own_pick = lax.optimization_barrier((mine, own_pick))
     theirs = swapped(mine)
-    w_descend, w_fine, w_src, w_dst, middle, picked = kernel_call(
-        functools.partial(ready_body, 2 * half),
-        [square] * 4 + [near(5 * mids, width), near(5 * mids, 2 * half)],
-        [],
-        stored=[cross_in, pair, mid_in, w_descend, w_fine, edge_w_src, edge_w_dst],
-        keep=[(3, 0), (4, 1), (5, 2), (6, 3)],
-        after=[mine, token],
-        scratch=[pltpu.VMEM((5 * mids, wide), BF16)],
-        flops=1_000_000_000,
-        name="final_ready",
-    )
 
     fine_out, mid_out, coarse_out = kernel_call(
         final_body,
         [free(count, width), free(mids, width), free(coarse_count, width)],
-        [mine, theirs] + [here(a) for a in (w_descend, w_fine, w_src, w_dst, middle, picked)],
-        stored=[target, select, edges, own_pick, fine_latent, node_w1, last, node, node_w3],
-        pieces=[1, 2],
+        [mine, theirs] + [here(a) for a in (w_descend, w_fine, middle, picked)],
+        stored=[edge_w_src, edge_w_dst, target, select, edges, own_pick, fine_latent, node_w1, last, node_w3],
+        pieces=[3, 4],
         scratch=[
             pltpu.VMEM((2 * half, width), BF16),
             pltpu.VMEM((8 * mids, width), BF16),

time: 80.4 us -> 79.3 us (0.986)
  starting transfers between devices: 38 us -> 32.2 us
  waiting for transfers between devices: 4.71 us -> 7.04 us
  Pallas kernels: 36.2 us -> 37.9 us
    ppermute x3 -> x0, starting transfers between devices: 10 us -> none  [paired(): lax.ppermute(values, 'z', [(i, i ^ step) for i in range(lax.axis_size('z'...]
    all_to_all x0 -> x1, starting transfers between devices: none -> 8.19 us  [on_device(): in_planes = lax.all_to_all(own_parts, 'z', 0, 0)]
    ppermute x5, starting transfers between devices: 7.75 us -> 5.24 us  [swapped(): return lax.ppermute(values, 'c', [(0, 1), (1, 0)])]
    all_to_all x1, waiting for transfers between devices: 0.01 us -> 1.83 us  [on_device(): parts = lax.all_to_all(blocks, PLANE, 0, 0)]
    pallas_call x12 -> x11, Pallas kernels: 36.2 us -> 37.9 us  [kernel_call(): pl.pallas_call(kernel, out_shape=outs, in_specs=[VMEM] * count + [STORED]...]
    all_to_all x1, starting transfers between devices: 7.65 us -> 6.07 us  [on_device(): mine = lax.all_to_all(results, PLANE, 0, 0).reshape(half, width)]
    ppermute x5, waiting for transfers between devices: 1.22 us -> 2.56 us  [swapped(): return lax.ppermute(values, 'c', [(0, 1), (1, 0)])]
    ppermute x3 -> x0, waiting for transfers between devices: 1.22 us -> none  [paired(): lax.ppermute(values, 'z', [(i, i ^ step) for i in range(lax.axis_size('z'...]
  transfers between devices with their start and end apart: 12 -> 10, of which waited for: 4 -> 6; matrix products, arithmetic and copies ran while one was open for 0% -> 0% of each run, Pallas kernels for 28% -> 31%
where the time goes in v6:
time: 79.3 us; the launch traced here: 78.8 us
  Pallas kernels  37.9 us (48%)
  starting transfers between devices  32.2 us (41%)
  waiting for transfers between devices  7.04 us (9%)
  between operations  0.98 us (1%)
    pallas_call x11, Pallas kernels, kernel_call(): pl.pallas_call(kernel, out_shape=outs, in_specs=[VMEM] * count + [STORED]...  37.9 us
    all_to_all x1, starting transfers between devices, on_device(): in_planes = lax.all_to_all(own_parts, 'z', 0, 0)  8.19 us
    all_to_all x1, starting transfers between devices, on_device(): parts = lax.all_to_all(blocks, PLANE, 0, 0)  6.86 us
    all_to_all x1, starting transfers between devices, on_device(): mine = lax.all_to_all(results, PLANE, 0, 0).reshape(half, width)  6.07 us
    ppermute x2, starting transfers between devices, crossed(): return lax.ppermute(values, TILE, pairs + [(b, a) for a, b in pairs])  5.84 us
    ppermute x5, starting transfers between devices, swapped(): return lax.ppermute(values, 'c', [(0, 1), (1, 0)])  5.24 us
    ppermute x5, waiting for transfers between devices, swapped(): return lax.ppermute(values, 'c', [(0, 1), (1, 0)])  2.56 us
    ppermute x2, waiting for transfers between devices, crossed(): return lax.ppermute(values, TILE, pairs + [(b, a) for a, b in pairs])  2.47 us
  transfers between devices with their start and end apart: 10, of which 6 were waited for; matrix products, arithmetic and copies ran while one was open for 0% of the time, Pallas kernels for 31%

profile of v6, /device:TPU:1, one launch (start us, length us, event | category | flops | bytes accessed | tf_op | source)
XLA Modules:
  0.0 78.8 jit_solution(10372572999340859578)
XLA Ops:
  0.6 1.3 %child_sums.1 = (f32[32,512]{1,0:T(8,128)S(1)}, bf16[32,512]{1,0:T(8,128)(2,1)S(1)}, bf16[32,512]{1,0:T(8,128)(2,1)S(1)}) custom-call(s32[4,128]{1,0:T(4,128)} %bitcast.12, bf16[512,512]{1,0:T(8,128)(2,1)} %refs_12_.1), custom_call_target="tpu_custom_call" | custom-call | bytes 1048576 | tf_op jit(solution)/shard_map/child_sums/pallas_call | solution.py:89
  1.9 3.3 %collective-permute-start = (bf16[32,512]{1,0:T(8,128)(2,1)S(1)}, bf16[32,512]{1,0:T(8,128)(2,1)S(1)}, u32[]{:S(2)}, u32[]{:S(2)}) collective-permute-start(bf16[32,512]{1,0:T(8,128)(2,1)S(1)} %get-tuple-element.40), channel_id=1, source_target_pairs={{0,1},{1,0},{2,3},{3,2},{4,5},{5,4},{6,7},{7,6},{8,9},{9,8},{10,11... | collective-permute-start | bytes 98312 | tf_op jit(solution)/shard_map/ppermute | solution.py:339
  5.3 1.9 %collective-permute-start.1 = (bf16[32,512]{1,0:T(8,128)(2,1)S(1)}, bf16[32,512]{1,0:T(8,128)(2,1)S(1)}, u32[]{:S(2)}, u32[]{:S(2)}) collective-permute-start(bf16[32,512]{1,0:T(8,128)(2,1)S(1)} %get-tuple-element.41), channel_id=1, source_target_pairs={{1,2},{3,4},{5,6},{7,8},{9,10},{11,12},{13,14},{15,16},{17,18},{19... | collective-permute-start | bytes 98312 | tf_op jit(solution)/shard_map/ppermute | solution.py:344
  7.2 1.6 %mid_ready.1 = (bf16[512,512]{1,0:T(8,128)(2,1)S(1)}, bf16[512,512]{1,0:T(8,128)(2,1)S(1)}, bf16[512,512]{1,0:T(8,128)(2,1)S(1)}, bf16[32,512]{1,0:T(8,128)(2,1)...) custom-call(bf16[32,512]{1,0:T(8,128)(2,1)} %refs_0_.3, s32[1,32]{1,0:T(1,128)} %bitcast.18, ...), custom_call_target="tpu_custom_call" | custom-call | flops 1000000000 | bytes 1048576 | tf_op jit(solution)/shard_map/mid_ready/pallas_call | solution.py:89
  8.8 0.0 collective-permute-done.refs_1_
  8.8 1.7 %collective-permute-done.1.refs_2_ = bf16[32,512]{1,0:T(8,128)(2,1)S(1)} collective-permute-done((bf16[32,512]{1,0:T(8,128)(2,1)S(1)}, bf16[32,512]{1,0:T(8,128)(2,1)S(1)}, u32[]{:S(2)}, u32[]{:S(2)}) %collective-permute-start.1) | collective-permute-done | bytes 32800 | tf_op jit(solution)/shard_map/ppermute | solution.py:344
  10.5 0.6 mid_update.1.refs_0_
  11.1 0.1 collective-permute-start.2
  11.2 1.2 %collective-permute-done.2.refs_1_ = bf16[32,640]{1,0:T(8,128)(2,1)S(1)} collective-permute-done((bf16[32,640]{1,0:T(8,128)(2,1)S(1)}, bf16[32,640]{1,0:T(8,128)(2,1)S(1)}, u32[]{:S(2)}, u32[]{:S(2)}) %collective-permute-start.2) | collective-permute-done | bytes 40992 | tf_op jit(solution)/shard_map/ppermute | solution.py:339
  12.4 1.2 %coarse_blocks.1 = (bf16[64,640]{1,0:T(8,128)(2,1)}, bf16[384,512]{1,0:T(8,128)(2,1)}) custom-call(bf16[32,640]{1,0:T(8,128)(2,1)S(1)} %mid_update.1.refs_0_, bf16[32,640]{1,0:T(8,128)(2,1)S(1)} %collective-permute-done.2.refs_1_), custom_call_target="tpu_custom_call" | custom-call | bytes 1048576 | tf_op jit(solution)/shard_map/coarse_blocks/pallas_call | solution.py:89
  13.6 6.9 %all-to-all-start = ((bf16[16,24,512]{2,1,0:T(8,128)(2,1)}), bf16[16,24,512]{2,1,0:T(8,128)(2,1)S(1)}, u32[]{:S(2)}, u32[]{:S(2)}) async-start(bf16[16,24,512]{2,1,0:T(8,128)(2,1)} %bitcast.2.refs_8_), calls=%async_computation | async-start | bytes 786432 | tf_op jit(solution)/shard_map/all_to_all | solution.py:433
  20.5 7.6 %own_edges.1 = (bf16[3072,512]{1,0:T(8,128)(2,1)}, bf16[128,640]{1,0:T(8,128)(2,1)}, bf16[192,640]{1,0:T(8,128)(2,1)}, bf16[8,128]{1,0:T(8,128)(2,1)S(1)}) custom-call(s32[4,128]{1,0:T(4,128)} %bitcast.13, s32[2,128]{1,0:T(2,128)} %bitcast.17, s32[24,128]{1,0:T(8,128)} %bitcast.15, s32[24,128]{1,0:T(8,128)} %bitcast.9, bf16[512,512]{1,0:T(8,128)(2,1)} %refs_12_.1, ...), custom_call_target="tpu_custom_call" | custom-call | flops 4000000000 | bytes 1048576 | tf_op jit(solution)/shard_map/own_edges/pallas_call | solution.py:89
  28.1 1.8 %all-to-all-done.refs_0_ = bf16[16,24,512]{2,1,0:T(8,128)(2,1)S(1)} async-done(((bf16[16,24,512]{2,1,0:T(8,128)(2,1)}), bf16[16,24,512]{2,1,0:T(8,128)(2,1)S(1)}, u32[]{:S(2)}, u32[]{:S(2)}) %all-to-all-start) | async-done | bytes 393248 | tf_op jit(solution)/shard_map/all_to_all | solution.py:433
  29.9 0.7 plane_sum.1.refs_2_
  30.7 8.2 %all-to-all-start.1 = ((bf16[8,24,512]{2,1,0:T(8,128)(2,1)}), bf16[8,24,512]{2,1,0:T(8,128)(2,1)S(1)}, u32[]{:S(2)}, u32[]{:S(2)}) async-start(bf16[8,24,512]{2,1,0:T(8,128)(2,1)} %plane_sum.1.refs_2_), calls=%async_computation.1 | async-start | bytes 393216 | tf_op jit(solution)/shard_map/all_to_all | solution.py:449
  38.9 2.2 %coarse_rows.1 = (bf16[24,512]{1,0:T(8,128)(2,1)}, f32[24,512]{1,0:T(8,128)}) custom-call(bf16[642,512]{1,0:T(8,128)(2,1)} %refs_0_.4, bf16[512,512]{1,0:T(8,128)(2,1)} %refs_1_.4, bf16[8,24,512]{2,1,0:T(8,128)(2,1)} %plane_sum.1.refs_2_), custom_call_target="tpu_custom_call" | custom-call | bytes 1048576 | tf_op jit(solution)/shard_map/coarse_rows/pallas_call | solution.py:89
  41.0 3.9 %collective-permute-start.3 = (bf16[192,640]{1,0:T(8,128)(2,1)}, bf16[192,640]{1,0:T(8,128)(2,1)S(1)}, u32[]{:S(2)}, u32[]{:S(2)}) collective-permute-start(bf16[192,640]{1,0:T(8,128)(2,1)} %get-tuple-element.54), channel_id=1, source_target_pairs={{1,2},{3,4},{5,6},{7,8},{9,10},{11,12},{13,14},{15,16},{17,18},{19... | collective-permute-start | bytes 737288 | tf_op jit(solution)/shard_map/ppermute | solution.py:344
  45.0 0.1 collective-permute-start.4
  45.1 3.5 %weights.1 = (bf16[512,512]{1,0:T(8,128)(2,1)S(1)}, bf16[512,512]{1,0:T(8,128)(2,1)S(1)}, bf16[512,512]{1,0:T(8,128)(2,1)}, bf16[24,512]{1,0:T(8,128)(2,1)S(1)}, f32[24,512]{1,0:T(8,128)S(1)}) custom-call(bf16[512,512]{1,0:T(8,128)(2,1)} %refs_0_.5, bf16[512,512]{1,0:T(8,128)(2,1)} %refs_1_.5, bf16[512,512]{1,0:T(8,128)(2,1)} %refs_2_.3, ...), custom_call_target="tpu_custom_call" | custom-call | flops 3000000000 | bytes 1048576 | tf_op jit(solution)/shard_map/weights/pallas_call | solution.py:89
  48.6 0.8 %collective-permute-done.3.refs_5_.refs_3_ = bf16[192,640]{1,0:T(8,128)(2,1)S(1)} collective-permute-done((bf16[192,640]{1,0:T(8,128)(2,1)}, bf16[192,640]{1,0:T(8,128)(2,1)S(1)}, u32[]{:S(2)}, u32[]{:S(2)}) %collective-permute-start.3) | collective-permute-done | bytes 245792 | tf_op jit(solution)/shard_map/ppermute | solution.py:344
  49.4 0.1 collective-permute-start.5
  49.5 0.0 collective-permute-done.4.refs_6_.refs_4_
  49.5 0.0 all-to-all-done.1.refs_0_
  49.5 1.2 %coarse_update.1.refs_11_ = bf16[16,24,512]{2,1,0:T(8,128)(2,1)} custom-call(bf16[8,24,512]{2,1,0:T(8,128)(2,1)S(1)} %all-to-all-done.1.refs_0_, bf16[24,512]{1,0:T(8,128)(2,1)S(1)} %get-tuple-element.58.refs_1_, f32[24,512]{1,0:T(8,128)S(1)} %get-tuple-element.59.refs_2_, bf16[512,512]{1,0:T(8,128)(2,1)S(1)} %get-tuple-element.60.refs_3_, ...), custom_call_target="tpu_custom_call" | custom-call | bytes 1048576 | tf_op jit(solution)/shard_map/coarse_update/pallas_call | solution.py:89
  50.7 6.1 %all-to-all-start.2 = ((bf16[16,24,512]{2,1,0:T(8,128)(2,1)}), bf16[16,24,512]{2,1,0:T(8,128)(2,1)S(1)}, u32[]{:S(2)}, u32[]{:S(2)}) async-start(bf16[16,24,512]{2,1,0:T(8,128)(2,1)} %coarse_update.1.refs_11_), calls=%async_computation.2 | async-start | bytes 786432 | tf_op jit(solution)/shard_map/all_to_all | solution.py:481
  56.8 0.0 collective-permute-done.5.refs_7_
  56.8 0.6 copy-done.2
  57.4 8.6 %rest_edges.1 = (bf16[512,512]{1,0:T(8,128)(2,1)S(1)}, bf16[512,512]{1,0:T(8,128)(2,1)S(1)}, bf16[3072,512]{1,0:T(8,128)(2,1)}, bf16[3072,256]{1,0:T(8,128)(2,1)...) custom-call(s32[4,128]{1,0:T(4,128)} %bitcast.14, s32[24,128]{1,0:T(8,128)} %bitcast.16, ...), custom_call_target="tpu_custom_call" | custom-call | flops 4000000000 | bytes 1048576 | tf_op jit(solution)/shard_map/rest_edges/pallas_call | solution.py:89
  66.0 0.2 all-to-all-done.2
  66.2 1.6 %collective-permute-start.6 = (bf16[384,512]{1,0:T(8,128)(2,1)S(1)}, bf16[384,512]{1,0:T(8,128)(2,1)S(1)}, u32[]{:S(2)}, u32[]{:S(2)}) collective-permute-start(bf16[384,512]{1,0:T(8,128)(2,1)S(1)} %bitcast.7), channel_id=1, source_target_pairs={{0,1},{1,0},{2,3},{3,2},{4,5},{5,4},{6,7},{7,6},{8,9},{9,8},{10,11... | collective-permute-start | bytes 1179656 | tf_op jit(solution)/shard_map/ppermute | solution.py:339
  67.8 1.3 %collective-permute-done.6.refs_1_ = bf16[384,512]{1,0:T(8,128)(2,1)S(1)} collective-permute-done((bf16[384,512]{1,0:T(8,128)(2,1)S(1)}, bf16[384,512]{1,0:T(8,128)(2,1)S(1)}, u32[]{:S(2)}, u32[]{:S(2)}) %collective-permute-start.6) | collective-permute-done | bytes 393248 | tf_op jit(solution)/shard_map/ppermute | solution.py:339
  69.2 9.4 %final.1 = (bf16[512,512]{1,0:T(8,128)(2,1)}, bf16[32,512]{1,0:T(8,128)(2,1)}, bf16[642,512]{1,0:T(8,128)(2,1)}) custom-call(bf16[384,512]{1,0:T(8,128)(2,1)S(1)} %bitcast.8, bf16[384,512]{1,0:T(8,128)(2,1)S(1)} %collective-permute-done.6.refs_1_, bf16[512,512]{1,0:T(8,128)(2,1)S(1)} %get-tuple-element.67.refs_2_, ...), custom_call_target="tpu_custom_call" | custom-call | bytes 1048576 | tf_op jit(solution)/shard_map/final/pallas_call | solution.py:89
  (6 shorter events, 0.0 us)
Async XLA Ops:
  1.9 6.9 %collective-permute-start = (bf16[32,512]{1,0:T(8,128)(2,1)S(1)}, bf16[32,512]{1,0:T(8,128)(2,1)S(1)}, u32[]{:S(2)}, u32[]{:S(2)}) collective-permute-start(bf16[32,512]{1,0:T(8,128)(2,1)S(1)} %get-tuple-element.40), channel_id=1, source_target_pairs={{0,1},{1,0},{2,3},{3,2},{4,5},{5,4},{6,7},{7,6},{8,9},{9,8},{10,11... | collective-permute-start | bytes 98312 | tf_op jit(solution)/shard_map/ppermute | solution.py:339
  5.3 5.2 %collective-permute-start.1 = (bf16[32,512]{1,0:T(8,128)(2,1)S(1)}, bf16[32,512]{1,0:T(8,128)(2,1)S(1)}, u32[]{:S(2)}, u32[]{:S(2)}) collective-permute-start(bf16[32,512]{1,0:T(8,128)(2,1)S(1)} %get-tuple-element.41), channel_id=1, source_target_pairs={{1,2},{3,4},{5,6},{7,8},{9,10},{11,12},{13,14},{15,16},{17,18},{19... | collective-permute-start | bytes 98312 | tf_op jit(solution)/shard_map/ppermute | solution.py:344
  11.1 1.3 %collective-permute-start.2 = (bf16[32,640]{1,0:T(8,128)(2,1)S(1)}, bf16[32,640]{1,0:T(8,128)(2,1)S(1)}, u32[]{:S(2)}, u32[]{:S(2)}) collective-permute-start(bf16[32,640]{1,0:T(8,128)(2,1)S(1)} %mid_update.1.refs_0_), channel_id=1, source_target_pairs={{0,1},{1,0},{2,3},{3,2},{4,5},{5,4},{6,7},{7,6},{8,9},{9,8},{10,11... | collective-permute-start | bytes 122888 | tf_op jit(solution)/shard_map/ppermute | solution.py:339
  13.6 16.3 %all-to-all-start = ((bf16[16,24,512]{2,1,0:T(8,128)(2,1)}), bf16[16,24,512]{2,1,0:T(8,128)(2,1)S(1)}, u32[]{:S(2)}, u32[]{:S(2)}) async-start(bf16[16,24,512]{2,1,0:T(8,128)(2,1)} %bitcast.2.refs_8_), calls=%async_computation | async-start | bytes 786432 | tf_op jit(solution)/shard_map/all_to_all | solution.py:433
  30.7 18.8 %all-to-all-start.1 = ((bf16[8,24,512]{2,1,0:T(8,128)(2,1)}), bf16[8,24,512]{2,1,0:T(8,128)(2,1)S(1)}, u32[]{:S(2)}, u32[]{:S(2)}) async-start(bf16[8,24,512]{2,1,0:T(8,128)(2,1)} %plane_sum.1.refs_2_), calls=%async_computation.1 | async-start | bytes 393216 | tf_op jit(solution)/shard_map/all_to_all | solution.py:449
  41.0 8.3 %collective-permute-start.3 = (bf16[192,640]{1,0:T(8,128)(2,1)}, bf16[192,640]{1,0:T(8,128)(2,1)S(1)}, u32[]{:S(2)}, u32[]{:S(2)}) collective-permute-start(bf16[192,640]{1,0:T(8,128)(2,1)} %get-tuple-element.54), channel_id=1, source_target_pairs={{1,2},{3,4},{5,6},{7,8},{9,10},{11,12},{13,14},{15,16},{17,18},{19... | collective-permute-start | bytes 737288 | tf_op jit(solution)/shard_map/ppermute | solution.py:344
  45.0 4.5 %collective-permute-start.4 = (bf16[128,640]{1,0:T(8,128)(2,1)}, bf16[128,640]{1,0:T(8,128)(2,1)S(1)}, u32[]{:S(2)}, u32[]{:S(2)}) collective-permute-start(bf16[128,640]{1,0:T(8,128)(2,1)} %get-tuple-element.62), channel_id=1, source_target_pairs={{0,1},{1,0},{2,3},{3,2},{4,5},{5,4},{6,7},{7,6},{8,9},{9,8},{10,11... | collective-permute-start | bytes 491528 | tf_op jit(solution)/shard_map/ppermute | solution.py:339
  49.4 7.5 %copy-start = (bf16[192,640]{1,0:T(8,128)(2,1)}, bf16[192,640]{1,0:T(8,128)(2,1)S(1)}, u32[]{:S(2)}) copy-start(bf16[192,640]{1,0:T(8,128)(2,1)S(1)} %collective-permute-done.3.refs_5_.refs_3_) | copy-start | bytes 737284
  49.4 7.4 %collective-permute-start.5 = (bf16[32,640]{1,0:T(8,128)(2,1)S(1)}, bf16[32,640]{1,0:T(8,128)(2,1)S(1)}, u32[]{:S(2)}, u32[]{:S(2)}) collective-permute-start(bf16[32,640]{1,0:T(8,128)(2,1)S(1)} %slice_select_fusion), channel_id=1, source_target_pairs={{0,1},{1,0},{2,3},{3,2},{4,5},{5,4},{6,7},{7,6},{8,9},{9,8},{10,11... | collective-permute-start | bytes 122888 | tf_op jit(solution)/shard_map/ppermute | solution.py:339
  49.5 7.4 %copy-start.1 = (bf16[128,640]{1,0:T(8,128)(2,1)}, bf16[128,640]{1,0:T(8,128)(2,1)S(1)}, u32[]{:S(2)}) copy-start(bf16[128,640]{1,0:T(8,128)(2,1)S(1)} %collective-permute-done.4.refs_6_.refs_4_) | copy-start | bytes 491524
  50.7 15.5 %all-to-all-start.2 = ((bf16[16,24,512]{2,1,0:T(8,128)(2,1)}), bf16[16,24,512]{2,1,0:T(8,128)(2,1)S(1)}, u32[]{:S(2)}, u32[]{:S(2)}) async-start(bf16[16,24,512]{2,1,0:T(8,128)(2,1)} %coarse_update.1.refs_11_), calls=%async_computation.2 | async-start | bytes 786432 | tf_op jit(solution)/shard_map/all_to_all | solution.py:481
  56.8 0.6 copy-start.2
  66.2 3.0 %collective-permute-start.6 = (bf16[384,512]{1,0:T(8,128)(2,1)S(1)}, bf16[384,512]{1,0:T(8,128)(2,1)S(1)}, u32[]{:S(2)}, u32[]{:S(2)}) collective-permute-start(bf16[384,512]{1,0:T(8,128)(2,1)S(1)} %bitcast.7), channel_id=1, source_target_pairs={{0,1},{1,0},{2,3},{3,2},{4,5},{5,4},{6,7},{7,6},{8,9},{9,8},{10,11... | collective-permute-start | bytes 1179656 | tf_op jit(solution)/shard_map/ppermute | solution.py:339

commit v7 on v6

--- a/solution.py
+++ b/solution.py
@@ -193,12 +193,22 @@
     values = fine[...]
     sent = product(values, w_src[...]).astype(BF16)
     received = product(values, w_dst[...]).astype(BF16)
-    for k in range(out.shape[0] // CHUNK):
-        marks = range(k * CHUNK // LANES, (k + 1) * CHUNK // LANES)
-        picked = [jnp.concatenate(picks(spread(source[r : r + 1, :]), 0, blocks), axis=1) for r in marks]
-        total = product(jnp.concatenate(picked, axis=0), sent)
-        picked = [jnp.concatenate(picks(spread(target[r : r + 1, :]), 0, blocks), axis=1) for r in marks]
-        total += product(jnp.concatenate(picked, axis=0), received)
+
+    def marks_of(k):
+        both = []
+        for ids in (source, target):
+            rows = range(k * CHUNK // LANES, (k + 1) * CHUNK // LANES)
+            rows = [jnp.concatenate(picks(spread(ids[r : r + 1, :]), 0, blocks), axis=1) for r in rows]
+            both.append(jnp.concatenate(rows, axis=0))
+        return both
+
+    chunks = out.shape[0] // CHUNK
+    following = marks_of(0)
+    for k in range(chunks):
+        sources, targets = following
+        if k + 1 < chunks:
+            following = marks_of(k + 1)
+        total = product(sources, sent) + product(targets, received)
         out[k * CHUNK : (k + 1) * CHUNK, :] = total.astype(BF16)
         if (k + 1) * CHUNK % PIECE == 0:
             sent_out.start(k * CHUNK // PIECE)
@@ -218,15 +228,16 @@
         out[i] = total
 
 
-def coarse_body(parts, own_latent, own_hidden, both, third, out):
+def coarse_body(parts, own_latent, own_hidden, w_coarse, second, third, out):
     total = jnp.sum(parts[...].astype(F32), axis=0).astype(BF16)
-    hidden = silu(own_hidden[...] + product(total, both[...]))
+    incoming = product(total, w_coarse[...]).astype(BF16)
+    hidden = silu(own_hidden[...] + product(incoming, second[...]))
     result = updated(own_latent[...], hidden, third[...])
     for i in range(out.shape[0]):
         out[i] = result
 
 
-def coarse_rows_body(coarse, coarse_w1, own_latent, own_hidden):
+def coarse_ready_body(coarse, coarse_w1, w_coarse, second, third, own_latent, own_hidden):
     rows, total = own_latent.shape[0], coarse.shape[0]
     chips = lax.axis_size("y") * lax.axis_size("x")
     chip = lax.axis_index("y") * lax.axis_size("x") + lax.axis_index("x")
@@ -238,13 +249,6 @@
     own_hidden[...] = product(latent, coarse_w1[...])
 
 
-def weights_body(w_coarse, coarse_w2, edge_w2, node_w2, third, rows, hidden, both, last, own_latent, own_hidden):
-    own_latent[...] = rows[...]
-    own_hidden[...] = hidden[...]
-    both[...] = product(w_coarse[...], coarse_w2[...]).astype(BF16)
-    last[...] = product(edge_w2[...], node_w2[...]).astype(BF16)
-
-
 def slots(codes, tile, count):
     parent = codes - 1
     side = parent // count
@@ -253,7 +257,7 @@
 
 
 def rest_edges_body(
-    mid_count, parent, source, target, cross, swap, w_src, pair, mid_swap, first, w_descend, w_fine,
+    mid_count, mid_swap, parent, source, target, cross, swap, w_src, pair, first, w_descend, w_fine, w_dst,
     sent_out, sent_select, own_pick, middle, picked, out, select, table, where, window
 ):
     core = lax.axis_index("c")
@@ -282,25 +286,33 @@
     near = window[...]
     middle[...] = near[:, :width]
     picked[...] = hot(row_ids(near, width) == lax.broadcasted_iota(I32, picked.shape, 1))
-    for k in range(out.shape[0] // CHUNK):
+    def marks_of(k):
         rows = []
         for r in range(k * CHUNK // LANES, (k + 1) * CHUNK // LANES):
             row = picks(spread(source[r : r + 1, :]), 0, blocks + 2)
             row += picks(spread(target[r : r + 1, :]), 0, blocks)
             rows.append(jnp.concatenate(row, axis=1))
-        marks = jnp.concatenate(rows, axis=0)
+        return jnp.concatenate(rows, axis=0)
+
+    chunks = out.shape[0] // CHUNK
+    following = marks_of(0)
+    for k in range(chunks):
         here = slice(k * CHUNK, (k + 1) * CHUNK)
+        first.get(k * CHUNK // PIECE)
+        marks = following
+        if k + 1 < chunks:
+            following = marks_of(k + 1)
         select[here, :] = product(marks, where[...]).astype(BF16)
         rest = product(marks[:, count : count + 2 * LANES], table[...])
-        out[here, :] = (first.get(k * CHUNK // PIECE)[here, :].astype(F32) + rest).astype(BF16)
+        out[here, :] = (first.target[here, :].astype(F32) + rest).astype(BF16)
         if (k + 1) * CHUNK % PIECE == 0:
             sent_out.start(k * CHUNK // PIECE)
             sent_select.start(k * CHUNK // PIECE)
 
 
 def final_body(
-    mine, theirs, w_descend, w_fine, near, picked, w_src, w_dst, target, select, edges, own_pick, fine,
-    w_node, last, node_w3, fine_out, mid_out, coarse_out, coarse, table, sums,
+    mine, theirs, w_src, w_descend, w_fine, w_dst, near, picked, target, select, edges, own_pick, fine,
+    w_node, edge_w2, node_w2, node_w3, fine_out, mid_out, coarse_out, coarse, table, sums,
 ):
     core = lax.axis_index("c")
     half, width = mine.shape
@@ -320,7 +332,7 @@
         here = slice(k * CHUNK, (k + 1) * CHUNK)
         piece = k * CHUNK // PIECE
         edge_sum = edges.get(piece)[here, :].astype(F32) + product(select.get(piece)[here, :], table[...])
-        hidden = silu(edge_sum).astype(BF16)
+        hidden = silu(edge_sum.astype(BF16))
         marks = range(k * CHUNK // LANES, (k + 1) * CHUNK // LANES)
         scatter = jnp.concatenate([hot(rows == target[r : r + 1, :]) for r in marks], axis=1)
         part = product(scatter, hidden)
@@ -331,7 +343,8 @@
     coarse_out[...] = coarse[: coarse_out.shape[0], :]
     reach = fine_down[count : 5 * count]
     lifted = (fine[...].astype(F32) + product(own_pick[...], reach)).astype(BF16)
-    hidden = silu(product(lifted, w_node[...]) + product(sums[...].astype(BF16), last[...]))
+    aggregate = product(sums[...].astype(BF16), edge_w2[...]).astype(BF16)
+    hidden = silu(product(lifted, w_node[...]) + product(aggregate, node_w2[...]))
     fine_out[...] = updated(lifted, hidden, node_w3[...])
 
 
@@ -447,26 +460,18 @@
         gather_body, [near(planes, BLOCK, width)], [parts], after=[token], name="plane_sum"
     )
     in_planes = lax.all_to_all(own_parts, "z", 0, 0)
-    rows, hidden = kernel_call(
-        coarse_rows_body,
-        [far(BLOCK, width), far(BLOCK, width, dtype=F32)],
-        [],
-        stored=[coarse_latent, coarse_w1],
-        after=[own_parts],
-
-        name="coarse_rows",
-    )
-    halo_swap, cross, rows = lax.optimization_barrier((halo_swap, cross, rows))
+    halo_swap, cross, _ = lax.optimization_barrier((halo_swap, cross, own_parts))
     cross_in = crossed(cross, tiles)
     halo_in = swapped(halo_swap)
-    coarse_w3, both, last, own_latent, own_hidden = kernel_call(
-        weights_body,
-        [square, square, far(width, width), near(BLOCK, width), near(BLOCK, width, dtype=F32)],
+    w_coarse, coarse_w2, coarse_w3, own_latent, own_hidden = kernel_call(
+        coarse_ready_body,
+        [square, square, square, near(BLOCK, width), near(BLOCK, width, dtype=F32)],
         [],
-        stored=[w_coarse, coarse_w2, edge_w2, node_w2, coarse_w3, rows, hidden],
-        keep=[(4, 0)],
-        flops=3_000_000_000,
-        name="weights",
+        stored=[coarse_latent, coarse_w1, w_coarse, coarse_w2, coarse_w3],
+        keep=[(2, 0), (3, 1), (4, 2)],
+        after=[own_parts],
+        flops=4_000_000_000,
+        name="coarse_ready",
     )
     nearest, own_latent = lax.optimization_barrier((cross_in, own_latent))
     mid_in = swapped(jnp.where(lax.axis_index("c") == 0, nearest[mids : 2 * mids], nearest[:mids]))
@@ -474,20 +479,21 @@
     (results,) = kernel_call(
         coarse_body,
         [near(chips, BLOCK, width)],
-        [in_planes] + [here(a) for a in (own_latent, own_hidden, both, coarse_w3)],
+        [in_planes] + [here(a) for a in (own_latent, own_hidden, w_coarse, coarse_w2, coarse_w3)],
         after=[cross_in, halo_in],
         name="coarse_update",
     )
     mine = lax.all_to_all(results, PLANE, 0, 0).reshape(half, width)
-    w_descend, w_fine, edges, select, own_pick, middle, picked = kernel_call(
+    w_src, w_descend, w_fine, w_dst, edges, select, own_pick, middle, picked = kernel_call(
         functools.partial(rest_edges_body, mids),
-        [square, square, far(edge_count, width), far(edge_count, 2 * LANES), far(count, LANES)]
+        [square] * 4
+        + [far(edge_count, width), far(edge_count, 2 * LANES), far(count, LANES)]
         + [near(5 * mids, width), near(5 * mids, 2 * half)],
-        [],
-        stored=[parent, source, target, cross_in, halo_in, edge_w_src, pair, mid_in, own_edges, w_descend, w_fine],
-        keep=[(9, 0), (10, 1)],
-        pieces=[8],
-        streams=[2, 3],
+        [mid_in],
+        stored=[parent, source, target, cross_in, halo_in, edge_w_src, pair, own_edges, w_descend, w_fine, edge_w_dst],
+        keep=[(5, 0), (8, 1), (9, 2), (10, 3)],
+        pieces=[7],
+        streams=[4, 5],
         after=[results],
         scratch=[
             pltpu.VMEM((2 * LANES, width), BF16),
@@ -504,9 +510,9 @@
     fine_out, mid_out, coarse_out = kernel_call(
         final_body,
         [free(count, width), free(mids, width), free(coarse_count, width)],
-        [mine, theirs] + [here(a) for a in (w_descend, w_fine, middle, picked)],
-        stored=[edge_w_src, edge_w_dst, target, select, edges, own_pick, fine_latent, node_w1, last, node_w3],
-        pieces=[3, 4],
+        [mine, theirs] + [here(a) for a in (w_src, w_descend, w_fine, w_dst, middle, picked)],
+        stored=[target, select, edges, own_pick, fine_latent, node_w1, edge_w2, node_w2, node_w3],
+        pieces=[1, 2],
         scratch=[
             pltpu.VMEM((2 * half, width), BF16),
             pltpu.VMEM((8 * mids, width), BF16),

time: 79.3 us -> 77.4 us (0.976)
  Pallas kernels: 37.9 us -> 33.5 us
  waiting for transfers between devices: 7.04 us -> 9.08 us
  starting transfers between devices: 32.2 us -> 33.3 us
    pallas_call x11 -> x10, Pallas kernels: 37.9 us -> 33.5 us  [kernel_call(): pl.pallas_call(kernel, out_shape=outs, in_specs=[VMEM] * count + [STORED]...]
    ppermute x2, waiting for transfers between devices: 2.47 us -> 4.18 us  [crossed(): return lax.ppermute(values, TILE, pairs + [(b, a) for a, b in pairs])]
    ppermute x5, starting transfers between devices: 5.24 us -> 6.59 us  [swapped(): return lax.ppermute(values, 'c', [(0, 1), (1, 0)])]
  transfers between devices with their start and end apart: 10 -> 10, of which waited for: 6 -> 7; matrix products, arithmetic and copies ran while one was open for 0% -> 0% of each run, Pallas kernels for 31% -> 27%
where the time goes in v7:
time: 77.4 us; the launch traced here: 76.9 us
  Pallas kernels  33.5 us (43%)
  starting transfers between devices  33.3 us (43%)
  waiting for transfers between devices  9.08 us (12%)
  between operations  0.96 us (1%)
    pallas_call x10, Pallas kernels, kernel_call(): pl.pallas_call(kernel, out_shape=outs, in_specs=[VMEM] * count + [STORED]...  33.5 us
    all_to_all x1, starting transfers between devices, on_device(): in_planes = lax.all_to_all(own_parts, 'z', 0, 0)  8.19 us
    all_to_all x1, starting transfers between devices, on_device(): parts = lax.all_to_all(blocks, PLANE, 0, 0)  6.86 us
    ppermute x5, starting transfers between devices, swapped(): return lax.ppermute(values, 'c', [(0, 1), (1, 0)])  6.59 us
    ppermute x2, starting transfers between devices, crossed(): return lax.ppermute(values, TILE, pairs + [(b, a) for a, b in pairs])  5.83 us
    all_to_all x1, starting transfers between devices, on_device(): mine = lax.all_to_all(results, PLANE, 0, 0).reshape(half, width)  5.79 us
    ppermute x2, waiting for transfers between devices, crossed(): return lax.ppermute(values, TILE, pairs + [(b, a) for a, b in pairs])  4.18 us
    ppermute x5, waiting for transfers between devices, swapped(): return lax.ppermute(values, 'c', [(0, 1), (1, 0)])  2.56 us
  transfers between devices with their start and end apart: 10, of which 7 were waited for; matrix products, arithmetic and copies ran while one was open for 0% of the time, Pallas kernels for 27%

profile of v7, /device:TPU:1, one launch (start us, length us, event | category | flops | bytes accessed | tf_op | source)
XLA Modules:
  0.0 76.9 jit_solution(12084624349802580295)
XLA Ops:
  0.6 1.3 %child_sums.1 = (f32[32,512]{1,0:T(8,128)S(1)}, bf16[32,512]{1,0:T(8,128)(2,1)S(1)}, bf16[32,512]{1,0:T(8,128)(2,1)S(1)}) custom-call(s32[4,128]{1,0:T(4,128)} %bitcast.12, bf16[512,512]{1,0:T(8,128)(2,1)} %refs_12_.1), custom_call_target="tpu_custom_call" | custom-call | bytes 1048576 | tf_op jit(solution)/shard_map/child_sums/pallas_call | solution.py:89
  1.9 3.3 %collective-permute-start = (bf16[32,512]{1,0:T(8,128)(2,1)S(1)}, bf16[32,512]{1,0:T(8,128)(2,1)S(1)}, u32[]{:S(2)}, u32[]{:S(2)}) collective-permute-start(bf16[32,512]{1,0:T(8,128)(2,1)S(1)} %get-tuple-element.39), channel_id=1, source_target_pairs={{0,1},{1,0},{2,3},{3,2},{4,5},{5,4},{6,7},{7,6},{8,9},{9,8},{10,11... | collective-permute-start | bytes 98312 | tf_op jit(solution)/shard_map/ppermute | solution.py:352
  5.3 1.9 %collective-permute-start.1 = (bf16[32,512]{1,0:T(8,128)(2,1)S(1)}, bf16[32,512]{1,0:T(8,128)(2,1)S(1)}, u32[]{:S(2)}, u32[]{:S(2)}) collective-permute-start(bf16[32,512]{1,0:T(8,128)(2,1)S(1)} %get-tuple-element.40), channel_id=1, source_target_pairs={{1,2},{3,4},{5,6},{7,8},{9,10},{11,12},{13,14},{15,16},{17,18},{19... | collective-permute-start | bytes 98312 | tf_op jit(solution)/shard_map/ppermute | solution.py:357
  7.2 1.6 %mid_ready.1 = (bf16[512,512]{1,0:T(8,128)(2,1)S(1)}, bf16[512,512]{1,0:T(8,128)(2,1)S(1)}, bf16[512,512]{1,0:T(8,128)(2,1)S(1)}, bf16[32,512]{1,0:T(8,128)(2,1)...) custom-call(bf16[32,512]{1,0:T(8,128)(2,1)} %refs_0_.2, s32[1,32]{1,0:T(1,128)} %bitcast.18, ...), custom_call_target="tpu_custom_call" | custom-call | flops 1000000000 | bytes 1048576 | tf_op jit(solution)/shard_map/mid_ready/pallas_call | solution.py:89
  8.8 0.0 collective-permute-done.refs_1_
  8.8 1.7 %collective-permute-done.1.refs_2_ = bf16[32,512]{1,0:T(8,128)(2,1)S(1)} collective-permute-done((bf16[32,512]{1,0:T(8,128)(2,1)S(1)}, bf16[32,512]{1,0:T(8,128)(2,1)S(1)}, u32[]{:S(2)}, u32[]{:S(2)}) %collective-permute-start.1) | collective-permute-done | bytes 32800 | tf_op jit(solution)/shard_map/ppermute | solution.py:357
  10.5 0.6 mid_update.1.refs_0_
  11.1 0.1 collective-permute-start.2
  11.2 1.2 %collective-permute-done.2.refs_1_ = bf16[32,640]{1,0:T(8,128)(2,1)S(1)} collective-permute-done((bf16[32,640]{1,0:T(8,128)(2,1)S(1)}, bf16[32,640]{1,0:T(8,128)(2,1)S(1)}, u32[]{:S(2)}, u32[]{:S(2)}) %collective-permute-start.2) | collective-permute-done | bytes 40992 | tf_op jit(solution)/shard_map/ppermute | solution.py:352
  12.4 1.2 %coarse_blocks.1 = (bf16[64,640]{1,0:T(8,128)(2,1)}, bf16[384,512]{1,0:T(8,128)(2,1)}) custom-call(bf16[32,640]{1,0:T(8,128)(2,1)S(1)} %mid_update.1.refs_0_, bf16[32,640]{1,0:T(8,128)(2,1)S(1)} %collective-permute-done.2.refs_1_), custom_call_target="tpu_custom_call" | custom-call | bytes 1048576 | tf_op jit(solution)/shard_map/coarse_blocks/pallas_call | solution.py:89
  13.6 6.9 %all-to-all-start = ((bf16[16,24,512]{2,1,0:T(8,128)(2,1)}), bf16[16,24,512]{2,1,0:T(8,128)(2,1)S(1)}, u32[]{:S(2)}, u32[]{:S(2)}) async-start(bf16[16,24,512]{2,1,0:T(8,128)(2,1)} %bitcast.2.refs_8_), calls=%async_computation | async-start | bytes 786432 | tf_op jit(solution)/shard_map/all_to_all | solution.py:446
  20.5 7.6 %own_edges.1 = (bf16[3072,512]{1,0:T(8,128)(2,1)}, bf16[128,640]{1,0:T(8,128)(2,1)}, bf16[192,640]{1,0:T(8,128)(2,1)}, bf16[8,128]{1,0:T(8,128)(2,1)S(1)}) custom-call(s32[4,128]{1,0:T(4,128)} %bitcast.13, s32[2,128]{1,0:T(2,128)} %bitcast.17, s32[24,128]{1,0:T(8,128)} %bitcast.15, s32[24,128]{1,0:T(8,128)} %bitcast.9, bf16[512,512]{1,0:T(8,128)(2,1)} %refs_12_.1, ...), custom_call_target="tpu_custom_call" | custom-call | flops 4000000000 | bytes 1048576 | tf_op jit(solution)/shard_map/own_edges/pallas_call | solution.py:89
  28.1 1.8 %all-to-all-done.refs_0_ = bf16[16,24,512]{2,1,0:T(8,128)(2,1)S(1)} async-done(((bf16[16,24,512]{2,1,0:T(8,128)(2,1)}), bf16[16,24,512]{2,1,0:T(8,128)(2,1)S(1)}, u32[]{:S(2)}, u32[]{:S(2)}) %all-to-all-start) | async-done | bytes 393248 | tf_op jit(solution)/shard_map/all_to_all | solution.py:446
  29.9 0.7 plane_sum.1.refs_5_
  30.7 8.2 %all-to-all-start.1 = ((bf16[8,24,512]{2,1,0:T(8,128)(2,1)}), bf16[8,24,512]{2,1,0:T(8,128)(2,1)S(1)}, u32[]{:S(2)}, u32[]{:S(2)}) async-start(bf16[8,24,512]{2,1,0:T(8,128)(2,1)} %plane_sum.1.refs_5_), calls=%async_computation.1 | async-start | bytes 393216 | tf_op jit(solution)/shard_map/all_to_all | solution.py:462
  38.9 3.9 %collective-permute-start.3 = (bf16[192,640]{1,0:T(8,128)(2,1)}, bf16[192,640]{1,0:T(8,128)(2,1)S(1)}, u32[]{:S(2)}, u32[]{:S(2)}) collective-permute-start(bf16[192,640]{1,0:T(8,128)(2,1)} %get-tuple-element.52), channel_id=1, source_target_pairs={{1,2},{3,4},{5,6},{7,8},{9,10},{11,12},{13,14},{15,16},{17,18},{19... | collective-permute-start | bytes 737288 | tf_op jit(solution)/shard_map/ppermute | solution.py:357
  42.8 0.1 collective-permute-start.4
  42.9 1.8 %coarse_ready.1 = (bf16[512,512]{1,0:T(8,128)(2,1)S(1)}, bf16[512,512]{1,0:T(8,128)(2,1)S(1)}, bf16[512,512]{1,0:T(8,128)(2,1)S(1)}, bf16[24,512]{1,0:T(8,128)(2,1)S(1)}, f32[24,512]{1,0:T(8,128)S(1)}) custom-call(bf16[642,512]{1,0:T(8,128)(2,1)} %refs_0_.3, bf16[512,512]{1,0:T(8,128)(2,1)} %refs_1_.3, bf16[512,512]{1,0:T(8,128)(2,1)} %refs_2_.3, ...), custom_call_target="tpu_custom_call" | custom-call | flops 4000000000 | bytes 1048576 | tf_op jit(solution)/shard_map/coarse_ready/pallas_call | solution.py:89
  44.7 2.5 %collective-permute-done.3.refs_6_.refs_4_ = bf16[192,640]{1,0:T(8,128)(2,1)S(1)} collective-permute-done((bf16[192,640]{1,0:T(8,128)(2,1)}, bf16[192,640]{1,0:T(8,128)(2,1)S(1)}, u32[]{:S(2)}, u32[]{:S(2)}) %collective-permute-start.3) | collective-permute-done | bytes 245792 | tf_op jit(solution)/shard_map/ppermute | solution.py:357
  47.2 0.1 collective-permute-start.5
  47.3 0.0 collective-permute-done.4.refs_7_.refs_5_
  47.3 0.0 copy-start.1
  47.3 0.3 all-to-all-done.1.refs_0_
  47.6 1.4 %coarse_update.1.refs_12_ = bf16[16,24,512]{2,1,0:T(8,128)(2,1)} custom-call(bf16[8,24,512]{2,1,0:T(8,128)(2,1)S(1)} %all-to-all-done.1.refs_0_, bf16[24,512]{1,0:T(8,128)(2,1)S(1)} %get-tuple-element.54.refs_1_, f32[24,512]{1,0:T(8,128)S(1)} %get-tuple-element.55.refs_2_, bf16[512,512]{1,0:T(8,128)(2,1)S(1)} %get-tuple-element.56.refs_3_, ...), custom_call_target="tpu_custom_call" | custom-call | bytes 1048576 | tf_op jit(solution)/shard_map/coarse_update/pallas_call | solution.py:89
  49.0 5.8 %all-to-all-start.2 = ((bf16[16,24,512]{2,1,0:T(8,128)(2,1)}), bf16[16,24,512]{2,1,0:T(8,128)(2,1)S(1)}, u32[]{:S(2)}, u32[]{:S(2)}) async-start(bf16[16,24,512]{2,1,0:T(8,128)(2,1)} %coarse_update.1.refs_12_), calls=%async_computation.2 | async-start | bytes 786432 | tf_op jit(solution)/shard_map/all_to_all | solution.py:486
  54.8 0.0 collective-permute-done.5.refs_0_
  54.8 0.0 copy-done
  54.8 8.2 %rest_edges.1 = (bf16[512,512]{1,0:T(8,128)(2,1)S(1)}, bf16[512,512]{1,0:T(8,128)(2,1)S(1)}, bf16[512,512]{1,0:T(8,128)(2,1)S(1)}, bf16[512,512]{1,0:T(8,128)(2,...) custom-call(bf16[32,640]{1,0:T(8,128)(2,1)S(1)} %collective-permute-, ...), custom_call_target="tpu_custom_call" | custom-call | flops 4000000000 | bytes 1048576 | tf_op jit(solution)/shard_map/rest_edges/pallas_call | solution.py:89
  63.0 0.2 all-to-all-done.2
  63.2 3.0 %collective-permute-start.6 = (bf16[384,512]{1,0:T(8,128)(2,1)S(1)}, bf16[384,512]{1,0:T(8,128)(2,1)S(1)}, u32[]{:S(2)}, u32[]{:S(2)}) collective-permute-start(bf16[384,512]{1,0:T(8,128)(2,1)S(1)} %bitcast.7), channel_id=1, source_target_pairs={{0,1},{1,0},{2,3},{3,2},{4,5},{5,4},{6,7},{7,6},{8,9},{9,8},{10,11... | collective-permute-start | bytes 1179656 | tf_op jit(solution)/shard_map/ppermute | solution.py:352
  66.2 1.3 %collective-permute-done.6.refs_1_ = bf16[384,512]{1,0:T(8,128)(2,1)S(1)} collective-permute-done((bf16[384,512]{1,0:T(8,128)(2,1)S(1)}, bf16[384,512]{1,0:T(8,128)(2,1)S(1)}, u32[]{:S(2)}, u32[]{:S(2)}) %collective-permute-start.6) | collective-permute-done | bytes 393248 | tf_op jit(solution)/shard_map/ppermute | solution.py:352
  67.5 9.2 %final.1 = (bf16[512,512]{1,0:T(8,128)(2,1)}, bf16[32,512]{1,0:T(8,128)(2,1)}, bf16[642,512]{1,0:T(8,128)(2,1)}) custom-call(bf16[384,512]{1,0:T(8,128)(2,1)S(1)} %bitcast.8, bf16[384,512]{1,0:T(8,128)(2,1)S(1)} %collective-permute-done.6.refs_1_, bf16[512,512]{1,0:T(8,128)(2,1)S(1)} %get-tuple-element.64.refs_2_, ...), custom_call_target="tpu_custom_call" | custom-call | bytes 1048576 | tf_op jit(solution)/shard_map/final/pallas_call | solution.py:89
  (3 shorter events, 0.0 us)
Async XLA Ops:
  1.9 6.9 %collective-permute-start = (bf16[32,512]{1,0:T(8,128)(2,1)S(1)}, bf16[32,512]{1,0:T(8,128)(2,1)S(1)}, u32[]{:S(2)}, u32[]{:S(2)}) collective-permute-start(bf16[32,512]{1,0:T(8,128)(2,1)S(1)} %get-tuple-element.39), channel_id=1, source_target_pairs={{0,1},{1,0},{2,3},{3,2},{4,5},{5,4},{6,7},{7,6},{8,9},{9,8},{10,11... | collective-permute-start | bytes 98312 | tf_op jit(solution)/shard_map/ppermute | solution.py:352
  5.3 5.2 %collective-permute-start.1 = (bf16[32,512]{1,0:T(8,128)(2,1)S(1)}, bf16[32,512]{1,0:T(8,128)(2,1)S(1)}, u32[]{:S(2)}, u32[]{:S(2)}) collective-permute-start(bf16[32,512]{1,0:T(8,128)(2,1)S(1)} %get-tuple-element.40), channel_id=1, source_target_pairs={{1,2},{3,4},{5,6},{7,8},{9,10},{11,12},{13,14},{15,16},{17,18},{19... | collective-permute-start | bytes 98312 | tf_op jit(solution)/shard_map/ppermute | solution.py:357
  11.1 1.3 %collective-permute-start.2 = (bf16[32,640]{1,0:T(8,128)(2,1)S(1)}, bf16[32,640]{1,0:T(8,128)(2,1)S(1)}, u32[]{:S(2)}, u32[]{:S(2)}) collective-permute-start(bf16[32,640]{1,0:T(8,128)(2,1)S(1)} %mid_update.1.refs_0_), channel_id=1, source_target_pairs={{0,1},{1,0},{2,3},{3,2},{4,5},{5,4},{6,7},{7,6},{8,9},{9,8},{10,11... | collective-permute-start | bytes 122888 | tf_op jit(solution)/shard_map/ppermute | solution.py:352
  13.6 16.3 %all-to-all-start = ((bf16[16,24,512]{2,1,0:T(8,128)(2,1)}), bf16[16,24,512]{2,1,0:T(8,128)(2,1)S(1)}, u32[]{:S(2)}, u32[]{:S(2)}) async-start(bf16[16,24,512]{2,1,0:T(8,128)(2,1)} %bitcast.2.refs_8_), calls=%async_computation | async-start | bytes 786432 | tf_op jit(solution)/shard_map/all_to_all | solution.py:446
  30.7 16.9 %all-to-all-start.1 = ((bf16[8,24,512]{2,1,0:T(8,128)(2,1)}), bf16[8,24,512]{2,1,0:T(8,128)(2,1)S(1)}, u32[]{:S(2)}, u32[]{:S(2)}) async-start(bf16[8,24,512]{2,1,0:T(8,128)(2,1)} %plane_sum.1.refs_5_), calls=%async_computation.1 | async-start | bytes 393216 | tf_op jit(solution)/shard_map/all_to_all | solution.py:462
  38.9 8.3 %collective-permute-start.3 = (bf16[192,640]{1,0:T(8,128)(2,1)}, bf16[192,640]{1,0:T(8,128)(2,1)S(1)}, u32[]{:S(2)}, u32[]{:S(2)}) collective-permute-start(bf16[192,640]{1,0:T(8,128)(2,1)} %get-tuple-element.52), channel_id=1, source_target_pairs={{1,2},{3,4},{5,6},{7,8},{9,10},{11,12},{13,14},{15,16},{17,18},{19... | collective-permute-start | bytes 737288 | tf_op jit(solution)/shard_map/ppermute | solution.py:357
  42.8 4.5 %collective-permute-start.4 = (bf16[128,640]{1,0:T(8,128)(2,1)}, bf16[128,640]{1,0:T(8,128)(2,1)S(1)}, u32[]{:S(2)}, u32[]{:S(2)}) collective-permute-start(bf16[128,640]{1,0:T(8,128)(2,1)} %get-tuple-element.59), channel_id=1, source_target_pairs={{0,1},{1,0},{2,3},{3,2},{4,5},{5,4},{6,7},{7,6},{8,9},{9,8},{10,11... | collective-permute-start | bytes 491528 | tf_op jit(solution)/shard_map/ppermute | solution.py:352
  47.2 7.6 %copy-start = (bf16[192,640]{1,0:T(8,128)(2,1)}, bf16[192,640]{1,0:T(8,128)(2,1)S(1)}, u32[]{:S(2)}) copy-start(bf16[192,640]{1,0:T(8,128)(2,1)S(1)} %collective-permute-done.3.refs_6_.refs_4_) | copy-start | bytes 737284
  47.2 7.6 %collective-permute-start.5 = (bf16[32,640]{1,0:T(8,128)(2,1)S(1)}, bf16[32,640]{1,0:T(8,128)(2,1)S(1)}, u32[]{:S(2)}, u32[]{:S(2)}) collective-permute-start(bf16[32,640]{1,0:T(8,128)(2,1)S(1)} %slice_select_fusion), channel_id=1, source_target_pairs={{0,1},{1,0},{2,3},{3,2},{4,5},{5,4},{6,7},{7,6},{8,9},{9,8},{10,11... | collective-permute-start | bytes 122888 | tf_op jit(solution)/shard_map/ppermute | solution.py:352
  47.3 7.5 %copy-start.1 = (bf16[128,640]{1,0:T(8,128)(2,1)}, bf16[128,640]{1,0:T(8,128)(2,1)S(1)}, u32[]{:S(2)}) copy-start(bf16[128,640]{1,0:T(8,128)(2,1)S(1)} %collective-permute-done.4.refs_7_.refs_5_) | copy-start | bytes 491524
  49.0 14.2 %all-to-all-start.2 = ((bf16[16,24,512]{2,1,0:T(8,128)(2,1)}), bf16[16,24,512]{2,1,0:T(8,128)(2,1)S(1)}, u32[]{:S(2)}, u32[]{:S(2)}) async-start(bf16[16,24,512]{2,1,0:T(8,128)(2,1)} %coarse_update.1.refs_12_), calls=%async_computation.2 | async-start | bytes 786432 | tf_op jit(solution)/shard_map/all_to_all | solution.py:486
  63.2 4.3 %collective-permute-start.6 = (bf16[384,512]{1,0:T(8,128)(2,1)S(1)}, bf16[384,512]{1,0:T(8,128)(2,1)S(1)}, u32[]{:S(2)}, u32[]{:S(2)}) collective-permute-start(bf16[384,512]{1,0:T(8,128)(2,1)S(1)} %bitcast.7), channel_id=1, source_target_pairs={{0,1},{1,0},{2,3},{3,2},{4,5},{5,4},{6,7},{7,6},{8,9},{9,8},{10,11... | collective-permute-start | bytes 1179656 | tf_op jit(solution)/shard_map/ppermute | solution.py:352

commit v8 on v7

--- a/solution.py
+++ b/solution.py
@@ -56,7 +56,7 @@
     count, held, skipped, given = len(operands), len(stored), len(after), len(outs)
     target = dict(keep)
     cuts = [stored[i].shape[0] // PIECE if i in pieces else 1 for i in range(held)]
-    flows = {o: outs[o].shape[0] // PIECE for o in streams}
+    flows = dict(streams)
 
     def kernel(*refs):
         inputs, refs = refs[:count], refs[count:]
@@ -65,8 +65,8 @@
         own, refs = refs[: len(scratch)], refs[len(scratch) :]
         buffers = iter(refs)
         places = [results[target[i]] if i in target else next(buffers) for i in range(held)]
-        leaving = {o: next(buffers) for o in streams}
-        semaphores = next(buffers) if held or streams else None
+        leaving = {o: next(buffers) for o in flows}
+        semaphores = next(buffers) if held or flows else None
         first, copies, fresh = 0, [], []
         for i in range(held):
             copies.append(Copied(sources[i], places[i], semaphores, first, cuts[i]).start())
@@ -77,14 +77,14 @@
                 first += flows[o]
             elif o not in target.values():
                 fresh.append(results[o])
-        body(*inputs, *copies, *fresh, *[leaving[o] for o in streams], *own)
+        body(*inputs, *copies, *fresh, *leaving.values(), *own)
         for copy in copies + fresh:
             if isinstance(copy, Copied):
                 copy.get()
 
     buffers = [pltpu.VMEM(stored[i].shape, stored[i].dtype) for i in range(held) if i not in target]
-    buffers += [pltpu.VMEM(outs[o].shape, outs[o].dtype) for o in streams]
-    if held or streams:
+    buffers += [pltpu.VMEM(outs[o].shape, outs[o].dtype) for o in flows]
+    if held or flows:
         buffers.append(pltpu.SemaphoreType.DMA((sum(cuts) + sum(flows.values()),)))
     return pl.pallas_call(
         kernel,
@@ -256,15 +256,13 @@
     return jnp.where(codes > 0, (tile + away) * count + (parent & (count - 1)), -1)
 
 
-def rest_edges_body(
-    mid_count, mid_swap, parent, source, target, cross, swap, w_src, pair, first, w_descend, w_fine, w_dst,
-    sent_out, sent_select, own_pick, middle, picked, out, select, table, where, window
-):
+def picks_body(mid_count, cross, swap, parent, source, target, sent_select, own_pick, token, select, where):
+    token[...] = jnp.zeros_like(token)
     core = lax.axis_index("c")
     count = own_pick.shape[0]
-    width = out.shape[1]
+    width = swap.shape[1] - LANES
     blocks = count // LANES
-    two = pair.shape[0]
+    two = cross.shape[0] - LANES
     for r in range(blocks):
         place = slots(spread(parent[r : r + 1, :]) + 1, 2, mid_count)
         rows = slice(r * LANES, (r + 1) * LANES)
@@ -274,24 +272,55 @@
         far = place + 4 * mid_count
         there = slice(count + 2 * LANES + r * LANES, count + 2 * LANES + (r + 1) * LANES)
         where[there, :] = jnp.concatenate(picks(far, 0, 2), axis=1)
-    for values, late in ((cross[two:], core), (swap[...], 1 - core)):
-        rows = pl.ds(pl.multiple_of(late * LANES, LANES), LANES)
-        table[rows, :] = product(values[:, :width], w_src[...]).astype(BF16)
-        place = slots(values[:, width:].astype(F32).astype(I32), 1 + 2 * late, mid_count)
+    for codes, late in ((cross[two:, width:], core), (swap[:, width:], 1 - core)):
+        place = slots(codes.astype(F32).astype(I32), 1 + 2 * late, mid_count)
         rows = pl.ds(pl.multiple_of(count + late * LANES, LANES), LANES)
         where[rows, :] = jnp.concatenate(picks(place, 0, 2), axis=1)
-    window[pl.ds(pl.multiple_of((1 - core) * 4 * mid_count, mid_count), mid_count), :] = mid_swap[...]
-    window[pl.ds(pl.multiple_of(core * 3 * mid_count, mid_count), two), :] = cross[:two]
-    window[pl.ds(pl.multiple_of((2 - core) * mid_count, mid_count), two), :] = pair[...]
-    near = window[...]
-    middle[...] = near[:, :width]
-    picked[...] = hot(row_ids(near, width) == lax.broadcasted_iota(I32, picked.shape, 1))
+
     def marks_of(k):
         rows = []
         for r in range(k * CHUNK // LANES, (k + 1) * CHUNK // LANES):
             row = picks(spread(source[r : r + 1, :]), 0, blocks + 2)
             row += picks(spread(target[r : r + 1, :]), 0, blocks)
             rows.append(jnp.concatenate(row, axis=1))
+        return jnp.concatenate(rows, axis=0)
+
+    chunks = select.shape[0] // CHUNK
+    following = marks_of(0)
+    for k in range(chunks):
+        marks = following
+        if k + 1 < chunks:
+            following = marks_of(k + 1)
+        select[k * CHUNK : (k + 1) * CHUNK, :] = product(marks, where[...]).astype(BF16)
+        if (k + 1) * CHUNK % PIECE == 0:
+            sent_select.start(k * CHUNK // PIECE)
+
+
+def halo_edges_body(
+    mid_count, mid_swap, source, cross, swap, w_src, pair, first, w_descend, w_fine, w_dst,
+    sent_out, middle, picked, out, table, window
+):
+    core = lax.axis_index("c")
+    count = 4 * LANES
+    width = out.shape[1]
+    half = picked.shape[1] // 2
+    two = pair.shape[0]
+    for values, late in ((cross[two:], core), (swap[...], 1 - core)):
+        rows = pl.ds(pl.multiple_of(late * LANES, LANES), LANES)
+        table[rows, :] = product(values[:, :width], w_src[...]).astype(BF16)
+    window[pl.ds(pl.multiple_of((1 - core) * 4 * mid_count, mid_count), mid_count), :] = mid_swap[...]
+    window[pl.ds(pl.multiple_of(core * 3 * mid_count, mid_count), two), :] = cross[:two]
+    window[pl.ds(pl.multiple_of((2 - core) * mid_count, mid_count), two), :] = pair[...]
+    near = window[...]
+    middle[...] = near[:, :width]
+    ids = row_ids(near, width)
+    mine = ids - core * half
+    place = jnp.where((mine >= 0) & (mine < half), mine, ids - (1 - core) * half + half)
+    picked[...] = hot(place == lax.broadcasted_iota(I32, picked.shape, 1))
+
+    def marks_of(k):
+        rows = range(k * CHUNK // LANES, (k + 1) * CHUNK // LANES)
+        rows = [jnp.concatenate(picks(spread(source[r : r + 1, :]), count, 2), axis=1) for r in rows]
         return jnp.concatenate(rows, axis=0)
 
     chunks = out.shape[0] // CHUNK
@@ -302,31 +331,30 @@
         marks = following
         if k + 1 < chunks:
             following = marks_of(k + 1)
-        select[here, :] = product(marks, where[...]).astype(BF16)
-        rest = product(marks[:, count : count + 2 * LANES], table[...])
-        out[here, :] = (first.target[here, :].astype(F32) + rest).astype(BF16)
+        out[here, :] = (first.target[here, :].astype(F32) + product(marks, table[...])).astype(BF16)
         if (k + 1) * CHUNK % PIECE == 0:
             sent_out.start(k * CHUNK // PIECE)
-            sent_select.start(k * CHUNK // PIECE)
 
 
 def final_body(
     mine, theirs, w_src, w_descend, w_fine, w_dst, near, picked, target, select, edges, own_pick, fine,
-    w_node, edge_w2, node_w2, node_w3, fine_out, mid_out, coarse_out, coarse, table, sums,
+    w_node, edge_w2, node_w2, node_w3, sent_fine, sent_mid, sent_coarse, fine_out, mid_out, coarse_out, table, sums,
 ):
     core = lax.axis_index("c")
-    half, width = mine.shape
+    half = mine.shape[0]
     count = near.shape[0] // 5
-    coarse[pl.ds(pl.multiple_of(core * half, half), half), :] = mine[...]
-    coarse[pl.ds(pl.multiple_of((1 - core) * half, half), half), :] = theirs[...]
-    parents = product(picked[...], coarse[...]).astype(BF16)
-    down = product(parents, w_descend[...]).astype(BF16)
+    parents = product(picked[:, :half], mine[...]) + product(picked[:, half:], theirs[...])
+    down = product(parents.astype(BF16), w_descend[...]).astype(BF16)
     middle = (near[...].astype(F32) + down.astype(F32)).astype(BF16)
     mid_out[...] = middle[2 * count : 3 * count]
+    sent_mid.start()
     fine_down = product(middle, w_fine[...]).astype(BF16)
     closer = fine_down[count : 4 * count]
     table[: 5 * count] = product(fine_down, w_src[...]).astype(BF16)
     table[5 * count :] = product(closer, w_dst[...]).astype(BF16)
+    coarse_out[:half] = jnp.where(core == 0, mine[...], theirs[...])
+    rest = coarse_out.shape[0] - half
+    coarse_out[half:] = jnp.where(core == 0, theirs[:rest], mine[:rest])
     rows = lax.broadcasted_iota(I32, (fine.shape[0], LANES), 0)
     for k in range(edges.shape[0] // CHUNK):
         here = slice(k * CHUNK, (k + 1) * CHUNK)
@@ -340,12 +368,17 @@
             sums[...] = part
         else:
             sums[...] += part
-    coarse_out[...] = coarse[: coarse_out.shape[0], :]
+    sent_coarse.start()
     reach = fine_down[count : 5 * count]
     lifted = (fine[...].astype(F32) + product(own_pick[...], reach)).astype(BF16)
     aggregate = product(sums[...].astype(BF16), edge_w2[...]).astype(BF16)
-    hidden = silu(product(lifted, w_node[...]) + product(aggregate, node_w2[...]))
-    fine_out[...] = updated(lifted, hidden, node_w3[...])
+    hidden = silu(product(lifted, w_node[...]) + product(aggregate, node_w2[...])).astype(BF16)
+    third = node_w3[...]
+    rows = fine_out.shape[0] // 2
+    for i in range(2):
+        here = slice(i * rows, (i + 1) * rows)
+        fine_out[here, :] = updated(lifted[here], hidden[here], third)
+        sent_fine.start(i)
 
 
 def swapped(values):
@@ -449,7 +482,7 @@
         [far(edge_count, width), far(LANES, wide), far(2 * mids + LANES, wide), free(8, LANES)],
         [],
         stored=[parent, halo, source, target, fine_latent, edge_w_src, edge_w_dst, pair],
-        streams=[0],
+        streams=[(0, edge_count // PIECE)],
         after=[blocks],
         limit=24,
         flops=4_000_000_000,
@@ -470,54 +503,57 @@
         stored=[coarse_latent, coarse_w1, w_coarse, coarse_w2, coarse_w3],
         keep=[(2, 0), (3, 1), (4, 2)],
         after=[own_parts],
-        flops=4_000_000_000,
+        flops=1_000_000_000,
         name="coarse_ready",
     )
     nearest, own_latent = lax.optimization_barrier((cross_in, own_latent))
     mid_in = swapped(jnp.where(lax.axis_index("c") == 0, nearest[mids : 2 * mids], nearest[:mids]))
+    select, own_pick, token = kernel_call(
+        functools.partial(picks_body, mids),
+        [far(edge_count, 2 * LANES), far(count, LANES), free(8, LANES)],
+        [cross_in, halo_in],
+        stored=[parent, source, target],
+        streams=[(0, edge_count // PIECE)],
+        after=[own_latent],
+        scratch=[pltpu.VMEM((2 * count + 2 * LANES, 2 * LANES), BF16)],
+        limit=16,
+        flops=3_000_000_000,
+        name="picks",
+    )
 
     (results,) = kernel_call(
         coarse_body,
         [near(chips, BLOCK, width)],
         [in_planes] + [here(a) for a in (own_latent, own_hidden, w_coarse, coarse_w2, coarse_w3)],
-        after=[cross_in, halo_in],
+        after=[token, mid_in],
         name="coarse_update",
     )
     mine = lax.all_to_all(results, PLANE, 0, 0).reshape(half, width)
-    w_src, w_descend, w_fine, w_dst, edges, select, own_pick, middle, picked = kernel_call(
-        functools.partial(rest_edges_body, mids),
-        [square] * 4
-        + [far(edge_count, width), far(edge_count, 2 * LANES), far(count, LANES)]
-        + [near(5 * mids, width), near(5 * mids, 2 * half)],
+    w_src, w_descend, w_fine, w_dst, edges, middle, picked = kernel_call(
+        functools.partial(halo_edges_body, mids),
+        [square] * 4 + [far(edge_count, width), near(5 * mids, width), near(5 * mids, 2 * half)],
         [mid_in],
-        stored=[parent, source, target, cross_in, halo_in, edge_w_src, pair, own_edges, w_descend, w_fine, edge_w_dst],
-        keep=[(5, 0), (8, 1), (9, 2), (10, 3)],
-        pieces=[7],
-        streams=[4, 5],
+        stored=[source, cross_in, halo_in, edge_w_src, pair, own_edges, w_descend, w_fine, edge_w_dst],
+        keep=[(3, 0), (6, 1), (7, 2), (8, 3)],
+        pieces=[5],
+        streams=[(4, edge_count // PIECE)],
         after=[results],
-        scratch=[
-            pltpu.VMEM((2 * LANES, width), BF16),
-            pltpu.VMEM((2 * count + 2 * LANES, 2 * LANES), BF16),
-            pltpu.VMEM((5 * mids, wide), BF16),
-        ],
+        scratch=[pltpu.VMEM((2 * LANES, width), BF16), pltpu.VMEM((5 * mids, wide), BF16)],
         limit=24,
         flops=4_000_000_000,
-        name="rest_edges",
-    )
-    mine, own_pick = lax.optimization_barrier((mine, own_pick))
+        name="halo_edges",
+    )
+    mine, edges = lax.optimization_barrier((mine, edges))
     theirs = swapped(mine)
 
     fine_out, mid_out, coarse_out = kernel_call(
         final_body,
-        [free(count, width), free(mids, width), free(coarse_count, width)],
+        [far(count, width), far(mids, width), far(coarse_count, width)],
         [mine, theirs] + [here(a) for a in (w_src, w_descend, w_fine, w_dst, middle, picked)],
         stored=[target, select, edges, own_pick, fine_latent, node_w1, edge_w2, node_w2, node_w3],
         pieces=[1, 2],
-        scratch=[
-            pltpu.VMEM((2 * half, width), BF16),
-            pltpu.VMEM((8 * mids, width), BF16),
-            pltpu.VMEM((count, width), F32),
-        ],
+        streams=[(0, 2), (1, 1), (2, 1)],
+        scratch=[pltpu.VMEM((8 * mids, width), BF16), pltpu.VMEM((count, width), F32)],
         limit=24,
         name="final",
     )

time: 77.4 us -> 81.6 us (1.054)
  waiting for transfers between devices: 9.08 us -> 13.6 us
  starting transfers between devices: 33.3 us -> 31.7 us
  Pallas kernels: 33.5 us -> 34.7 us
    all_to_all x1, waiting for transfers between devices: 0.22 us -> 5.06 us  [on_device(): mine = lax.all_to_all(results, PLANE, 0, 0).reshape(half, width)]
    ppermute x2, waiting for transfers between devices: 4.18 us -> 1.68 us  [crossed(): return lax.ppermute(values, TILE, pairs + [(b, a) for a, b in pairs])]
    all_to_all x1, waiting for transfers between devices: 0.3 us -> 2.51 us  [on_device(): in_planes = lax.all_to_all(own_parts, 'z', 0, 0)]
    pallas_call x10 -> x11, Pallas kernels: 33.5 us -> 34.7 us  [kernel_call(): pl.pallas_call(kernel, out_shape=outs, in_specs=[VMEM] * count + [STORED]...]
    ppermute x5, starting transfers between devices: 6.59 us -> 5.55 us  [swapped(): return lax.ppermute(values, 'c', [(0, 1), (1, 0)])]
  transfers between devices with their start and end apart: 10 -> 10, of which waited for: 7 -> 6; matrix products, arithmetic and copies ran while one was open for 0% -> 0% of each run, Pallas kernels for 27% -> 25%
where the time goes in v8:
time: 81.6 us; the launch traced here: 81 us
  Pallas kernels  34.7 us (43%)
  starting transfers between devices  31.7 us (39%)
  waiting for transfers between devices  13.6 us (17%)
  between operations  0.96 us (1%)
    pallas_call x11, Pallas kernels, kernel_call(): pl.pallas_call(kernel, out_shape=outs, in_specs=[VMEM] * count + [STORED]...  34.7 us
    all_to_all x1, starting transfers between devices, on_device(): in_planes = lax.all_to_all(own_parts, 'z', 0, 0)  8.2 us
    all_to_all x1, starting transfers between devices, on_device(): parts = lax.all_to_all(blocks, PLANE, 0, 0)  6.86 us
    ppermute x5, starting transfers between devices, swapped(): return lax.ppermute(values, 'c', [(0, 1), (1, 0)])  5.55 us
    ppermute x2, starting transfers between devices, crossed(): return lax.ppermute(values, TILE, pairs + [(b, a) for a, b in pairs])  5.55 us
    all_to_all x1, starting transfers between devices, on_device(): mine = lax.all_to_all(results, PLANE, 0, 0).reshape(half, width)  5.51 us
    all_to_all x1, waiting for transfers between devices, on_device(): mine = lax.all_to_all(results, PLANE, 0, 0).reshape(half, width)  5.06 us
    ppermute x5, waiting for transfers between devices, swapped(): return lax.ppermute(values, 'c', [(0, 1), (1, 0)])  2.56 us
  transfers between devices with their start and end apart: 10, of which 6 were waited for; matrix products, arithmetic and copies ran while one was open for 0% of the time, Pallas kernels for 25%

profile of v8, /device:TPU:1, one launch (start us, length us, event | category | flops | bytes accessed | tf_op | source)
XLA Modules:
  0.0 81.0 jit_solution(14882003163738152267)
XLA Ops:
  0.6 1.3 %child_sums.1 = (f32[32,512]{1,0:T(8,128)S(1)}, bf16[32,512]{1,0:T(8,128)(2,1)S(1)}, bf16[32,512]{1,0:T(8,128)(2,1)S(1)}) custom-call(s32[4,128]{1,0:T(4,128)} %bitcast.12, bf16[512,512]{1,0:T(8,128)(2,1)} %refs_12_.1), custom_call_target="tpu_custom_call" | custom-call | bytes 1048576 | tf_op jit(solution)/shard_map/child_sums/pallas_call | solution.py:89
  1.9 3.3 %collective-permute-start = (bf16[32,512]{1,0:T(8,128)(2,1)S(1)}, bf16[32,512]{1,0:T(8,128)(2,1)S(1)}, u32[]{:S(2)}, u32[]{:S(2)}) collective-permute-start(bf16[32,512]{1,0:T(8,128)(2,1)S(1)} %get-tuple-element.40), channel_id=1, source_target_pairs={{0,1},{1,0},{2,3},{3,2},{4,5},{5,4},{6,7},{7,6},{8,9},{9,8},{10,11... | collective-permute-start | bytes 98312 | tf_op jit(solution)/shard_map/ppermute | solution.py:385
  5.3 1.9 %collective-permute-start.1 = (bf16[32,512]{1,0:T(8,128)(2,1)S(1)}, bf16[32,512]{1,0:T(8,128)(2,1)S(1)}, u32[]{:S(2)}, u32[]{:S(2)}) collective-permute-start(bf16[32,512]{1,0:T(8,128)(2,1)S(1)} %get-tuple-element.41), channel_id=1, source_target_pairs={{1,2},{3,4},{5,6},{7,8},{9,10},{11,12},{13,14},{15,16},{17,18},{19... | collective-permute-start | bytes 98312 | tf_op jit(solution)/shard_map/ppermute | solution.py:390
  7.2 1.6 %mid_ready.1 = (bf16[512,512]{1,0:T(8,128)(2,1)S(1)}, bf16[512,512]{1,0:T(8,128)(2,1)S(1)}, bf16[512,512]{1,0:T(8,128)(2,1)S(1)}, bf16[32,512]{1,0:T(8,128)(2,1)...) custom-call(bf16[32,512]{1,0:T(8,128)(2,1)} %refs_0_.2, s32[1,32]{1,0:T(1,128)} %bitcast.19, ...), custom_call_target="tpu_custom_call" | custom-call | flops 1000000000 | bytes 1048576 | tf_op jit(solution)/shard_map/mid_ready/pallas_call | solution.py:89
  8.8 0.0 collective-permute-done.refs_1_
  8.8 1.7 %collective-permute-done.1.refs_2_ = bf16[32,512]{1,0:T(8,128)(2,1)S(1)} collective-permute-done((bf16[32,512]{1,0:T(8,128)(2,1)S(1)}, bf16[32,512]{1,0:T(8,128)(2,1)S(1)}, u32[]{:S(2)}, u32[]{:S(2)}) %collective-permute-start.1) | collective-permute-done | bytes 32800 | tf_op jit(solution)/shard_map/ppermute | solution.py:390
  10.5 0.6 mid_update.1.refs_0_
  11.1 0.1 collective-permute-start.2
  11.2 1.2 %collective-permute-done.2.refs_1_ = bf16[32,640]{1,0:T(8,128)(2,1)S(1)} collective-permute-done((bf16[32,640]{1,0:T(8,128)(2,1)S(1)}, bf16[32,640]{1,0:T(8,128)(2,1)S(1)}, u32[]{:S(2)}, u32[]{:S(2)}) %collective-permute-start.2) | collective-permute-done | bytes 40992 | tf_op jit(solution)/shard_map/ppermute | solution.py:385
  12.4 1.2 %coarse_blocks.1 = (bf16[64,640]{1,0:T(8,128)(2,1)}, bf16[384,512]{1,0:T(8,128)(2,1)}) custom-call(bf16[32,640]{1,0:T(8,128)(2,1)S(1)} %mid_update.1.refs_0_, bf16[32,640]{1,0:T(8,128)(2,1)S(1)} %collective-permute-done.2.refs_1_), custom_call_target="tpu_custom_call" | custom-call | bytes 1048576 | tf_op jit(solution)/shard_map/coarse_blocks/pallas_call | solution.py:89
  13.6 6.9 %all-to-all-start = ((bf16[16,24,512]{2,1,0:T(8,128)(2,1)}), bf16[16,24,512]{2,1,0:T(8,128)(2,1)S(1)}, u32[]{:S(2)}, u32[]{:S(2)}) async-start(bf16[16,24,512]{2,1,0:T(8,128)(2,1)} %bitcast.2.refs_8_), calls=%async_computation | async-start | bytes 786432 | tf_op jit(solution)/shard_map/all_to_all | solution.py:479
  20.5 7.6 %own_edges.1 = (bf16[3072,512]{1,0:T(8,128)(2,1)}, bf16[128,640]{1,0:T(8,128)(2,1)}, bf16[192,640]{1,0:T(8,128)(2,1)}, bf16[8,128]{1,0:T(8,128)(2,1)S(1)}) custom-call(s32[4,128]{1,0:T(4,128)} %bitcast.13, s32[2,128]{1,0:T(2,128)} %bitcast.18, s32[24,128]{1,0:T(8,128)} %bitcast.15, s32[24,128]{1,0:T(8,128)} %bitcast.9, bf16[512,512]{1,0:T(8,128)(2,1)} %refs_12_.1, ...), custom_call_target="tpu_custom_call" | custom-call | flops 4000000000 | bytes 1048576 | tf_op jit(solution)/shard_map/own_edges/pallas_call | solution.py:89
  28.1 1.8 %all-to-all-done.refs_0_ = bf16[16,24,512]{2,1,0:T(8,128)(2,1)S(1)} async-done(((bf16[16,24,512]{2,1,0:T(8,128)(2,1)}), bf16[16,24,512]{2,1,0:T(8,128)(2,1)S(1)}, u32[]{:S(2)}, u32[]{:S(2)}) %all-to-all-start) | async-done | bytes 393248 | tf_op jit(solution)/shard_map/all_to_all | solution.py:479
  29.9 0.7 plane_sum.1.refs_5_
  30.7 3.6 %collective-permute-start.3 = (bf16[192,640]{1,0:T(8,128)(2,1)}, bf16[192,640]{1,0:T(8,128)(2,1)S(1)}, u32[]{:S(2)}, u32[]{:S(2)}) collective-permute-start(bf16[192,640]{1,0:T(8,128)(2,1)} %get-tuple-element.53), channel_id=1, source_target_pairs={{1,2},{3,4},{5,6},{7,8},{9,10},{11,12},{13,14},{15,16},{17,18},{19... | collective-permute-start | bytes 737288 | tf_op jit(solution)/shard_map/ppermute | solution.py:390
  34.3 8.2 %all-to-all-start.1 = ((bf16[8,24,512]{2,1,0:T(8,128)(2,1)}), bf16[8,24,512]{2,1,0:T(8,128)(2,1)S(1)}, u32[]{:S(2)}, u32[]{:S(2)}) async-start(bf16[8,24,512]{2,1,0:T(8,128)(2,1)} %plane_sum.1.refs_5_), calls=%async_computation.1 | async-start | bytes 393216 | tf_op jit(solution)/shard_map/all_to_all | solution.py:495
  42.5 0.0 collective-permute-start.4
  42.6 1.8 %coarse_ready.1 = (bf16[512,512]{1,0:T(8,128)(2,1)S(1)}, bf16[512,512]{1,0:T(8,128)(2,1)S(1)}, bf16[512,512]{1,0:T(8,128)(2,1)S(1)}, bf16[24,512]{1,0:T(8,128)(2,1)S(1)}, f32[24,512]{1,0:T(8,128)S(1)}) custom-call(bf16[642,512]{1,0:T(8,128)(2,1)} %refs_0_.3, bf16[512,512]{1,0:T(8,128)(2,1)} %refs_1_.3, bf16[512,512]{1,0:T(8,128)(2,1)} %refs_2_.3, ...), custom_call_target="tpu_custom_call" | custom-call | flops 1000000000 | bytes 1048576 | tf_op jit(solution)/shard_map/coarse_ready/pallas_call | solution.py:89
  44.3 0.0 collective-permute-done.3.refs_0_.refs_2_
  44.3 0.0 copy-start
  44.4 0.6 collective-permute-start.5
  44.9 0.0 collective-permute-done.4.refs_1_.refs_3_
  45.0 5.1 %picks.1 = (bf16[3072,256]{1,0:T(8,128)(2,1)}, bf16[512,128]{1,0:T(8,128)(2,1)}, bf16[8,128]{1,0:T(8,128)(2,1)S(1)}) custom-call(bf16[192,640]{1,0:T(8,128)(2,1)S(1)} %collective-permute-done.3.refs_0_.refs_2_, bf16[128,640]{1,0:T(8,128)(2,1)S(1)} %collective-permute-done.4.refs_1_.refs_3_, s32[4,128]{1,0:T(4,128)} %bitcast.14, s32[24,128]{1,0:T(8,128)} %bitcast.16, ...), custom_call_target="tpu_custom_call" | custom-call | flops 3000000000 | bytes 1048576 | tf_op jit(solution)/shard_map/picks/pallas_call | solution.py:89
  50.1 0.0 collective-permute-done.5.refs_7_.refs_0_
  50.1 2.5 %all-to-all-done.1.refs_0_ = bf16[8,24,512]{2,1,0:T(8,128)(2,1)S(1)} async-done(((bf16[8,24,512]{2,1,0:T(8,128)(2,1)}), bf16[8,24,512]{2,1,0:T(8,128)(2,1)S(1)}, u32[]{:S(2)}, u32[]{:S(2)}) %all-to-all-start.1) | async-done | bytes 196640 | tf_op jit(solution)/shard_map/all_to_all | solution.py:495
  52.6 1.4 %coarse_update.1.refs_10_ = bf16[16,24,512]{2,1,0:T(8,128)(2,1)} custom-call(bf16[8,24,512]{2,1,0:T(8,128)(2,1)S(1)} %all-to-all-done.1.refs_0_, bf16[24,512]{1,0:T(8,128)(2,1)S(1)} %get-tuple-element.55.refs_5_.refs_1_, f32[24,512]{1,0:T(8,128)S(1)} %get-tuple-element.56.refs_2_, bf16[512,512]{1,0:T(8,128)(2,1)S(1)} %get-tuple-element.57.refs_3_, ...), custom_call_target="tpu_custom_call" | custom-call | bytes 1048576 | tf_op jit(solution)/shard_map/coarse_update/pallas_call | solution.py:89
  54.0 5.5 %all-to-all-start.2 = ((bf16[16,24,512]{2,1,0:T(8,128)(2,1)}), bf16[16,24,512]{2,1,0:T(8,128)(2,1)S(1)}, u32[]{:S(2)}, u32[]{:S(2)}) async-start(bf16[16,24,512]{2,1,0:T(8,128)(2,1)} %coarse_update.1.refs_10_), calls=%async_computation.2 | async-start | bytes 786432 | tf_op jit(solution)/shard_map/all_to_all | solution.py:531
  59.5 4.4 %halo_edges.1 = (bf16[512,512]{1,0:T(8,128)(2,1)S(1)}, bf16[512,512]{1,0:T(8,128)(2,1)S(1)}, bf16[512,512]{1,0:T(8,128)(2,1)S(1)}, bf16[512,512]{1,0:T(8,128)(2,...) custom-call(bf16[32,640]{1,0:T(8,128)(2,1)S(1)} %collective-permute-done.5.refs_7_.ref, ...), custom_call_target="tpu_custom_call" | custom-call | flops 4000000000 | bytes 1048576 | tf_op jit(solution)/shard_map/halo_edges/pallas_call | solution.py:89
  63.9 5.1 %all-to-all-done.2 = bf16[16,24,512]{2,1,0:T(8,128)(2,1)S(1)} async-done(((bf16[16,24,512]{2,1,0:T(8,128)(2,1)}), bf16[16,24,512]{2,1,0:T(8,128)(2,1)S(1)}, u32[]{:S(2)}, u32[]{:S(2)}) %all-to-all-start.2) | async-done | bytes 393248 | tf_op jit(solution)/shard_map/all_to_all | solution.py:531
  69.0 1.5 %collective-permute-start.6 = (bf16[384,512]{1,0:T(8,128)(2,1)S(1)}, bf16[384,512]{1,0:T(8,128)(2,1)S(1)}, u32[]{:S(2)}, u32[]{:S(2)}) collective-permute-start(bf16[384,512]{1,0:T(8,128)(2,1)S(1)} %bitcast.7), channel_id=1, source_target_pairs={{0,1},{1,0},{2,3},{3,2},{4,5},{5,4},{6,7},{7,6},{8,9},{9,8},{10,11... | collective-permute-start | bytes 1179656 | tf_op jit(solution)/shard_map/ppermute | solution.py:385
  70.5 1.3 %collective-permute-done.6.refs_1_ = bf16[384,512]{1,0:T(8,128)(2,1)S(1)} collective-permute-done((bf16[384,512]{1,0:T(8,128)(2,1)S(1)}, bf16[384,512]{1,0:T(8,128)(2,1)S(1)}, u32[]{:S(2)}, u32[]{:S(2)}) %collective-permute-start.6) | collective-permute-done | bytes 393248 | tf_op jit(solution)/shard_map/ppermute | solution.py:385
  71.9 8.9 %final.1 = (bf16[512,512]{1,0:T(8,128)(2,1)}, bf16[32,512]{1,0:T(8,128)(2,1)}, bf16[642,512]{1,0:T(8,128)(2,1)}) custom-call(bf16[384,512]{1,0:T(8,128)(2,1)S(1)} %bitcast.8, bf16[384,512]{1,0:T(8,128)(2,1)S(1)} %collective-permute-done.6.refs_1_, bf16[512,512]{1,0:T(8,128)(2,1)S(1)} %get-tuple-element.66.refs_2_, ...), custom_call_target="tpu_custom_call" | custom-call | bytes 1048576 | tf_op jit(solution)/shard_map/final/pallas_call | solution.py:89
  (4 shorter events, 0.0 us)
Async XLA Ops:
  1.9 6.9 %collective-permute-start = (bf16[32,512]{1,0:T(8,128)(2,1)S(1)}, bf16[32,512]{1,0:T(8,128)(2,1)S(1)}, u32[]{:S(2)}, u32[]{:S(2)}) collective-permute-start(bf16[32,512]{1,0:T(8,128)(2,1)S(1)} %get-tuple-element.40), channel_id=1, source_target_pairs={{0,1},{1,0},{2,3},{3,2},{4,5},{5,4},{6,7},{7,6},{8,9},{9,8},{10,11... | collective-permute-start | bytes 98312 | tf_op jit(solution)/shard_map/ppermute | solution.py:385
  5.3 5.2 %collective-permute-start.1 = (bf16[32,512]{1,0:T(8,128)(2,1)S(1)}, bf16[32,512]{1,0:T(8,128)(2,1)S(1)}, u32[]{:S(2)}, u32[]{:S(2)}) collective-permute-start(bf16[32,512]{1,0:T(8,128)(2,1)S(1)} %get-tuple-element.41), channel_id=1, source_target_pairs={{1,2},{3,4},{5,6},{7,8},{9,10},{11,12},{13,14},{15,16},{17,18},{19... | collective-permute-start | bytes 98312 | tf_op jit(solution)/shard_map/ppermute | solution.py:390
  11.1 1.3 %collective-permute-start.2 = (bf16[32,640]{1,0:T(8,128)(2,1)S(1)}, bf16[32,640]{1,0:T(8,128)(2,1)S(1)}, u32[]{:S(2)}, u32[]{:S(2)}) collective-permute-start(bf16[32,640]{1,0:T(8,128)(2,1)S(1)} %mid_update.1.refs_0_), channel_id=1, source_target_pairs={{0,1},{1,0},{2,3},{3,2},{4,5},{5,4},{6,7},{7,6},{8,9},{9,8},{10,11... | collective-permute-start | bytes 122888 | tf_op jit(solution)/shard_map/ppermute | solution.py:385
  13.6 16.3 %all-to-all-start = ((bf16[16,24,512]{2,1,0:T(8,128)(2,1)}), bf16[16,24,512]{2,1,0:T(8,128)(2,1)S(1)}, u32[]{:S(2)}, u32[]{:S(2)}) async-start(bf16[16,24,512]{2,1,0:T(8,128)(2,1)} %bitcast.2.refs_8_), calls=%async_computation | async-start | bytes 786432 | tf_op jit(solution)/shard_map/all_to_all | solution.py:479
  30.7 13.6 %collective-permute-start.3 = (bf16[192,640]{1,0:T(8,128)(2,1)}, bf16[192,640]{1,0:T(8,128)(2,1)S(1)}, u32[]{:S(2)}, u32[]{:S(2)}) collective-permute-start(bf16[192,640]{1,0:T(8,128)(2,1)} %get-tuple-element.53), channel_id=1, source_target_pairs={{1,2},{3,4},{5,6},{7,8},{9,10},{11,12},{13,14},{15,16},{17,18},{19... | collective-permute-start | bytes 737288 | tf_op jit(solution)/shard_map/ppermute | solution.py:390
  34.3 18.3 %all-to-all-start.1 = ((bf16[8,24,512]{2,1,0:T(8,128)(2,1)}), bf16[8,24,512]{2,1,0:T(8,128)(2,1)S(1)}, u32[]{:S(2)}, u32[]{:S(2)}) async-start(bf16[8,24,512]{2,1,0:T(8,128)(2,1)} %plane_sum.1.refs_5_), calls=%async_computation.1 | async-start | bytes 393216 | tf_op jit(solution)/shard_map/all_to_all | solution.py:495
  42.5 2.4 %collective-permute-start.4 = (bf16[128,640]{1,0:T(8,128)(2,1)}, bf16[128,640]{1,0:T(8,128)(2,1)S(1)}, u32[]{:S(2)}, u32[]{:S(2)}) collective-permute-start(bf16[128,640]{1,0:T(8,128)(2,1)} %get-tuple-element.60), channel_id=1, source_target_pairs={{0,1},{1,0},{2,3},{3,2},{4,5},{5,4},{6,7},{7,6},{8,9},{9,8},{10,11... | collective-permute-start | bytes 491528 | tf_op jit(solution)/shard_map/ppermute | solution.py:385
  44.3 5.8 %copy-start = (bf16[192,640]{1,0:T(8,128)(2,1)}, bf16[192,640]{1,0:T(8,128)(2,1)S(1)}, u32[]{:S(2)}) copy-start(bf16[192,640]{1,0:T(8,128)(2,1)S(1)} %collective-permute-done.3.refs_0_.refs_2_) | copy-start | bytes 737284
  44.4 5.7 %collective-permute-start.5 = (bf16[32,640]{1,0:T(8,128)(2,1)S(1)}, bf16[32,640]{1,0:T(8,128)(2,1)S(1)}, u32[]{:S(2)}, u32[]{:S(2)}) collective-permute-start(bf16[32,640]{1,0:T(8,128)(2,1)S(1)} %slice_select_fusion), channel_id=1, source_target_pairs={{0,1},{1,0},{2,3},{3,2},{4,5},{5,4},{6,7},{7,6},{8,9},{9,8},{10,11... | collective-permute-start | bytes 122888 | tf_op jit(solution)/shard_map/ppermute | solution.py:385
  45.0 5.1 %copy-start.1 = (bf16[128,640]{1,0:T(8,128)(2,1)}, bf16[128,640]{1,0:T(8,128)(2,1)S(1)}, u32[]{:S(2)}) copy-start(bf16[128,640]{1,0:T(8,128)(2,1)S(1)} %collective-permute-done.4.refs_1_.refs_3_) | copy-start | bytes 491524
  54.0 15.0 %all-to-all-start.2 = ((bf16[16,24,512]{2,1,0:T(8,128)(2,1)}), bf16[16,24,512]{2,1,0:T(8,128)(2,1)S(1)}, u32[]{:S(2)}, u32[]{:S(2)}) async-start(bf16[16,24,512]{2,1,0:T(8,128)(2,1)} %coarse_update.1.refs_10_), calls=%async_computation.2 | async-start | bytes 786432 | tf_op jit(solution)/shard_map/all_to_all | solution.py:531
  69.0 2.9 %collective-permute-start.6 = (bf16[384,512]{1,0:T(8,128)(2,1)S(1)}, bf16[384,512]{1,0:T(8,128)(2,1)S(1)}, u32[]{:S(2)}, u32[]{:S(2)}) collective-permute-start(bf16[384,512]{1,0:T(8,128)(2,1)S(1)} %bitcast.7), channel_id=1, source_target_pairs={{0,1},{1,0},{2,3},{3,2},{4,5},{5,4},{6,7},{7,6},{8,9},{9,8},{10,11... | collective-permute-start | bytes 1179656 | tf_op jit(solution)/shard_map/ppermute | solution.py:385

commit v9 on v7

--- a/solution.py
+++ b/solution.py
@@ -56,7 +56,7 @@
     count, held, skipped, given = len(operands), len(stored), len(after), len(outs)
     target = dict(keep)
     cuts = [stored[i].shape[0] // PIECE if i in pieces else 1 for i in range(held)]
-    flows = {o: outs[o].shape[0] // PIECE for o in streams}
+    flows = dict(streams)
 
     def kernel(*refs):
         inputs, refs = refs[:count], refs[count:]
@@ -65,8 +65,8 @@
         own, refs = refs[: len(scratch)], refs[len(scratch) :]
         buffers = iter(refs)
         places = [results[target[i]] if i in target else next(buffers) for i in range(held)]
-        leaving = {o: next(buffers) for o in streams}
-        semaphores = next(buffers) if held or streams else None
+        leaving = {o: next(buffers) for o in flows}
+        semaphores = next(buffers) if held or flows else None
         first, copies, fresh = 0, [], []
         for i in range(held):
             copies.append(Copied(sources[i], places[i], semaphores, first, cuts[i]).start())
@@ -77,14 +77,14 @@
                 first += flows[o]
             elif o not in target.values():
                 fresh.append(results[o])
-        body(*inputs, *copies, *fresh, *[leaving[o] for o in streams], *own)
+        body(*inputs, *copies, *fresh, *leaving.values(), *own)
         for copy in copies + fresh:
             if isinstance(copy, Copied):
                 copy.get()
 
     buffers = [pltpu.VMEM(stored[i].shape, stored[i].dtype) for i in range(held) if i not in target]
-    buffers += [pltpu.VMEM(outs[o].shape, outs[o].dtype) for o in streams]
-    if held or streams:
+    buffers += [pltpu.VMEM(outs[o].shape, outs[o].dtype) for o in flows]
+    if held or flows:
         buffers.append(pltpu.SemaphoreType.DMA((sum(cuts) + sum(flows.values()),)))
     return pl.pallas_call(
         kernel,
@@ -228,16 +228,17 @@
         out[i] = total
 
 
-def coarse_body(parts, own_latent, own_hidden, w_coarse, second, third, out):
+def coarse_body(parts, own_latent, own_hidden, both, third, out):
     total = jnp.sum(parts[...].astype(F32), axis=0).astype(BF16)
-    incoming = product(total, w_coarse[...]).astype(BF16)
-    hidden = silu(own_hidden[...] + product(incoming, second[...]))
+    hidden = silu(own_hidden[...] + product(total, both[...]))
     result = updated(own_latent[...], hidden, third[...])
     for i in range(out.shape[0]):
         out[i] = result
 
 
-def coarse_ready_body(coarse, coarse_w1, w_coarse, second, third, own_latent, own_hidden):
+def coarse_ready_body(
+    coarse, coarse_w1, w_coarse, coarse_w2, edge_w2, node_w2, third, both, last, own_latent, own_hidden
+):
     rows, total = own_latent.shape[0], coarse.shape[0]
     chips = lax.axis_size("y") * lax.axis_size("x")
     chip = lax.axis_index("y") * lax.axis_size("x") + lax.axis_index("x")
@@ -247,6 +248,8 @@
     latent = product(picked, coarse[...]).astype(BF16)
     own_latent[...] = latent
     own_hidden[...] = product(latent, coarse_w1[...])
+    both[...] = product(w_coarse[...], coarse_w2[...]).astype(BF16)
+    last[...] = product(edge_w2[...], node_w2[...]).astype(BF16)
 
 
 def slots(codes, tile, count):
@@ -285,7 +288,12 @@
     window[pl.ds(pl.multiple_of((2 - core) * mid_count, mid_count), two), :] = pair[...]
     near = window[...]
     middle[...] = near[:, :width]
-    picked[...] = hot(row_ids(near, width) == lax.broadcasted_iota(I32, picked.shape, 1))
+    half = picked.shape[1] // 2
+    ids = row_ids(near, width)
+    mine = ids - core * half
+    place = jnp.where((mine >= 0) & (mine < half), mine, ids - (1 - core) * half + half)
+    picked[...] = hot(place == lax.broadcasted_iota(I32, picked.shape, 1))
+
     def marks_of(k):
         rows = []
         for r in range(k * CHUNK // LANES, (k + 1) * CHUNK // LANES):
@@ -295,6 +303,7 @@
         return jnp.concatenate(rows, axis=0)
 
     chunks = out.shape[0] // CHUNK
+    ready = []
     following = marks_of(0)
     for k in range(chunks):
         here = slice(k * CHUNK, (k + 1) * CHUNK)
@@ -305,28 +314,33 @@
         select[here, :] = product(marks, where[...]).astype(BF16)
         rest = product(marks[:, count : count + 2 * LANES], table[...])
         out[here, :] = (first.target[here, :].astype(F32) + rest).astype(BF16)
-        if (k + 1) * CHUNK % PIECE == 0:
-            sent_out.start(k * CHUNK // PIECE)
-            sent_select.start(k * CHUNK // PIECE)
+        ready += [k]
+        if k % 2 == 1 or k >= chunks - 2:
+            for i in ready:
+                sent_out.start(i)
+                sent_select.start(i)
+            ready = []
 
 
 def final_body(
     mine, theirs, w_src, w_descend, w_fine, w_dst, near, picked, target, select, edges, own_pick, fine,
-    w_node, edge_w2, node_w2, node_w3, fine_out, mid_out, coarse_out, coarse, table, sums,
+    w_node, last, node_w3, sent_fine, sent_mid, sent_coarse, fine_out, mid_out, coarse_out, table, sums,
 ):
     core = lax.axis_index("c")
-    half, width = mine.shape
+    half = mine.shape[0]
     count = near.shape[0] // 5
-    coarse[pl.ds(pl.multiple_of(core * half, half), half), :] = mine[...]
-    coarse[pl.ds(pl.multiple_of((1 - core) * half, half), half), :] = theirs[...]
-    parents = product(picked[...], coarse[...]).astype(BF16)
-    down = product(parents, w_descend[...]).astype(BF16)
+    parents = product(picked[:, :half], mine[...]) + product(picked[:, half:], theirs[...])
+    down = product(parents.astype(BF16), w_descend[...]).astype(BF16)
     middle = (near[...].astype(F32) + down.astype(F32)).astype(BF16)
     mid_out[...] = middle[2 * count : 3 * count]
+    sent_mid.start()
     fine_down = product(middle, w_fine[...]).astype(BF16)
     closer = fine_down[count : 4 * count]
     table[: 5 * count] = product(fine_down, w_src[...]).astype(BF16)
     table[5 * count :] = product(closer, w_dst[...]).astype(BF16)
+    coarse_out[:half] = jnp.where(core == 0, mine[...], theirs[...])
+    rest = coarse_out.shape[0] - half
+    coarse_out[half:] = jnp.where(core == 0, theirs[:rest], mine[:rest])
     rows = lax.broadcasted_iota(I32, (fine.shape[0], LANES), 0)
     for k in range(edges.shape[0] // CHUNK):
         here = slice(k * CHUNK, (k + 1) * CHUNK)
@@ -340,12 +354,16 @@
             sums[...] = part
         else:
             sums[...] += part
-    coarse_out[...] = coarse[: coarse_out.shape[0], :]
+    sent_coarse.start()
     reach = fine_down[count : 5 * count]
     lifted = (fine[...].astype(F32) + product(own_pick[...], reach)).astype(BF16)
-    aggregate = product(sums[...].astype(BF16), edge_w2[...]).astype(BF16)
-    hidden = silu(product(lifted, w_node[...]) + product(aggregate, node_w2[...]))
-    fine_out[...] = updated(lifted, hidden, node_w3[...])
+    hidden = silu(product(lifted, w_node[...]) + product(sums[...].astype(BF16), last[...])).astype(BF16)
+    third = node_w3[...]
+    rows = fine_out.shape[0] // 2
+    for i in range(2):
+        here = slice(i * rows, (i + 1) * rows)
+        fine_out[here, :] = updated(lifted[here], hidden[here], third)
+        sent_fine.start(i)
 
 
 def swapped(values):
@@ -449,7 +467,7 @@
         [far(edge_count, width), far(LANES, wide), far(2 * mids + LANES, wide), free(8, LANES)],
         [],
         stored=[parent, halo, source, target, fine_latent, edge_w_src, edge_w_dst, pair],
-        streams=[0],
+        streams=[(0, edge_count // PIECE)],
         after=[blocks],
         limit=24,
         flops=4_000_000_000,
@@ -463,12 +481,12 @@
     halo_swap, cross, _ = lax.optimization_barrier((halo_swap, cross, own_parts))
     cross_in = crossed(cross, tiles)
     halo_in = swapped(halo_swap)
-    w_coarse, coarse_w2, coarse_w3, own_latent, own_hidden = kernel_call(
+    coarse_w3, both, last, own_latent, own_hidden = kernel_call(
         coarse_ready_body,
-        [square, square, square, near(BLOCK, width), near(BLOCK, width, dtype=F32)],
+        [square, square, far(width, width), near(BLOCK, width), near(BLOCK, width, dtype=F32)],
         [],
-        stored=[coarse_latent, coarse_w1, w_coarse, coarse_w2, coarse_w3],
-        keep=[(2, 0), (3, 1), (4, 2)],
+        stored=[coarse_latent, coarse_w1, w_coarse, coarse_w2, edge_w2, node_w2, coarse_w3],
+        keep=[(6, 0)],
         after=[own_parts],
         flops=4_000_000_000,
         name="coarse_ready",
@@ -479,7 +497,7 @@
     (results,) = kernel_call(
         coarse_body,
         [near(chips, BLOCK, width)],
-        [in_planes] + [here(a) for a in (own_latent, own_hidden, w_coarse, coarse_w2, coarse_w3)],
+        [in_planes] + [here(a) for a in (own_latent, own_hidden, both, coarse_w3)],
         after=[cross_in, halo_in],
         name="coarse_update",
     )
@@ -493,7 +511,7 @@
         stored=[parent, source, target, cross_in, halo_in, edge_w_src, pair, own_edges, w_descend, w_fine, edge_w_dst],
         keep=[(5, 0), (8, 1), (9, 2), (10, 3)],
         pieces=[7],
-        streams=[4, 5],
+        streams=[(4, edge_count // CHUNK), (5, edge_count // CHUNK)],
         after=[results],
         scratch=[
             pltpu.VMEM((2 * LANES, width), BF16),
@@ -509,15 +527,12 @@
 
     fine_out, mid_out, coarse_out = kernel_call(
         final_body,
-        [free(count, width), free(mids, width), free(coarse_count, width)],
+        [far(count, width), far(mids, width), far(coarse_count, width)],
         [mine, theirs] + [here(a) for a in (w_src, w_descend, w_fine, w_dst, middle, picked)],
-        stored=[target, select, edges, own_pick, fine_latent, node_w1, edge_w2, node_w2, node_w3],
+        stored=[target, select, edges, own_pick, fine_latent, node_w1, last, node_w3],
         pieces=[1, 2],
-        scratch=[
-            pltpu.VMEM((2 * half, width), BF16),
-            pltpu.VMEM((8 * mids, width), BF16),
-            pltpu.VMEM((count, width), F32),
-        ],
+        streams=[(0, 2), (1, 1), (2, 1)],
+        scratch=[pltpu.VMEM((8 * mids, width), BF16), pltpu.VMEM((count, width), F32)],
         limit=24,
         name="final",
     )

time: 77.4 us -> 76.6 us (0.990)
  waiting for transfers between devices: 9.08 us -> 7.69 us
    ppermute x2, waiting for transfers between devices: 4.18 us -> 2.58 us  [crossed(): return lax.ppermute(values, TILE, pairs + [(b, a) for a, b in pairs])]
  transfers between devices with their start and end apart: 10 -> 10, of which waited for: 7 -> 7; matrix products, arithmetic and copies ran while one was open for 0% -> 0% of each run, Pallas kernels for 27% -> 29%
where the time goes in v9:
time: 76.6 us; the launch traced here: 76 us
  Pallas kernels  34.1 us (45%)
  starting transfers between devices  33.3 us (43%)
  waiting for transfers between devices  7.69 us (10%)
  between operations  0.96 us (1%)
    pallas_call x10, Pallas kernels, kernel_call(): pl.pallas_call(kernel, out_shape=outs, in_specs=[VMEM] * count + [STORED]...  34.1 us
    all_to_all x1, starting transfers between devices, on_device(): in_planes = lax.all_to_all(own_parts, 'z', 0, 0)  8.19 us
    all_to_all x1, starting transfers between devices, on_device(): parts = lax.all_to_all(blocks, PLANE, 0, 0)  6.86 us
    ppermute x5, starting transfers between devices, swapped(): return lax.ppermute(values, 'c', [(0, 1), (1, 0)])  6.59 us
    ppermute x2, starting transfers between devices, crossed(): return lax.ppermute(values, TILE, pairs + [(b, a) for a, b in pairs])  5.83 us
    all_to_all x1, starting transfers between devices, on_device(): mine = lax.all_to_all(results, PLANE, 0, 0).reshape(half, width)  5.79 us
    ppermute x2, waiting for transfers between devices, crossed(): return lax.ppermute(values, TILE, pairs + [(b, a) for a, b in pairs])  2.58 us
    ppermute x5, waiting for transfers between devices, swapped(): return lax.ppermute(values, 'c', [(0, 1), (1, 0)])  2.56 us
  transfers between devices with their start and end apart: 10, of which 7 were waited for; matrix products, arithmetic and copies ran while one was open for 0% of the time, Pallas kernels for 29%

profile of v9, /device:TPU:1, one launch (start us, length us, event | category | flops | bytes accessed | tf_op | source)
XLA Modules:
  0.0 76.0 jit_solution(4338304040737899199)
XLA Ops:
  0.6 1.3 %child_sums.1 = (f32[32,512]{1,0:T(8,128)S(1)}, bf16[32,512]{1,0:T(8,128)(2,1)S(1)}, bf16[32,512]{1,0:T(8,128)(2,1)S(1)}) custom-call(s32[4,128]{1,0:T(4,128)} %bitcast.12, bf16[512,512]{1,0:T(8,128)(2,1)} %refs_12_.1), custom_call_target="tpu_custom_call" | custom-call | bytes 1048576 | tf_op jit(solution)/shard_map/child_sums/pallas_call | solution.py:89
  1.9 3.3 %collective-permute-start = (bf16[32,512]{1,0:T(8,128)(2,1)S(1)}, bf16[32,512]{1,0:T(8,128)(2,1)S(1)}, u32[]{:S(2)}, u32[]{:S(2)}) collective-permute-start(bf16[32,512]{1,0:T(8,128)(2,1)S(1)} %get-tuple-element.39), channel_id=1, source_target_pairs={{0,1},{1,0},{2,3},{3,2},{4,5},{5,4},{6,7},{7,6},{8,9},{9,8},{10,11... | collective-permute-start | bytes 98312 | tf_op jit(solution)/shard_map/ppermute | solution.py:370
  5.3 1.9 %collective-permute-start.1 = (bf16[32,512]{1,0:T(8,128)(2,1)S(1)}, bf16[32,512]{1,0:T(8,128)(2,1)S(1)}, u32[]{:S(2)}, u32[]{:S(2)}) collective-permute-start(bf16[32,512]{1,0:T(8,128)(2,1)S(1)} %get-tuple-element.40), channel_id=1, source_target_pairs={{1,2},{3,4},{5,6},{7,8},{9,10},{11,12},{13,14},{15,16},{17,18},{19... | collective-permute-start | bytes 98312 | tf_op jit(solution)/shard_map/ppermute | solution.py:375
  7.2 1.6 %mid_ready.1 = (bf16[512,512]{1,0:T(8,128)(2,1)S(1)}, bf16[512,512]{1,0:T(8,128)(2,1)S(1)}, bf16[512,512]{1,0:T(8,128)(2,1)S(1)}, bf16[32,512]{1,0:T(8,128)(2,1)...) custom-call(bf16[32,512]{1,0:T(8,128)(2,1)} %refs_0_.2, s32[1,32]{1,0:T(1,128)} %bitcast.18, ...), custom_call_target="tpu_custom_call" | custom-call | flops 1000000000 | bytes 1048576 | tf_op jit(solution)/shard_map/mid_ready/pallas_call | solution.py:89
  8.8 0.0 collective-permute-done.refs_1_
  8.8 1.7 %collective-permute-done.1.refs_2_ = bf16[32,512]{1,0:T(8,128)(2,1)S(1)} collective-permute-done((bf16[32,512]{1,0:T(8,128)(2,1)S(1)}, bf16[32,512]{1,0:T(8,128)(2,1)S(1)}, u32[]{:S(2)}, u32[]{:S(2)}) %collective-permute-start.1) | collective-permute-done | bytes 32800 | tf_op jit(solution)/shard_map/ppermute | solution.py:375
  10.5 0.6 mid_update.1.refs_0_
  11.1 0.1 collective-permute-start.2
  11.2 1.2 %collective-permute-done.2.refs_1_ = bf16[32,640]{1,0:T(8,128)(2,1)S(1)} collective-permute-done((bf16[32,640]{1,0:T(8,128)(2,1)S(1)}, bf16[32,640]{1,0:T(8,128)(2,1)S(1)}, u32[]{:S(2)}, u32[]{:S(2)}) %collective-permute-start.2) | collective-permute-done | bytes 40992 | tf_op jit(solution)/shard_map/ppermute | solution.py:370
  12.4 1.2 %coarse_blocks.1 = (bf16[64,640]{1,0:T(8,128)(2,1)}, bf16[384,512]{1,0:T(8,128)(2,1)}) custom-call(bf16[32,640]{1,0:T(8,128)(2,1)S(1)} %mid_update.1.refs_0_, bf16[32,640]{1,0:T(8,128)(2,1)S(1)} %collective-permute-done.2.refs_1_), custom_call_target="tpu_custom_call" | custom-call | bytes 1048576 | tf_op jit(solution)/shard_map/coarse_blocks/pallas_call | solution.py:89
  13.6 6.9 %all-to-all-start = ((bf16[16,24,512]{2,1,0:T(8,128)(2,1)}), bf16[16,24,512]{2,1,0:T(8,128)(2,1)S(1)}, u32[]{:S(2)}, u32[]{:S(2)}) async-start(bf16[16,24,512]{2,1,0:T(8,128)(2,1)} %bitcast.2.refs_8_), calls=%async_computation | async-start | bytes 786432 | tf_op jit(solution)/shard_map/all_to_all | solution.py:464
  20.5 7.6 %own_edges.1 = (bf16[3072,512]{1,0:T(8,128)(2,1)}, bf16[128,640]{1,0:T(8,128)(2,1)}, bf16[192,640]{1,0:T(8,128)(2,1)}, bf16[8,128]{1,0:T(8,128)(2,1)S(1)}) custom-call(s32[4,128]{1,0:T(4,128)} %bitcast.13, s32[2,128]{1,0:T(2,128)} %bitcast.17, s32[24,128]{1,0:T(8,128)} %bitcast.15, s32[24,128]{1,0:T(8,128)} %bitcast.9, bf16[512,512]{1,0:T(8,128)(2,1)} %refs_12_.1, ...), custom_call_target="tpu_custom_call" | custom-call | flops 4000000000 | bytes 1048576 | tf_op jit(solution)/shard_map/own_edges/pallas_call | solution.py:89
  28.1 1.8 %all-to-all-done.refs_0_ = bf16[16,24,512]{2,1,0:T(8,128)(2,1)S(1)} async-done(((bf16[16,24,512]{2,1,0:T(8,128)(2,1)}), bf16[16,24,512]{2,1,0:T(8,128)(2,1)S(1)}, u32[]{:S(2)}, u32[]{:S(2)}) %all-to-all-start) | async-done | bytes 393248 | tf_op jit(solution)/shard_map/all_to_all | solution.py:464
  29.9 0.7 plane_sum.1.refs_7_
  30.7 8.2 %all-to-all-start.1 = ((bf16[8,24,512]{2,1,0:T(8,128)(2,1)}), bf16[8,24,512]{2,1,0:T(8,128)(2,1)S(1)}, u32[]{:S(2)}, u32[]{:S(2)}) async-start(bf16[8,24,512]{2,1,0:T(8,128)(2,1)} %plane_sum.1.refs_7_), calls=%async_computation.1 | async-start | bytes 393216 | tf_op jit(solution)/shard_map/all_to_all | solution.py:480
  38.9 3.9 %collective-permute-start.3 = (bf16[192,640]{1,0:T(8,128)(2,1)}, bf16[192,640]{1,0:T(8,128)(2,1)S(1)}, u32[]{:S(2)}, u32[]{:S(2)}) collective-permute-start(bf16[192,640]{1,0:T(8,128)(2,1)} %get-tuple-element.52), channel_id=1, source_target_pairs={{1,2},{3,4},{5,6},{7,8},{9,10},{11,12},{13,14},{15,16},{17,18},{19... | collective-permute-start | bytes 737288 | tf_op jit(solution)/shard_map/ppermute | solution.py:375
  42.8 0.1 collective-permute-start.4
  42.9 3.4 %coarse_ready.1 = (bf16[512,512]{1,0:T(8,128)(2,1)S(1)}, bf16[512,512]{1,0:T(8,128)(2,1)S(1)}, bf16[512,512]{1,0:T(8,128)(2,1)}, bf16[24,512]{1,0:T(8,128)(2,1)S(1)}, f32[24,512]{1,0:T(8,128)S(1)}) custom-call(bf16[642,512]{1,0:T(8,128)(2,1)} %refs_0_.3, bf16[512,512]{1,0:T(8,128)(2,1)} %refs_1_.3, bf16[512,512]{1,0:T(8,128)(2,1)} %refs_2_.3, ...), custom_call_target="tpu_custom_call" | custom-call | flops 4000000000 | bytes 1048576 | tf_op jit(solution)/shard_map/coarse_ready/pallas_call | solution.py:89
  46.3 0.9 %collective-permute-done.3.refs_5_.refs_4_ = bf16[192,640]{1,0:T(8,128)(2,1)S(1)} collective-permute-done((bf16[192,640]{1,0:T(8,128)(2,1)}, bf16[192,640]{1,0:T(8,128)(2,1)S(1)}, u32[]{:S(2)}, u32[]{:S(2)}) %collective-permute-start.3) | collective-permute-done | bytes 245792 | tf_op jit(solution)/shard_map/ppermute | solution.py:375
  47.2 0.1 collective-permute-start.5
  47.3 0.0 collective-permute-done.4.refs_6_.refs_5_
  47.3 0.0 copy-start.1
  47.3 0.3 all-to-all-done.1.refs_0_
  47.6 1.2 %coarse_update.1.refs_12_ = bf16[16,24,512]{2,1,0:T(8,128)(2,1)} custom-call(bf16[8,24,512]{2,1,0:T(8,128)(2,1)S(1)} %all-to-all-done.1.refs_0_, bf16[24,512]{1,0:T(8,128)(2,1)S(1)} %get-tuple-element.54.refs_1_, f32[24,512]{1,0:T(8,128)S(1)} %get-tuple-element.55.refs_2_, bf16[512,512]{1,0:T(8,128)(2,1)S(1)} %get-tuple-element.56.refs_3_, ...), custom_call_target="tpu_custom_call" | custom-call | bytes 1048576 | tf_op jit(solution)/shard_map/coarse_update/pallas_call | solution.py:89
  48.8 5.8 %all-to-all-start.2 = ((bf16[16,24,512]{2,1,0:T(8,128)(2,1)}), bf16[16,24,512]{2,1,0:T(8,128)(2,1)S(1)}, u32[]{:S(2)}, u32[]{:S(2)}) async-start(bf16[16,24,512]{2,1,0:T(8,128)(2,1)} %coarse_update.1.refs_12_), calls=%async_computation.2 | async-start | bytes 786432 | tf_op jit(solution)/shard_map/all_to_all | solution.py:504
  54.6 0.0 collective-permute-done.5.refs_0_
  54.6 0.0 copy-done
  54.7 8.0 %rest_edges.1 = (bf16[512,512]{1,0:T(8,128)(2,1)S(1)}, bf16[512,512]{1,0:T(8,128)(2,1)S(1)}, bf16[512,512]{1,0:T(8,128)(2,1)S(1)}, bf16[512,512]{1,0:T(8,128)(2,...) custom-call(bf16[32,640]{1,0:T(8,128)(2,1)S(1)} %collective-permute-, ...), custom_call_target="tpu_custom_call" | custom-call | flops 4000000000 | bytes 1048576 | tf_op jit(solution)/shard_map/rest_edges/pallas_call | solution.py:89
  62.6 0.4 all-to-all-done.2
  63.1 3.0 %collective-permute-start.6 = (bf16[384,512]{1,0:T(8,128)(2,1)S(1)}, bf16[384,512]{1,0:T(8,128)(2,1)S(1)}, u32[]{:S(2)}, u32[]{:S(2)}) collective-permute-start(bf16[384,512]{1,0:T(8,128)(2,1)S(1)} %bitcast.7), channel_id=1, source_target_pairs={{0,1},{1,0},{2,3},{3,2},{4,5},{5,4},{6,7},{7,6},{8,9},{9,8},{10,11... | collective-permute-start | bytes 1179656 | tf_op jit(solution)/shard_map/ppermute | solution.py:370
  66.0 1.3 %collective-permute-done.6.refs_1_ = bf16[384,512]{1,0:T(8,128)(2,1)S(1)} collective-permute-done((bf16[384,512]{1,0:T(8,128)(2,1)S(1)}, bf16[384,512]{1,0:T(8,128)(2,1)S(1)}, u32[]{:S(2)}, u32[]{:S(2)}) %collective-permute-start.6) | collective-permute-done | bytes 393248 | tf_op jit(solution)/shard_map/ppermute | solution.py:370
  67.4 8.5 %final.1 = (bf16[512,512]{1,0:T(8,128)(2,1)}, bf16[32,512]{1,0:T(8,128)(2,1)}, bf16[642,512]{1,0:T(8,128)(2,1)}) custom-call(bf16[384,512]{1,0:T(8,128)(2,1)S(1)} %bitcast.8, bf16[384,512]{1,0:T(8,128)(2,1)S(1)} %collective-permute-done.6.refs_1_, bf16[512,512]{1,0:T(8,128)(2,1)S(1)} %get-tuple-element.63.refs_2_, ...), custom_call_target="tpu_custom_call" | custom-call | bytes 1048576 | tf_op jit(solution)/shard_map/final/pallas_call | solution.py:89
  (3 shorter events, 0.0 us)
Async XLA Ops:
  1.9 6.9 %collective-permute-start = (bf16[32,512]{1,0:T(8,128)(2,1)S(1)}, bf16[32,512]{1,0:T(8,128)(2,1)S(1)}, u32[]{:S(2)}, u32[]{:S(2)}) collective-permute-start(bf16[32,512]{1,0:T(8,128)(2,1)S(1)} %get-tuple-element.39), channel_id=1, source_target_pairs={{0,1},{1,0},{2,3},{3,2},{4,5},{5,4},{6,7},{7,6},{8,9},{9,8},{10,11... | collective-permute-start | bytes 98312 | tf_op jit(solution)/shard_map/ppermute | solution.py:370
  5.3 5.2 %collective-permute-start.1 = (bf16[32,512]{1,0:T(8,128)(2,1)S(1)}, bf16[32,512]{1,0:T(8,128)(2,1)S(1)}, u32[]{:S(2)}, u32[]{:S(2)}) collective-permute-start(bf16[32,512]{1,0:T(8,128)(2,1)S(1)} %get-tuple-element.40), channel_id=1, source_target_pairs={{1,2},{3,4},{5,6},{7,8},{9,10},{11,12},{13,14},{15,16},{17,18},{19... | collective-permute-start | bytes 98312 | tf_op jit(solution)/shard_map/ppermute | solution.py:375
  11.1 1.3 %collective-permute-start.2 = (bf16[32,640]{1,0:T(8,128)(2,1)S(1)}, bf16[32,640]{1,0:T(8,128)(2,1)S(1)}, u32[]{:S(2)}, u32[]{:S(2)}) collective-permute-start(bf16[32,640]{1,0:T(8,128)(2,1)S(1)} %mid_update.1.refs_0_), channel_id=1, source_target_pairs={{0,1},{1,0},{2,3},{3,2},{4,5},{5,4},{6,7},{7,6},{8,9},{9,8},{10,11... | collective-permute-start | bytes 122888 | tf_op jit(solution)/shard_map/ppermute | solution.py:370
  13.6 16.3 %all-to-all-start = ((bf16[16,24,512]{2,1,0:T(8,128)(2,1)}), bf16[16,24,512]{2,1,0:T(8,128)(2,1)S(1)}, u32[]{:S(2)}, u32[]{:S(2)}) async-start(bf16[16,24,512]{2,1,0:T(8,128)(2,1)} %bitcast.2.refs_8_), calls=%async_computation | async-start | bytes 786432 | tf_op jit(solution)/shard_map/all_to_all | solution.py:464
  30.7 16.9 %all-to-all-start.1 = ((bf16[8,24,512]{2,1,0:T(8,128)(2,1)}), bf16[8,24,512]{2,1,0:T(8,128)(2,1)S(1)}, u32[]{:S(2)}, u32[]{:S(2)}) async-start(bf16[8,24,512]{2,1,0:T(8,128)(2,1)} %plane_sum.1.refs_7_), calls=%async_computation.1 | async-start | bytes 393216 | tf_op jit(solution)/shard_map/all_to_all | solution.py:480
  38.9 8.3 %collective-permute-start.3 = (bf16[192,640]{1,0:T(8,128)(2,1)}, bf16[192,640]{1,0:T(8,128)(2,1)S(1)}, u32[]{:S(2)}, u32[]{:S(2)}) collective-permute-start(bf16[192,640]{1,0:T(8,128)(2,1)} %get-tuple-element.52), channel_id=1, source_target_pairs={{1,2},{3,4},{5,6},{7,8},{9,10},{11,12},{13,14},{15,16},{17,18},{19... | collective-permute-start | bytes 737288 | tf_op jit(solution)/shard_map/ppermute | solution.py:375
  42.8 4.5 %collective-permute-start.4 = (bf16[128,640]{1,0:T(8,128)(2,1)}, bf16[128,640]{1,0:T(8,128)(2,1)S(1)}, u32[]{:S(2)}, u32[]{:S(2)}) collective-permute-start(bf16[128,640]{1,0:T(8,128)(2,1)} %get-tuple-element.58), channel_id=1, source_target_pairs={{0,1},{1,0},{2,3},{3,2},{4,5},{5,4},{6,7},{7,6},{8,9},{9,8},{10,11... | collective-permute-start | bytes 491528 | tf_op jit(solution)/shard_map/ppermute | solution.py:370
  47.2 7.5 %copy-start = (bf16[192,640]{1,0:T(8,128)(2,1)}, bf16[192,640]{1,0:T(8,128)(2,1)S(1)}, u32[]{:S(2)}) copy-start(bf16[192,640]{1,0:T(8,128)(2,1)S(1)} %collective-permute-done.3.refs_5_.refs_4_) | copy-start | bytes 737284
  47.2 7.4 %collective-permute-start.5 = (bf16[32,640]{1,0:T(8,128)(2,1)S(1)}, bf16[32,640]{1,0:T(8,128)(2,1)S(1)}, u32[]{:S(2)}, u32[]{:S(2)}) collective-permute-start(bf16[32,640]{1,0:T(8,128)(2,1)S(1)} %slice_select_fusion), channel_id=1, source_target_pairs={{0,1},{1,0},{2,3},{3,2},{4,5},{5,4},{6,7},{7,6},{8,9},{9,8},{10,11... | collective-permute-start | bytes 122888 | tf_op jit(solution)/shard_map/ppermute | solution.py:370
  47.3 7.3 %copy-start.1 = (bf16[128,640]{1,0:T(8,128)(2,1)}, bf16[128,640]{1,0:T(8,128)(2,1)S(1)}, u32[]{:S(2)}) copy-start(bf16[128,640]{1,0:T(8,128)(2,1)S(1)} %collective-permute-done.4.refs_6_.refs_5_) | copy-start | bytes 491524
  48.8 14.2 %all-to-all-start.2 = ((bf16[16,24,512]{2,1,0:T(8,128)(2,1)}), bf16[16,24,512]{2,1,0:T(8,128)(2,1)S(1)}, u32[]{:S(2)}, u32[]{:S(2)}) async-start(bf16[16,24,512]{2,1,0:T(8,128)(2,1)} %coarse_update.1.refs_12_), calls=%async_computation.2 | async-start | bytes 786432 | tf_op jit(solution)/shard_map/all_to_all | solution.py:504
  63.1 4.3 %collective-permute-start.6 = (bf16[384,512]{1,0:T(8,128)(2,1)S(1)}, bf16[384,512]{1,0:T(8,128)(2,1)S(1)}, u32[]{:S(2)}, u32[]{:S(2)}) collective-permute-start(bf16[384,512]{1,0:T(8,128)(2,1)S(1)} %bitcast.7), channel_id=1, source_target_pairs={{0,1},{1,0},{2,3},{3,2},{4,5},{5,4},{6,7},{7,6},{8,9},{9,8},{10,11... | collective-permute-start | bytes 1179656 | tf_op jit(solution)/shard_map/ppermute | solution.py:370

commit v10 on v9

--- a/solution.py
+++ b/solution.py
@@ -478,7 +478,6 @@
         gather_body, [near(planes, BLOCK, width)], [parts], after=[token], name="plane_sum"
     )
     in_planes = lax.all_to_all(own_parts, "z", 0, 0)
-    halo_swap, cross, _ = lax.optimization_barrier((halo_swap, cross, own_parts))
     cross_in = crossed(cross, tiles)
     halo_in = swapped(halo_swap)
     coarse_w3, both, last, own_latent, own_hidden = kernel_call(

time: 76.6 us -> 80.1 us (1.046)
  waiting for transfers between devices: 7.69 us -> 9.68 us
  starting transfers between devices: 33.3 us -> 34.8 us
    all_to_all x1, waiting for transfers between devices: 0.3 us -> 4.98 us  [on_device(): in_planes = lax.all_to_all(own_parts, 'z', 0, 0)]
    all_to_all x1, waiting for transfers between devices: 1.83 us -> 0.01 us  [on_device(): parts = lax.all_to_all(blocks, PLANE, 0, 0)]
    ppermute x2, waiting for transfers between devices: 2.58 us -> 1.68 us  [crossed(): return lax.ppermute(values, TILE, pairs + [(b, a) for a, b in pairs])]
    all_to_all x1, starting transfers between devices: 5.79 us -> 6.59 us  [on_device(): mine = lax.all_to_all(results, PLANE, 0, 0).reshape(half, width)]
  transfers between devices with their start and end apart: 10 -> 10, of which waited for: 7 -> 5; matrix products, arithmetic and copies ran while one was open for 0% -> 0% of each run, Pallas kernels for 29% -> 28%
where the time goes in v10:
time: 80.1 us; the launch traced here: 79.6 us
  starting transfers between devices  34.8 us (43%)
  Pallas kernels  34.1 us (43%)
  waiting for transfers between devices  9.68 us (12%)
  between operations  0.96 us (1%)
    pallas_call x10, Pallas kernels, kernel_call(): pl.pallas_call(kernel, out_shape=outs, in_specs=[VMEM] * count + [STORED]...  34.1 us
    all_to_all x1, starting transfers between devices, on_device(): in_planes = lax.all_to_all(own_parts, 'z', 0, 0)  8.19 us
    ppermute x5, starting transfers between devices, swapped(): return lax.ppermute(values, 'c', [(0, 1), (1, 0)])  7.35 us
    all_to_all x1, starting transfers between devices, on_device(): parts = lax.all_to_all(blocks, PLANE, 0, 0)  6.86 us
    all_to_all x1, starting transfers between devices, on_device(): mine = lax.all_to_all(results, PLANE, 0, 0).reshape(half, width)  6.59 us
    ppermute x2, starting transfers between devices, crossed(): return lax.ppermute(values, TILE, pairs + [(b, a) for a, b in pairs])  5.78 us
    all_to_all x1, waiting for transfers between devices, on_device(): in_planes = lax.all_to_all(own_parts, 'z', 0, 0)  4.98 us
    ppermute x5, waiting for transfers between devices, swapped(): return lax.ppermute(values, 'c', [(0, 1), (1, 0)])  2.56 us
  transfers between devices with their start and end apart: 10, of which 5 were waited for; matrix products, arithmetic and copies ran while one was open for 0% of the time, Pallas kernels for 28%

profile of v10, /device:TPU:1, one launch (start us, length us, event | category | flops | bytes accessed | tf_op | source)
XLA Modules:
  0.0 79.6 jit_solution(3862808432169817180)
XLA Ops:
  0.6 1.3 %child_sums.1 = (f32[32,512]{1,0:T(8,128)S(1)}, bf16[32,512]{1,0:T(8,128)(2,1)S(1)}, bf16[32,512]{1,0:T(8,128)(2,1)S(1)}) custom-call(s32[4,128]{1,0:T(4,128)} %bitcast.12, bf16[512,512]{1,0:T(8,128)(2,1)} %refs_12_.1), custom_call_target="tpu_custom_call" | custom-call | bytes 1048576 | tf_op jit(solution)/shard_map/child_sums/pallas_call | solution.py:89
  1.9 3.3 %collective-permute-start = (bf16[32,512]{1,0:T(8,128)(2,1)S(1)}, bf16[32,512]{1,0:T(8,128)(2,1)S(1)}, u32[]{:S(2)}, u32[]{:S(2)}) collective-permute-start(bf16[32,512]{1,0:T(8,128)(2,1)S(1)} %get-tuple-element.37), channel_id=1, source_target_pairs={{0,1},{1,0},{2,3},{3,2},{4,5},{5,4},{6,7},{7,6},{8,9},{9,8},{10,11... | collective-permute-start | bytes 98312 | tf_op jit(solution)/shard_map/ppermute | solution.py:370
  5.3 1.9 %collective-permute-start.1 = (bf16[32,512]{1,0:T(8,128)(2,1)S(1)}, bf16[32,512]{1,0:T(8,128)(2,1)S(1)}, u32[]{:S(2)}, u32[]{:S(2)}) collective-permute-start(bf16[32,512]{1,0:T(8,128)(2,1)S(1)} %get-tuple-element.38), channel_id=1, source_target_pairs={{1,2},{3,4},{5,6},{7,8},{9,10},{11,12},{13,14},{15,16},{17,18},{19... | collective-permute-start | bytes 98312 | tf_op jit(solution)/shard_map/ppermute | solution.py:375
  7.2 1.6 %mid_ready.1 = (bf16[512,512]{1,0:T(8,128)(2,1)S(1)}, bf16[512,512]{1,0:T(8,128)(2,1)S(1)}, bf16[512,512]{1,0:T(8,128)(2,1)S(1)}, bf16[32,512]{1,0:T(8,128)(2,1)...) custom-call(bf16[32,512]{1,0:T(8,128)(2,1)} %refs_0_.2, s32[1,32]{1,0:T(1,128)} %bitcast.18, ...), custom_call_target="tpu_custom_call" | custom-call | flops 1000000000 | bytes 1048576 | tf_op jit(solution)/shard_map/mid_ready/pallas_call | solution.py:89
  8.8 0.0 collective-permute-done.refs_1_
  8.8 1.7 %collective-permute-done.1.refs_2_ = bf16[32,512]{1,0:T(8,128)(2,1)S(1)} collective-permute-done((bf16[32,512]{1,0:T(8,128)(2,1)S(1)}, bf16[32,512]{1,0:T(8,128)(2,1)S(1)}, u32[]{:S(2)}, u32[]{:S(2)}) %collective-permute-start.1) | collective-permute-done | bytes 32800 | tf_op jit(solution)/shard_map/ppermute | solution.py:375
  10.5 0.6 mid_update.1.refs_0_
  11.1 0.1 collective-permute-start.2
  11.2 1.2 %collective-permute-done.2.refs_1_ = bf16[32,640]{1,0:T(8,128)(2,1)S(1)} collective-permute-done((bf16[32,640]{1,0:T(8,128)(2,1)S(1)}, bf16[32,640]{1,0:T(8,128)(2,1)S(1)}, u32[]{:S(2)}, u32[]{:S(2)}) %collective-permute-start.2) | collective-permute-done | bytes 40992 | tf_op jit(solution)/shard_map/ppermute | solution.py:370
  12.4 1.2 %coarse_blocks.1 = (bf16[64,640]{1,0:T(8,128)(2,1)}, bf16[384,512]{1,0:T(8,128)(2,1)}) custom-call(bf16[32,640]{1,0:T(8,128)(2,1)S(1)} %mid_update.1.refs_0_, bf16[32,640]{1,0:T(8,128)(2,1)S(1)} %collective-permute-done.2.refs_1_), custom_call_target="tpu_custom_call" | custom-call | bytes 1048576 | tf_op jit(solution)/shard_map/coarse_blocks/pallas_call | solution.py:89
  13.6 6.9 %all-to-all-start = ((bf16[16,24,512]{2,1,0:T(8,128)(2,1)}), bf16[16,24,512]{2,1,0:T(8,128)(2,1)S(1)}, u32[]{:S(2)}, u32[]{:S(2)}) async-start(bf16[16,24,512]{2,1,0:T(8,128)(2,1)} %bitcast.2.refs_8_), calls=%async_computation | async-start | bytes 786432 | tf_op jit(solution)/shard_map/all_to_all | solution.py:464
  20.5 7.6 %own_edges.1 = (bf16[3072,512]{1,0:T(8,128)(2,1)}, bf16[128,640]{1,0:T(8,128)(2,1)}, bf16[192,640]{1,0:T(8,128)(2,1)}, bf16[8,128]{1,0:T(8,128)(2,1)S(1)}) custom-call(s32[4,128]{1,0:T(4,128)} %bitcast.13, s32[2,128]{1,0:T(2,128)} %bitcast.17, s32[24,128]{1,0:T(8,128)} %bitcast.15, s32[24,128]{1,0:T(8,128)} %bitcast.9, bf16[512,512]{1,0:T(8,128)(2,1)} %refs_12_.1, ...), custom_call_target="tpu_custom_call" | custom-call | flops 4000000000 | bytes 1048576 | tf_op jit(solution)/shard_map/own_edges/pallas_call | solution.py:89
  28.1 3.9 %collective-permute-start.3 = (bf16[192,640]{1,0:T(8,128)(2,1)}, bf16[192,640]{1,0:T(8,128)(2,1)S(1)}, u32[]{:S(2)}, u32[]{:S(2)}) collective-permute-start(bf16[192,640]{1,0:T(8,128)(2,1)} %get-tuple-element.48), channel_id=1, source_target_pairs={{1,2},{3,4},{5,6},{7,8},{9,10},{11,12},{13,14},{15,16},{17,18},{19... | collective-permute-start | bytes 737288 | tf_op jit(solution)/shard_map/ppermute | solution.py:375
  32.0 0.1 collective-permute-start.4
  32.1 0.0 all-to-all-done.refs_0_
  32.1 0.7 plane_sum.1.refs_7_
  32.8 8.2 %all-to-all-start.1 = ((bf16[8,24,512]{2,1,0:T(8,128)(2,1)}), bf16[8,24,512]{2,1,0:T(8,128)(2,1)S(1)}, u32[]{:S(2)}, u32[]{:S(2)}) async-start(bf16[8,24,512]{2,1,0:T(8,128)(2,1)} %plane_sum.1.refs_7_), calls=%async_computation.1 | async-start | bytes 393216 | tf_op jit(solution)/shard_map/all_to_all | solution.py:480
  41.0 3.4 %coarse_ready.1 = (bf16[512,512]{1,0:T(8,128)(2,1)S(1)}, bf16[512,512]{1,0:T(8,128)(2,1)S(1)}, bf16[512,512]{1,0:T(8,128)(2,1)}, bf16[24,512]{1,0:T(8,128)(2,1)S(1)}, f32[24,512]{1,0:T(8,128)S(1)}) custom-call(bf16[642,512]{1,0:T(8,128)(2,1)} %refs_0_.3, bf16[512,512]{1,0:T(8,128)(2,1)} %refs_1_.3, bf16[512,512]{1,0:T(8,128)(2,1)} %refs_2_.3, ...), custom_call_target="tpu_custom_call" | custom-call | flops 4000000000 | bytes 1048576 | tf_op jit(solution)/shard_map/coarse_ready/pallas_call | solution.py:89
  44.4 0.0 collective-permute-done.3.refs_5_.refs_4_
  44.4 0.0 copy-start
  44.4 0.9 %collective-permute-start.5 = (bf16[32,640]{1,0:T(8,128)(2,1)S(1)}, bf16[32,640]{1,0:T(8,128)(2,1)S(1)}, u32[]{:S(2)}, u32[]{:S(2)}) collective-permute-start(bf16[32,640]{1,0:T(8,128)(2,1)S(1)} %slice_select_fusion), channel_id=1, source_target_pairs={{0,1},{1,0},{2,3},{3,2},{4,5},{5,4},{6,7},{7,6},{8,9},{9,8},{10,11... | collective-permute-start | bytes 122888 | tf_op jit(solution)/shard_map/ppermute | solution.py:370
  45.3 0.0 collective-permute-done.4.refs_6_.refs_5_
  45.3 5.0 %all-to-all-done.1.refs_0_ = bf16[8,24,512]{2,1,0:T(8,128)(2,1)S(1)} async-done(((bf16[8,24,512]{2,1,0:T(8,128)(2,1)}), bf16[8,24,512]{2,1,0:T(8,128)(2,1)S(1)}, u32[]{:S(2)}, u32[]{:S(2)}) %all-to-all-start.1) | async-done | bytes 196640 | tf_op jit(solution)/shard_map/all_to_all | solution.py:480
  50.3 1.2 %coarse_update.1.refs_12_ = bf16[16,24,512]{2,1,0:T(8,128)(2,1)} custom-call(bf16[8,24,512]{2,1,0:T(8,128)(2,1)S(1)} %all-to-all-done.1.refs_0_, bf16[24,512]{1,0:T(8,128)(2,1)S(1)} %get-tuple-element.50.refs_1_, f32[24,512]{1,0:T(8,128)S(1)} %get-tuple-element.51.refs_2_, bf16[512,512]{1,0:T(8,128)(2,1)S(1)} %get-tuple-element.52.refs_3_, ...), custom_call_target="tpu_custom_call" | custom-call | bytes 1048576 | tf_op jit(solution)/shard_map/coarse_update/pallas_call | solution.py:89
  51.5 6.6 %all-to-all-start.2 = ((bf16[16,24,512]{2,1,0:T(8,128)(2,1)}), bf16[16,24,512]{2,1,0:T(8,128)(2,1)S(1)}, u32[]{:S(2)}, u32[]{:S(2)}) async-start(bf16[16,24,512]{2,1,0:T(8,128)(2,1)} %coarse_update.1.refs_12_), calls=%async_computation.2 | async-start | bytes 786432 | tf_op jit(solution)/shard_map/all_to_all | solution.py:503
  58.1 0.0 collective-permute-done.5.refs_0_
  58.1 0.0 copy-done
  58.1 8.0 %rest_edges.1 = (bf16[512,512]{1,0:T(8,128)(2,1)S(1)}, bf16[512,512]{1,0:T(8,128)(2,1)S(1)}, bf16[512,512]{1,0:T(8,128)(2,1)S(1)}, bf16[512,512]{1,0:T(8,128)(2,...) custom-call(bf16[32,640]{1,0:T(8,128)(2,1)S(1)} %collective-permute-, ...), custom_call_target="tpu_custom_call" | custom-call | flops 4000000000 | bytes 1048576 | tf_op jit(solution)/shard_map/rest_edges/pallas_call | solution.py:89
  66.1 0.5 all-to-all-done.2
  66.6 3.0 %collective-permute-start.6 = (bf16[384,512]{1,0:T(8,128)(2,1)S(1)}, bf16[384,512]{1,0:T(8,128)(2,1)S(1)}, u32[]{:S(2)}, u32[]{:S(2)}) collective-permute-start(bf16[384,512]{1,0:T(8,128)(2,1)S(1)} %bitcast.7), channel_id=1, source_target_pairs={{0,1},{1,0},{2,3},{3,2},{4,5},{5,4},{6,7},{7,6},{8,9},{9,8},{10,11... | collective-permute-start | bytes 1179656 | tf_op jit(solution)/shard_map/ppermute | solution.py:370
  69.5 1.3 %collective-permute-done.6.refs_1_ = bf16[384,512]{1,0:T(8,128)(2,1)S(1)} collective-permute-done((bf16[384,512]{1,0:T(8,128)(2,1)S(1)}, bf16[384,512]{1,0:T(8,128)(2,1)S(1)}, u32[]{:S(2)}, u32[]{:S(2)}) %collective-permute-start.6) | collective-permute-done | bytes 393248 | tf_op jit(solution)/shard_map/ppermute | solution.py:370
  70.9 8.5 %final.1 = (bf16[512,512]{1,0:T(8,128)(2,1)}, bf16[32,512]{1,0:T(8,128)(2,1)}, bf16[642,512]{1,0:T(8,128)(2,1)}) custom-call(bf16[384,512]{1,0:T(8,128)(2,1)S(1)} %bitcast.8, bf16[384,512]{1,0:T(8,128)(2,1)S(1)} %collective-permute-done.6.refs_1_, bf16[512,512]{1,0:T(8,128)(2,1)S(1)} %get-tuple-element.59.refs_2_, ...), custom_call_target="tpu_custom_call" | custom-call | bytes 1048576 | tf_op jit(solution)/shard_map/final/pallas_call | solution.py:89
  (3 shorter events, 0.0 us)
Async XLA Ops:
  1.9 6.9 %collective-permute-start = (bf16[32,512]{1,0:T(8,128)(2,1)S(1)}, bf16[32,512]{1,0:T(8,128)(2,1)S(1)}, u32[]{:S(2)}, u32[]{:S(2)}) collective-permute-start(bf16[32,512]{1,0:T(8,128)(2,1)S(1)} %get-tuple-element.37), channel_id=1, source_target_pairs={{0,1},{1,0},{2,3},{3,2},{4,5},{5,4},{6,7},{7,6},{8,9},{9,8},{10,11... | collective-permute-start | bytes 98312 | tf_op jit(solution)/shard_map/ppermute | solution.py:370
  5.3 5.2 %collective-permute-start.1 = (bf16[32,512]{1,0:T(8,128)(2,1)S(1)}, bf16[32,512]{1,0:T(8,128)(2,1)S(1)}, u32[]{:S(2)}, u32[]{:S(2)}) collective-permute-start(bf16[32,512]{1,0:T(8,128)(2,1)S(1)} %get-tuple-element.38), channel_id=1, source_target_pairs={{1,2},{3,4},{5,6},{7,8},{9,10},{11,12},{13,14},{15,16},{17,18},{19... | collective-permute-start | bytes 98312 | tf_op jit(solution)/shard_map/ppermute | solution.py:375
  11.1 1.3 %collective-permute-start.2 = (bf16[32,640]{1,0:T(8,128)(2,1)S(1)}, bf16[32,640]{1,0:T(8,128)(2,1)S(1)}, u32[]{:S(2)}, u32[]{:S(2)}) collective-permute-start(bf16[32,640]{1,0:T(8,128)(2,1)S(1)} %mid_update.1.refs_0_), channel_id=1, source_target_pairs={{0,1},{1,0},{2,3},{3,2},{4,5},{5,4},{6,7},{7,6},{8,9},{9,8},{10,11... | collective-permute-start | bytes 122888 | tf_op jit(solution)/shard_map/ppermute | solution.py:370
  13.6 18.5 %all-to-all-start = ((bf16[16,24,512]{2,1,0:T(8,128)(2,1)}), bf16[16,24,512]{2,1,0:T(8,128)(2,1)S(1)}, u32[]{:S(2)}, u32[]{:S(2)}) async-start(bf16[16,24,512]{2,1,0:T(8,128)(2,1)} %bitcast.2.refs_8_), calls=%async_computation | async-start | bytes 786432 | tf_op jit(solution)/shard_map/all_to_all | solution.py:464
  28.1 16.3 %collective-permute-start.3 = (bf16[192,640]{1,0:T(8,128)(2,1)}, bf16[192,640]{1,0:T(8,128)(2,1)S(1)}, u32[]{:S(2)}, u32[]{:S(2)}) collective-permute-start(bf16[192,640]{1,0:T(8,128)(2,1)} %get-tuple-element.48), channel_id=1, source_target_pairs={{1,2},{3,4},{5,6},{7,8},{9,10},{11,12},{13,14},{15,16},{17,18},{19... | collective-permute-start | bytes 737288 | tf_op jit(solution)/shard_map/ppermute | solution.py:375
  32.0 13.3 %collective-permute-start.4 = (bf16[128,640]{1,0:T(8,128)(2,1)}, bf16[128,640]{1,0:T(8,128)(2,1)S(1)}, u32[]{:S(2)}, u32[]{:S(2)}) collective-permute-start(bf16[128,640]{1,0:T(8,128)(2,1)} %get-tuple-element.54), channel_id=1, source_target_pairs={{0,1},{1,0},{2,3},{3,2},{4,5},{5,4},{6,7},{7,6},{8,9},{9,8},{10,11... | collective-permute-start | bytes 491528 | tf_op jit(solution)/shard_map/ppermute | solution.py:370
  32.8 17.4 %all-to-all-start.1 = ((bf16[8,24,512]{2,1,0:T(8,128)(2,1)}), bf16[8,24,512]{2,1,0:T(8,128)(2,1)S(1)}, u32[]{:S(2)}, u32[]{:S(2)}) async-start(bf16[8,24,512]{2,1,0:T(8,128)(2,1)} %plane_sum.1.refs_7_), calls=%async_computation.1 | async-start | bytes 393216 | tf_op jit(solution)/shard_map/all_to_all | solution.py:480
  44.4 13.7 %copy-start = (bf16[192,640]{1,0:T(8,128)(2,1)}, bf16[192,640]{1,0:T(8,128)(2,1)S(1)}, u32[]{:S(2)}) copy-start(bf16[192,640]{1,0:T(8,128)(2,1)S(1)} %collective-permute-done.3.refs_5_.refs_4_) | copy-start | bytes 737284
  44.4 13.7 %collective-permute-start.5 = (bf16[32,640]{1,0:T(8,128)(2,1)S(1)}, bf16[32,640]{1,0:T(8,128)(2,1)S(1)}, u32[]{:S(2)}, u32[]{:S(2)}) collective-permute-start(bf16[32,640]{1,0:T(8,128)(2,1)S(1)} %slice_select_fusion), channel_id=1, source_target_pairs={{0,1},{1,0},{2,3},{3,2},{4,5},{5,4},{6,7},{7,6},{8,9},{9,8},{10,11... | collective-permute-start | bytes 122888 | tf_op jit(solution)/shard_map/ppermute | solution.py:370
  45.3 12.8 %copy-start.1 = (bf16[128,640]{1,0:T(8,128)(2,1)}, bf16[128,640]{1,0:T(8,128)(2,1)S(1)}, u32[]{:S(2)}) copy-start(bf16[128,640]{1,0:T(8,128)(2,1)S(1)} %collective-permute-done.4.refs_6_.refs_5_) | copy-start | bytes 491524
  51.5 15.1 %all-to-all-start.2 = ((bf16[16,24,512]{2,1,0:T(8,128)(2,1)}), bf16[16,24,512]{2,1,0:T(8,128)(2,1)S(1)}, u32[]{:S(2)}, u32[]{:S(2)}) async-start(bf16[16,24,512]{2,1,0:T(8,128)(2,1)} %coarse_update.1.refs_12_), calls=%async_computation.2 | async-start | bytes 786432 | tf_op jit(solution)/shard_map/all_to_all | solution.py:503
  66.6 4.3 %collective-permute-start.6 = (bf16[384,512]{1,0:T(8,128)(2,1)S(1)}, bf16[384,512]{1,0:T(8,128)(2,1)S(1)}, u32[]{:S(2)}, u32[]{:S(2)}) collective-permute-start(bf16[384,512]{1,0:T(8,128)(2,1)S(1)} %bitcast.7), channel_id=1, source_target_pairs={{0,1},{1,0},{2,3},{3,2},{4,5},{5,4},{6,7},{7,6},{8,9},{9,8},{10,11... | collective-permute-start | bytes 1179656 | tf_op jit(solution)/shard_map/ppermute | solution.py:370
